TPU v7x, 256 devices: a whole 4x4x8 slice. The times are simulated.
256 devices in a mesh: gx: 8 (over y, x_lo), gy: 8 (over z), wa: 4 (over x_hi, core).
Axes of the slice: x: 4 (x_hi: 2, x_lo: 2; x = x_hi * 2 + x_lo), y: 4, z: 8, core: 2. Of those that a mesh axis runs over, the one named last changes fastest.
Arguments:
- adjoint_init: float32 [5, 64, 128, 512], P(None, 'gx', 'gy', 'wa'), may hold values from -6 to 6
- objective_grad: float32 [5, 64, 128, 512], P(None, 'gx', 'gy', 'wa'), may hold values from -6 to 6
- diag_term: float32 [64, 128, 512], P('gx', 'gy', 'wa'), may hold values from 1.5 to 3
- face_metric: float32 [12, 64, 128, 512], P(None, 'gx', 'gy', 'wa'), may hold values from 0.05 to 0.3
- flux_jacobian: bfloat16 [5, 5, 64, 128, 512], P(None, None, 'gx', 'gy', 'wa'), may hold values from -2 to 2
- wall_coef: float32 [3, 10, 64, 128], P(None, None, 'gx', 'gy'), may hold values from -2 to 2
- ffd_ids: int32 [4, 64, 128], P(None, 'gx', 'gy'), may hold values from 0 to 4095
- ffd_weight: float32 [4, 64, 128], P(None, 'gx', 'gy'), may hold values from 0.1 to 1
Outputs:
- adjoint: float32 [5, 64, 128, 512], P(None, 'gx', 'gy', 'wa')
- shape_grad: float32 [3, 4096], P(None, ('gx', 'gy', 'wa'))
All inputs are finite; a program needn't handle non-finite values.
Results may differ from a plain program's by a relative error of at most 0.0003.
Values sent between devices are 32-bit elements; how exact they have to be, the bound alone decides.
No kernel may reach another device: no remote copies, remote signals or barrier semaphores. Data moves between devices by JAX's collectives and lax.ppermute only.
A program may use at most 192 MiB of HBM per device.

v0:
```python
import jax
import jax.numpy as jnp
from jax import lax
from jax.sharding import PartitionSpec as P

SWEEPS = 4
POINTS = 4096


OMEGA = 0.6
OFFSET_LIST = [
    (1, 1),
    (1, -1),
    (1, 2),
    (1, -2),
    (2, 1),
    (2, -1),
    (2, 2),
    (2, -2),
    (3, 1),
    (3, -1),
    (3, 2),
    (3, -2),
]


def with_halo(block, sides, width):
    for axis, dim in sides:
        count = lax.axis_size(axis)
        forward = [(i, i + 1) for i in range(count - 1)]
        backward = [(target, source) for source, target in forward]
        low = lax.ppermute(
            lax.slice_in_dim(block, block.shape[dim] - width, None, axis=dim), axis, forward
        )
        high = lax.ppermute(lax.slice_in_dim(block, 0, width, axis=dim), axis, backward)
        block = jnp.concatenate([low, block, high], axis=dim)
    return block


def take_shifted(field, dim, step):
    starts = [0, 2, 2, 2]
    starts[dim] = 2 - step
    limits = [field.shape[0]] + [starts[d] + field.shape[d] - 4 for d in (1, 2, 3)]
    return lax.slice(field, starts, limits)


def sweep(padded_psi, padded_coef, diag, rhs, jac):
    total = jnp.zeros(
        (padded_psi.shape[0],) + tuple((s - 4 for s in padded_psi.shape[1:])), jnp.float32
    )
    for index, (dim, step) in enumerate(OFFSET_LIST):
        total = total + take_shifted(padded_coef[index][None] * padded_psi, dim, step)
    centre = padded_psi[:, 2:-2, 2:-2, 2:-2]
    coupled = (jac * total[:, None]).sum(0)
    return centre + OMEGA * (rhs - diag * centre + coupled) / diag


def local(
    adjoint_init,
    objective_grad,
    diag_term,
    face_metric,
    flux_jacobian,
    wall_coef,
    ffd_ids,
    ffd_weight,
):
    fields = adjoint_init.shape[0]
    psi = adjoint_init
    coef_ext = with_halo(face_metric, (("gx", 1), ("gy", 2), ("wa", 3)), 2)
    for sweep_index in range(SWEEPS):
        psi_ext = with_halo(psi, (("gx", 1), ("gy", 2), ("wa", 3)), 2)
        psi = sweep(psi_ext, coef_ext, diag_term[None], objective_grad, flux_jacobian)
    wall_on = (lax.axis_index("wa") == 0).astype(jnp.float32)
    sens = jnp.zeros(wall_coef.shape[:1] + wall_coef.shape[2:], jnp.float32)
    for field in range(fields):
        for layer in range(2):
            sens = sens + wall_coef[:, 2 * field + layer] * psi[field, :, :, layer][None]
    values = ffd_weight[None] * sens[:, None]
    flat = values.reshape(values.shape[0], -1).T
    summed = jax.ops.segment_sum(flat, ffd_ids.reshape(-1), num_segments=POINTS).T * wall_on
    grad = lax.psum_scatter(summed, ("gx", "gy", "wa"), scatter_dimension=1, tiled=True)
    return (psi, grad)


def solution(mesh):
    in_specs = (
        P(None, "gx", "gy", "wa"),
        P(None, "gx", "gy", "wa"),
        P("gx", "gy", "wa"),
        P(None, "gx", "gy", "wa"),
        P(None, None, "gx", "gy", "wa"),
        P(None, None, "gx", "gy"),
        P(None, "gx", "gy"),
        P(None, "gx", "gy"),
    )
    out_specs = (P(None, "gx", "gy", "wa"), P(None, ("gx", "gy", "wa")))
    return jax.shard_map(local, mesh=mesh, in_specs=in_specs, out_specs=out_specs, check_vma=False)
```

profile of v0, /device:TPU:1, one launch (start us, length us, event | category | flops | bytes accessed | tf_op | source)
XLA Modules:
  0.0 1473.4 jit_solution(5379851136659286217)
XLA Ops:
  7.2 1.0 fusion.61
  8.2 3.9 collective-permute-start.6
  12.2 1.1 fusion.52
  13.2 3.2 collective-permute-start
  16.4 1.3 collective-permute-start.1
  17.7 1.3 collective-permute-start.7
  20.1 7.5 collective-permute-done.7
  27.6 3.5 collective-permute-start.8
  31.2 1.3 collective-permute-start.9
  32.8 3.6 collective-permute-done.9
  37.0 3.5 collective-permute-start.2
  40.5 1.3 collective-permute-start.3
  42.6 7.6 collective-permute-start.10
  50.7 1.9 collective-permute-start.11
  52.6 1.3 copy.92
  53.9 3.8 collective-permute-done.11
  57.7 1.4 copy.93
  59.4 2.0 fusion.51
  61.4 3.5 copy.85
  64.8 1.9 collective-permute-start.4
  66.8 1.9 copy.86
  68.7 3.2 collective-permute-start.5
  71.9 2.4 pad_maximum_fusion.2
  74.4 3.6 copy.87
  77.9 2.6 copy.88
  80.6 5.0 pad_maximum_fusion
  87.4 1.0 fusion.39
  89.7 2.9 collective-permute-start.12
  92.6 1.3 collective-permute-start.13
  94.8 4.2 collective-permute-done.13
  99.0 5.3 collective-permute-start.14
  104.3 1.3 collective-permute-start.15
  105.6 5.1 collective-permute-done.15
  111.9 6.0 collective-permute-start.16
  118.3 1.9 collective-permute-start.17
  120.7 4.6 collective-permute-done.17
  125.9 1.9 pad_maximum_fusion.3
  128.0 1.0 fusion.28
  129.3 3.1 collective-permute-start.18
  132.4 1.3 collective-permute-start.19
  133.9 3.7 collective-permute-done.19
  137.6 3.6 collective-permute-start.20
  141.3 1.3 collective-permute-start.21
  142.6 3.9 collective-permute-done.21
  147.6 5.3 collective-permute-start.22
  153.4 1.9 collective-permute-start.23
  155.8 4.6 collective-permute-done.23
  160.9 1.9 pad_maximum_fusion.4
  163.0 1.0 fusion.17
  164.3 2.6 collective-permute-start.24
  166.9 1.3 collective-permute-start.25
  168.3 3.8 collective-permute-done.25
  172.2 4.1 collective-permute-start.26
  176.2 1.3 collective-permute-start.27
  177.6 3.9 collective-permute-done.27
  182.6 5.0 collective-permute-start.28
  188.0 1.9 collective-permute-start.29
  190.6 4.4 collective-permute-done.29
  195.6 1.9 pad_maximum_fusion.5
  197.7 1.0 fusion.6
  199.9 2.8 scatter_custom_fusion
  202.7 1.5 multiply_bitcast_fusion
  204.2 1261.0 %reduce-scatter.2.cloned.1.call-done = f32[3,16]{0,1:T(8,128)} async-done(((f32[3,4096]{0,1:T(8,128)}), f32[3,16]{0,1:T(8,128)}) %reduce-scatter.2.cloned.1.call-update) | async-done | bytes 208 | tf_op jit(solution)/shard_map/reduce_scatter | solution.py:82
  1465.2 1.3 copy.118
  (214 shorter events, 17.0 us)
Async XLA Ops:
  7.2 25.3 %copy-start.5 = (f32[12,8,16,128]{3,2,1,0:T(8,128)S(1)}, f32[12,8,16,128]{3,2,1,0:T(8,128)}, u32[]{:S(2)}) copy-start(f32[12,8,16,128]{3,2,1,0:T(8,128)} %param.11) | copy-start | bytes 2359300
  7.2 1458.1 %reduce-scatter.2.cloned.1.call-start = ((), (), s32[]{:S(2)}) async-start(), calls=%async_computation.1 | async-start | bytes 2105344 | tf_op jit(solution)/shard_map/reduce_scatter | solution.py:82
  8.2 10.8 collective-permute-start.6
  13.2 23.2 %collective-permute-start = (f32[12,2,16,128]{3,2,1,0:T(8,128)S(1)}, f32[12,2,16,128]{3,2,1,0:T(8,128)S(1)}, u32[]{:S(2)}, u32[]{:S(2)}) collective-permute-start(f32[12,2,16,128]{3,2,1,0:T(8,128)S(1)} %get-tuple-element.36), channel_id=1, source_target_pairs={{0,32},{32,64},{64,96},{96,128},{128,160},{160,192},{192,224},{1,3... | collective-permute-start | bytes 589832 | tf_op jit(solution)/shard_map/ppermute | solution.py:32
  16.4 20.2 %collective-permute-start.1 = (f32[12,2,16,128]{3,2,1,0:T(8,128)S(1)}, f32[12,2,16,128]{3,2,1,0:T(8,128)S(1)}, u32[]{:S(2)}, u32[]{:S(2)}) collective-permute-start(f32[12,2,16,128]{3,2,1,0:T(8,128)S(1)} %get-tuple-element.37), channel_id=1, source_target_pairs={{32,0},{64,32},{96,64},{128,96},{160,128},{192,160},{224,192},{33,... | collective-permute-start | bytes 589832 | tf_op jit(solution)/shard_map/ppermute | solution.py:35
  17.7 9.8 collective-permute-start.7
  27.6 9.0 copy-start.3
  27.6 5.1 collective-permute-start.8
  31.2 5.2 collective-permute-start.9
  32.8 4.0 copy-start.48
  37.0 22.1 %collective-permute-start.2 = (f32[12,12,2,128]{3,1,2,0:T(8,128)S(1)}, f32[12,12,2,128]{3,1,2,0:T(8,128)S(1)}, u32[]{:S(2)}, u32[]{:S(2)}) collective-permute-start(f32[12,12,2,128]{3,1,2,0:T(8,128)S(1)} %get-tuple-element.34), channel_id=1, source_target_pairs={{0,4},{4,8},{8,12},{12,16},{16,20},{20,24},{24,28},{1,5},{5,9},{9,... | collective-permute-start | bytes 442376 | tf_op jit(solution)/shard_map/ppermute | solution.py:32
  40.5 18.6 %collective-permute-start.3 = (f32[12,12,2,128]{3,1,2,0:T(8,128)S(1)}, f32[12,12,2,128]{3,1,2,0:T(8,128)S(1)}, u32[]{:S(2)}, u32[]{:S(2)}) collective-permute-start(f32[12,12,2,128]{3,1,2,0:T(8,128)S(1)} %get-tuple-element.35), channel_id=1, source_target_pairs={{4,0},{8,4},{12,8},{16,12},{20,16},{24,20},{28,24},{5,1},{9,5},{13... | collective-permute-start | bytes 442376 | tf_op jit(solution)/shard_map/ppermute | solution.py:35
  42.6 10.0 collective-permute-start.10
  50.7 7.0 collective-permute-start.11
  64.8 9.5 collective-permute-start.4
  68.7 9.3 collective-permute-start.5
  89.7 5.0 collective-permute-start.12
  92.6 6.4 collective-permute-start.13
  94.8 16.4 %copy-start.44 = (f32[5,2,16,128]{3,2,1,0:T(8,128)}, f32[5,2,16,128]{3,2,1,0:T(8,128)S(1)}, u32[]{:S(2)}) copy-start(f32[5,2,16,128]{3,2,1,0:T(8,128)S(1)} %collective-permute-done.12) | copy-start | bytes 245764
  99.0 12.2 copy-start.46
  99.0 6.6 collective-permute-start.14
  104.3 6.5 collective-permute-start.15
  105.6 5.5 copy-start.52
  111.9 8.4 collective-permute-start.16
  118.3 7.0 collective-permute-start.17
  125.9 2.0 copy-start.15
  125.9 2.0 copy-start.19
  125.9 2.0 copy-start.23
  125.9 2.0 copy-start.27
  125.9 2.0 copy-start.31
  125.9 2.0 copy-start.35
  129.3 4.6 collective-permute-start.18
  132.4 5.2 collective-permute-start.19
  133.9 13.0 copy-start.45
  137.6 9.3 copy-start.47
  137.6 5.0 collective-permute-start.20
  141.3 5.2 collective-permute-start.21
  142.6 4.3 copy-start.53
  147.6 7.7 collective-permute-start.22
  153.4 7.0 collective-permute-start.23
  160.9 2.0 copy-start.16
  160.9 2.0 copy-start.20
  160.9 2.0 copy-start.24
  160.9 2.0 copy-start.28
  160.9 2.0 copy-start.32
  160.9 2.0 copy-start.36
  164.3 4.0 collective-permute-start.24
  166.9 5.3 collective-permute-start.25
  168.3 13.6 copy-start.42
  172.1 9.8 copy-start.43
  172.2 5.4 collective-permute-start.26
  176.2 5.2 collective-permute-start.27
  177.6 4.4 copy-start.50
  181.6 8.4 copy-start.57
  181.6 8.4 copy-start.58
  182.6 7.6 collective-permute-start.28
  188.0 7.0 collective-permute-start.29
  195.6 2.0 copy-start.17
  195.6 2.0 copy-start.21
  195.6 2.0 copy-start.25
  195.6 2.0 copy-start.29
  195.6 2.0 copy-start.33
  195.6 2.0 copy-start.37
  199.0 3.7 copy-start.2
  (26 other events, 35.6 us)
Sparse Core Ops, SparseCore 0:
  204.3 1260.8 reduce-scatter.1
where the time goes:
time: 1480 us; the launch traced here: 1470 us
  waiting for transfers between devices  1320 us (89%)
  starting transfers between devices  85.4 us (6%)
  local copies, waits for them, and re-layouts  33.4 us (2%)
  other arithmetic  23.7 us (2%)
  between operations  15.5 us (1%)
    reduce_scatter x1, waiting for transfers between devices, local(): lax.psum_scatter(summed, ('gx', 'gy', 'wa'), scatter_dimension=1, tiled=T...  1260 us
    ppermute x15, starting transfers between devices, with_halo(): lax.ppermute(lax.slice_in_dim(block, block.shape[dim] - width, None, axis...  61.5 us
    ppermute x15, waiting for transfers between devices, with_halo(): lax.ppermute(lax.slice_in_dim(block, 0, width, axis=dim), axis, backward)  53.2 us
  transfers between devices with their start and end apart: 31, of which 16 were waited for; matrix products, arithmetic and copies ran while one was open for 1% of the time, Pallas kernels for 0%

commit v1 on v0

v1 whole, which is shorter than its diff:
```python
import jax
import jax.numpy as jnp
from jax import lax
from jax.sharding import PartitionSpec as P

SWEEPS = 4
POINTS = 4096
OMEGA = 0.6
AXES = ("gx", "gy", "wa")


def pairs(count, odd):
    table = {}
    for i in range(0, count, 2):
        a, b = (i + odd) % count, (i + 1 + odd) % count
        table[a], table[b] = b, a
    return sorted(table.items())


def send(high, low, axis):
    count = lax.axis_size(axis)
    even = lax.axis_index(axis) % 2 == 0
    first = lax.ppermute(jnp.where(even, high, low), axis, pairs(count, 0))
    second = lax.ppermute(jnp.where(even, low, high), axis, pairs(count, 1))
    return first, second


def receive(first, second, axis):
    count = lax.axis_size(axis)
    index = lax.axis_index(axis)
    even = index % 2 == 0
    below = jnp.where(even, second, first) * (index > 0).astype(jnp.float32)
    above = jnp.where(even, first, second) * (index < count - 1).astype(jnp.float32)
    return below, above


def part(a, dim, start, stop):
    return lax.slice_in_dim(a, start, stop, axis=dim)


def padded(a, dim, before, after):
    widths = [(0, 0)] * a.ndim
    widths[dim] = (before, after)
    return jnp.pad(a, widths)


def sweep(psi, metric, diag, rhs, jac):
    flights = []
    for axis, dim, base in (("wa", 3, 8), ("gy", 2, 4), ("gx", 1, 0)):
        n = psi.shape[dim]
        def term(o, start, stop):
            return part(metric[base + o][None], dim, start, stop) * part(psi, dim, start, stop)
        high = jnp.concatenate([term(0, n - 1, n) + term(2, n - 2, n - 1), term(2, n - 1, n)], axis=dim)
        low = jnp.concatenate([term(3, 0, 1), term(1, 0, 1) + term(3, 1, 2)], axis=dim)
        flights.append(send(high, low, axis))
    z = jnp.zeros_like(psi)
    for dim, base in ((1, 0), (2, 4), (3, 8)):
        n = psi.shape[dim]
        for o, step in enumerate((1, -1, 2, -2)):
            p = metric[base + o][None] * psi
            if step > 0:
                z = z + padded(part(p, dim, 0, n - step), dim, step, 0)
            else:
                z = z + padded(part(p, dim, -step, n), dim, 0, -step)
    for (first, second), (axis, dim) in zip(flights, (("wa", 3), ("gy", 2), ("gx", 1))):
        n = psi.shape[dim]
        below, above = receive(first, second, axis)
        z = z + padded(below, dim, 0, n - 2) + padded(above, dim, n - 2, 0)
    coupled = (jac * z[:, None]).sum(0)
    return psi + OMEGA * (rhs - diag * psi + coupled) / diag


def local(adjoint_init, objective_grad, diag_term, face_metric, flux_jacobian, wall_coef, ffd_ids, ffd_weight):
    psi = adjoint_init
    for _ in range(SWEEPS):
        psi = sweep(psi, face_metric, diag_term[None], objective_grad, flux_jacobian)
    wall_on = (lax.axis_index("wa") == 0).astype(jnp.float32)
    sens = jnp.zeros(wall_coef.shape[:1] + wall_coef.shape[2:], jnp.float32)
    for field in range(psi.shape[0]):
        for layer in range(2):
            sens = sens + wall_coef[:, 2 * field + layer] * psi[field, :, :, layer][None]
    values = ffd_weight[None] * sens[:, None] * wall_on
    flat = values.reshape(values.shape[0], -1).T
    summed = jax.ops.segment_sum(flat, ffd_ids.reshape(-1), num_segments=POINTS)
    owners = lax.axis_size(AXES)
    slots = jnp.swapaxes(summed.reshape(owners, POINTS // owners, -1), 1, 2).reshape(owners, 1, -1)
    got = lax.all_to_all(slots, AXES, 0, 0)
    return psi, got.sum((0, 1)).reshape(wall_coef.shape[0], -1)


def solution(mesh):
    in_specs = (
        P(None, "gx", "gy", "wa"),
        P(None, "gx", "gy", "wa"),
        P("gx", "gy", "wa"),
        P(None, "gx", "gy", "wa"),
        P(None, None, "gx", "gy", "wa"),
        P(None, None, "gx", "gy"),
        P(None, "gx", "gy"),
        P(None, "gx", "gy"),
    )
    out_specs = (P(None, "gx", "gy", "wa"), P(None, AXES))
    return jax.shard_map(local, mesh=mesh, in_specs=in_specs, out_specs=out_specs, check_vma=False)
```

time: 1480 us -> 112 us (0.08)
  waiting for transfers between devices: 1320 us -> 24.4 us
  starting transfers between devices: 85.4 us -> 34.5 us
  local copies, waits for them, and re-layouts: 33.4 us -> 8.84 us
  blocking collectives: 0 us -> 23.5 us
    reduce_scatter x1 -> x0, waiting for transfers between devices: 1260 us -> none  [local(): lax.psum_scatter(summed, ('gx', 'gy', 'wa'), scatter_dimension=1, tiled=T...]
    ppermute x30 -> x24, starting transfers between devices: 85.3 us -> 34.5 us  [the longest x12 31.9 us: send(): second = lax.ppermute(jnp.where(even, low, high), axis, pairs(count, 1))]
    ppermute x30 -> x24, waiting for transfers between devices: 54.5 us -> 24.4 us  [the longest x12 16.1 us: send(): second = lax.ppermute(jnp.where(even, low, high), axis, pairs(count, 1))]
    all_to_all x0 -> x1, blocking collectives: none -> 23.5 us  [local(): got = lax.all_to_all(slots, AXES, 0, 0)]
  transfers between devices with their start and end apart: 31 -> 24, of which waited for: 16 -> 10; matrix products, arithmetic and copies ran while one was open for 1% -> 8% of each run, Pallas kernels for 0% -> 0%
where the time goes in v1:
time: 112 us
  starting transfers between devices  34.5 us (31%)
  waiting for transfers between devices  24.4 us (22%)
  blocking collectives  23.5 us (21%)
  other arithmetic  19.1 us (17%)
  local copies, waits for them, and re-layouts  8.84 us (8%)
  between operations  1.43 us (1%)
    ppermute x12, starting transfers between devices, send(): second = lax.ppermute(jnp.where(even, low, high), axis, pairs(count, 1))  31.9 us
    all_to_all x1, blocking collectives, local(): got = lax.all_to_all(slots, AXES, 0, 0)  23.5 us
    ppermute x12, waiting for transfers between devices, send(): second = lax.ppermute(jnp.where(even, low, high), axis, pairs(count, 1))  16.1 us
    ppermute x12, waiting for transfers between devices, send(): first = lax.ppermute(jnp.where(even, high, low), axis, pairs(count, 0))  8.29 us
    mul x24, other arithmetic, sweep(): p = metric[base + o][None] * psi  4.4 us
    mul x12, other arithmetic, receive(): below = jnp.where(even, second, first) * (index > 0).astype(jnp.float32)  3.35 us
    select_n x12, other arithmetic, send(): second = lax.ppermute(jnp.where(even, low, high), axis, pairs(count, 1))  2.81 us
    scatter-add x1, other arithmetic, local(): summed = jax.ops.segment_sum(flat, ffd_ids.reshape(-1), num_segments=POINTS)  2.77 us
  transfers between devices with their start and end apart: 24, of which 10 were waited for; matrix products, arithmetic and copies ran while one was open for 8% of the time, Pallas kernels for 0%

profile of v1, /device:TPU:1, one launch (start us, length us, event | category | flops | bytes accessed | tf_op | source)
XLA Modules:
  0.0 111.7 jit_solution(653316459751180453)
XLA Ops:
  0.7 1.2 %fusion.34 = (f32[1,8,16,1]{3,2,1,0:T(8,128)S(1)}, f32[1,8,16,1]{3,2,1,0:T(8,128)S(1)}, f32[1,8,16,1]{3,2,1,0:T(8,128)S(1)}, f32[1,8,16,1]{3,2,1,0:T(8,128)S(1)}...) fusion(f32[12,8,16,128]{3,2,1,0:T(8,128)} %param.11), kind=kLoop, calls=%fused_computation.237 | loop fusion | bytes 6144 | tf_op jit(solution)/shard_map/slice | solution.py:38
  2.5 0.4 slice_multiply_fusion.45
  3.0 1.1 broadcast_select_fusion.7
  4.1 4.1 %collective-permute-start = (f32[5,8,16,2]{3,2,1,0:T(8,128)}, f32[5,8,16,2]{3,2,1,0:T(8,128)}, u32[]{:S(2)}, u32[]{:S(2)}) collective-permute-start(f32[5,8,16,2]{3,2,1,0:T(8,128)} %get-tuple-element.22), channel_id=1, source_target_pairs={{0,3},{1,2},{2,1},{3,0},{4,7},{5,6},{6,5},{7,4},{8,11},{9,10},{10,... | collective-permute-start | bytes 15368 | tf_op jit(solution)/shard_map/ppermute | solution.py:24
  8.4 0.6 copy.436
  9.0 5.6 %collective-permute-start.2 = (f32[5,8,2,128]{3,1,2,0:T(8,128)}, f32[5,8,2,128]{3,1,2,0:T(8,128)}, u32[]{:S(2)}, u32[]{:S(2)}) collective-permute-start(f32[5,8,2,128]{3,1,2,0:T(8,128)} %copy.436), channel_id=1, source_target_pairs={{0,28},{4,8},{8,4},{12,16},{16,12},{20,24},{24,20},{28,0},{1,29},{... | collective-permute-start | bytes 122888 | tf_op jit(solution)/shard_map/ppermute | solution.py:24
  14.6 0.6 copy.437
  15.3 0.6 fusion.21
  15.9 2.8 %collective-permute-start.4 = (f32[5,2,16,128]{3,2,1,0:T(8,128)}, f32[5,2,16,128]{3,2,1,0:T(8,128)}, u32[]{:S(2)}, u32[]{:S(2)}) collective-permute-start(f32[5,2,16,128]{3,2,1,0:T(8,128)} %get-tuple-element.172), channel_id=1, source_target_pairs={{0,224},{32,64},{64,32},{96,128},{128,96},{160,192},{192,160},{224... | collective-permute-start | bytes 245768 | tf_op jit(solution)/shard_map/ppermute | solution.py:24
  19.3 0.9 slice_multiply_fusion.31
  20.2 0.9 slice_multiply_fusion.53
  21.1 0.8 slice_multiply_fusion.61
  21.9 0.7 mul.1382
  22.6 0.8 reshape.74
  23.5 1.2 %select_multiply_fusion.7 = (f32[5,8,16,2]{3,2,1,0:T(8,128)S(1)}, f32[5,8,16,2]{3,2,1,0:T(8,128)S(1)}) fusion(f32[5,8,16,2]{3,2,1,0:T(8,128)} %collective-permute-done, f32[5,8,16,2]{3,2,1,0:T(8,128)} %collective-permute-done.1, f32[]{:T(128)S(6)} %convert_element_type.136, pred[]{:T(512)S(6)} %eq.58, f32[]{:T(128)S(6)} %convert_element_type.137), kind=kLoop, calls=%fused_computation.78 | loop fusion | flops 5120 | bytes 20489 | tf_op jit(solution)/shard_map/mul | solution.py:32
  24.8 0.8 select_multiply_fusion.23
  25.6 1.2 %collective-permute-done.5 = f32[5,2,16,128]{3,2,1,0:T(8,128)S(1)} collective-permute-done((f32[5,2,16,128]{3,2,1,0:T(8,128)S(1)}, f32[5,2,16,128]{3,2,1,0:T(8,128)S(1)}, u32[]{:S(2)}, u32[]{:S(2)}) %collective-permute-start.5) | collective-permute-done | bytes 81952 | tf_op jit(solution)/shard_map/ppermute | solution.py:23
  26.8 0.9 select_multiply_fusion.15
  27.8 0.6 pad_add_fusion.3
  28.3 0.6 copy-done.1
  28.9 0.2 fusion
  29.1 0.8 copy-done.2
  30.0 0.4 slice_multiply_fusion.43
  30.5 0.2 slice_multiply_fusion.25
  30.7 0.2 slice_multiply_fusion.23
  31.1 0.2 broadcast_select_fusion.5
  31.3 3.9 %collective-permute-start.6 = (f32[5,8,16,2]{3,2,1,0:T(8,128)S(1)}, f32[5,8,16,2]{3,2,1,0:T(8,128)S(1)}, u32[]{:S(2)}, u32[]{:S(2)}) collective-permute-start(f32[5,8,16,2]{3,2,1,0:T(8,128)S(1)} %get-tuple-element.20), channel_id=1, source_target_pairs={{0,3},{1,2},{2,1},{3,0},{4,7},{5,6},{6,5},{7,4},{8,11},{9,10},{10,... | collective-permute-start | bytes 15368 | tf_op jit(solution)/shard_map/ppermute | solution.py:24
  35.3 1.8 %collective-permute-start.8 = (f32[5,8,2,128]{3,1,2,0:T(8,128)S(1)}, f32[5,8,2,128]{3,1,2,0:T(8,128)S(1)}, u32[]{:S(2)}, u32[]{:S(2)}) collective-permute-start(f32[5,8,2,128]{3,1,2,0:T(8,128)S(1)} %copy.442), channel_id=1, source_target_pairs={{0,28},{4,8},{8,4},{12,16},{16,12},{20,24},{24,20},{28,0},{1,29},{... | collective-permute-start | bytes 122888 | tf_op jit(solution)/shard_map/ppermute | solution.py:24
  37.1 0.7 collective-permute-start.9
  38.0 4.9 %collective-permute-done.6 = f32[5,8,16,2]{3,2,1,0:T(8,128)S(1)} collective-permute-done((f32[5,8,16,2]{3,2,1,0:T(8,128)S(1)}, f32[5,8,16,2]{3,2,1,0:T(8,128)S(1)}, u32[]{:S(2)}, u32[]{:S(2)}) %collective-permute-start.6) | collective-permute-done | bytes 5152 | tf_op jit(solution)/shard_map/ppermute | solution.py:24
  43.0 0.7 collective-permute-done.10
  43.7 2.5 %collective-permute-done.11 = f32[5,2,16,128]{3,2,1,0:T(8,128)S(1)} collective-permute-done((f32[5,2,16,128]{3,2,1,0:T(8,128)S(1)}, f32[5,2,16,128]{3,2,1,0:T(8,128)S(1)}, u32[]{:S(2)}, u32[]{:S(2)}) %collective-permute-start.11) | collective-permute-done | bytes 81952 | tf_op jit(solution)/shard_map/ppermute | solution.py:23
  46.2 0.5 pad_add_fusion.2
  46.7 0.2 fusion.1
  47.0 0.4 slice_multiply_fusion.41
  47.5 0.2 slice_multiply_fusion.15
  48.1 0.2 broadcast_select_fusion.3
  48.3 4.6 %collective-permute-start.12 = (f32[5,8,16,2]{3,2,1,0:T(8,128)S(1)}, f32[5,8,16,2]{3,2,1,0:T(8,128)S(1)}, u32[]{:S(2)}, u32[]{:S(2)}) collective-permute-start(f32[5,8,16,2]{3,2,1,0:T(8,128)S(1)} %get-tuple-element.18), channel_id=1, source_target_pairs={{0,3},{1,2},{2,1},{3,0},{4,7},{5,6},{6,5},{7,4},{8,11},{9,10},{10,... | collective-permute-start | bytes 15368 | tf_op jit(solution)/shard_map/ppermute | solution.py:24
  53.0 1.8 %collective-permute-start.14 = (f32[5,8,2,128]{3,1,2,0:T(8,128)S(1)}, f32[5,8,2,128]{3,1,2,0:T(8,128)S(1)}, u32[]{:S(2)}, u32[]{:S(2)}) collective-permute-start(f32[5,8,2,128]{3,1,2,0:T(8,128)S(1)} %copy.448), channel_id=1, source_target_pairs={{0,28},{4,8},{8,4},{12,16},{16,12},{20,24},{24,20},{28,0},{1,29},{... | collective-permute-start | bytes 122888 | tf_op jit(solution)/shard_map/ppermute | solution.py:24
  54.8 0.7 collective-permute-start.15
  55.5 0.4 collective-permute-start.16
  55.9 4.7 %collective-permute-done.12 = f32[5,8,16,2]{3,2,1,0:T(8,128)S(1)} collective-permute-done((f32[5,8,16,2]{3,2,1,0:T(8,128)S(1)}, f32[5,8,16,2]{3,2,1,0:T(8,128)S(1)}, u32[]{:S(2)}, u32[]{:S(2)}) %collective-permute-start.12) | collective-permute-done | bytes 5152 | tf_op jit(solution)/shard_map/ppermute | solution.py:24
  60.7 0.6 collective-permute-done.16
  61.3 2.6 %collective-permute-done.17 = f32[5,2,16,128]{3,2,1,0:T(8,128)S(1)} collective-permute-done((f32[5,2,16,128]{3,2,1,0:T(8,128)S(1)}, f32[5,2,16,128]{3,2,1,0:T(8,128)S(1)}, u32[]{:S(2)}, u32[]{:S(2)}) %collective-permute-start.17) | collective-permute-done | bytes 81952 | tf_op jit(solution)/shard_map/ppermute | solution.py:23
  63.9 0.5 pad_add_fusion.1
  64.4 0.2 fusion.2
  64.7 0.4 slice_multiply_fusion.39
  65.8 0.2 broadcast_select_fusion.1
  66.0 4.4 %collective-permute-start.18 = (f32[5,8,16,2]{3,2,1,0:T(8,128)S(1)}, f32[5,8,16,2]{3,2,1,0:T(8,128)S(1)}, u32[]{:S(2)}, u32[]{:S(2)}) collective-permute-start(f32[5,8,16,2]{3,2,1,0:T(8,128)S(1)} %get-tuple-element.16), channel_id=1, source_target_pairs={{0,3},{1,2},{2,1},{3,0},{4,7},{5,6},{6,5},{7,4},{8,11},{9,10},{10,... | collective-permute-start | bytes 15368 | tf_op jit(solution)/shard_map/ppermute | solution.py:24
  70.5 2.4 %collective-permute-start.20 = (f32[5,8,2,128]{3,1,2,0:T(8,128)S(1)}, f32[5,8,2,128]{3,1,2,0:T(8,128)S(1)}, u32[]{:S(2)}, u32[]{:S(2)}) collective-permute-start(f32[5,8,2,128]{3,1,2,0:T(8,128)S(1)} %copy.454), channel_id=1, source_target_pairs={{0,28},{4,8},{8,4},{12,16},{16,12},{20,24},{24,20},{28,0},{1,29},{... | collective-permute-start | bytes 122888 | tf_op jit(solution)/shard_map/ppermute | solution.py:24
  72.9 0.7 collective-permute-start.21
  73.8 4.2 %collective-permute-done.18 = f32[5,8,16,2]{3,2,1,0:T(8,128)S(1)} collective-permute-done((f32[5,8,16,2]{3,2,1,0:T(8,128)S(1)}, f32[5,8,16,2]{3,2,1,0:T(8,128)S(1)}, u32[]{:S(2)}, u32[]{:S(2)}) %collective-permute-start.18) | collective-permute-done | bytes 5152 | tf_op jit(solution)/shard_map/ppermute | solution.py:24
  78.0 0.3 collective-permute-start.23
  78.4 1.1 collective-permute-done.22
  79.5 2.1 %collective-permute-done.23 = f32[5,2,16,128]{3,2,1,0:T(8,128)S(1)} collective-permute-done((f32[5,2,16,128]{3,2,1,0:T(8,128)S(1)}, f32[5,2,16,128]{3,2,1,0:T(8,128)S(1)}, u32[]{:S(2)}, u32[]{:S(2)}) %collective-permute-start.23) | collective-permute-done | bytes 81952 | tf_op jit(solution)/shard_map/ppermute | solution.py:23
  81.6 0.5 pad_add_fusion
  82.1 0.2 fusion.3
  82.4 0.4 slice_reduce_fusion.9
  82.8 0.2 copy-done.11
  83.3 2.8 %scatter_custom_fusion = f32[4096,3]{1,0:T(8,128)S(1)} fusion(s32[512]{0:T(512)S(1)} %reshape.74, f32[]{:T(128)} %constant.76.clone.1, f32[3,512]{0,1:T(8,128)S(1)} %fusion.13), kind=kCustom, calls=%fused_computation.9 | custom fusion | flops 1536 | bytes 311300 | tf_op jit(solution)/shard_map/scatter-add | solution.py:84
  86.1 1.1 copy.461
  87.2 23.5 %all_to_all.5 = f32[256,1,48]{2,1,0:T(1,128)S(1)} all-to-all(f32[256,1,48]{2,1,0:T(1,128)S(1)} %copy.462), channel_id=1, replica_groups=mesh['gx'=8,'gy'=8,'wa'=4] {'gx','gy','wa'}, dimensions={0} | all-to-all | bytes 98304 | tf_op jit(solution)/shard_map/all_to_all | solution.py:87
  110.7 0.3 reduce_sum.49
  111.0 0.7 reshape.71
  (122 shorter events, 4.6 us)
Async XLA Ops:
  0.6 1.9 %copy-start = (f32[5,8,16,128]{3,2,1,0:T(8,128)S(1)}, f32[5,8,16,128]{3,2,1,0:T(8,128)}, u32[]{:S(2)}) copy-start(f32[5,8,16,128]{3,2,1,0:T(8,128)} %param.8) | copy-start | bytes 983044
  3.0 5.2 %copy-start.4 = (f32[12,8,16,128]{3,2,1,0:T(8,128)S(1)}, f32[12,8,16,128]{3,2,1,0:T(8,128)}, u32[]{:S(2)}) copy-start(f32[12,8,16,128]{3,2,1,0:T(8,128)} %param.11) | copy-start | bytes 2359300
  4.1 19.3 %collective-permute-start = (f32[5,8,16,2]{3,2,1,0:T(8,128)}, f32[5,8,16,2]{3,2,1,0:T(8,128)}, u32[]{:S(2)}, u32[]{:S(2)}) collective-permute-start(f32[5,8,16,2]{3,2,1,0:T(8,128)} %get-tuple-element.22), channel_id=1, source_target_pairs={{0,3},{1,2},{2,1},{3,0},{4,7},{5,6},{6,5},{7,4},{8,11},{9,10},{10,... | collective-permute-start | bytes 15368 | tf_op jit(solution)/shard_map/ppermute | solution.py:24
  8.2 15.3 %collective-permute-start.1 = (f32[5,8,16,2]{3,2,1,0:T(8,128)}, f32[5,8,16,2]{3,2,1,0:T(8,128)}, u32[]{:S(2)}, u32[]{:S(2)}) collective-permute-start(f32[5,8,16,2]{3,2,1,0:T(8,128)} %get-tuple-element.23), channel_id=1, source_target_pairs={{0,1},{1,0},{2,3},{3,2},{4,5},{5,4},{6,7},{7,6},{8,9},{9,8},{10,11... | collective-permute-start | bytes 15368 | tf_op jit(solution)/shard_map/ppermute | solution.py:23
  9.0 15.7 %collective-permute-start.2 = (f32[5,8,2,128]{3,1,2,0:T(8,128)}, f32[5,8,2,128]{3,1,2,0:T(8,128)}, u32[]{:S(2)}, u32[]{:S(2)}) collective-permute-start(f32[5,8,2,128]{3,1,2,0:T(8,128)} %copy.436), channel_id=1, source_target_pairs={{0,28},{4,8},{8,4},{12,16},{16,12},{20,24},{24,20},{28,0},{1,29},{... | collective-permute-start | bytes 122888 | tf_op jit(solution)/shard_map/ppermute | solution.py:24
  15.2 9.5 %collective-permute-start.3 = (f32[5,8,2,128]{3,1,2,0:T(8,128)}, f32[5,8,2,128]{3,1,2,0:T(8,128)}, u32[]{:S(2)}, u32[]{:S(2)}) collective-permute-start(f32[5,8,2,128]{3,1,2,0:T(8,128)} %copy.437), channel_id=1, source_target_pairs={{0,4},{4,0},{8,12},{12,8},{16,20},{20,16},{24,28},{28,24},{1,5},{5... | collective-permute-start | bytes 122888 | tf_op jit(solution)/shard_map/ppermute | solution.py:23
  15.9 9.7 %collective-permute-start.4 = (f32[5,2,16,128]{3,2,1,0:T(8,128)}, f32[5,2,16,128]{3,2,1,0:T(8,128)}, u32[]{:S(2)}, u32[]{:S(2)}) collective-permute-start(f32[5,2,16,128]{3,2,1,0:T(8,128)} %get-tuple-element.172), channel_id=1, source_target_pairs={{0,224},{32,64},{64,32},{96,128},{128,96},{160,192},{192,160},{224... | collective-permute-start | bytes 245768 | tf_op jit(solution)/shard_map/ppermute | solution.py:24
  19.3 2.6 %copy-start.12 = (f32[4,8,16]{2,1,0:T(8,128)S(1)}, f32[4,8,16]{2,1,0:T(8,128)}, u32[]{:S(2)}) copy-start(f32[4,8,16]{2,1,0:T(8,128)} %param.15) | copy-start | bytes 6148
  23.3 4.3 %copy-start.5 = (f32[5,8,16,126]{3,2,1,0:T(8,128)S(1)}, f32[5,8,16,126]{3,2,1,0:T(8,128)}, u32[]{:S(2)}) copy-start(f32[5,8,16,126]{3,2,1,0:T(8,128)} %get-tuple-element.145) | copy-start | bytes 967684
  23.3 4.3 %copy-start.6 = (f32[5,7,16,128]{3,2,1,0:T(8,128)S(1)}, f32[5,7,16,128]{3,2,1,0:T(8,128)}, u32[]{:S(2)}) copy-start(f32[5,7,16,128]{3,2,1,0:T(8,128)} %get-tuple-element.134) | copy-start | bytes 860164
  23.4 4.3 %copy-start.7 = (f32[5,7,16,128]{3,2,1,0:T(8,128)S(1)}, f32[5,7,16,128]{3,2,1,0:T(8,128)}, u32[]{:S(2)}) copy-start(f32[5,7,16,128]{3,2,1,0:T(8,128)} %get-tuple-element.135) | copy-start | bytes 860164
  23.4 4.3 %copy-start.9 = (f32[5,6,16,128]{3,2,1,0:T(8,128)S(1)}, f32[5,6,16,128]{3,2,1,0:T(8,128)}, u32[]{:S(2)}) copy-start(f32[5,6,16,128]{3,2,1,0:T(8,128)} %get-tuple-element.136) | copy-start | bytes 737284
  23.4 4.3 %copy-start.10 = (f32[5,6,16,128]{3,2,1,0:T(8,128)S(1)}, f32[5,6,16,128]{3,2,1,0:T(8,128)}, u32[]{:S(2)}) copy-start(f32[5,6,16,128]{3,2,1,0:T(8,128)} %get-tuple-element.137) | copy-start | bytes 737284
  23.4 3.4 %collective-permute-start.5 = (f32[5,2,16,128]{3,2,1,0:T(8,128)S(1)}, f32[5,2,16,128]{3,2,1,0:T(8,128)S(1)}, u32[]{:S(2)}, u32[]{:S(2)}) collective-permute-start(f32[5,2,16,128]{3,2,1,0:T(8,128)S(1)} %get-tuple-element.173), channel_id=1, source_target_pairs={{0,32},{32,0},{64,96},{96,64},{128,160},{160,128},{192,224},{224,1... | collective-permute-start | bytes 245768 | tf_op jit(solution)/shard_map/ppermute | solution.py:23
  27.7 1.1 %copy-start.1 = (bf16[5,5,8,16,128]{4,3,2,1,0:T(8,128)(2,1)S(1)}, bf16[5,5,8,16,128]{4,3,2,1,0:T(8,128)(2,1)}, u32[]{:S(2)}) copy-start(bf16[5,5,8,16,128]{4,3,2,1,0:T(8,128)(2,1)} %param.12) | copy-start | bytes 2457604
  27.7 1.3 %copy-start.8 = (f32[8,16,128]{2,1,0:T(8,128)S(1)}, f32[8,16,128]{2,1,0:T(8,128)}, u32[]{:S(2)}) copy-start(f32[8,16,128]{2,1,0:T(8,128)} %param.10) | copy-start | bytes 196612
  28.9 1.0 copy-start.2
  31.3 11.6 %collective-permute-start.6 = (f32[5,8,16,2]{3,2,1,0:T(8,128)S(1)}, f32[5,8,16,2]{3,2,1,0:T(8,128)S(1)}, u32[]{:S(2)}, u32[]{:S(2)}) collective-permute-start(f32[5,8,16,2]{3,2,1,0:T(8,128)S(1)} %get-tuple-element.20), channel_id=1, source_target_pairs={{0,3},{1,2},{2,1},{3,0},{4,7},{5,6},{6,5},{7,4},{8,11},{9,10},{10,... | collective-permute-start | bytes 15368 | tf_op jit(solution)/shard_map/ppermute | solution.py:24
  35.2 7.6 %collective-permute-start.7 = (f32[5,8,16,2]{3,2,1,0:T(8,128)S(1)}, f32[5,8,16,2]{3,2,1,0:T(8,128)S(1)}, u32[]{:S(2)}, u32[]{:S(2)}) collective-permute-start(f32[5,8,16,2]{3,2,1,0:T(8,128)S(1)} %get-tuple-element.21), channel_id=1, source_target_pairs={{0,1},{1,0},{2,3},{3,2},{4,5},{5,4},{6,7},{7,6},{8,9},{9,8},{10,11... | collective-permute-start | bytes 15368 | tf_op jit(solution)/shard_map/ppermute | solution.py:23
  35.3 7.6 %collective-permute-start.8 = (f32[5,8,2,128]{3,1,2,0:T(8,128)S(1)}, f32[5,8,2,128]{3,1,2,0:T(8,128)S(1)}, u32[]{:S(2)}, u32[]{:S(2)}) collective-permute-start(f32[5,8,2,128]{3,1,2,0:T(8,128)S(1)} %copy.442), channel_id=1, source_target_pairs={{0,28},{4,8},{8,4},{12,16},{16,12},{20,24},{24,20},{28,0},{1,29},{... | collective-permute-start | bytes 122888 | tf_op jit(solution)/shard_map/ppermute | solution.py:24
  37.1 5.8 %collective-permute-start.9 = (f32[5,8,2,128]{3,1,2,0:T(8,128)S(1)}, f32[5,8,2,128]{3,1,2,0:T(8,128)S(1)}, u32[]{:S(2)}, u32[]{:S(2)}) collective-permute-start(f32[5,8,2,128]{3,1,2,0:T(8,128)S(1)} %copy.443), channel_id=1, source_target_pairs={{0,4},{4,0},{8,12},{12,8},{16,20},{20,16},{24,28},{28,24},{1,5},{5... | collective-permute-start | bytes 122888 | tf_op jit(solution)/shard_map/ppermute | solution.py:23
  37.9 5.8 %collective-permute-start.10 = (f32[5,2,16,128]{3,2,1,0:T(8,128)S(1)}, f32[5,2,16,128]{3,2,1,0:T(8,128)S(1)}, u32[]{:S(2)}, u32[]{:S(2)}) collective-permute-start(f32[5,2,16,128]{3,2,1,0:T(8,128)S(1)} %get-tuple-element.168), channel_id=1, source_target_pairs={{0,224},{32,64},{64,32},{96,128},{128,96},{160,192},{192,160},{224... | collective-permute-start | bytes 245768 | tf_op jit(solution)/shard_map/ppermute | solution.py:24
  42.9 3.3 %collective-permute-start.11 = (f32[5,2,16,128]{3,2,1,0:T(8,128)S(1)}, f32[5,2,16,128]{3,2,1,0:T(8,128)S(1)}, u32[]{:S(2)}, u32[]{:S(2)}) collective-permute-start(f32[5,2,16,128]{3,2,1,0:T(8,128)S(1)} %get-tuple-element.169), channel_id=1, source_target_pairs={{0,32},{32,0},{64,96},{96,64},{128,160},{160,128},{192,224},{224,1... | collective-permute-start | bytes 245768 | tf_op jit(solution)/shard_map/ppermute | solution.py:23
  48.3 12.3 %collective-permute-start.12 = (f32[5,8,16,2]{3,2,1,0:T(8,128)S(1)}, f32[5,8,16,2]{3,2,1,0:T(8,128)S(1)}, u32[]{:S(2)}, u32[]{:S(2)}) collective-permute-start(f32[5,8,16,2]{3,2,1,0:T(8,128)S(1)} %get-tuple-element.18), channel_id=1, source_target_pairs={{0,3},{1,2},{2,1},{3,0},{4,7},{5,6},{6,5},{7,4},{8,11},{9,10},{10,... | collective-permute-start | bytes 15368 | tf_op jit(solution)/shard_map/ppermute | solution.py:24
  52.9 7.7 %collective-permute-start.13 = (f32[5,8,16,2]{3,2,1,0:T(8,128)S(1)}, f32[5,8,16,2]{3,2,1,0:T(8,128)S(1)}, u32[]{:S(2)}, u32[]{:S(2)}) collective-permute-start(f32[5,8,16,2]{3,2,1,0:T(8,128)S(1)} %get-tuple-element.19), channel_id=1, source_target_pairs={{0,1},{1,0},{2,3},{3,2},{4,5},{5,4},{6,7},{7,6},{8,9},{9,8},{10,11... | collective-permute-start | bytes 15368 | tf_op jit(solution)/shard_map/ppermute | solution.py:23
  53.0 7.7 %collective-permute-start.14 = (f32[5,8,2,128]{3,1,2,0:T(8,128)S(1)}, f32[5,8,2,128]{3,1,2,0:T(8,128)S(1)}, u32[]{:S(2)}, u32[]{:S(2)}) collective-permute-start(f32[5,8,2,128]{3,1,2,0:T(8,128)S(1)} %copy.448), channel_id=1, source_target_pairs={{0,28},{4,8},{8,4},{12,16},{16,12},{20,24},{24,20},{28,0},{1,29},{... | collective-permute-start | bytes 122888 | tf_op jit(solution)/shard_map/ppermute | solution.py:24
  54.8 5.9 %collective-permute-start.15 = (f32[5,8,2,128]{3,1,2,0:T(8,128)S(1)}, f32[5,8,2,128]{3,1,2,0:T(8,128)S(1)}, u32[]{:S(2)}, u32[]{:S(2)}) collective-permute-start(f32[5,8,2,128]{3,1,2,0:T(8,128)S(1)} %copy.449), channel_id=1, source_target_pairs={{0,4},{4,0},{8,12},{12,8},{16,20},{20,16},{24,28},{28,24},{1,5},{5... | collective-permute-start | bytes 122888 | tf_op jit(solution)/shard_map/ppermute | solution.py:23
  55.5 5.8 %collective-permute-start.16 = (f32[5,2,16,128]{3,2,1,0:T(8,128)S(1)}, f32[5,2,16,128]{3,2,1,0:T(8,128)S(1)}, u32[]{:S(2)}, u32[]{:S(2)}) collective-permute-start(f32[5,2,16,128]{3,2,1,0:T(8,128)S(1)} %get-tuple-element.164), channel_id=1, source_target_pairs={{0,224},{32,64},{64,32},{96,128},{128,96},{160,192},{192,160},{224... | collective-permute-start | bytes 245768 | tf_op jit(solution)/shard_map/ppermute | solution.py:24
  60.6 3.3 %collective-permute-start.17 = (f32[5,2,16,128]{3,2,1,0:T(8,128)S(1)}, f32[5,2,16,128]{3,2,1,0:T(8,128)S(1)}, u32[]{:S(2)}, u32[]{:S(2)}) collective-permute-start(f32[5,2,16,128]{3,2,1,0:T(8,128)S(1)} %get-tuple-element.165), channel_id=1, source_target_pairs={{0,32},{32,0},{64,96},{96,64},{128,160},{160,128},{192,224},{224,1... | collective-permute-start | bytes 245768 | tf_op jit(solution)/shard_map/ppermute | solution.py:23
  66.0 11.9 %collective-permute-start.18 = (f32[5,8,16,2]{3,2,1,0:T(8,128)S(1)}, f32[5,8,16,2]{3,2,1,0:T(8,128)S(1)}, u32[]{:S(2)}, u32[]{:S(2)}) collective-permute-start(f32[5,8,16,2]{3,2,1,0:T(8,128)S(1)} %get-tuple-element.16), channel_id=1, source_target_pairs={{0,3},{1,2},{2,1},{3,0},{4,7},{5,6},{6,5},{7,4},{8,11},{9,10},{10,... | collective-permute-start | bytes 15368 | tf_op jit(solution)/shard_map/ppermute | solution.py:24
  70.4 7.8 %collective-permute-start.19 = (f32[5,8,16,2]{3,2,1,0:T(8,128)S(1)}, f32[5,8,16,2]{3,2,1,0:T(8,128)S(1)}, u32[]{:S(2)}, u32[]{:S(2)}) collective-permute-start(f32[5,8,16,2]{3,2,1,0:T(8,128)S(1)} %get-tuple-element.17), channel_id=1, source_target_pairs={{0,1},{1,0},{2,3},{3,2},{4,5},{5,4},{6,7},{7,6},{8,9},{9,8},{10,11... | collective-permute-start | bytes 15368 | tf_op jit(solution)/shard_map/ppermute | solution.py:23
  70.5 7.7 %collective-permute-start.20 = (f32[5,8,2,128]{3,1,2,0:T(8,128)S(1)}, f32[5,8,2,128]{3,1,2,0:T(8,128)S(1)}, u32[]{:S(2)}, u32[]{:S(2)}) collective-permute-start(f32[5,8,2,128]{3,1,2,0:T(8,128)S(1)} %copy.454), channel_id=1, source_target_pairs={{0,28},{4,8},{8,4},{12,16},{16,12},{20,24},{24,20},{28,0},{1,29},{... | collective-permute-start | bytes 122888 | tf_op jit(solution)/shard_map/ppermute | solution.py:24
  72.9 5.4 %collective-permute-start.21 = (f32[5,8,2,128]{3,1,2,0:T(8,128)S(1)}, f32[5,8,2,128]{3,1,2,0:T(8,128)S(1)}, u32[]{:S(2)}, u32[]{:S(2)}) collective-permute-start(f32[5,8,2,128]{3,1,2,0:T(8,128)S(1)} %copy.455), channel_id=1, source_target_pairs={{0,4},{4,0},{8,12},{12,8},{16,20},{20,16},{24,28},{28,24},{1,5},{5... | collective-permute-start | bytes 122888 | tf_op jit(solution)/shard_map/ppermute | solution.py:23
  73.7 5.8 %collective-permute-start.22 = (f32[5,2,16,128]{3,2,1,0:T(8,128)S(1)}, f32[5,2,16,128]{3,2,1,0:T(8,128)S(1)}, u32[]{:S(2)}, u32[]{:S(2)}) collective-permute-start(f32[5,2,16,128]{3,2,1,0:T(8,128)S(1)} %get-tuple-element.160), channel_id=1, source_target_pairs={{0,224},{32,64},{64,32},{96,128},{128,96},{160,192},{192,160},{224... | collective-permute-start | bytes 245768 | tf_op jit(solution)/shard_map/ppermute | solution.py:24
  78.0 3.6 %collective-permute-start.23 = (f32[5,2,16,128]{3,2,1,0:T(8,128)S(1)}, f32[5,2,16,128]{3,2,1,0:T(8,128)S(1)}, u32[]{:S(2)}, u32[]{:S(2)}) collective-permute-start(f32[5,2,16,128]{3,2,1,0:T(8,128)S(1)} %get-tuple-element.161), channel_id=1, source_target_pairs={{0,32},{32,0},{64,96},{96,64},{128,160},{160,128},{192,224},{224,1... | collective-permute-start | bytes 245768 | tf_op jit(solution)/shard_map/ppermute | solution.py:23
  82.1 0.9 copy-start.11
  82.1 1.0 copy-start.13
  82.4 3.7 %copy-start.3 = (f32[5,8,16,128]{3,2,1,0:T(8,128)}, f32[5,8,16,128]{3,2,1,0:T(8,128)S(1)}, u32[]{:S(2)}) copy-start(f32[5,8,16,128]{3,2,1,0:T(8,128)S(1)} %divide_add_fusion) | copy-start | bytes 983044

commit v2 on v1

v2 whole, which is shorter than its diff:
```python
import jax
import jax.numpy as jnp
from jax import lax
from jax.experimental import pallas as pl
from jax.experimental.pallas import tpu as pltpu
from jax.sharding import PartitionSpec as P

SWEEPS = 4
OMEGA = 0.6
AXES = ("gx", "gy", "wa")
FIELDS, NX, NY, NZ = 5, 8, 16, 128
ROWS = NX * NY
F32 = jnp.float32
VMEM = pl.BlockSpec(memory_space=pltpu.VMEM)


def pairs(count, odd):
    table = {}
    for i in range(0, count, 2):
        a, b = (i + odd) % count, (i + 1 + odd) % count
        table[a], table[b] = b, a
    return sorted(table.items())


def iota(shape, dim):
    return lax.broadcasted_iota(jnp.int32, shape, dim)


def lane_roll(v, shift):
    return pltpu.roll(v, shift % NZ, axis=1) if shift % NZ else v


def row_roll(v, shift):
    return pltpu.roll(v, shift % v.shape[0], axis=0)


def is_even(axis):
    return lax.axis_index(axis) % 2 == 0


def slab(x):
    return slice(NY * x, NY * (x + 1))


def edge_rows(y):
    return pl.ds(y, NX, stride=NY)


def tile_rows(x, t):
    return slice(NY * x + 8 * t, NY * x + 8 * t + 8)


def pack_edges(psi_ref):
    lane = iota((8, NZ), 1)
    edge = (lane < 2) | (lane >= NZ - 2)
    groups = []
    for g in range((FIELDS + 1) // 2):
        total = jnp.zeros((8, NZ), F32)
        for e in range(2 * g, min(2 * g + 2, FIELDS)):
            for x in range(NX):
                for t in range(2):
                    v = jnp.where(edge, psi_ref[e, tile_rows(x, t), :], 0.0)
                    total = total + lane_roll(v, 2 + 64 * (e % 2) + 4 * (2 * x + t))
        groups.append(total)
    return groups


def pack_metric(metric_ref, out_ref):
    lane = iota((8, NZ), 1)
    same = jnp.zeros((8, NZ), F32)
    after = jnp.zeros((8, NZ), F32)
    before = jnp.zeros((8, NZ), F32)
    for x in range(NX):
        for t in range(2):
            j, rows = 4 * (2 * x + t), tile_rows(x, t)
            v = jnp.where(lane >= NZ - 2, metric_ref[10, rows, :], jnp.where(lane < 2, metric_ref[11, rows, :], 0.0))
            same = same + lane_roll(v, 2 + j)
            after = after + lane_roll(jnp.where(lane == NZ - 1, metric_ref[8, rows, :], 0.0), 1 + j)
            before = before + lane_roll(jnp.where(lane == 0, metric_ref[9, rows, :], 0.0), 3 + j)
    for i, v in enumerate((same, after, before)):
        out_ref[8 * i : 8 * i + 8, :] = v + lane_roll(v, 64)


def emit_sends(psi_ref, metric_ref, packed_metric, groups, sends):
    x0, x1, y0, y1, zz = sends
    lane = iota((8, NZ), 1)
    same, after, before = (packed_metric[8 * i : 8 * i + 8, :] for i in range(3))
    for g, p in enumerate(groups):
        v = same * p + after * lane_roll(p, -1) + before * lane_roll(p, 1)
        zz[8 * g : 8 * g + 8, :] = jnp.where(lane % 4 < 2, lane_roll(v, -2), lane_roll(v, 2))
    even = is_even("gy")
    m4, m6a, m6b = metric_ref[4, edge_rows(15), :], metric_ref[6, edge_rows(14), :], metric_ref[6, edge_rows(15), :]
    m5, m7a, m7b = metric_ref[5, edge_rows(0), :], metric_ref[7, edge_rows(0), :], metric_ref[7, edge_rows(1), :]
    for e in range(FIELDS):
        q14, q15 = psi_ref[e, edge_rows(14), :], psi_ref[e, edge_rows(15), :]
        q0, q1 = psi_ref[e, edge_rows(0), :], psi_ref[e, edge_rows(1), :]
        high = (m4 * q15 + m6a * q14, m6b * q15)
        low = (m7a * q0, m5 * q0 + m7b * q1)
        for r in range(2):
            y0[e, r] = jnp.where(even, high[r], low[r])
            y1[e, r] = jnp.where(even, low[r], high[r])
    even = is_even("gx")
    last, near = slab(NX - 1), slab(NX - 2)
    m0, m2a, m2b = metric_ref[0, last, :], metric_ref[2, near, :], metric_ref[2, last, :]
    m1, m3a, m3b = metric_ref[1, slab(0), :], metric_ref[3, slab(0), :], metric_ref[3, slab(1), :]
    for e in range(FIELDS):
        q6, q7, q0, q1 = psi_ref[e, near, :], psi_ref[e, last, :], psi_ref[e, slab(0), :], psi_ref[e, slab(1), :]
        high = (m0 * q7 + m2a * q6, m2b * q7)
        low = (m3a * q0, m1 * q0 + m3b * q1)
        for r in range(2):
            x0[e, r] = jnp.where(even, high[r], low[r])
            x1[e, r] = jnp.where(even, low[r], high[r])


def first_body(psi_ref, metric_ref, x0, x1, y0, y1, zz, packed_metric):
    pack_metric(metric_ref, packed_metric)
    emit_sends(psi_ref, metric_ref, packed_metric, pack_edges(psi_ref), (x0, x1, y0, y1, zz))


def inner_body(psi_ref, metric_ref, z_ref):
    lane, row = iota((NY, NZ), 1), iota((NY, NZ), 0)
    for x in range(NX):
        s = slab(x)
        ms = []
        for o, keep in (
            (4, row < NY - 1), (5, row >= 1), (6, row < NY - 2), (7, row >= 2),
            (8, lane < NZ - 1), (9, lane >= 1), (10, lane < NZ - 2), (11, lane >= 2),
        ):
            ms.append(jnp.where(keep, metric_ref[o, s, :], 0.0))
        for e in range(FIELDS):
            q = psi_ref[e, s, :]
            total = row_roll(ms[0] * q, 1) + row_roll(ms[1] * q, -1)
            total = total + (row_roll(ms[2] * q, 2) + row_roll(ms[3] * q, -2))
            total = total + (lane_roll(ms[4] * q, 1) + lane_roll(ms[5] * q, -1))
            total = total + (lane_roll(ms[6] * q, 2) + lane_roll(ms[7] * q, -2))
            for o, step in enumerate((1, -1, 2, -2)):
                if 0 <= x - step < NX:
                    total = total + metric_ref[o, slab(x - step), :] * psi_ref[e, slab(x - step), :]
            z_ref[e, s, :] = total


def from_sides(axis, first, second):
    index = lax.axis_index(axis)
    even = index % 2 == 0
    below = jnp.where(even, second, first)
    above = jnp.where(even, first, second)
    return jnp.where(index > 0, below, 0.0), jnp.where(index < lax.axis_size(axis) - 1, above, 0.0)


def update(psi_ref, z_ref, received, diag_ref, rhs_ref, jac_ref, new_ref, total_ref):
    x0, x1, y0, y1, z0, z1 = received
    lane8 = iota((8, NZ), 1)
    edge = (lane8 < 2) | (lane8 >= NZ - 2)
    for g in range((FIELDS + 1) // 2):
        rows = slice(8 * g, 8 * g + 8)
        below, above = from_sides("wa", z0[rows, :], z1[rows, :])
        both = jnp.where(lane8 % 4 >= 2, below, above)
        for e in range(2 * g, min(2 * g + 2, FIELDS)):
            for x in range(NX):
                for t in range(2):
                    shift = -(2 + 64 * (e % 2) + 4 * (2 * x + t))
                    total_ref[e, tile_rows(x, t), :] = z_ref[e, tile_rows(x, t), :] + jnp.where(edge, lane_roll(both, shift), 0.0)
    for e in range(FIELDS):
        for r in range(2):
            below, above = from_sides("gx", x0[e, r], x1[e, r])
            total_ref[e, slab(r), :] += below
            total_ref[e, slab(NX - 2 + r), :] += above
        for r in range(2):
            below, above = from_sides("gy", y0[e, r], y1[e, r])
            total_ref[e, edge_rows(r), :] += below
            total_ref[e, edge_rows(NY - 2 + r), :] += above
    for x in range(NX):
        s = slab(x)
        d = diag_ref[s, :]
        scale = OMEGA / d
        zs = [total_ref[e, s, :] for e in range(FIELDS)]
        for f in range(FIELDS):
            c = jac_ref[f, s, :].astype(F32) * zs[0]
            for e in range(1, FIELDS):
                c = c + jac_ref[FIELDS * e + f, s, :].astype(F32) * zs[e]
            q = psi_ref[f, s, :]
            new_ref[f, s, :] = q + (rhs_ref[f, s, :] - d * q + c) * scale


def middle_body(psi_ref, z_ref, r0, r1, r2, r3, r4, r5, diag_ref, rhs_ref, jac_ref, metric_ref, packed_metric,
                new_ref, x0, x1, y0, y1, zz, total_ref):
    update(psi_ref, z_ref, (r0, r1, r2, r3, r4, r5), diag_ref, rhs_ref, jac_ref, new_ref, total_ref)
    emit_sends(new_ref, metric_ref, packed_metric, pack_edges(new_ref), (x0, x1, y0, y1, zz))


def wall_body(coef_ref, ids_ref, weight_ref, coef_out, weight_out, hot_out, low_out):
    def spread(rows, place):
        at = lax.broadcasted_iota(jnp.int32, (rows, 2 * NZ), 1)
        r = lax.broadcasted_iota(jnp.int32, (rows, 2 * NZ), 0)
        return (at % NZ == place(r) + 4 * (at // NZ)).astype(F32)

    def packed(table, chooser):
        v = lax.dot_general(table, chooser, (((0,), (0,)), ((), ())), precision=lax.Precision.HIGHEST,
                            preferred_element_type=F32)
        return v[:8, :NZ] + v[8:, NZ:]

    chooser = spread(4 * NX, lambda r: 64 * (r // 16) + 8 * (r % NX) + 2 + (r // NX) % 2)
    for c in range(3):
        for g in range((FIELDS + 1) // 2):
            count = 4 * NX if g < FIELDS // 2 else 2 * NX
            start = c * 10 * NX + g * 4 * NX
            coef_out[c, 8 * g : 8 * g + 8, :] = packed(coef_ref[start : start + count, :], chooser[:count])
    chooser = spread(4 * NX, lambda r: 8 * (r % NX) + r // NX)
    lane, row = iota((8, NZ), 1), iota((8, NZ), 0)

    def halves(v):
        return jnp.where(lane < 64, v, lane_roll(row_roll(v, 4), 64))

    on = jnp.where(lax.axis_index("wa") == 0, 1.0, 0.0)
    weight_out[...] = halves(packed(weight_ref[...], chooser)) * on
    ids = halves(packed(ids_ref[...].astype(F32), chooser)).astype(jnp.int32)
    low_out[...] = ids % 16
    owner = ids // 16
    slot = iota((256, NZ), 0)
    for s in range(4):
        hit = slot == jnp.broadcast_to(owner[s : s + 1, :], (256, NZ))
        hot_out[:, NZ * s : NZ * s + NZ] = jnp.where(hit, 1.0, 0.0).astype(jnp.bfloat16)


def last_body(psi_ref, z_ref, r0, r1, r2, r3, r4, r5, diag_ref, rhs_ref, jac_ref, coef_ref, weight_ref, hot_ref, low_ref,
              new_ref, slots_ref, total_ref, high_part, low_part):
    update(psi_ref, z_ref, (r0, r1, r2, r3, r4, r5), diag_ref, rhs_ref, jac_ref, new_ref, total_ref)
    lane = iota((8, NZ), 1)
    groups = pack_edges(new_ref)
    low = low_ref[...]
    point = iota((16, NZ), 0)
    for c in range(3):
        v = coef_ref[c, 0:8, :] * groups[0]
        for g in range(1, len(groups)):
            v = v + coef_ref[c, 8 * g : 8 * g + 8, :] * groups[g]
        v = v + lane_roll(v, 64)
        v = jnp.where(lane % 4 == 3, v + lane_roll(v, 1), 0.0)
        v = v + lane_roll(v, -1)
        v = v + lane_roll(v, -2)
        v = jnp.where(lane < 64, v, row_roll(v, 4)) * weight_ref[...]
        for s in range(4):
            here = point == jnp.broadcast_to(low[s : s + 1, :], (16, NZ))
            w = jnp.where(here, jnp.broadcast_to(v[s : s + 1, :], (16, NZ)), 0.0)
            top = w.astype(jnp.bfloat16)
            at = (slice(16 * c, 16 * c + 16), slice(NZ * s, NZ * s + NZ))
            high_part[at] = top
            low_part[at] = (w - top.astype(F32)).astype(jnp.bfloat16)
    high_part[48:, :] = jnp.zeros((NZ - 48, 512), jnp.bfloat16)
    low_part[48:, :] = jnp.zeros((NZ - 48, 512), jnp.bfloat16)
    hot = hot_ref[...]
    dims = (((1,), (1,)), ((), ()))
    slots_ref[...] = lax.dot_general(hot, high_part[...], dims, preferred_element_type=F32) + lax.dot_general(
        hot, low_part[...], dims, preferred_element_type=F32
    )


def sum_body(got_ref, out_ref):
    v = got_ref[...].sum(axis=0, keepdims=True)
    v = jnp.broadcast_to(v, (8, NZ))
    for c in range(3):
        out_ref[c : c + 1, :] = lane_roll(v, -16 * c)[0:1, :16]


def run(body, args, *rest, **kw):
    shapes = [jax.ShapeDtypeStruct(s, d) for s, d in rest[0]]
    return pl.pallas_call(
        body,
        out_shape=shapes,
        in_specs=[VMEM] * len(args),
        out_specs=[VMEM] * len(shapes),
        scratch_shapes=[pltpu.VMEM(s, d) for s, d in kw.get("scratch", ())],
        compiler_params=pltpu.CompilerParams(vmem_limit_bytes=24 << 20),
        cost_estimate=pl.CostEstimate(flops=kw.get("flops", 1000000), bytes_accessed=kw.get("traffic", 1000000), transcendentals=0),
    )(*args)


EDGE_X = ((FIELDS, 2, NY, NZ), F32)
EDGE_Y = ((FIELDS, 2, NX, NZ), F32)
EDGE_Z = ((24, NZ), F32)
SENDS = [EDGE_X, EDGE_X, EDGE_Y, EDGE_Y, EDGE_Z]
FIELD = ((FIELDS, ROWS, NZ), F32)


def exchange(sends):
    x0, x1, y0, y1, zz = sends
    def swap(v, axis, odd):
        return lax.ppermute(v, axis, pairs(lax.axis_size(axis), odd))
    z = swap(zz, "wa", 0), swap(zz, "wa", 1)
    y = swap(y0, "gy", 0), swap(y1, "gy", 1)
    x = swap(x0, "gx", 0), swap(x1, "gx", 1)
    return (*x, *y, *z)


def local(adjoint_init, objective_grad, diag_term, face_metric, flux_jacobian, wall_coef, ffd_ids, ffd_weight):
    psi = adjoint_init.reshape(FIELDS, ROWS, NZ)
    rhs = objective_grad.reshape(FIELDS, ROWS, NZ)
    diag = diag_term.reshape(ROWS, NZ)
    metric = face_metric.reshape(12, ROWS, NZ)
    jac = flux_jacobian.reshape(FIELDS * FIELDS, ROWS, NZ)
    *sends, packed_metric = run(first_body, (psi, metric), SENDS + [((24, NZ), F32)])
    wall = run(
        wall_body,
        (wall_coef.reshape(30 * NX, NY), ffd_ids.reshape(4 * NX, NY), ffd_weight.reshape(4 * NX, NY)),
        [((3, 24, NZ), F32), ((8, NZ), F32), ((256, 512), jnp.bfloat16), ((8, NZ), jnp.int32)],
    )
    for step in range(SWEEPS):
        received = exchange(sends)
        (z,) = run(inner_body, (psi, metric), [FIELD])
        if step < SWEEPS - 1:
            psi, *sends = run(
                middle_body, (psi, z, *received, diag, rhs, jac, metric, packed_metric), [FIELD] + SENDS, scratch=[FIELD]
            )
        else:
            psi, slots = run(
                last_body, (psi, z, *received, diag, rhs, jac, *wall), [FIELD, ((256, NZ), F32)],
                scratch=[FIELD, ((NZ, 512), jnp.bfloat16), ((NZ, 512), jnp.bfloat16)],
            )
    got = lax.all_to_all(slots.reshape(256, 1, NZ), AXES, 0, 0).reshape(256, NZ)
    (grad,) = run(sum_body, (got,), [((3, 16), F32)])
    return psi.reshape(adjoint_init.shape), grad


def solution(mesh):
    in_specs = (
        P(None, "gx", "gy", "wa"),
        P(None, "gx", "gy", "wa"),
        P("gx", "gy", "wa"),
        P(None, "gx", "gy", "wa"),
        P(None, None, "gx", "gy", "wa"),
        P(None, None, "gx", "gy"),
        P(None, "gx", "gy"),
        P(None, "gx", "gy"),
    )
    out_specs = (P(None, "gx", "gy", "wa"), P(None, AXES))
    return jax.shard_map(local, mesh=mesh, in_specs=in_specs, out_specs=out_specs, check_vma=False)
```

time: 112 us -> 78.9 us (0.70)
  other arithmetic: 19.1 us -> 0 us
  waiting for transfers between devices: 24.4 us -> 8.1 us
  local copies, waits for them, and re-layouts: 8.84 us -> 2.14 us
  Pallas kernels: 0 us -> 6.6 us
  starting transfers between devices: 34.5 us -> 39.1 us
  blocking collectives: 23.5 us -> 22 us
    ppermute x24, waiting for transfers between devices: 24.4 us -> 8.1 us  [swap(): return lax.ppermute(v, axis, pairs(lax.axis_size(axis), odd))]
    mul x50 -> x0, other arithmetic: 10 us -> none  [the longest x24 4.4 us: sweep(): p = metric[base + o][None] * psi]
    pallas_call x0 -> x11, Pallas kernels: none -> 6.6 us  [run(): pl.pallas_call(body, out_shape=shapes, in_specs=[VMEM] * len(args), out_s...]
    ppermute x24, starting transfers between devices: 34.5 us -> 39.1 us  [swap(): return lax.ppermute(v, axis, pairs(lax.axis_size(axis), odd))]
    select_n x12 -> x0, other arithmetic: 2.81 us -> none  [send(): second = lax.ppermute(jnp.where(even, low, high), axis, pairs(count, 1))]
    scatter-add x1 -> x0, other arithmetic: 2.77 us -> none  [local(): summed = jax.ops.segment_sum(flat, ffd_ids.reshape(-1), num_segments=POINTS)]
    add x8 -> x0, other arithmetic: 2.46 us -> none  [the longest x4 2.14 us: sweep(): z = z + padded(below, dim, 0, n - 2) + padded(above, dim, n - 2, 0)]
    reshape x3 -> x0, local copies, waits for them, and re-layouts: 1.81 us -> none  [the longest x1 1.05 us: local(): summed.reshape(owners, POINTS // owners, -1)]
  transfers between devices with their start and end apart: 24 -> 24, of which waited for: 10 -> 8; matrix products, arithmetic and copies ran while one was open for 8% -> 0% of each run, Pallas kernels for 0% -> 3%
where the time goes in v2:
time: 78.9 us; the launch traced here: 78.8 us
  starting transfers between devices  39.1 us (50%)
  blocking collectives  22 us (28%)
  waiting for transfers between devices  8.1 us (10%)
  Pallas kernels  6.6 us (8%)
  local copies, waits for them, and re-layouts  2.14 us (3%)
  between operations  0.81 us (1%)
    ppermute x24, starting transfers between devices, swap(): return lax.ppermute(v, axis, pairs(lax.axis_size(axis), odd))  39.1 us
    all_to_all x1, blocking collectives, local(): got = lax.all_to_all(slots.reshape(256, 1, NZ), AXES, 0, 0).reshape(256, NZ)  22 us
    ppermute x24, waiting for transfers between devices, swap(): return lax.ppermute(v, axis, pairs(lax.axis_size(axis), odd))  8.1 us
    pallas_call x11, Pallas kernels, run(): pl.pallas_call(body, out_shape=shapes, in_specs=[VMEM] * len(args), out_s...  6.6 us
    unnamed x18, local copies, waits for them, and re-layouts  2.14 us
  transfers between devices with their start and end apart: 24, of which 8 were waited for; matrix products, arithmetic and copies ran while one was open for 0% of the time, Pallas kernels for 3%

profile of v2, /device:TPU:1, one launch (start us, length us, event | category | flops | bytes accessed | tf_op | source)
XLA Modules:
  0.0 78.8 jit_solution(14018608640924199470)
XLA Ops:
  0.6 0.0 copy-start
  0.6 1.1 %copy-done = f32[12,8,16,128]{3,2,1,0:T(8,128)S(1)} copy-done((f32[12,8,16,128]{3,2,1,0:T(8,128)S(1)}, f32[12,8,16,128]{3,2,1,0:T(8,128)}, u32[]{:S(2)}) %copy-start) | copy-done | bytes 786456
  1.8 1.0 %copy-done.4 = f32[5,8,16,128]{3,2,1,0:T(8,128)S(1)} copy-done((f32[5,8,16,128]{3,2,1,0:T(8,128)S(1)}, f32[5,8,16,128]{3,2,1,0:T(8,128)}, u32[]{:S(2)}) %copy-start.4) | copy-done | bytes 327704
  2.7 0.3 shard_map.96
  3.1 2.1 %collective-permute-start = (f32[5,2,16,128]{3,2,1,0:T(8,128)S(1)}, f32[5,2,16,128]{3,2,1,0:T(8,128)S(1)}, u32[]{:S(2)}, u32[]{:S(2)}) collective-permute-start(f32[5,2,16,128]{3,2,1,0:T(8,128)S(1)} %get-tuple-element.32), channel_id=1, source_target_pairs={{0,32},{32,0},{64,96},{96,64},{128,160},{160,128},{192,224},{224,1... | collective-permute-start | bytes 245768 | tf_op jit(solution)/shard_map/ppermute | solution.py:287
  5.2 2.7 %collective-permute-start.1 = (f32[5,2,16,128]{3,2,1,0:T(8,128)S(1)}, f32[5,2,16,128]{3,2,1,0:T(8,128)S(1)}, u32[]{:S(2)}, u32[]{:S(2)}) collective-permute-start(f32[5,2,16,128]{3,2,1,0:T(8,128)S(1)} %get-tuple-element.33), channel_id=1, source_target_pairs={{0,224},{32,64},{64,32},{96,128},{128,96},{160,192},{192,160},{224... | collective-permute-start | bytes 245768 | tf_op jit(solution)/shard_map/ppermute | solution.py:287
  7.9 1.6 %collective-permute-start.2 = (f32[5,2,8,128]{3,2,1,0:T(8,128)S(1)}, f32[5,2,8,128]{3,2,1,0:T(8,128)S(1)}, u32[]{:S(2)}, u32[]{:S(2)}) collective-permute-start(f32[5,2,8,128]{3,2,1,0:T(8,128)S(1)} %get-tuple-element.34), channel_id=1, source_target_pairs={{0,4},{4,0},{8,12},{12,8},{16,20},{20,16},{24,28},{28,24},{1,5},{5... | collective-permute-start | bytes 122888 | tf_op jit(solution)/shard_map/ppermute | solution.py:287
  9.5 4.7 %collective-permute-start.3 = (f32[5,2,8,128]{3,2,1,0:T(8,128)S(1)}, f32[5,2,8,128]{3,2,1,0:T(8,128)S(1)}, u32[]{:S(2)}, u32[]{:S(2)}) collective-permute-start(f32[5,2,8,128]{3,2,1,0:T(8,128)S(1)} %get-tuple-element.35), channel_id=1, source_target_pairs={{0,28},{4,8},{8,4},{12,16},{16,12},{20,24},{24,20},{28,0},{1,29},{... | collective-permute-start | bytes 122888 | tf_op jit(solution)/shard_map/ppermute | solution.py:287
  14.2 1.8 %collective-permute-start.4 = (f32[24,128]{1,0:T(8,128)S(1)}, f32[24,128]{1,0:T(8,128)S(1)}, u32[]{:S(2)}, u32[]{:S(2)}) collective-permute-start(f32[24,128]{1,0:T(8,128)S(1)} %get-tuple-element.36), channel_id=1, source_target_pairs={{0,1},{1,0},{2,3},{3,2},{4,5},{5,4},{6,7},{7,6},{8,9},{9,8},{10,11... | collective-permute-start | bytes 36872 | tf_op jit(solution)/shard_map/ppermute | solution.py:287
  16.0 0.8 %collective-permute-done.4.r4 = f32[24,128]{1,0:T(8,128)S(1)} collective-permute-done((f32[24,128]{1,0:T(8,128)S(1)}, f32[24,128]{1,0:T(8,128)S(1)}, u32[]{:S(2)}, u32[]{:S(2)}) %collective-permute-start.4) | collective-permute-done | bytes 12320 | tf_op jit(solution)/shard_map/ppermute | solution.py:287
  16.8 3.0 %collective-permute-start.5 = (f32[24,128]{1,0:T(8,128)S(1)}, f32[24,128]{1,0:T(8,128)S(1)}, u32[]{:S(2)}, u32[]{:S(2)}) collective-permute-start(f32[24,128]{1,0:T(8,128)S(1)} %get-tuple-element.36), channel_id=1, source_target_pairs={{0,3},{1,2},{2,1},{3,0},{4,7},{5,6},{6,5},{7,4},{8,11},{9,10},{10,... | collective-permute-start | bytes 36872 | tf_op jit(solution)/shard_map/ppermute | solution.py:287
  19.8 0.4 shard_map.95.z_ref
  20.2 1.2 %collective-permute-done.5.r5 = f32[24,128]{1,0:T(8,128)S(1)} collective-permute-done((f32[24,128]{1,0:T(8,128)S(1)}, f32[24,128]{1,0:T(8,128)S(1)}, u32[]{:S(2)}, u32[]{:S(2)}) %collective-permute-start.5) | collective-permute-done | bytes 12320 | tf_op jit(solution)/shard_map/ppermute | solution.py:287
  21.5 0.0 collective-permute-done.2.r2
  21.5 0.0 collective-permute-done.3.r3
  21.5 0.0 collective-permute-done.r0
  21.5 0.0 collective-permute-done.1.r1
  21.5 0.0 copy-start.1
  21.5 0.7 shard_map.97
  22.2 0.0 collective-permute-start.6
  22.3 1.6 %collective-permute-start.7 = (f32[5,2,16,128]{3,2,1,0:T(8,128)S(1)}, f32[5,2,16,128]{3,2,1,0:T(8,128)S(1)}, u32[]{:S(2)}, u32[]{:S(2)}) collective-permute-start(f32[5,2,16,128]{3,2,1,0:T(8,128)S(1)} %get-tuple-element.40), channel_id=1, source_target_pairs={{0,224},{32,64},{64,32},{96,128},{128,96},{160,192},{192,160},{224... | collective-permute-start | bytes 245768 | tf_op jit(solution)/shard_map/ppermute | solution.py:287
  23.9 0.0 collective-permute-start.8
  23.9 1.5 %collective-permute-start.9 = (f32[5,2,8,128]{3,2,1,0:T(8,128)S(1)}, f32[5,2,8,128]{3,2,1,0:T(8,128)S(1)}, u32[]{:S(2)}, u32[]{:S(2)}) collective-permute-start(f32[5,2,8,128]{3,2,1,0:T(8,128)S(1)} %get-tuple-element.42), channel_id=1, source_target_pairs={{0,28},{4,8},{8,4},{12,16},{16,12},{20,24},{24,20},{28,0},{1,29},{... | collective-permute-start | bytes 122888 | tf_op jit(solution)/shard_map/ppermute | solution.py:287
  25.4 1.5 %collective-permute-start.10 = (f32[24,128]{1,0:T(8,128)S(1)}, f32[24,128]{1,0:T(8,128)S(1)}, u32[]{:S(2)}, u32[]{:S(2)}) collective-permute-start(f32[24,128]{1,0:T(8,128)S(1)} %get-tuple-element.43), channel_id=1, source_target_pairs={{0,1},{1,0},{2,3},{3,2},{4,5},{5,4},{6,7},{7,6},{8,9},{9,8},{10,11... | collective-permute-start | bytes 36872 | tf_op jit(solution)/shard_map/ppermute | solution.py:287
  26.8 0.8 %collective-permute-done.10.r4 = f32[24,128]{1,0:T(8,128)S(1)} collective-permute-done((f32[24,128]{1,0:T(8,128)S(1)}, f32[24,128]{1,0:T(8,128)S(1)}, u32[]{:S(2)}, u32[]{:S(2)}) %collective-permute-start.10) | collective-permute-done | bytes 12320 | tf_op jit(solution)/shard_map/ppermute | solution.py:287
  27.7 3.0 %collective-permute-start.11 = (f32[24,128]{1,0:T(8,128)S(1)}, f32[24,128]{1,0:T(8,128)S(1)}, u32[]{:S(2)}, u32[]{:S(2)}) collective-permute-start(f32[24,128]{1,0:T(8,128)S(1)} %get-tuple-element.43), channel_id=1, source_target_pairs={{0,3},{1,2},{2,1},{3,0},{4,7},{5,6},{6,5},{7,4},{8,11},{9,10},{10,... | collective-permute-start | bytes 36872 | tf_op jit(solution)/shard_map/ppermute | solution.py:287
  30.6 0.4 shard_map.98.z_ref
  31.1 1.2 %collective-permute-done.11.r5 = f32[24,128]{1,0:T(8,128)S(1)} collective-permute-done((f32[24,128]{1,0:T(8,128)S(1)}, f32[24,128]{1,0:T(8,128)S(1)}, u32[]{:S(2)}, u32[]{:S(2)}) %collective-permute-start.11) | collective-permute-done | bytes 12320 | tf_op jit(solution)/shard_map/ppermute | solution.py:287
  32.3 0.0 collective-permute-done.8.r2
  32.3 0.0 collective-permute-done.9.r3
  32.3 0.0 collective-permute-done.6.r0
  32.3 0.7 shard_map.99
  33.0 0.6 collective-permute-start.12
  33.6 1.2 %collective-permute-start.13 = (f32[5,2,16,128]{3,2,1,0:T(8,128)S(1)}, f32[5,2,16,128]{3,2,1,0:T(8,128)S(1)}, u32[]{:S(2)}, u32[]{:S(2)}) collective-permute-start(f32[5,2,16,128]{3,2,1,0:T(8,128)S(1)} %get-tuple-element.46), channel_id=1, source_target_pairs={{0,224},{32,64},{64,32},{96,128},{128,96},{160,192},{192,160},{224... | collective-permute-start | bytes 245768 | tf_op jit(solution)/shard_map/ppermute | solution.py:287
  34.9 0.7 collective-permute-start.14
  35.6 0.2 collective-permute-start.15
  35.8 1.1 %collective-permute-start.16 = (f32[24,128]{1,0:T(8,128)S(1)}, f32[24,128]{1,0:T(8,128)S(1)}, u32[]{:S(2)}, u32[]{:S(2)}) collective-permute-start(f32[24,128]{1,0:T(8,128)S(1)} %get-tuple-element.49), channel_id=1, source_target_pairs={{0,1},{1,0},{2,3},{3,2},{4,5},{5,4},{6,7},{7,6},{8,9},{9,8},{10,11... | collective-permute-start | bytes 36872 | tf_op jit(solution)/shard_map/ppermute | solution.py:287
  36.9 0.8 %collective-permute-done.16.r4 = f32[24,128]{1,0:T(8,128)S(1)} collective-permute-done((f32[24,128]{1,0:T(8,128)S(1)}, f32[24,128]{1,0:T(8,128)S(1)}, u32[]{:S(2)}, u32[]{:S(2)}) %collective-permute-start.16) | collective-permute-done | bytes 12320 | tf_op jit(solution)/shard_map/ppermute | solution.py:287
  37.8 2.8 %collective-permute-start.17 = (f32[24,128]{1,0:T(8,128)S(1)}, f32[24,128]{1,0:T(8,128)S(1)}, u32[]{:S(2)}, u32[]{:S(2)}) collective-permute-start(f32[24,128]{1,0:T(8,128)S(1)} %get-tuple-element.49), channel_id=1, source_target_pairs={{0,3},{1,2},{2,1},{3,0},{4,7},{5,6},{6,5},{7,4},{8,11},{9,10},{10,... | collective-permute-start | bytes 36872 | tf_op jit(solution)/shard_map/ppermute | solution.py:287
  40.6 0.4 shard_map.100.z_ref
  41.0 0.0 copy-start.6
  41.0 1.4 %collective-permute-done.17.r5 = f32[24,128]{1,0:T(8,128)S(1)} collective-permute-done((f32[24,128]{1,0:T(8,128)S(1)}, f32[24,128]{1,0:T(8,128)S(1)}, u32[]{:S(2)}, u32[]{:S(2)}) %collective-permute-start.17) | collective-permute-done | bytes 12320 | tf_op jit(solution)/shard_map/ppermute | solution.py:287
  42.4 0.0 collective-permute-done.14.r2
  42.4 0.0 collective-permute-done.15.r3
  42.4 0.0 collective-permute-done.12.r0
  42.4 0.0 copy-start.7
  42.4 0.0 copy-start.8
  42.4 0.7 shard_map.101
  43.1 1.1 %collective-permute-start.18 = (f32[5,2,16,128]{3,2,1,0:T(8,128)S(1)}, f32[5,2,16,128]{3,2,1,0:T(8,128)S(1)}, u32[]{:S(2)}, u32[]{:S(2)}) collective-permute-start(f32[5,2,16,128]{3,2,1,0:T(8,128)S(1)} %get-tuple-element.51), channel_id=1, source_target_pairs={{0,32},{32,0},{64,96},{96,64},{128,160},{160,128},{192,224},{224,1... | collective-permute-start | bytes 245768 | tf_op jit(solution)/shard_map/ppermute | solution.py:287
  44.2 1.5 %collective-permute-start.19 = (f32[5,2,16,128]{3,2,1,0:T(8,128)S(1)}, f32[5,2,16,128]{3,2,1,0:T(8,128)S(1)}, u32[]{:S(2)}, u32[]{:S(2)}) collective-permute-start(f32[5,2,16,128]{3,2,1,0:T(8,128)S(1)} %get-tuple-element.52), channel_id=1, source_target_pairs={{0,224},{32,64},{64,32},{96,128},{128,96},{160,192},{192,160},{224... | collective-permute-start | bytes 245768 | tf_op jit(solution)/shard_map/ppermute | solution.py:287
  45.7 1.5 %collective-permute-start.20 = (f32[5,2,8,128]{3,2,1,0:T(8,128)S(1)}, f32[5,2,8,128]{3,2,1,0:T(8,128)S(1)}, u32[]{:S(2)}, u32[]{:S(2)}) collective-permute-start(f32[5,2,8,128]{3,2,1,0:T(8,128)S(1)} %get-tuple-element.53), channel_id=1, source_target_pairs={{0,4},{4,0},{8,12},{12,8},{16,20},{20,16},{24,28},{28,24},{1,5},{5... | collective-permute-start | bytes 122888 | tf_op jit(solution)/shard_map/ppermute | solution.py:287
  47.2 1.2 %collective-permute-start.21 = (f32[5,2,8,128]{3,2,1,0:T(8,128)S(1)}, f32[5,2,8,128]{3,2,1,0:T(8,128)S(1)}, u32[]{:S(2)}, u32[]{:S(2)}) collective-permute-start(f32[5,2,8,128]{3,2,1,0:T(8,128)S(1)} %get-tuple-element.54), channel_id=1, source_target_pairs={{0,28},{4,8},{8,4},{12,16},{16,12},{20,24},{24,20},{28,0},{1,29},{... | collective-permute-start | bytes 122888 | tf_op jit(solution)/shard_map/ppermute | solution.py:287
  48.5 0.9 %collective-permute-start.22 = (f32[24,128]{1,0:T(8,128)S(1)}, f32[24,128]{1,0:T(8,128)S(1)}, u32[]{:S(2)}, u32[]{:S(2)}) collective-permute-start(f32[24,128]{1,0:T(8,128)S(1)} %get-tuple-element.55), channel_id=1, source_target_pairs={{0,1},{1,0},{2,3},{3,2},{4,5},{5,4},{6,7},{7,6},{8,9},{9,8},{10,11... | collective-permute-start | bytes 36872 | tf_op jit(solution)/shard_map/ppermute | solution.py:287
  49.4 0.8 %collective-permute-done.22.r4 = f32[24,128]{1,0:T(8,128)S(1)} collective-permute-done((f32[24,128]{1,0:T(8,128)S(1)}, f32[24,128]{1,0:T(8,128)S(1)}, u32[]{:S(2)}, u32[]{:S(2)}) %collective-permute-start.22) | collective-permute-done | bytes 12320 | tf_op jit(solution)/shard_map/ppermute | solution.py:287
  50.2 2.7 %collective-permute-start.23 = (f32[24,128]{1,0:T(8,128)S(1)}, f32[24,128]{1,0:T(8,128)S(1)}, u32[]{:S(2)}, u32[]{:S(2)}) collective-permute-start(f32[24,128]{1,0:T(8,128)S(1)} %get-tuple-element.55), channel_id=1, source_target_pairs={{0,3},{1,2},{2,1},{3,0},{4,7},{5,6},{6,5},{7,4},{8,11},{9,10},{10,... | collective-permute-start | bytes 36872 | tf_op jit(solution)/shard_map/ppermute | solution.py:287
  52.9 0.6 shard_map.103
  53.5 0.4 shard_map.102.z_ref
  53.9 0.9 %collective-permute-done.23.r5 = f32[24,128]{1,0:T(8,128)S(1)} collective-permute-done((f32[24,128]{1,0:T(8,128)S(1)}, f32[24,128]{1,0:T(8,128)S(1)}, u32[]{:S(2)}, u32[]{:S(2)}) %collective-permute-start.23) | collective-permute-done | bytes 12320 | tf_op jit(solution)/shard_map/ppermute | solution.py:287
  54.8 0.0 collective-permute-done.20.r2
  54.8 0.0 collective-permute-done.21.r3
  54.8 0.0 collective-permute-done.18.r0
  54.8 1.2 %shard_map.104 = (f32[5,128,128]{2,1,0:T(8,128)}, f32[256,128]{1,0:T(8,128)S(1)}) custom-call(f32[5,128,128]{2,1,0:T(8,128)S(1)} %get-tuple-element.50.psi_ref, f32[5,128,128]{2,1,0:T(8,128)S(1)} %shard_map.102.z_ref, f32[5,2,16,128]{3,2,1,0:T(8,128)S(1)} %collective-permute-done.18.r0, f32[5,2,16,128]{3,2,1,0:T(8,128)S(1)} %collective-permute-done.19.r1, ...), custom_call_target="tpu_custom_call" | custom-call | flops 1000000 | bytes 1000000 | tf_op jit(solution)/shard_map/pallas_call | solution.py:266
  56.0 22.0 %all_to_all.5 = f32[256,1,128]{2,1,0:T(1,128)S(1)} all-to-all(f32[256,1,128]{2,1,0:T(1,128)S(1)} %bitcast.37), channel_id=1, replica_groups=mesh['gx'=8,'gy'=8,'wa'=4] {'gx','gy','wa'}, dimensions={0} | all-to-all | bytes 262144 | tf_op jit(solution)/shard_map/all_to_all | solution.py:318
  78.1 0.7 shard_map.105
  (14 shorter events, 0.0 us)
Async XLA Ops:
  0.6 1.1 %copy-start = (f32[12,8,16,128]{3,2,1,0:T(8,128)S(1)}, f32[12,8,16,128]{3,2,1,0:T(8,128)}, u32[]{:S(2)}) copy-start(f32[12,8,16,128]{3,2,1,0:T(8,128)} %param.11) | copy-start | bytes 2359300
  1.8 1.0 %copy-start.4 = (f32[5,8,16,128]{3,2,1,0:T(8,128)S(1)}, f32[5,8,16,128]{3,2,1,0:T(8,128)}, u32[]{:S(2)}) copy-start(f32[5,8,16,128]{3,2,1,0:T(8,128)} %param.8) | copy-start | bytes 983044
  3.1 18.4 %copy-start.2 = (bf16[5,5,8,16,128]{4,3,2,1,0:T(8,128)(2,1)S(1)}, bf16[5,5,8,16,128]{4,3,2,1,0:T(8,128)(2,1)}, u32[]{:S(2)}) copy-start(bf16[5,5,8,16,128]{4,3,2,1,0:T(8,128)(2,1)} %param.12) | copy-start | bytes 2457604
  3.1 18.4 %collective-permute-start = (f32[5,2,16,128]{3,2,1,0:T(8,128)S(1)}, f32[5,2,16,128]{3,2,1,0:T(8,128)S(1)}, u32[]{:S(2)}, u32[]{:S(2)}) collective-permute-start(f32[5,2,16,128]{3,2,1,0:T(8,128)S(1)} %get-tuple-element.32), channel_id=1, source_target_pairs={{0,32},{32,0},{64,96},{96,64},{128,160},{160,128},{192,224},{224,1... | collective-permute-start | bytes 245768 | tf_op jit(solution)/shard_map/ppermute | solution.py:287
  5.2 16.3 %collective-permute-start.1 = (f32[5,2,16,128]{3,2,1,0:T(8,128)S(1)}, f32[5,2,16,128]{3,2,1,0:T(8,128)S(1)}, u32[]{:S(2)}, u32[]{:S(2)}) collective-permute-start(f32[5,2,16,128]{3,2,1,0:T(8,128)S(1)} %get-tuple-element.33), channel_id=1, source_target_pairs={{0,224},{32,64},{64,32},{96,128},{128,96},{160,192},{192,160},{224... | collective-permute-start | bytes 245768 | tf_op jit(solution)/shard_map/ppermute | solution.py:287
  7.9 13.6 %collective-permute-start.2 = (f32[5,2,8,128]{3,2,1,0:T(8,128)S(1)}, f32[5,2,8,128]{3,2,1,0:T(8,128)S(1)}, u32[]{:S(2)}, u32[]{:S(2)}) collective-permute-start(f32[5,2,8,128]{3,2,1,0:T(8,128)S(1)} %get-tuple-element.34), channel_id=1, source_target_pairs={{0,4},{4,0},{8,12},{12,8},{16,20},{20,16},{24,28},{28,24},{1,5},{5... | collective-permute-start | bytes 122888 | tf_op jit(solution)/shard_map/ppermute | solution.py:287
  9.5 11.9 %collective-permute-start.3 = (f32[5,2,8,128]{3,2,1,0:T(8,128)S(1)}, f32[5,2,8,128]{3,2,1,0:T(8,128)S(1)}, u32[]{:S(2)}, u32[]{:S(2)}) collective-permute-start(f32[5,2,8,128]{3,2,1,0:T(8,128)S(1)} %get-tuple-element.35), channel_id=1, source_target_pairs={{0,28},{4,8},{8,4},{12,16},{16,12},{20,24},{24,20},{28,0},{1,29},{... | collective-permute-start | bytes 122888 | tf_op jit(solution)/shard_map/ppermute | solution.py:287
  14.2 7.3 %copy-start.3 = (f32[5,8,16,128]{3,2,1,0:T(8,128)S(1)}, f32[5,8,16,128]{3,2,1,0:T(8,128)}, u32[]{:S(2)}) copy-start(f32[5,8,16,128]{3,2,1,0:T(8,128)} %param.9) | copy-start | bytes 983044
  14.2 7.3 %copy-start.5 = (f32[8,16,128]{2,1,0:T(8,128)S(1)}, f32[8,16,128]{2,1,0:T(8,128)}, u32[]{:S(2)}) copy-start(f32[8,16,128]{2,1,0:T(8,128)} %param.10) | copy-start | bytes 196612
  14.2 2.6 %collective-permute-start.4 = (f32[24,128]{1,0:T(8,128)S(1)}, f32[24,128]{1,0:T(8,128)S(1)}, u32[]{:S(2)}, u32[]{:S(2)}) collective-permute-start(f32[24,128]{1,0:T(8,128)S(1)} %get-tuple-element.36), channel_id=1, source_target_pairs={{0,1},{1,0},{2,3},{3,2},{4,5},{5,4},{6,7},{7,6},{8,9},{9,8},{10,11... | collective-permute-start | bytes 36872 | tf_op jit(solution)/shard_map/ppermute | solution.py:287
  16.8 4.6 %collective-permute-start.5 = (f32[24,128]{1,0:T(8,128)S(1)}, f32[24,128]{1,0:T(8,128)S(1)}, u32[]{:S(2)}, u32[]{:S(2)}) collective-permute-start(f32[24,128]{1,0:T(8,128)S(1)} %get-tuple-element.36), channel_id=1, source_target_pairs={{0,3},{1,2},{2,1},{3,0},{4,7},{5,6},{6,5},{7,4},{8,11},{9,10},{10,... | collective-permute-start | bytes 36872 | tf_op jit(solution)/shard_map/ppermute | solution.py:287
  21.5 9.1 %copy-start.1 = (f32[12,8,16,128]{3,2,1,0:T(8,128)S(1)}, f32[12,8,16,128]{3,2,1,0:T(8,128)}, u32[]{:S(2)}) copy-start(f32[12,8,16,128]{3,2,1,0:T(8,128)} %param.11) | copy-start | bytes 2359300
  22.2 10.1 %collective-permute-start.6 = (f32[5,2,16,128]{3,2,1,0:T(8,128)S(1)}, f32[5,2,16,128]{3,2,1,0:T(8,128)S(1)}, u32[]{:S(2)}, u32[]{:S(2)}) collective-permute-start(f32[5,2,16,128]{3,2,1,0:T(8,128)S(1)} %get-tuple-element.39), channel_id=1, source_target_pairs={{0,32},{32,0},{64,96},{96,64},{128,160},{160,128},{192,224},{224,1... | collective-permute-start | bytes 245768 | tf_op jit(solution)/shard_map/ppermute | solution.py:287
  22.3 10.0 %collective-permute-start.7 = (f32[5,2,16,128]{3,2,1,0:T(8,128)S(1)}, f32[5,2,16,128]{3,2,1,0:T(8,128)S(1)}, u32[]{:S(2)}, u32[]{:S(2)}) collective-permute-start(f32[5,2,16,128]{3,2,1,0:T(8,128)S(1)} %get-tuple-element.40), channel_id=1, source_target_pairs={{0,224},{32,64},{64,32},{96,128},{128,96},{160,192},{192,160},{224... | collective-permute-start | bytes 245768 | tf_op jit(solution)/shard_map/ppermute | solution.py:287
  23.9 8.4 %collective-permute-start.8 = (f32[5,2,8,128]{3,2,1,0:T(8,128)S(1)}, f32[5,2,8,128]{3,2,1,0:T(8,128)S(1)}, u32[]{:S(2)}, u32[]{:S(2)}) collective-permute-start(f32[5,2,8,128]{3,2,1,0:T(8,128)S(1)} %get-tuple-element.41), channel_id=1, source_target_pairs={{0,4},{4,0},{8,12},{12,8},{16,20},{20,16},{24,28},{28,24},{1,5},{5... | collective-permute-start | bytes 122888 | tf_op jit(solution)/shard_map/ppermute | solution.py:287
  23.9 8.4 %collective-permute-start.9 = (f32[5,2,8,128]{3,2,1,0:T(8,128)S(1)}, f32[5,2,8,128]{3,2,1,0:T(8,128)S(1)}, u32[]{:S(2)}, u32[]{:S(2)}) collective-permute-start(f32[5,2,8,128]{3,2,1,0:T(8,128)S(1)} %get-tuple-element.42), channel_id=1, source_target_pairs={{0,28},{4,8},{8,4},{12,16},{16,12},{20,24},{24,20},{28,0},{1,29},{... | collective-permute-start | bytes 122888 | tf_op jit(solution)/shard_map/ppermute | solution.py:287
  25.4 2.3 %collective-permute-start.10 = (f32[24,128]{1,0:T(8,128)S(1)}, f32[24,128]{1,0:T(8,128)S(1)}, u32[]{:S(2)}, u32[]{:S(2)}) collective-permute-start(f32[24,128]{1,0:T(8,128)S(1)} %get-tuple-element.43), channel_id=1, source_target_pairs={{0,1},{1,0},{2,3},{3,2},{4,5},{5,4},{6,7},{7,6},{8,9},{9,8},{10,11... | collective-permute-start | bytes 36872 | tf_op jit(solution)/shard_map/ppermute | solution.py:287
  27.7 4.6 %collective-permute-start.11 = (f32[24,128]{1,0:T(8,128)S(1)}, f32[24,128]{1,0:T(8,128)S(1)}, u32[]{:S(2)}, u32[]{:S(2)}) collective-permute-start(f32[24,128]{1,0:T(8,128)S(1)} %get-tuple-element.43), channel_id=1, source_target_pairs={{0,3},{1,2},{2,1},{3,0},{4,7},{5,6},{6,5},{7,4},{8,11},{9,10},{10,... | collective-permute-start | bytes 36872 | tf_op jit(solution)/shard_map/ppermute | solution.py:287
  33.0 9.4 %collective-permute-start.12 = (f32[5,2,16,128]{3,2,1,0:T(8,128)S(1)}, f32[5,2,16,128]{3,2,1,0:T(8,128)S(1)}, u32[]{:S(2)}, u32[]{:S(2)}) collective-permute-start(f32[5,2,16,128]{3,2,1,0:T(8,128)S(1)} %get-tuple-element.45), channel_id=1, source_target_pairs={{0,32},{32,0},{64,96},{96,64},{128,160},{160,128},{192,224},{224,1... | collective-permute-start | bytes 245768 | tf_op jit(solution)/shard_map/ppermute | solution.py:287
  33.6 8.8 %collective-permute-start.13 = (f32[5,2,16,128]{3,2,1,0:T(8,128)S(1)}, f32[5,2,16,128]{3,2,1,0:T(8,128)S(1)}, u32[]{:S(2)}, u32[]{:S(2)}) collective-permute-start(f32[5,2,16,128]{3,2,1,0:T(8,128)S(1)} %get-tuple-element.46), channel_id=1, source_target_pairs={{0,224},{32,64},{64,32},{96,128},{128,96},{160,192},{192,160},{224... | collective-permute-start | bytes 245768 | tf_op jit(solution)/shard_map/ppermute | solution.py:287
  34.9 7.5 %collective-permute-start.14 = (f32[5,2,8,128]{3,2,1,0:T(8,128)S(1)}, f32[5,2,8,128]{3,2,1,0:T(8,128)S(1)}, u32[]{:S(2)}, u32[]{:S(2)}) collective-permute-start(f32[5,2,8,128]{3,2,1,0:T(8,128)S(1)} %get-tuple-element.47), channel_id=1, source_target_pairs={{0,4},{4,0},{8,12},{12,8},{16,20},{20,16},{24,28},{28,24},{1,5},{5... | collective-permute-start | bytes 122888 | tf_op jit(solution)/shard_map/ppermute | solution.py:287
  35.6 6.8 %collective-permute-start.15 = (f32[5,2,8,128]{3,2,1,0:T(8,128)S(1)}, f32[5,2,8,128]{3,2,1,0:T(8,128)S(1)}, u32[]{:S(2)}, u32[]{:S(2)}) collective-permute-start(f32[5,2,8,128]{3,2,1,0:T(8,128)S(1)} %get-tuple-element.48), channel_id=1, source_target_pairs={{0,28},{4,8},{8,4},{12,16},{16,12},{20,24},{24,20},{28,0},{1,29},{... | collective-permute-start | bytes 122888 | tf_op jit(solution)/shard_map/ppermute | solution.py:287
  35.8 1.9 %collective-permute-start.16 = (f32[24,128]{1,0:T(8,128)S(1)}, f32[24,128]{1,0:T(8,128)S(1)}, u32[]{:S(2)}, u32[]{:S(2)}) collective-permute-start(f32[24,128]{1,0:T(8,128)S(1)} %get-tuple-element.49), channel_id=1, source_target_pairs={{0,1},{1,0},{2,3},{3,2},{4,5},{5,4},{6,7},{7,6},{8,9},{9,8},{10,11... | collective-permute-start | bytes 36872 | tf_op jit(solution)/shard_map/ppermute | solution.py:287
  37.8 4.6 %collective-permute-start.17 = (f32[24,128]{1,0:T(8,128)S(1)}, f32[24,128]{1,0:T(8,128)S(1)}, u32[]{:S(2)}, u32[]{:S(2)}) collective-permute-start(f32[24,128]{1,0:T(8,128)S(1)} %get-tuple-element.49), channel_id=1, source_target_pairs={{0,3},{1,2},{2,1},{3,0},{4,7},{5,6},{6,5},{7,4},{8,11},{9,10},{10,... | collective-permute-start | bytes 36872 | tf_op jit(solution)/shard_map/ppermute | solution.py:287
  41.0 11.9 %copy-start.6 = (f32[3,10,8,16]{3,2,1,0:T(8,128)S(1)}, f32[3,10,8,16]{3,2,1,0:T(8,128)}, u32[]{:S(2)}) copy-start(f32[3,10,8,16]{3,2,1,0:T(8,128)} %param.13) | copy-start | bytes 46084
  42.4 10.5 %copy-start.7 = (s32[4,8,16]{2,1,0:T(8,128)S(1)}, s32[4,8,16]{2,1,0:T(8,128)}, u32[]{:S(2)}) copy-start(s32[4,8,16]{2,1,0:T(8,128)} %param.14) | copy-start | bytes 6148
  42.4 10.5 %copy-start.8 = (f32[4,8,16]{2,1,0:T(8,128)S(1)}, f32[4,8,16]{2,1,0:T(8,128)}, u32[]{:S(2)}) copy-start(f32[4,8,16]{2,1,0:T(8,128)} %param.15) | copy-start | bytes 6148
  43.1 11.7 %collective-permute-start.18 = (f32[5,2,16,128]{3,2,1,0:T(8,128)S(1)}, f32[5,2,16,128]{3,2,1,0:T(8,128)S(1)}, u32[]{:S(2)}, u32[]{:S(2)}) collective-permute-start(f32[5,2,16,128]{3,2,1,0:T(8,128)S(1)} %get-tuple-element.51), channel_id=1, source_target_pairs={{0,32},{32,0},{64,96},{96,64},{128,160},{160,128},{192,224},{224,1... | collective-permute-start | bytes 245768 | tf_op jit(solution)/shard_map/ppermute | solution.py:287
  44.2 10.6 %collective-permute-start.19 = (f32[5,2,16,128]{3,2,1,0:T(8,128)S(1)}, f32[5,2,16,128]{3,2,1,0:T(8,128)S(1)}, u32[]{:S(2)}, u32[]{:S(2)}) collective-permute-start(f32[5,2,16,128]{3,2,1,0:T(8,128)S(1)} %get-tuple-element.52), channel_id=1, source_target_pairs={{0,224},{32,64},{64,32},{96,128},{128,96},{160,192},{192,160},{224... | collective-permute-start | bytes 245768 | tf_op jit(solution)/shard_map/ppermute | solution.py:287
  45.7 9.1 %collective-permute-start.20 = (f32[5,2,8,128]{3,2,1,0:T(8,128)S(1)}, f32[5,2,8,128]{3,2,1,0:T(8,128)S(1)}, u32[]{:S(2)}, u32[]{:S(2)}) collective-permute-start(f32[5,2,8,128]{3,2,1,0:T(8,128)S(1)} %get-tuple-element.53), channel_id=1, source_target_pairs={{0,4},{4,0},{8,12},{12,8},{16,20},{20,16},{24,28},{28,24},{1,5},{5... | collective-permute-start | bytes 122888 | tf_op jit(solution)/shard_map/ppermute | solution.py:287
  47.2 7.6 %collective-permute-start.21 = (f32[5,2,8,128]{3,2,1,0:T(8,128)S(1)}, f32[5,2,8,128]{3,2,1,0:T(8,128)S(1)}, u32[]{:S(2)}, u32[]{:S(2)}) collective-permute-start(f32[5,2,8,128]{3,2,1,0:T(8,128)S(1)} %get-tuple-element.54), channel_id=1, source_target_pairs={{0,28},{4,8},{8,4},{12,16},{16,12},{20,24},{24,20},{28,0},{1,29},{... | collective-permute-start | bytes 122888 | tf_op jit(solution)/shard_map/ppermute | solution.py:287
  48.5 1.7 %collective-permute-start.22 = (f32[24,128]{1,0:T(8,128)S(1)}, f32[24,128]{1,0:T(8,128)S(1)}, u32[]{:S(2)}, u32[]{:S(2)}) collective-permute-start(f32[24,128]{1,0:T(8,128)S(1)} %get-tuple-element.55), channel_id=1, source_target_pairs={{0,1},{1,0},{2,3},{3,2},{4,5},{5,4},{6,7},{7,6},{8,9},{9,8},{10,11... | collective-permute-start | bytes 36872 | tf_op jit(solution)/shard_map/ppermute | solution.py:287
  50.2 4.6 %collective-permute-start.23 = (f32[24,128]{1,0:T(8,128)S(1)}, f32[24,128]{1,0:T(8,128)S(1)}, u32[]{:S(2)}, u32[]{:S(2)}) collective-permute-start(f32[24,128]{1,0:T(8,128)S(1)} %get-tuple-element.55), channel_id=1, source_target_pairs={{0,3},{1,2},{2,1},{3,0},{4,7},{5,6},{6,5},{7,4},{8,11},{9,10},{10,... | collective-permute-start | bytes 36872 | tf_op jit(solution)/shard_map/ppermute | solution.py:287

commit v3 on v2

--- a/solution.py
+++ b/solution.py
@@ -285,9 +285,12 @@
     x0, x1, y0, y1, zz = sends
     def swap(v, axis, odd):
         return lax.ppermute(v, axis, pairs(lax.axis_size(axis), odd))
-    z = swap(zz, "wa", 0), swap(zz, "wa", 1)
+    x = swap(x0, "gx", 0), swap(x1, "gx", 1)
     y = swap(y0, "gy", 0), swap(y1, "gy", 1)
-    x = swap(x0, "gx", 0), swap(x1, "gx", 1)
+    far = swap(zz, "wa", 1)
+    zz, first = lax.optimization_barrier((zz, x[0]))
+    x = first, x[1]
+    z = swap(zz, "wa", 0), far
     return (*x, *y, *z)
 
 

time: 78.9 us -> 74.2 us (0.940)
  waiting for transfers between devices: 8.1 us -> 4.17 us
  starting transfers between devices: 39.1 us -> 37.7 us
    ppermute x24, waiting for transfers between devices: 8.1 us -> 4.17 us  [swap(): return lax.ppermute(v, axis, pairs(lax.axis_size(axis), odd))]
    ppermute x24, starting transfers between devices: 39.1 us -> 37.7 us  [swap(): return lax.ppermute(v, axis, pairs(lax.axis_size(axis), odd))]
  transfers between devices with their start and end apart: 24 -> 24, of which waited for: 8 -> 4; matrix products, arithmetic and copies ran while one was open for 0% -> 0% of each run, Pallas kernels for 3% -> 3%
where the time goes in v3:
time: 74.2 us; the launch traced here: 74 us
  starting transfers between devices  37.7 us (51%)
  blocking collectives  22.6 us (30%)
  Pallas kernels  6.59 us (9%)
  waiting for transfers between devices  4.17 us (6%)
  local copies, waits for them, and re-layouts  2.14 us (3%)
  between operations  0.84 us (1%)
    ppermute x24, starting transfers between devices, swap(): return lax.ppermute(v, axis, pairs(lax.axis_size(axis), odd))  37.7 us
    all_to_all x1, blocking collectives, local(): got = lax.all_to_all(slots.reshape(256, 1, NZ), AXES, 0, 0).reshape(256, NZ)  22.6 us
    pallas_call x11, Pallas kernels, run(): pl.pallas_call(body, out_shape=shapes, in_specs=[VMEM] * len(args), out_s...  6.59 us
    ppermute x24, waiting for transfers between devices, swap(): return lax.ppermute(v, axis, pairs(lax.axis_size(axis), odd))  4.17 us
    unnamed x18, local copies, waits for them, and re-layouts  2.14 us
  transfers between devices with their start and end apart: 24, of which 4 were waited for; matrix products, arithmetic and copies ran while one was open for 0% of the time, Pallas kernels for 3%

profile of v3, /device:TPU:1, one launch (start us, length us, event | category | flops | bytes accessed | tf_op | source)
XLA Modules:
  0.0 74.0 jit_solution(9558038502212755469)
XLA Ops:
  0.6 0.0 copy-start
  0.6 1.1 %copy-done = f32[12,8,16,128]{3,2,1,0:T(8,128)S(1)} copy-done((f32[12,8,16,128]{3,2,1,0:T(8,128)S(1)}, f32[12,8,16,128]{3,2,1,0:T(8,128)}, u32[]{:S(2)}) %copy-start) | copy-done | bytes 786456
  1.8 1.0 %copy-done.4 = f32[5,8,16,128]{3,2,1,0:T(8,128)S(1)} copy-done((f32[5,8,16,128]{3,2,1,0:T(8,128)S(1)}, f32[5,8,16,128]{3,2,1,0:T(8,128)}, u32[]{:S(2)}) %copy-start.4) | copy-done | bytes 327704
  2.7 0.3 shard_map.96
  3.1 2.1 %collective-permute-start = (f32[5,2,16,128]{3,2,1,0:T(8,128)S(1)}, f32[5,2,16,128]{3,2,1,0:T(8,128)S(1)}, u32[]{:S(2)}, u32[]{:S(2)}) collective-permute-start(f32[5,2,16,128]{3,2,1,0:T(8,128)S(1)} %get-tuple-element.41), channel_id=1, source_target_pairs={{0,32},{32,0},{64,96},{96,64},{128,160},{160,128},{192,224},{224,1... | collective-permute-start | bytes 245768 | tf_op jit(solution)/shard_map/ppermute | solution.py:287
  5.2 2.7 %collective-permute-start.1 = (f32[5,2,16,128]{3,2,1,0:T(8,128)S(1)}, f32[5,2,16,128]{3,2,1,0:T(8,128)S(1)}, u32[]{:S(2)}, u32[]{:S(2)}) collective-permute-start(f32[5,2,16,128]{3,2,1,0:T(8,128)S(1)} %get-tuple-element.43), channel_id=1, source_target_pairs={{0,224},{32,64},{64,32},{96,128},{128,96},{160,192},{192,160},{224... | collective-permute-start | bytes 245768 | tf_op jit(solution)/shard_map/ppermute | solution.py:287
  7.9 1.6 %collective-permute-start.2 = (f32[5,2,8,128]{3,2,1,0:T(8,128)S(1)}, f32[5,2,8,128]{3,2,1,0:T(8,128)S(1)}, u32[]{:S(2)}, u32[]{:S(2)}) collective-permute-start(f32[5,2,8,128]{3,2,1,0:T(8,128)S(1)} %get-tuple-element.44), channel_id=1, source_target_pairs={{0,4},{4,0},{8,12},{12,8},{16,20},{20,16},{24,28},{28,24},{1,5},{5... | collective-permute-start | bytes 122888 | tf_op jit(solution)/shard_map/ppermute | solution.py:287
  9.5 4.7 %collective-permute-start.3 = (f32[5,2,8,128]{3,2,1,0:T(8,128)S(1)}, f32[5,2,8,128]{3,2,1,0:T(8,128)S(1)}, u32[]{:S(2)}, u32[]{:S(2)}) collective-permute-start(f32[5,2,8,128]{3,2,1,0:T(8,128)S(1)} %get-tuple-element.45), channel_id=1, source_target_pairs={{0,28},{4,8},{8,4},{12,16},{16,12},{20,24},{24,20},{28,0},{1,29},{... | collective-permute-start | bytes 122888 | tf_op jit(solution)/shard_map/ppermute | solution.py:287
  14.2 4.4 %collective-permute-start.5 = (f32[24,128]{1,0:T(8,128)S(1)}, f32[24,128]{1,0:T(8,128)S(1)}, u32[]{:S(2)}, u32[]{:S(2)}) collective-permute-start(f32[24,128]{1,0:T(8,128)S(1)} %get-tuple-element.46), channel_id=1, source_target_pairs={{0,3},{1,2},{2,1},{3,0},{4,7},{5,6},{6,5},{7,4},{8,11},{9,10},{10,... | collective-permute-start | bytes 36872 | tf_op jit(solution)/shard_map/ppermute | solution.py:287
  18.6 0.0 collective-permute-done.r0
  18.6 0.0 collective-permute-start.4
  18.6 0.4 shard_map.95.z_ref
  19.1 1.2 %collective-permute-done.5.r5 = f32[24,128]{1,0:T(8,128)S(1)} collective-permute-done((f32[24,128]{1,0:T(8,128)S(1)}, f32[24,128]{1,0:T(8,128)S(1)}, u32[]{:S(2)}, u32[]{:S(2)}) %collective-permute-start.5) | collective-permute-done | bytes 12320 | tf_op jit(solution)/shard_map/ppermute | solution.py:287
  20.3 0.0 collective-permute-done.2.r2
  20.3 0.0 collective-permute-done.3.r3
  20.3 0.0 collective-permute-done.1.r1
  20.3 0.0 collective-permute-done.4.r4
  20.4 0.0 copy-start.1
  20.4 0.7 shard_map.97
  21.1 0.0 collective-permute-start.6
  21.1 1.6 %collective-permute-start.7 = (f32[5,2,16,128]{3,2,1,0:T(8,128)S(1)}, f32[5,2,16,128]{3,2,1,0:T(8,128)S(1)}, u32[]{:S(2)}, u32[]{:S(2)}) collective-permute-start(f32[5,2,16,128]{3,2,1,0:T(8,128)S(1)} %get-tuple-element.52), channel_id=1, source_target_pairs={{0,224},{32,64},{64,32},{96,128},{128,96},{160,192},{192,160},{224... | collective-permute-start | bytes 245768 | tf_op jit(solution)/shard_map/ppermute | solution.py:287
  22.7 0.0 collective-permute-start.8
  22.7 1.5 %collective-permute-start.9 = (f32[5,2,8,128]{3,2,1,0:T(8,128)S(1)}, f32[5,2,8,128]{3,2,1,0:T(8,128)S(1)}, u32[]{:S(2)}, u32[]{:S(2)}) collective-permute-start(f32[5,2,8,128]{3,2,1,0:T(8,128)S(1)} %get-tuple-element.54), channel_id=1, source_target_pairs={{0,28},{4,8},{8,4},{12,16},{16,12},{20,24},{24,20},{28,0},{1,29},{... | collective-permute-start | bytes 122888 | tf_op jit(solution)/shard_map/ppermute | solution.py:287
  24.2 4.1 %collective-permute-start.11 = (f32[24,128]{1,0:T(8,128)S(1)}, f32[24,128]{1,0:T(8,128)S(1)}, u32[]{:S(2)}, u32[]{:S(2)}) collective-permute-start(f32[24,128]{1,0:T(8,128)S(1)} %get-tuple-element.55), channel_id=1, source_target_pairs={{0,3},{1,2},{2,1},{3,0},{4,7},{5,6},{6,5},{7,4},{8,11},{9,10},{10,... | collective-permute-start | bytes 36872 | tf_op jit(solution)/shard_map/ppermute | solution.py:287
  28.3 0.0 collective-permute-done.6.r0
  28.3 0.0 collective-permute-start.10
  28.3 0.4 shard_map.98.z_ref
  28.7 1.3 %collective-permute-done.11.r5 = f32[24,128]{1,0:T(8,128)S(1)} collective-permute-done((f32[24,128]{1,0:T(8,128)S(1)}, f32[24,128]{1,0:T(8,128)S(1)}, u32[]{:S(2)}, u32[]{:S(2)}) %collective-permute-start.11) | collective-permute-done | bytes 12320 | tf_op jit(solution)/shard_map/ppermute | solution.py:287
  30.1 0.0 collective-permute-done.8.r2
  30.1 0.0 collective-permute-done.9.r3
  30.1 0.0 collective-permute-done.7.r1
  30.1 0.0 collective-permute-done.10.r4
  30.1 0.7 shard_map.99
  30.8 0.0 collective-permute-start.12
  30.8 1.0 %collective-permute-start.13 = (f32[5,2,16,128]{3,2,1,0:T(8,128)S(1)}, f32[5,2,16,128]{3,2,1,0:T(8,128)S(1)}, u32[]{:S(2)}, u32[]{:S(2)}) collective-permute-start(f32[5,2,16,128]{3,2,1,0:T(8,128)S(1)} %get-tuple-element.60), channel_id=1, source_target_pairs={{0,224},{32,64},{64,32},{96,128},{128,96},{160,192},{192,160},{224... | collective-permute-start | bytes 245768 | tf_op jit(solution)/shard_map/ppermute | solution.py:287
  31.9 0.7 collective-permute-start.14
  32.6 0.3 collective-permute-start.15
  32.9 4.4 %collective-permute-start.17 = (f32[24,128]{1,0:T(8,128)S(1)}, f32[24,128]{1,0:T(8,128)S(1)}, u32[]{:S(2)}, u32[]{:S(2)}) collective-permute-start(f32[24,128]{1,0:T(8,128)S(1)} %get-tuple-element.63), channel_id=1, source_target_pairs={{0,3},{1,2},{2,1},{3,0},{4,7},{5,6},{6,5},{7,4},{8,11},{9,10},{10,... | collective-permute-start | bytes 36872 | tf_op jit(solution)/shard_map/ppermute | solution.py:287
  37.4 0.0 collective-permute-done.12.r0
  37.4 0.0 collective-permute-start.16
  37.4 0.4 shard_map.100.z_ref
  37.8 0.0 copy-start.6
  37.8 1.2 %collective-permute-done.17.r5 = f32[24,128]{1,0:T(8,128)S(1)} collective-permute-done((f32[24,128]{1,0:T(8,128)S(1)}, f32[24,128]{1,0:T(8,128)S(1)}, u32[]{:S(2)}, u32[]{:S(2)}) %collective-permute-start.17) | collective-permute-done | bytes 12320 | tf_op jit(solution)/shard_map/ppermute | solution.py:287
  39.1 0.0 collective-permute-done.14.r2
  39.1 0.0 collective-permute-done.15.r3
  39.1 0.0 collective-permute-done.16.r4
  39.1 0.0 copy-start.7
  39.1 0.0 copy-start.8
  39.1 0.7 shard_map.101
  39.8 0.0 collective-permute-start.18
  39.9 1.5 %collective-permute-start.19 = (f32[5,2,16,128]{3,2,1,0:T(8,128)S(1)}, f32[5,2,16,128]{3,2,1,0:T(8,128)S(1)}, u32[]{:S(2)}, u32[]{:S(2)}) collective-permute-start(f32[5,2,16,128]{3,2,1,0:T(8,128)S(1)} %get-tuple-element.68), channel_id=1, source_target_pairs={{0,224},{32,64},{64,32},{96,128},{128,96},{160,192},{192,160},{224... | collective-permute-start | bytes 245768 | tf_op jit(solution)/shard_map/ppermute | solution.py:287
  41.3 1.2 %collective-permute-start.20 = (f32[5,2,8,128]{3,2,1,0:T(8,128)S(1)}, f32[5,2,8,128]{3,2,1,0:T(8,128)S(1)}, u32[]{:S(2)}, u32[]{:S(2)}) collective-permute-start(f32[5,2,8,128]{3,2,1,0:T(8,128)S(1)} %get-tuple-element.69), channel_id=1, source_target_pairs={{0,4},{4,0},{8,12},{12,8},{16,20},{20,16},{24,28},{28,24},{1,5},{5... | collective-permute-start | bytes 122888 | tf_op jit(solution)/shard_map/ppermute | solution.py:287
  42.5 1.2 %collective-permute-start.21 = (f32[5,2,8,128]{3,2,1,0:T(8,128)S(1)}, f32[5,2,8,128]{3,2,1,0:T(8,128)S(1)}, u32[]{:S(2)}, u32[]{:S(2)}) collective-permute-start(f32[5,2,8,128]{3,2,1,0:T(8,128)S(1)} %get-tuple-element.70), channel_id=1, source_target_pairs={{0,28},{4,8},{8,4},{12,16},{16,12},{20,24},{24,20},{28,0},{1,29},{... | collective-permute-start | bytes 122888 | tf_op jit(solution)/shard_map/ppermute | solution.py:287
  43.7 4.4 %collective-permute-start.23 = (f32[24,128]{1,0:T(8,128)S(1)}, f32[24,128]{1,0:T(8,128)S(1)}, u32[]{:S(2)}, u32[]{:S(2)}) collective-permute-start(f32[24,128]{1,0:T(8,128)S(1)} %get-tuple-element.71), channel_id=1, source_target_pairs={{0,3},{1,2},{2,1},{3,0},{4,7},{5,6},{6,5},{7,4},{8,11},{9,10},{10,... | collective-permute-start | bytes 36872 | tf_op jit(solution)/shard_map/ppermute | solution.py:287
  48.2 0.0 collective-permute-done.18.r0
  48.2 0.0 collective-permute-start.22
  48.2 0.6 shard_map.103
  48.8 0.4 shard_map.102.z_ref
  49.2 0.3 collective-permute-done.23.r5
  49.5 0.0 collective-permute-done.19.r1
  49.5 0.0 collective-permute-done.22.r4
  49.6 1.2 %shard_map.104 = (f32[5,128,128]{2,1,0:T(8,128)}, f32[256,128]{1,0:T(8,128)S(1)}) custom-call(f32[5,128,128]{2,1,0:T(8,128)S(1)} %get-tuple-element.64.psi_ref, f32[5,128,128]{2,1,0:T(8,128)S(1)} %shard_map.102.z_ref, f32[5,2,16,128]{3,2,1,0:T(8,128)S(1)} %collective-permute-done.18.r0, f32[5,2,16,128]{3,2,1,0:T(8,128)S(1)} %collective-permute-done.19.r1, ...), custom_call_target="tpu_custom_call" | custom-call | flops 1000000 | bytes 1000000 | tf_op jit(solution)/shard_map/pallas_call | solution.py:266
  50.7 22.6 %all_to_all.5 = f32[256,1,128]{2,1,0:T(1,128)S(1)} all-to-all(f32[256,1,128]{2,1,0:T(1,128)S(1)} %bitcast.37), channel_id=1, replica_groups=mesh['gx'=8,'gy'=8,'wa'=4] {'gx','gy','wa'}, dimensions={0} | all-to-all | bytes 262144 | tf_op jit(solution)/shard_map/all_to_all | solution.py:321
  73.3 0.7 shard_map.105
  (14 shorter events, 0.0 us)
Async XLA Ops:
  0.6 1.1 %copy-start = (f32[12,8,16,128]{3,2,1,0:T(8,128)S(1)}, f32[12,8,16,128]{3,2,1,0:T(8,128)}, u32[]{:S(2)}) copy-start(f32[12,8,16,128]{3,2,1,0:T(8,128)} %param.11) | copy-start | bytes 2359300
  1.8 1.0 %copy-start.4 = (f32[5,8,16,128]{3,2,1,0:T(8,128)S(1)}, f32[5,8,16,128]{3,2,1,0:T(8,128)}, u32[]{:S(2)}) copy-start(f32[5,8,16,128]{3,2,1,0:T(8,128)} %param.8) | copy-start | bytes 983044
  3.1 17.2 %copy-start.2 = (bf16[5,5,8,16,128]{4,3,2,1,0:T(8,128)(2,1)S(1)}, bf16[5,5,8,16,128]{4,3,2,1,0:T(8,128)(2,1)}, u32[]{:S(2)}) copy-start(bf16[5,5,8,16,128]{4,3,2,1,0:T(8,128)(2,1)} %param.12) | copy-start | bytes 2457604
  3.1 15.6 %collective-permute-start = (f32[5,2,16,128]{3,2,1,0:T(8,128)S(1)}, f32[5,2,16,128]{3,2,1,0:T(8,128)S(1)}, u32[]{:S(2)}, u32[]{:S(2)}) collective-permute-start(f32[5,2,16,128]{3,2,1,0:T(8,128)S(1)} %get-tuple-element.41), channel_id=1, source_target_pairs={{0,32},{32,0},{64,96},{96,64},{128,160},{160,128},{192,224},{224,1... | collective-permute-start | bytes 245768 | tf_op jit(solution)/shard_map/ppermute | solution.py:287
  5.2 15.1 %collective-permute-start.1 = (f32[5,2,16,128]{3,2,1,0:T(8,128)S(1)}, f32[5,2,16,128]{3,2,1,0:T(8,128)S(1)}, u32[]{:S(2)}, u32[]{:S(2)}) collective-permute-start(f32[5,2,16,128]{3,2,1,0:T(8,128)S(1)} %get-tuple-element.43), channel_id=1, source_target_pairs={{0,224},{32,64},{64,32},{96,128},{128,96},{160,192},{192,160},{224... | collective-permute-start | bytes 245768 | tf_op jit(solution)/shard_map/ppermute | solution.py:287
  7.9 12.4 %collective-permute-start.2 = (f32[5,2,8,128]{3,2,1,0:T(8,128)S(1)}, f32[5,2,8,128]{3,2,1,0:T(8,128)S(1)}, u32[]{:S(2)}, u32[]{:S(2)}) collective-permute-start(f32[5,2,8,128]{3,2,1,0:T(8,128)S(1)} %get-tuple-element.44), channel_id=1, source_target_pairs={{0,4},{4,0},{8,12},{12,8},{16,20},{20,16},{24,28},{28,24},{1,5},{5... | collective-permute-start | bytes 122888 | tf_op jit(solution)/shard_map/ppermute | solution.py:287
  9.5 10.8 %collective-permute-start.3 = (f32[5,2,8,128]{3,2,1,0:T(8,128)S(1)}, f32[5,2,8,128]{3,2,1,0:T(8,128)S(1)}, u32[]{:S(2)}, u32[]{:S(2)}) collective-permute-start(f32[5,2,8,128]{3,2,1,0:T(8,128)S(1)} %get-tuple-element.45), channel_id=1, source_target_pairs={{0,28},{4,8},{8,4},{12,16},{16,12},{20,24},{24,20},{28,0},{1,29},{... | collective-permute-start | bytes 122888 | tf_op jit(solution)/shard_map/ppermute | solution.py:287
  14.2 6.1 %copy-start.3 = (f32[5,8,16,128]{3,2,1,0:T(8,128)S(1)}, f32[5,8,16,128]{3,2,1,0:T(8,128)}, u32[]{:S(2)}) copy-start(f32[5,8,16,128]{3,2,1,0:T(8,128)} %param.9) | copy-start | bytes 983044
  14.2 6.1 %copy-start.5 = (f32[8,16,128]{2,1,0:T(8,128)S(1)}, f32[8,16,128]{2,1,0:T(8,128)}, u32[]{:S(2)}) copy-start(f32[8,16,128]{2,1,0:T(8,128)} %param.10) | copy-start | bytes 196612
  14.2 6.1 %collective-permute-start.5 = (f32[24,128]{1,0:T(8,128)S(1)}, f32[24,128]{1,0:T(8,128)S(1)}, u32[]{:S(2)}, u32[]{:S(2)}) collective-permute-start(f32[24,128]{1,0:T(8,128)S(1)} %get-tuple-element.46), channel_id=1, source_target_pairs={{0,3},{1,2},{2,1},{3,0},{4,7},{5,6},{6,5},{7,4},{8,11},{9,10},{10,... | collective-permute-start | bytes 36872 | tf_op jit(solution)/shard_map/ppermute | solution.py:287
  18.6 1.7 %collective-permute-start.4 = (f32[24,128]{1,0:T(8,128)S(1)}, f32[24,128]{1,0:T(8,128)S(1)}, u32[]{:S(2)}, u32[]{:S(2)}) collective-permute-start(f32[24,128]{1,0:T(8,128)S(1)} %get-tuple-element.46), channel_id=1, source_target_pairs={{0,1},{1,0},{2,3},{3,2},{4,5},{5,4},{6,7},{7,6},{8,9},{9,8},{10,11... | collective-permute-start | bytes 36872 | tf_op jit(solution)/shard_map/ppermute | solution.py:287
  20.4 7.9 %copy-start.1 = (f32[12,8,16,128]{3,2,1,0:T(8,128)S(1)}, f32[12,8,16,128]{3,2,1,0:T(8,128)}, u32[]{:S(2)}) copy-start(f32[12,8,16,128]{3,2,1,0:T(8,128)} %param.11) | copy-start | bytes 2359300
  21.1 7.2 %collective-permute-start.6 = (f32[5,2,16,128]{3,2,1,0:T(8,128)S(1)}, f32[5,2,16,128]{3,2,1,0:T(8,128)S(1)}, u32[]{:S(2)}, u32[]{:S(2)}) collective-permute-start(f32[5,2,16,128]{3,2,1,0:T(8,128)S(1)} %get-tuple-element.50), channel_id=1, source_target_pairs={{0,32},{32,0},{64,96},{96,64},{128,160},{160,128},{192,224},{224,1... | collective-permute-start | bytes 245768 | tf_op jit(solution)/shard_map/ppermute | solution.py:287
  21.1 9.0 %collective-permute-start.7 = (f32[5,2,16,128]{3,2,1,0:T(8,128)S(1)}, f32[5,2,16,128]{3,2,1,0:T(8,128)S(1)}, u32[]{:S(2)}, u32[]{:S(2)}) collective-permute-start(f32[5,2,16,128]{3,2,1,0:T(8,128)S(1)} %get-tuple-element.52), channel_id=1, source_target_pairs={{0,224},{32,64},{64,32},{96,128},{128,96},{160,192},{192,160},{224... | collective-permute-start | bytes 245768 | tf_op jit(solution)/shard_map/ppermute | solution.py:287
  22.7 7.3 %collective-permute-start.8 = (f32[5,2,8,128]{3,2,1,0:T(8,128)S(1)}, f32[5,2,8,128]{3,2,1,0:T(8,128)S(1)}, u32[]{:S(2)}, u32[]{:S(2)}) collective-permute-start(f32[5,2,8,128]{3,2,1,0:T(8,128)S(1)} %get-tuple-element.53), channel_id=1, source_target_pairs={{0,4},{4,0},{8,12},{12,8},{16,20},{20,16},{24,28},{28,24},{1,5},{5... | collective-permute-start | bytes 122888 | tf_op jit(solution)/shard_map/ppermute | solution.py:287
  22.7 7.3 %collective-permute-start.9 = (f32[5,2,8,128]{3,2,1,0:T(8,128)S(1)}, f32[5,2,8,128]{3,2,1,0:T(8,128)S(1)}, u32[]{:S(2)}, u32[]{:S(2)}) collective-permute-start(f32[5,2,8,128]{3,2,1,0:T(8,128)S(1)} %get-tuple-element.54), channel_id=1, source_target_pairs={{0,28},{4,8},{8,4},{12,16},{16,12},{20,24},{24,20},{28,0},{1,29},{... | collective-permute-start | bytes 122888 | tf_op jit(solution)/shard_map/ppermute | solution.py:287
  24.2 5.9 %collective-permute-start.11 = (f32[24,128]{1,0:T(8,128)S(1)}, f32[24,128]{1,0:T(8,128)S(1)}, u32[]{:S(2)}, u32[]{:S(2)}) collective-permute-start(f32[24,128]{1,0:T(8,128)S(1)} %get-tuple-element.55), channel_id=1, source_target_pairs={{0,3},{1,2},{2,1},{3,0},{4,7},{5,6},{6,5},{7,4},{8,11},{9,10},{10,... | collective-permute-start | bytes 36872 | tf_op jit(solution)/shard_map/ppermute | solution.py:287
  28.3 1.8 %collective-permute-start.10 = (f32[24,128]{1,0:T(8,128)S(1)}, f32[24,128]{1,0:T(8,128)S(1)}, u32[]{:S(2)}, u32[]{:S(2)}) collective-permute-start(f32[24,128]{1,0:T(8,128)S(1)} %get-tuple-element.55), channel_id=1, source_target_pairs={{0,1},{1,0},{2,3},{3,2},{4,5},{5,4},{6,7},{7,6},{8,9},{9,8},{10,11... | collective-permute-start | bytes 36872 | tf_op jit(solution)/shard_map/ppermute | solution.py:287
  30.8 6.6 %collective-permute-start.12 = (f32[5,2,16,128]{3,2,1,0:T(8,128)S(1)}, f32[5,2,16,128]{3,2,1,0:T(8,128)S(1)}, u32[]{:S(2)}, u32[]{:S(2)}) collective-permute-start(f32[5,2,16,128]{3,2,1,0:T(8,128)S(1)} %get-tuple-element.58), channel_id=1, source_target_pairs={{0,32},{32,0},{64,96},{96,64},{128,160},{160,128},{192,224},{224,1... | collective-permute-start | bytes 245768 | tf_op jit(solution)/shard_map/ppermute | solution.py:287
  30.8 8.3 %collective-permute-start.13 = (f32[5,2,16,128]{3,2,1,0:T(8,128)S(1)}, f32[5,2,16,128]{3,2,1,0:T(8,128)S(1)}, u32[]{:S(2)}, u32[]{:S(2)}) collective-permute-start(f32[5,2,16,128]{3,2,1,0:T(8,128)S(1)} %get-tuple-element.60), channel_id=1, source_target_pairs={{0,224},{32,64},{64,32},{96,128},{128,96},{160,192},{192,160},{224... | collective-permute-start | bytes 245768 | tf_op jit(solution)/shard_map/ppermute | solution.py:287
  31.9 7.2 %collective-permute-start.14 = (f32[5,2,8,128]{3,2,1,0:T(8,128)S(1)}, f32[5,2,8,128]{3,2,1,0:T(8,128)S(1)}, u32[]{:S(2)}, u32[]{:S(2)}) collective-permute-start(f32[5,2,8,128]{3,2,1,0:T(8,128)S(1)} %get-tuple-element.61), channel_id=1, source_target_pairs={{0,4},{4,0},{8,12},{12,8},{16,20},{20,16},{24,28},{28,24},{1,5},{5... | collective-permute-start | bytes 122888 | tf_op jit(solution)/shard_map/ppermute | solution.py:287
  32.6 6.5 %collective-permute-start.15 = (f32[5,2,8,128]{3,2,1,0:T(8,128)S(1)}, f32[5,2,8,128]{3,2,1,0:T(8,128)S(1)}, u32[]{:S(2)}, u32[]{:S(2)}) collective-permute-start(f32[5,2,8,128]{3,2,1,0:T(8,128)S(1)} %get-tuple-element.62), channel_id=1, source_target_pairs={{0,28},{4,8},{8,4},{12,16},{16,12},{20,24},{24,20},{28,0},{1,29},{... | collective-permute-start | bytes 122888 | tf_op jit(solution)/shard_map/ppermute | solution.py:287
  32.9 6.1 %collective-permute-start.17 = (f32[24,128]{1,0:T(8,128)S(1)}, f32[24,128]{1,0:T(8,128)S(1)}, u32[]{:S(2)}, u32[]{:S(2)}) collective-permute-start(f32[24,128]{1,0:T(8,128)S(1)} %get-tuple-element.63), channel_id=1, source_target_pairs={{0,3},{1,2},{2,1},{3,0},{4,7},{5,6},{6,5},{7,4},{8,11},{9,10},{10,... | collective-permute-start | bytes 36872 | tf_op jit(solution)/shard_map/ppermute | solution.py:287
  37.4 1.7 %collective-permute-start.16 = (f32[24,128]{1,0:T(8,128)S(1)}, f32[24,128]{1,0:T(8,128)S(1)}, u32[]{:S(2)}, u32[]{:S(2)}) collective-permute-start(f32[24,128]{1,0:T(8,128)S(1)} %get-tuple-element.63), channel_id=1, source_target_pairs={{0,1},{1,0},{2,3},{3,2},{4,5},{5,4},{6,7},{7,6},{8,9},{9,8},{10,11... | collective-permute-start | bytes 36872 | tf_op jit(solution)/shard_map/ppermute | solution.py:287
  37.8 10.4 %copy-start.6 = (f32[3,10,8,16]{3,2,1,0:T(8,128)S(1)}, f32[3,10,8,16]{3,2,1,0:T(8,128)}, u32[]{:S(2)}) copy-start(f32[3,10,8,16]{3,2,1,0:T(8,128)} %param.13) | copy-start | bytes 46084
  39.1 9.1 %copy-start.7 = (s32[4,8,16]{2,1,0:T(8,128)S(1)}, s32[4,8,16]{2,1,0:T(8,128)}, u32[]{:S(2)}) copy-start(s32[4,8,16]{2,1,0:T(8,128)} %param.14) | copy-start | bytes 6148
  39.1 9.1 %copy-start.8 = (f32[4,8,16]{2,1,0:T(8,128)S(1)}, f32[4,8,16]{2,1,0:T(8,128)}, u32[]{:S(2)}) copy-start(f32[4,8,16]{2,1,0:T(8,128)} %param.15) | copy-start | bytes 6148
  39.8 8.3 %collective-permute-start.18 = (f32[5,2,16,128]{3,2,1,0:T(8,128)S(1)}, f32[5,2,16,128]{3,2,1,0:T(8,128)S(1)}, u32[]{:S(2)}, u32[]{:S(2)}) collective-permute-start(f32[5,2,16,128]{3,2,1,0:T(8,128)S(1)} %get-tuple-element.66), channel_id=1, source_target_pairs={{0,32},{32,0},{64,96},{96,64},{128,160},{160,128},{192,224},{224,1... | collective-permute-start | bytes 245768 | tf_op jit(solution)/shard_map/ppermute | solution.py:287
  39.9 9.7 %collective-permute-start.19 = (f32[5,2,16,128]{3,2,1,0:T(8,128)S(1)}, f32[5,2,16,128]{3,2,1,0:T(8,128)S(1)}, u32[]{:S(2)}, u32[]{:S(2)}) collective-permute-start(f32[5,2,16,128]{3,2,1,0:T(8,128)S(1)} %get-tuple-element.68), channel_id=1, source_target_pairs={{0,224},{32,64},{64,32},{96,128},{128,96},{160,192},{192,160},{224... | collective-permute-start | bytes 245768 | tf_op jit(solution)/shard_map/ppermute | solution.py:287
  41.3 8.2 %collective-permute-start.20 = (f32[5,2,8,128]{3,2,1,0:T(8,128)S(1)}, f32[5,2,8,128]{3,2,1,0:T(8,128)S(1)}, u32[]{:S(2)}, u32[]{:S(2)}) collective-permute-start(f32[5,2,8,128]{3,2,1,0:T(8,128)S(1)} %get-tuple-element.69), channel_id=1, source_target_pairs={{0,4},{4,0},{8,12},{12,8},{16,20},{20,16},{24,28},{28,24},{1,5},{5... | collective-permute-start | bytes 122888 | tf_op jit(solution)/shard_map/ppermute | solution.py:287
  42.5 7.0 %collective-permute-start.21 = (f32[5,2,8,128]{3,2,1,0:T(8,128)S(1)}, f32[5,2,8,128]{3,2,1,0:T(8,128)S(1)}, u32[]{:S(2)}, u32[]{:S(2)}) collective-permute-start(f32[5,2,8,128]{3,2,1,0:T(8,128)S(1)} %get-tuple-element.70), channel_id=1, source_target_pairs={{0,28},{4,8},{8,4},{12,16},{16,12},{20,24},{24,20},{28,0},{1,29},{... | collective-permute-start | bytes 122888 | tf_op jit(solution)/shard_map/ppermute | solution.py:287
  43.7 5.8 %collective-permute-start.23 = (f32[24,128]{1,0:T(8,128)S(1)}, f32[24,128]{1,0:T(8,128)S(1)}, u32[]{:S(2)}, u32[]{:S(2)}) collective-permute-start(f32[24,128]{1,0:T(8,128)S(1)} %get-tuple-element.71), channel_id=1, source_target_pairs={{0,3},{1,2},{2,1},{3,0},{4,7},{5,6},{6,5},{7,4},{8,11},{9,10},{10,... | collective-permute-start | bytes 36872 | tf_op jit(solution)/shard_map/ppermute | solution.py:287
  48.2 1.4 %collective-permute-start.22 = (f32[24,128]{1,0:T(8,128)S(1)}, f32[24,128]{1,0:T(8,128)S(1)}, u32[]{:S(2)}, u32[]{:S(2)}) collective-permute-start(f32[24,128]{1,0:T(8,128)S(1)} %get-tuple-element.71), channel_id=1, source_target_pairs={{0,1},{1,0},{2,3},{3,2},{4,5},{5,4},{6,7},{7,6},{8,9},{9,8},{10,11... | collective-permute-start | bytes 36872 | tf_op jit(solution)/shard_map/ppermute | solution.py:287

commit v4 on v3

--- a/solution.py
+++ b/solution.py
@@ -112,9 +112,22 @@
             x1[e, r] = jnp.where(even, low[r], high[r])
 
 
-def first_body(psi_ref, metric_ref, x0, x1, y0, y1, zz, packed_metric):
+def first_body(psi_hbm, metric_hbm, x0, x1, y0, y1, zz, packed_metric, psi_ref, metric_ref, sems):
+    copies = [
+        pltpu.make_async_copy(metric_hbm.at[8:12], metric_ref.at[8:12], sems.at[0]),
+        pltpu.make_async_copy(psi_hbm, psi_ref, sems.at[1]),
+        pltpu.make_async_copy(metric_hbm.at[4:8], metric_ref.at[4:8], sems.at[2]),
+        pltpu.make_async_copy(metric_hbm.at[0:4], metric_ref.at[0:4], sems.at[3]),
+    ]
+    for copy in copies:
+        copy.start()
+    copies[0].wait()
     pack_metric(metric_ref, packed_metric)
-    emit_sends(psi_ref, metric_ref, packed_metric, pack_edges(psi_ref), (x0, x1, y0, y1, zz))
+    copies[1].wait()
+    groups = pack_edges(psi_ref)
+    copies[2].wait()
+    copies[3].wait()
+    emit_sends(psi_ref, metric_ref, packed_metric, groups, (x0, x1, y0, y1, zz))
 
 
 def inner_body(psi_ref, metric_ref, z_ref):
@@ -223,8 +236,10 @@
 
 
 def last_body(psi_ref, z_ref, r0, r1, r2, r3, r4, r5, diag_ref, rhs_ref, jac_ref, coef_ref, weight_ref, hot_ref, low_ref,
-              new_ref, slots_ref, total_ref, high_part, low_part):
+              out_hbm, slots_ref, new_ref, total_ref, high_part, low_part, sem):
     update(psi_ref, z_ref, (r0, r1, r2, r3, r4, r5), diag_ref, rhs_ref, jac_ref, new_ref, total_ref)
+    copy = pltpu.make_async_copy(new_ref, out_hbm, sem)
+    copy.start()
     lane = iota((8, NZ), 1)
     groups = pack_edges(new_ref)
     low = low_ref[...]
@@ -245,32 +260,31 @@
             at = (slice(16 * c, 16 * c + 16), slice(NZ * s, NZ * s + NZ))
             high_part[at] = top
             low_part[at] = (w - top.astype(F32)).astype(jnp.bfloat16)
-    high_part[48:, :] = jnp.zeros((NZ - 48, 512), jnp.bfloat16)
-    low_part[48:, :] = jnp.zeros((NZ - 48, 512), jnp.bfloat16)
     hot = hot_ref[...]
     dims = (((1,), (1,)), ((), ()))
     slots_ref[...] = lax.dot_general(hot, high_part[...], dims, preferred_element_type=F32) + lax.dot_general(
         hot, low_part[...], dims, preferred_element_type=F32
     )
+    copy.wait()
 
 
 def sum_body(got_ref, out_ref):
     v = got_ref[...].sum(axis=0, keepdims=True)
-    v = jnp.broadcast_to(v, (8, NZ))
     for c in range(3):
-        out_ref[c : c + 1, :] = lane_roll(v, -16 * c)[0:1, :16]
-
-
-def run(body, args, *rest, **kw):
-    shapes = [jax.ShapeDtypeStruct(s, d) for s, d in rest[0]]
+        out_ref[c : c + 1, :] = v[:, 16 * c : 16 * c + 16]
+
+
+def run(body, args, outs, scratch=(), sems=(), far=(), far_outs=()):
+    hbm = pl.BlockSpec(memory_space=pltpu.HBM)
+    args = [pltpu.with_memory_space_constraint(v, pltpu.HBM) if i in far else v for i, v in enumerate(args)]
     return pl.pallas_call(
         body,
-        out_shape=shapes,
-        in_specs=[VMEM] * len(args),
-        out_specs=[VMEM] * len(shapes),
-        scratch_shapes=[pltpu.VMEM(s, d) for s, d in kw.get("scratch", ())],
+        out_shape=[jax.ShapeDtypeStruct(s, d) for s, d in outs],
+        in_specs=[hbm if i in far else VMEM for i in range(len(args))],
+        out_specs=[hbm if i in far_outs else VMEM for i in range(len(outs))],
+        scratch_shapes=[pltpu.VMEM(s, d) for s, d in scratch] + [pltpu.SemaphoreType.DMA(s) for s in sems],
         compiler_params=pltpu.CompilerParams(vmem_limit_bytes=24 << 20),
-        cost_estimate=pl.CostEstimate(flops=kw.get("flops", 1000000), bytes_accessed=kw.get("traffic", 1000000), transcendentals=0),
+        cost_estimate=pl.CostEstimate(flops=1000000, bytes_accessed=1000000, transcendentals=0),
     )(*args)
 
 
@@ -300,7 +314,9 @@
     diag = diag_term.reshape(ROWS, NZ)
     metric = face_metric.reshape(12, ROWS, NZ)
     jac = flux_jacobian.reshape(FIELDS * FIELDS, ROWS, NZ)
-    *sends, packed_metric = run(first_body, (psi, metric), SENDS + [((24, NZ), F32)])
+    *sends, packed_metric, psi, metric = run(
+        first_body, (psi, metric), SENDS + [((24, NZ), F32), FIELD, ((12, ROWS, NZ), F32)], sems=[(4,)], far=(0, 1)
+    )
     wall = run(
         wall_body,
         (wall_coef.reshape(30 * NX, NY), ffd_ids.reshape(4 * NX, NY), ffd_weight.reshape(4 * NX, NY)),
@@ -309,16 +325,18 @@
     for step in range(SWEEPS):
         received = exchange(sends)
         (z,) = run(inner_body, (psi, metric), [FIELD])
+        if step == 0:
+            z, wall = lax.optimization_barrier((z, wall))
         if step < SWEEPS - 1:
             psi, *sends = run(
                 middle_body, (psi, z, *received, diag, rhs, jac, metric, packed_metric), [FIELD] + SENDS, scratch=[FIELD]
             )
         else:
             psi, slots = run(
-                last_body, (psi, z, *received, diag, rhs, jac, *wall), [FIELD, ((256, NZ), F32)],
-                scratch=[FIELD, ((NZ, 512), jnp.bfloat16), ((NZ, 512), jnp.bfloat16)],
+                last_body, (psi, z, *received, diag, rhs, jac, *wall), [FIELD, ((256, 48), F32)],
+                scratch=[FIELD, FIELD, ((48, 512), jnp.bfloat16), ((48, 512), jnp.bfloat16)], sems=[()], far_outs=(0,),
             )
-    got = lax.all_to_all(slots.reshape(256, 1, NZ), AXES, 0, 0).reshape(256, NZ)
+    got = lax.all_to_all(slots.reshape(256, 1, 48), AXES, 0, 0).reshape(256, 48)
     (grad,) = run(sum_body, (got,), [((3, 16), F32)])
     return psi.reshape(adjoint_init.shape), grad
 

time: 74.2 us -> 73.3 us (0.988)
  local copies, waits for them, and re-layouts: 2.14 us -> 0.52 us
  Pallas kernels: 6.59 us -> 7.75 us
  waiting for transfers between devices: 4.17 us -> 3.33 us
    unnamed x18 -> x12, local copies, waits for them, and re-layouts: 2.14 us -> 0.52 us
    pallas_call x11, Pallas kernels: 6.59 us -> 7.75 us  [run(): pl.pallas_call(body, out_shape=[jax.ShapeDtypeStruct(s, d) for s, d in ou...]
    ppermute x24, waiting for transfers between devices: 4.17 us -> 3.33 us  [swap(): return lax.ppermute(v, axis, pairs(lax.axis_size(axis), odd))]
where the time goes in v4:
time: 73.3 us; the launch traced here: 73.1 us
  starting transfers between devices  38 us (52%)
  blocking collectives  22.6 us (31%)
  Pallas kernels  7.75 us (11%)
  waiting for transfers between devices  3.33 us (5%)
  between operations  0.82 us (1%)
    ppermute x24, starting transfers between devices, swap(): return lax.ppermute(v, axis, pairs(lax.axis_size(axis), odd))  38 us
    all_to_all x1, blocking collectives, local(): got = lax.all_to_all(slots.reshape(256, 1, 48), AXES, 0, 0).reshape(256, 48)  22.6 us
    pallas_call x11, Pallas kernels, run(): pl.pallas_call(body, out_shape=[jax.ShapeDtypeStruct(s, d) for s, d in ou...  7.75 us
    ppermute x24, waiting for transfers between devices, swap(): return lax.ppermute(v, axis, pairs(lax.axis_size(axis), odd))  3.33 us
  transfers between devices with their start and end apart: 24, of which 4 were waited for; matrix products, arithmetic and copies ran while one was open for 0% of the time, Pallas kernels for 3%

profile of v4, /device:TPU:1, one launch (start us, length us, event | category | flops | bytes accessed | tf_op | source)
XLA Modules:
  0.0 73.1 jit_solution(11785014411026219753)
XLA Ops:
  0.6 1.5 %shard_map.95 = (f32[5,2,16,128]{3,2,1,0:T(8,128)S(1)}, f32[5,2,16,128]{3,2,1,0:T(8,128)S(1)}, f32[5,2,8,128]{3,2,1,0:T(8,128)S(1)}, f32[5,2,8,128]{3,2,1,0:T(8,...) custom-call(f32[5,128,128]{2,1,0:T(8,128)} %bitcast.31, ...), custom_call_target="tpu_custom_call" | custom-call | flops 1000000 | bytes 1000000 | tf_op jit(solution)/shard_map/pallas_call | solution.py:280
  2.1 0.0 copy-start
  2.1 2.1 %collective-permute-start = (f32[5,2,16,128]{3,2,1,0:T(8,128)S(1)}, f32[5,2,16,128]{3,2,1,0:T(8,128)S(1)}, u32[]{:S(2)}, u32[]{:S(2)}) collective-permute-start(f32[5,2,16,128]{3,2,1,0:T(8,128)S(1)} %get-tuple-element.55), channel_id=1, source_target_pairs={{0,32},{32,0},{64,96},{96,64},{128,160},{160,128},{192,224},{224,1... | collective-permute-start | bytes 245768 | tf_op jit(solution)/shard_map/ppermute | solution.py:301
  4.3 2.7 %collective-permute-start.1 = (f32[5,2,16,128]{3,2,1,0:T(8,128)S(1)}, f32[5,2,16,128]{3,2,1,0:T(8,128)S(1)}, u32[]{:S(2)}, u32[]{:S(2)}) collective-permute-start(f32[5,2,16,128]{3,2,1,0:T(8,128)S(1)} %get-tuple-element.57), channel_id=1, source_target_pairs={{0,224},{32,64},{64,32},{96,128},{128,96},{160,192},{192,160},{224... | collective-permute-start | bytes 245768 | tf_op jit(solution)/shard_map/ppermute | solution.py:301
  7.0 1.6 %collective-permute-start.2 = (f32[5,2,8,128]{3,2,1,0:T(8,128)S(1)}, f32[5,2,8,128]{3,2,1,0:T(8,128)S(1)}, u32[]{:S(2)}, u32[]{:S(2)}) collective-permute-start(f32[5,2,8,128]{3,2,1,0:T(8,128)S(1)} %get-tuple-element.58), channel_id=1, source_target_pairs={{0,4},{4,0},{8,12},{12,8},{16,20},{20,16},{24,28},{28,24},{1,5},{5... | collective-permute-start | bytes 122888 | tf_op jit(solution)/shard_map/ppermute | solution.py:301
  8.6 4.7 %collective-permute-start.3 = (f32[5,2,8,128]{3,2,1,0:T(8,128)S(1)}, f32[5,2,8,128]{3,2,1,0:T(8,128)S(1)}, u32[]{:S(2)}, u32[]{:S(2)}) collective-permute-start(f32[5,2,8,128]{3,2,1,0:T(8,128)S(1)} %get-tuple-element.59), channel_id=1, source_target_pairs={{0,28},{4,8},{8,4},{12,16},{16,12},{20,24},{24,20},{28,0},{1,29},{... | collective-permute-start | bytes 122888 | tf_op jit(solution)/shard_map/ppermute | solution.py:301
  13.3 4.4 %collective-permute-start.5 = (f32[24,128]{1,0:T(8,128)S(1)}, f32[24,128]{1,0:T(8,128)S(1)}, u32[]{:S(2)}, u32[]{:S(2)}) collective-permute-start(f32[24,128]{1,0:T(8,128)S(1)} %get-tuple-element.60), channel_id=1, source_target_pairs={{0,3},{1,2},{2,1},{3,0},{4,7},{5,6},{6,5},{7,4},{8,11},{9,10},{10,... | collective-permute-start | bytes 36872 | tf_op jit(solution)/shard_map/ppermute | solution.py:301
  17.7 0.0 collective-permute-done.r0
  17.7 0.0 collective-permute-start.4
  17.7 0.0 copy-start.4
  17.7 0.0 copy-start.5
  17.7 0.0 copy-start.1
  17.7 0.4 shard_map.96.z_ref
  18.2 0.4 copy-done.3
  18.6 0.6 shard_map.97
  19.2 0.2 collective-permute-done.5.r5
  19.4 0.0 collective-permute-done.2.r2
  19.4 0.0 collective-permute-done.3.r3
  19.4 0.0 collective-permute-done.1.r1
  19.4 0.0 collective-permute-done.4.r4
  19.4 0.1 copy-done.2
  19.5 0.7 shard_map.98
  20.2 0.0 collective-permute-start.6
  20.2 1.6 %collective-permute-start.7 = (f32[5,2,16,128]{3,2,1,0:T(8,128)S(1)}, f32[5,2,16,128]{3,2,1,0:T(8,128)S(1)}, u32[]{:S(2)}, u32[]{:S(2)}) collective-permute-start(f32[5,2,16,128]{3,2,1,0:T(8,128)S(1)} %get-tuple-element.66), channel_id=1, source_target_pairs={{0,224},{32,64},{64,32},{96,128},{128,96},{160,192},{192,160},{224... | collective-permute-start | bytes 245768 | tf_op jit(solution)/shard_map/ppermute | solution.py:301
  21.8 0.0 collective-permute-start.8
  21.8 1.5 %collective-permute-start.9 = (f32[5,2,8,128]{3,2,1,0:T(8,128)S(1)}, f32[5,2,8,128]{3,2,1,0:T(8,128)S(1)}, u32[]{:S(2)}, u32[]{:S(2)}) collective-permute-start(f32[5,2,8,128]{3,2,1,0:T(8,128)S(1)} %get-tuple-element.68), channel_id=1, source_target_pairs={{0,28},{4,8},{8,4},{12,16},{16,12},{20,24},{24,20},{28,0},{1,29},{... | collective-permute-start | bytes 122888 | tf_op jit(solution)/shard_map/ppermute | solution.py:301
  23.3 4.0 %collective-permute-start.11 = (f32[24,128]{1,0:T(8,128)S(1)}, f32[24,128]{1,0:T(8,128)S(1)}, u32[]{:S(2)}, u32[]{:S(2)}) collective-permute-start(f32[24,128]{1,0:T(8,128)S(1)} %get-tuple-element.69), channel_id=1, source_target_pairs={{0,3},{1,2},{2,1},{3,0},{4,7},{5,6},{6,5},{7,4},{8,11},{9,10},{10,... | collective-permute-start | bytes 36872 | tf_op jit(solution)/shard_map/ppermute | solution.py:301
  27.3 0.0 collective-permute-done.6.r0
  27.3 0.0 collective-permute-start.10
  27.3 0.4 shard_map.99.z_ref
  27.8 0.9 %collective-permute-done.11.r5 = f32[24,128]{1,0:T(8,128)S(1)} collective-permute-done((f32[24,128]{1,0:T(8,128)S(1)}, f32[24,128]{1,0:T(8,128)S(1)}, u32[]{:S(2)}, u32[]{:S(2)}) %collective-permute-start.11) | collective-permute-done | bytes 12320 | tf_op jit(solution)/shard_map/ppermute | solution.py:301
  28.7 0.0 collective-permute-done.8.r2
  28.7 0.0 collective-permute-done.9.r3
  28.7 0.0 collective-permute-done.7.r1
  28.7 0.0 collective-permute-done.10.r4
  28.7 0.7 shard_map.100
  29.4 0.0 collective-permute-start.12
  29.5 1.4 %collective-permute-start.13 = (f32[5,2,16,128]{3,2,1,0:T(8,128)S(1)}, f32[5,2,16,128]{3,2,1,0:T(8,128)S(1)}, u32[]{:S(2)}, u32[]{:S(2)}) collective-permute-start(f32[5,2,16,128]{3,2,1,0:T(8,128)S(1)} %get-tuple-element.74), channel_id=1, source_target_pairs={{0,224},{32,64},{64,32},{96,128},{128,96},{160,192},{192,160},{224... | collective-permute-start | bytes 245768 | tf_op jit(solution)/shard_map/ppermute | solution.py:301
  30.9 0.7 %collective-permute-start.14 = (f32[5,2,8,128]{3,2,1,0:T(8,128)S(1)}, f32[5,2,8,128]{3,2,1,0:T(8,128)S(1)}, u32[]{:S(2)}, u32[]{:S(2)}) collective-permute-start(f32[5,2,8,128]{3,2,1,0:T(8,128)S(1)} %get-tuple-element.75), channel_id=1, source_target_pairs={{0,4},{4,0},{8,12},{12,8},{16,20},{20,16},{24,28},{28,24},{1,5},{5... | collective-permute-start | bytes 122888 | tf_op jit(solution)/shard_map/ppermute | solution.py:301
  31.7 0.4 collective-permute-start.15
  32.1 4.4 %collective-permute-start.17 = (f32[24,128]{1,0:T(8,128)S(1)}, f32[24,128]{1,0:T(8,128)S(1)}, u32[]{:S(2)}, u32[]{:S(2)}) collective-permute-start(f32[24,128]{1,0:T(8,128)S(1)} %get-tuple-element.77), channel_id=1, source_target_pairs={{0,3},{1,2},{2,1},{3,0},{4,7},{5,6},{6,5},{7,4},{8,11},{9,10},{10,... | collective-permute-start | bytes 36872 | tf_op jit(solution)/shard_map/ppermute | solution.py:301
  36.4 0.0 collective-permute-done.12.r0
  36.4 0.0 collective-permute-start.16
  36.4 0.4 shard_map.101.z_ref
  36.9 1.3 %collective-permute-done.17.r5 = f32[24,128]{1,0:T(8,128)S(1)} collective-permute-done((f32[24,128]{1,0:T(8,128)S(1)}, f32[24,128]{1,0:T(8,128)S(1)}, u32[]{:S(2)}, u32[]{:S(2)}) %collective-permute-start.17) | collective-permute-done | bytes 12320 | tf_op jit(solution)/shard_map/ppermute | solution.py:301
  38.1 0.0 collective-permute-done.14.r2
  38.1 0.0 collective-permute-done.15.r3
  38.1 0.0 collective-permute-done.13.r1
  38.1 0.0 collective-permute-done.16.r4
  38.1 0.7 shard_map.102
  38.8 0.0 collective-permute-start.18
  38.9 1.5 %collective-permute-start.19 = (f32[5,2,16,128]{3,2,1,0:T(8,128)S(1)}, f32[5,2,16,128]{3,2,1,0:T(8,128)S(1)}, u32[]{:S(2)}, u32[]{:S(2)}) collective-permute-start(f32[5,2,16,128]{3,2,1,0:T(8,128)S(1)} %get-tuple-element.82), channel_id=1, source_target_pairs={{0,224},{32,64},{64,32},{96,128},{128,96},{160,192},{192,160},{224... | collective-permute-start | bytes 245768 | tf_op jit(solution)/shard_map/ppermute | solution.py:301
  40.4 1.2 %collective-permute-start.20 = (f32[5,2,8,128]{3,2,1,0:T(8,128)S(1)}, f32[5,2,8,128]{3,2,1,0:T(8,128)S(1)}, u32[]{:S(2)}, u32[]{:S(2)}) collective-permute-start(f32[5,2,8,128]{3,2,1,0:T(8,128)S(1)} %get-tuple-element.83), channel_id=1, source_target_pairs={{0,4},{4,0},{8,12},{12,8},{16,20},{20,16},{24,28},{28,24},{1,5},{5... | collective-permute-start | bytes 122888 | tf_op jit(solution)/shard_map/ppermute | solution.py:301
  41.6 1.2 %collective-permute-start.21 = (f32[5,2,8,128]{3,2,1,0:T(8,128)S(1)}, f32[5,2,8,128]{3,2,1,0:T(8,128)S(1)}, u32[]{:S(2)}, u32[]{:S(2)}) collective-permute-start(f32[5,2,8,128]{3,2,1,0:T(8,128)S(1)} %get-tuple-element.84), channel_id=1, source_target_pairs={{0,28},{4,8},{8,4},{12,16},{16,12},{20,24},{24,20},{28,0},{1,29},{... | collective-permute-start | bytes 122888 | tf_op jit(solution)/shard_map/ppermute | solution.py:301
  42.8 4.4 %collective-permute-start.23 = (f32[24,128]{1,0:T(8,128)S(1)}, f32[24,128]{1,0:T(8,128)S(1)}, u32[]{:S(2)}, u32[]{:S(2)}) collective-permute-start(f32[24,128]{1,0:T(8,128)S(1)} %get-tuple-element.85), channel_id=1, source_target_pairs={{0,3},{1,2},{2,1},{3,0},{4,7},{5,6},{6,5},{7,4},{8,11},{9,10},{10,... | collective-permute-start | bytes 36872 | tf_op jit(solution)/shard_map/ppermute | solution.py:301
  47.2 0.0 collective-permute-done.18.r0
  47.2 0.4 shard_map.103.z_ref
  47.6 0.9 %collective-permute-done.23.r5 = f32[24,128]{1,0:T(8,128)S(1)} collective-permute-done((f32[24,128]{1,0:T(8,128)S(1)}, f32[24,128]{1,0:T(8,128)S(1)}, u32[]{:S(2)}, u32[]{:S(2)}) %collective-permute-start.23) | collective-permute-done | bytes 12320 | tf_op jit(solution)/shard_map/ppermute | solution.py:301
  48.6 0.0 collective-permute-done.20.r2
  48.6 0.0 collective-permute-done.21.r3
  48.6 0.0 collective-permute-done.19.r1
  48.6 1.2 %shard_map.104 = (f32[5,128,128]{2,1,0:T(8,128)}, f32[256,48]{1,0:T(8,128)S(1)}) custom-call(f32[5,128,128]{2,1,0:T(8,128)S(1)} %get-tuple-element.78.psi_ref, f32[5,128,128]{2,1,0:T(8,128)S(1)} %shard_map.103.z_ref, f32[5,2,16,128]{3,2,1,0:T(8,128)S(1)} %collective-permute-done.18.r0, f32[5,2,16,128]{3,2,1,0:T(8,128)S(1)} %collective-permute-done.19.r1, ...), custom_call_target="tpu_custom_call" | custom-call | flops 1000000 | bytes 1000000 | tf_op jit(solution)/shard_map/pallas_call | solution.py:280
  49.8 22.6 %all_to_all.5 = f32[256,1,48]{2,1,0:T(1,128)S(1)} all-to-all(f32[256,1,48]{2,1,0:T(1,128)S(1)} %bitcast.26), channel_id=1, replica_groups=mesh['gx'=8,'gy'=8,'wa'=4] {'gx','gy','wa'}, dimensions={0} | all-to-all | bytes 98304 | tf_op jit(solution)/shard_map/all_to_all | solution.py:339
  72.4 0.7 shard_map.105
  (8 shorter events, 0.0 us)
Async XLA Ops:
  2.1 17.3 %copy-start = (bf16[5,5,8,16,128]{4,3,2,1,0:T(8,128)(2,1)S(1)}, bf16[5,5,8,16,128]{4,3,2,1,0:T(8,128)(2,1)}, u32[]{:S(2)}) copy-start(bf16[5,5,8,16,128]{4,3,2,1,0:T(8,128)(2,1)} %param.12) | copy-start | bytes 2457604
  2.1 15.6 %collective-permute-start = (f32[5,2,16,128]{3,2,1,0:T(8,128)S(1)}, f32[5,2,16,128]{3,2,1,0:T(8,128)S(1)}, u32[]{:S(2)}, u32[]{:S(2)}) collective-permute-start(f32[5,2,16,128]{3,2,1,0:T(8,128)S(1)} %get-tuple-element.55), channel_id=1, source_target_pairs={{0,32},{32,0},{64,96},{96,64},{128,160},{160,128},{192,224},{224,1... | collective-permute-start | bytes 245768 | tf_op jit(solution)/shard_map/ppermute | solution.py:301
  4.3 15.1 %collective-permute-start.1 = (f32[5,2,16,128]{3,2,1,0:T(8,128)S(1)}, f32[5,2,16,128]{3,2,1,0:T(8,128)S(1)}, u32[]{:S(2)}, u32[]{:S(2)}) collective-permute-start(f32[5,2,16,128]{3,2,1,0:T(8,128)S(1)} %get-tuple-element.57), channel_id=1, source_target_pairs={{0,224},{32,64},{64,32},{96,128},{128,96},{160,192},{192,160},{224... | collective-permute-start | bytes 245768 | tf_op jit(solution)/shard_map/ppermute | solution.py:301
  7.0 12.4 %collective-permute-start.2 = (f32[5,2,8,128]{3,2,1,0:T(8,128)S(1)}, f32[5,2,8,128]{3,2,1,0:T(8,128)S(1)}, u32[]{:S(2)}, u32[]{:S(2)}) collective-permute-start(f32[5,2,8,128]{3,2,1,0:T(8,128)S(1)} %get-tuple-element.58), channel_id=1, source_target_pairs={{0,4},{4,0},{8,12},{12,8},{16,20},{20,16},{24,28},{28,24},{1,5},{5... | collective-permute-start | bytes 122888 | tf_op jit(solution)/shard_map/ppermute | solution.py:301
  8.6 10.8 %collective-permute-start.3 = (f32[5,2,8,128]{3,2,1,0:T(8,128)S(1)}, f32[5,2,8,128]{3,2,1,0:T(8,128)S(1)}, u32[]{:S(2)}, u32[]{:S(2)}) collective-permute-start(f32[5,2,8,128]{3,2,1,0:T(8,128)S(1)} %get-tuple-element.59), channel_id=1, source_target_pairs={{0,28},{4,8},{8,4},{12,16},{16,12},{20,24},{24,20},{28,0},{1,29},{... | collective-permute-start | bytes 122888 | tf_op jit(solution)/shard_map/ppermute | solution.py:301
  13.3 6.1 %collective-permute-start.5 = (f32[24,128]{1,0:T(8,128)S(1)}, f32[24,128]{1,0:T(8,128)S(1)}, u32[]{:S(2)}, u32[]{:S(2)}) collective-permute-start(f32[24,128]{1,0:T(8,128)S(1)} %get-tuple-element.60), channel_id=1, source_target_pairs={{0,3},{1,2},{2,1},{3,0},{4,7},{5,6},{6,5},{7,4},{8,11},{9,10},{10,... | collective-permute-start | bytes 36872 | tf_op jit(solution)/shard_map/ppermute | solution.py:301
  17.7 1.7 %collective-permute-start.4 = (f32[24,128]{1,0:T(8,128)S(1)}, f32[24,128]{1,0:T(8,128)S(1)}, u32[]{:S(2)}, u32[]{:S(2)}) collective-permute-start(f32[24,128]{1,0:T(8,128)S(1)} %get-tuple-element.60), channel_id=1, source_target_pairs={{0,1},{1,0},{2,3},{3,2},{4,5},{5,4},{6,7},{7,6},{8,9},{9,8},{10,11... | collective-permute-start | bytes 36872 | tf_op jit(solution)/shard_map/ppermute | solution.py:301
  17.7 0.9 %copy-start.3 = (f32[3,10,8,16]{3,2,1,0:T(8,128)S(1)}, f32[3,10,8,16]{3,2,1,0:T(8,128)}, u32[]{:S(2)}) copy-start(f32[3,10,8,16]{3,2,1,0:T(8,128)} %param.13) | copy-start | bytes 46084
  17.7 0.9 %copy-start.4 = (s32[4,8,16]{2,1,0:T(8,128)S(1)}, s32[4,8,16]{2,1,0:T(8,128)}, u32[]{:S(2)}) copy-start(s32[4,8,16]{2,1,0:T(8,128)} %param.14) | copy-start | bytes 6148
  17.7 0.9 %copy-start.5 = (f32[4,8,16]{2,1,0:T(8,128)S(1)}, f32[4,8,16]{2,1,0:T(8,128)}, u32[]{:S(2)}) copy-start(f32[4,8,16]{2,1,0:T(8,128)} %param.15) | copy-start | bytes 6148
  17.7 1.7 %copy-start.1 = (f32[5,8,16,128]{3,2,1,0:T(8,128)S(1)}, f32[5,8,16,128]{3,2,1,0:T(8,128)}, u32[]{:S(2)}) copy-start(f32[5,8,16,128]{3,2,1,0:T(8,128)} %param.9) | copy-start | bytes 983044
  18.6 0.9 %copy-start.2 = (f32[8,16,128]{2,1,0:T(8,128)S(1)}, f32[8,16,128]{2,1,0:T(8,128)}, u32[]{:S(2)}) copy-start(f32[8,16,128]{2,1,0:T(8,128)} %param.10) | copy-start | bytes 196612
  20.2 7.2 %collective-permute-start.6 = (f32[5,2,16,128]{3,2,1,0:T(8,128)S(1)}, f32[5,2,16,128]{3,2,1,0:T(8,128)S(1)}, u32[]{:S(2)}, u32[]{:S(2)}) collective-permute-start(f32[5,2,16,128]{3,2,1,0:T(8,128)S(1)} %get-tuple-element.64), channel_id=1, source_target_pairs={{0,32},{32,0},{64,96},{96,64},{128,160},{160,128},{192,224},{224,1... | collective-permute-start | bytes 245768 | tf_op jit(solution)/shard_map/ppermute | solution.py:301
  20.2 8.5 %collective-permute-start.7 = (f32[5,2,16,128]{3,2,1,0:T(8,128)S(1)}, f32[5,2,16,128]{3,2,1,0:T(8,128)S(1)}, u32[]{:S(2)}, u32[]{:S(2)}) collective-permute-start(f32[5,2,16,128]{3,2,1,0:T(8,128)S(1)} %get-tuple-element.66), channel_id=1, source_target_pairs={{0,224},{32,64},{64,32},{96,128},{128,96},{160,192},{192,160},{224... | collective-permute-start | bytes 245768 | tf_op jit(solution)/shard_map/ppermute | solution.py:301
  21.8 6.9 %collective-permute-start.8 = (f32[5,2,8,128]{3,2,1,0:T(8,128)S(1)}, f32[5,2,8,128]{3,2,1,0:T(8,128)S(1)}, u32[]{:S(2)}, u32[]{:S(2)}) collective-permute-start(f32[5,2,8,128]{3,2,1,0:T(8,128)S(1)} %get-tuple-element.67), channel_id=1, source_target_pairs={{0,4},{4,0},{8,12},{12,8},{16,20},{20,16},{24,28},{28,24},{1,5},{5... | collective-permute-start | bytes 122888 | tf_op jit(solution)/shard_map/ppermute | solution.py:301
  21.8 6.9 %collective-permute-start.9 = (f32[5,2,8,128]{3,2,1,0:T(8,128)S(1)}, f32[5,2,8,128]{3,2,1,0:T(8,128)S(1)}, u32[]{:S(2)}, u32[]{:S(2)}) collective-permute-start(f32[5,2,8,128]{3,2,1,0:T(8,128)S(1)} %get-tuple-element.68), channel_id=1, source_target_pairs={{0,28},{4,8},{8,4},{12,16},{16,12},{20,24},{24,20},{28,0},{1,29},{... | collective-permute-start | bytes 122888 | tf_op jit(solution)/shard_map/ppermute | solution.py:301
  23.3 5.4 %collective-permute-start.11 = (f32[24,128]{1,0:T(8,128)S(1)}, f32[24,128]{1,0:T(8,128)S(1)}, u32[]{:S(2)}, u32[]{:S(2)}) collective-permute-start(f32[24,128]{1,0:T(8,128)S(1)} %get-tuple-element.69), channel_id=1, source_target_pairs={{0,3},{1,2},{2,1},{3,0},{4,7},{5,6},{6,5},{7,4},{8,11},{9,10},{10,... | collective-permute-start | bytes 36872 | tf_op jit(solution)/shard_map/ppermute | solution.py:301
  27.3 1.4 %collective-permute-start.10 = (f32[24,128]{1,0:T(8,128)S(1)}, f32[24,128]{1,0:T(8,128)S(1)}, u32[]{:S(2)}, u32[]{:S(2)}) collective-permute-start(f32[24,128]{1,0:T(8,128)S(1)} %get-tuple-element.69), channel_id=1, source_target_pairs={{0,1},{1,0},{2,3},{3,2},{4,5},{5,4},{6,7},{7,6},{8,9},{9,8},{10,11... | collective-permute-start | bytes 36872 | tf_op jit(solution)/shard_map/ppermute | solution.py:301
  29.4 7.0 %collective-permute-start.12 = (f32[5,2,16,128]{3,2,1,0:T(8,128)S(1)}, f32[5,2,16,128]{3,2,1,0:T(8,128)S(1)}, u32[]{:S(2)}, u32[]{:S(2)}) collective-permute-start(f32[5,2,16,128]{3,2,1,0:T(8,128)S(1)} %get-tuple-element.72), channel_id=1, source_target_pairs={{0,32},{32,0},{64,96},{96,64},{128,160},{160,128},{192,224},{224,1... | collective-permute-start | bytes 245768 | tf_op jit(solution)/shard_map/ppermute | solution.py:301
  29.5 8.7 %collective-permute-start.13 = (f32[5,2,16,128]{3,2,1,0:T(8,128)S(1)}, f32[5,2,16,128]{3,2,1,0:T(8,128)S(1)}, u32[]{:S(2)}, u32[]{:S(2)}) collective-permute-start(f32[5,2,16,128]{3,2,1,0:T(8,128)S(1)} %get-tuple-element.74), channel_id=1, source_target_pairs={{0,224},{32,64},{64,32},{96,128},{128,96},{160,192},{192,160},{224... | collective-permute-start | bytes 245768 | tf_op jit(solution)/shard_map/ppermute | solution.py:301
  30.9 7.2 %collective-permute-start.14 = (f32[5,2,8,128]{3,2,1,0:T(8,128)S(1)}, f32[5,2,8,128]{3,2,1,0:T(8,128)S(1)}, u32[]{:S(2)}, u32[]{:S(2)}) collective-permute-start(f32[5,2,8,128]{3,2,1,0:T(8,128)S(1)} %get-tuple-element.75), channel_id=1, source_target_pairs={{0,4},{4,0},{8,12},{12,8},{16,20},{20,16},{24,28},{28,24},{1,5},{5... | collective-permute-start | bytes 122888 | tf_op jit(solution)/shard_map/ppermute | solution.py:301
  31.7 6.5 %collective-permute-start.15 = (f32[5,2,8,128]{3,2,1,0:T(8,128)S(1)}, f32[5,2,8,128]{3,2,1,0:T(8,128)S(1)}, u32[]{:S(2)}, u32[]{:S(2)}) collective-permute-start(f32[5,2,8,128]{3,2,1,0:T(8,128)S(1)} %get-tuple-element.76), channel_id=1, source_target_pairs={{0,28},{4,8},{8,4},{12,16},{16,12},{20,24},{24,20},{28,0},{1,29},{... | collective-permute-start | bytes 122888 | tf_op jit(solution)/shard_map/ppermute | solution.py:301
  32.1 6.0 %collective-permute-start.17 = (f32[24,128]{1,0:T(8,128)S(1)}, f32[24,128]{1,0:T(8,128)S(1)}, u32[]{:S(2)}, u32[]{:S(2)}) collective-permute-start(f32[24,128]{1,0:T(8,128)S(1)} %get-tuple-element.77), channel_id=1, source_target_pairs={{0,3},{1,2},{2,1},{3,0},{4,7},{5,6},{6,5},{7,4},{8,11},{9,10},{10,... | collective-permute-start | bytes 36872 | tf_op jit(solution)/shard_map/ppermute | solution.py:301
  36.4 1.7 %collective-permute-start.16 = (f32[24,128]{1,0:T(8,128)S(1)}, f32[24,128]{1,0:T(8,128)S(1)}, u32[]{:S(2)}, u32[]{:S(2)}) collective-permute-start(f32[24,128]{1,0:T(8,128)S(1)} %get-tuple-element.77), channel_id=1, source_target_pairs={{0,1},{1,0},{2,3},{3,2},{4,5},{5,4},{6,7},{7,6},{8,9},{9,8},{10,11... | collective-permute-start | bytes 36872 | tf_op jit(solution)/shard_map/ppermute | solution.py:301
  38.8 8.3 %collective-permute-start.18 = (f32[5,2,16,128]{3,2,1,0:T(8,128)S(1)}, f32[5,2,16,128]{3,2,1,0:T(8,128)S(1)}, u32[]{:S(2)}, u32[]{:S(2)}) collective-permute-start(f32[5,2,16,128]{3,2,1,0:T(8,128)S(1)} %get-tuple-element.80), channel_id=1, source_target_pairs={{0,32},{32,0},{64,96},{96,64},{128,160},{160,128},{192,224},{224,1... | collective-permute-start | bytes 245768 | tf_op jit(solution)/shard_map/ppermute | solution.py:301
  38.9 9.7 %collective-permute-start.19 = (f32[5,2,16,128]{3,2,1,0:T(8,128)S(1)}, f32[5,2,16,128]{3,2,1,0:T(8,128)S(1)}, u32[]{:S(2)}, u32[]{:S(2)}) collective-permute-start(f32[5,2,16,128]{3,2,1,0:T(8,128)S(1)} %get-tuple-element.82), channel_id=1, source_target_pairs={{0,224},{32,64},{64,32},{96,128},{128,96},{160,192},{192,160},{224... | collective-permute-start | bytes 245768 | tf_op jit(solution)/shard_map/ppermute | solution.py:301
  40.4 8.2 %collective-permute-start.20 = (f32[5,2,8,128]{3,2,1,0:T(8,128)S(1)}, f32[5,2,8,128]{3,2,1,0:T(8,128)S(1)}, u32[]{:S(2)}, u32[]{:S(2)}) collective-permute-start(f32[5,2,8,128]{3,2,1,0:T(8,128)S(1)} %get-tuple-element.83), channel_id=1, source_target_pairs={{0,4},{4,0},{8,12},{12,8},{16,20},{20,16},{24,28},{28,24},{1,5},{5... | collective-permute-start | bytes 122888 | tf_op jit(solution)/shard_map/ppermute | solution.py:301
  41.6 7.0 %collective-permute-start.21 = (f32[5,2,8,128]{3,2,1,0:T(8,128)S(1)}, f32[5,2,8,128]{3,2,1,0:T(8,128)S(1)}, u32[]{:S(2)}, u32[]{:S(2)}) collective-permute-start(f32[5,2,8,128]{3,2,1,0:T(8,128)S(1)} %get-tuple-element.84), channel_id=1, source_target_pairs={{0,28},{4,8},{8,4},{12,16},{16,12},{20,24},{24,20},{28,0},{1,29},{... | collective-permute-start | bytes 122888 | tf_op jit(solution)/shard_map/ppermute | solution.py:301
  42.8 5.8 %collective-permute-start.23 = (f32[24,128]{1,0:T(8,128)S(1)}, f32[24,128]{1,0:T(8,128)S(1)}, u32[]{:S(2)}, u32[]{:S(2)}) collective-permute-start(f32[24,128]{1,0:T(8,128)S(1)} %get-tuple-element.85), channel_id=1, source_target_pairs={{0,3},{1,2},{2,1},{3,0},{4,7},{5,6},{6,5},{7,4},{8,11},{9,10},{10,... | collective-permute-start | bytes 36872 | tf_op jit(solution)/shard_map/ppermute | solution.py:301
  47.2 1.4 %collective-permute-start.22 = (f32[24,128]{1,0:T(8,128)S(1)}, f32[24,128]{1,0:T(8,128)S(1)}, u32[]{:S(2)}, u32[]{:S(2)}) collective-permute-start(f32[24,128]{1,0:T(8,128)S(1)} %get-tuple-element.85), channel_id=1, source_target_pairs={{0,1},{1,0},{2,3},{3,2},{4,5},{5,4},{6,7},{7,6},{8,9},{9,8},{10,11... | collective-permute-start | bytes 36872 | tf_op jit(solution)/shard_map/ppermute | solution.py:301

commit v5 on v4

--- a/solution.py
+++ b/solution.py
@@ -10,6 +10,7 @@
 AXES = ("gx", "gy", "wa")
 FIELDS, NX, NY, NZ = 5, 8, 16, 128
 ROWS = NX * NY
+SLOTS, SLOT = 128, 32
 F32 = jnp.float32
 VMEM = pl.BlockSpec(memory_space=pltpu.VMEM)
 
@@ -227,11 +228,11 @@
     on = jnp.where(lax.axis_index("wa") == 0, 1.0, 0.0)
     weight_out[...] = halves(packed(weight_ref[...], chooser)) * on
     ids = halves(packed(ids_ref[...].astype(F32), chooser)).astype(jnp.int32)
-    low_out[...] = ids % 16
-    owner = ids // 16
-    slot = iota((256, NZ), 0)
+    low_out[...] = ids % SLOT
+    owner = ids // SLOT
+    slot = iota((SLOTS, NZ), 0)
     for s in range(4):
-        hit = slot == jnp.broadcast_to(owner[s : s + 1, :], (256, NZ))
+        hit = slot == jnp.broadcast_to(owner[s : s + 1, :], (SLOTS, NZ))
         hot_out[:, NZ * s : NZ * s + NZ] = jnp.where(hit, 1.0, 0.0).astype(jnp.bfloat16)
 
 
@@ -243,7 +244,7 @@
     lane = iota((8, NZ), 1)
     groups = pack_edges(new_ref)
     low = low_ref[...]
-    point = iota((16, NZ), 0)
+    point = iota((SLOT, NZ), 0)
     for c in range(3):
         v = coef_ref[c, 0:8, :] * groups[0]
         for g in range(1, len(groups)):
@@ -254,10 +255,10 @@
         v = v + lane_roll(v, -2)
         v = jnp.where(lane < 64, v, row_roll(v, 4)) * weight_ref[...]
         for s in range(4):
-            here = point == jnp.broadcast_to(low[s : s + 1, :], (16, NZ))
-            w = jnp.where(here, jnp.broadcast_to(v[s : s + 1, :], (16, NZ)), 0.0)
+            here = point == jnp.broadcast_to(low[s : s + 1, :], (SLOT, NZ))
+            w = jnp.where(here, jnp.broadcast_to(v[s : s + 1, :], (SLOT, NZ)), 0.0)
             top = w.astype(jnp.bfloat16)
-            at = (slice(16 * c, 16 * c + 16), slice(NZ * s, NZ * s + NZ))
+            at = (slice(SLOT * c, SLOT * c + SLOT), slice(NZ * s, NZ * s + NZ))
             high_part[at] = top
             low_part[at] = (w - top.astype(F32)).astype(jnp.bfloat16)
     hot = hot_ref[...]
@@ -269,9 +270,15 @@
 
 
 def sum_body(got_ref, out_ref):
-    v = got_ref[...].sum(axis=0, keepdims=True)
+    out_ref[...] = jnp.broadcast_to(got_ref[...].sum(axis=0, keepdims=True), out_ref.shape)
+
+
+def pick_body(own_ref, other_ref, out_ref):
+    own, other = own_ref[0:1, :], other_ref[0:1, :]
+    even = is_even("wa")
     for c in range(3):
-        out_ref[c : c + 1, :] = v[:, 16 * c : 16 * c + 16]
+        at = SLOT * c
+        out_ref[c : c + 1, :] = jnp.where(even, own[:, at : at + SLOT // 2], other[:, at + SLOT // 2 : at + SLOT])
 
 
 def run(body, args, outs, scratch=(), sems=(), far=(), far_outs=()):
@@ -320,7 +327,7 @@
     wall = run(
         wall_body,
         (wall_coef.reshape(30 * NX, NY), ffd_ids.reshape(4 * NX, NY), ffd_weight.reshape(4 * NX, NY)),
-        [((3, 24, NZ), F32), ((8, NZ), F32), ((256, 512), jnp.bfloat16), ((8, NZ), jnp.int32)],
+        [((3, 24, NZ), F32), ((8, NZ), F32), ((SLOTS, 512), jnp.bfloat16), ((8, NZ), jnp.int32)],
     )
     for step in range(SWEEPS):
         received = exchange(sends)
@@ -333,11 +340,15 @@
             )
         else:
             psi, slots = run(
-                last_body, (psi, z, *received, diag, rhs, jac, *wall), [FIELD, ((256, 48), F32)],
-                scratch=[FIELD, FIELD, ((48, 512), jnp.bfloat16), ((48, 512), jnp.bfloat16)], sems=[()], far_outs=(0,),
+                last_body, (psi, z, *received, diag, rhs, jac, *wall), [FIELD, ((SLOTS, 3 * SLOT), F32)],
+                scratch=[FIELD, FIELD, ((3 * SLOT, 512), jnp.bfloat16), ((3 * SLOT, 512), jnp.bfloat16)], sems=[()], far_outs=(0,),
             )
-    got = lax.all_to_all(slots.reshape(256, 1, 48), AXES, 0, 0).reshape(256, 48)
-    (grad,) = run(sum_body, (got,), [((3, 16), F32)])
+    columns = lax.axis_size("gx") * lax.axis_size("gy")
+    groups = [[4 * i + w for i in range(columns) for w in (core, core + 2)] for core in range(2)]
+    got = lax.all_to_all(slots.reshape(SLOTS, 1, 3 * SLOT), AXES, 0, 0, axis_index_groups=groups).reshape(SLOTS, 3 * SLOT)
+    (own,) = run(sum_body, (got,), [((8, 3 * SLOT), F32)])
+    other = lax.ppermute(own, "wa", pairs(lax.axis_size("wa"), 0))
+    (grad,) = run(pick_body, (own, other), [((3, 16), F32)])
     return psi.reshape(adjoint_init.shape), grad
 
 

time: 73.3 us -> 74.5 us (1.016)
  starting transfers between devices: 38 us -> 42 us
  blocking collectives: 22.6 us -> 19 us
  waiting for transfers between devices: 3.33 us -> 4.21 us
    ppermute x0 -> x1, starting transfers between devices: none -> 4 us  [local(): other = lax.ppermute(own, 'wa', pairs(lax.axis_size('wa'), 0))]
    all_to_all x1, blocking collectives: 22.6 us -> 19 us  [local(): lax.all_to_all(slots.reshape(SLOTS, 1, 3 * SLOT), AXES, 0, 0, axis_index_...]
    ppermute x0 -> x1, waiting for transfers between devices: none -> 0.82 us  [local(): other = lax.ppermute(own, 'wa', pairs(lax.axis_size('wa'), 0))]
    pallas_call x11 -> x12, Pallas kernels: 7.75 us -> 7.7 us  [run(): pl.pallas_call(body, out_shape=[jax.ShapeDtypeStruct(s, d) for s, d in ou...]
  transfers between devices with their start and end apart: 24 -> 25, of which waited for: 4 -> 5; matrix products, arithmetic and copies ran while one was open for 0% -> 0% of each run, Pallas kernels for 3% -> 3%
where the time goes in v5:
time: 74.5 us; the launch traced here: 74.3 us
  starting transfers between devices  42 us (56%)
  blocking collectives  19 us (26%)
  Pallas kernels  7.7 us (10%)
  waiting for transfers between devices  4.21 us (6%)
  between operations  0.82 us (1%)
    ppermute x24, starting transfers between devices, swap(): return lax.ppermute(v, axis, pairs(lax.axis_size(axis), odd))  38 us
    all_to_all x1, blocking collectives, local(): lax.all_to_all(slots.reshape(SLOTS, 1, 3 * SLOT), AXES, 0, 0, axis_index_...  19 us
    pallas_call x12, Pallas kernels, run(): pl.pallas_call(body, out_shape=[jax.ShapeDtypeStruct(s, d) for s, d in ou...  7.7 us
    ppermute x1, starting transfers between devices, local(): other = lax.ppermute(own, 'wa', pairs(lax.axis_size('wa'), 0))  4 us
    ppermute x24, waiting for transfers between devices, swap(): return lax.ppermute(v, axis, pairs(lax.axis_size(axis), odd))  3.39 us
  transfers between devices with their start and end apart: 25, of which 5 were waited for; matrix products, arithmetic and copies ran while one was open for 0% of the time, Pallas kernels for 3%

profile of v5, /device:TPU:1, one launch (start us, length us, event | category | flops | bytes accessed | tf_op | source)
XLA Modules:
  0.0 74.3 jit_solution(14913491828597127514)
XLA Ops:
  0.6 1.5 %shard_map.95 = (f32[5,2,16,128]{3,2,1,0:T(8,128)S(1)}, f32[5,2,16,128]{3,2,1,0:T(8,128)S(1)}, f32[5,2,8,128]{3,2,1,0:T(8,128)S(1)}, f32[5,2,8,128]{3,2,1,0:T(8,...) custom-call(f32[5,128,128]{2,1,0:T(8,128)} %bitcast.31, ...), custom_call_target="tpu_custom_call" | custom-call | flops 1000000 | bytes 1000000 | tf_op jit(solution)/shard_map/pallas_call | solution.py:287
  2.1 0.0 copy-start
  2.1 2.1 %collective-permute-start = (f32[5,2,16,128]{3,2,1,0:T(8,128)S(1)}, f32[5,2,16,128]{3,2,1,0:T(8,128)S(1)}, u32[]{:S(2)}, u32[]{:S(2)}) collective-permute-start(f32[5,2,16,128]{3,2,1,0:T(8,128)S(1)} %get-tuple-element.55), channel_id=1, source_target_pairs={{0,32},{32,0},{64,96},{96,64},{128,160},{160,128},{192,224},{224,1... | collective-permute-start | bytes 245768 | tf_op jit(solution)/shard_map/ppermute | solution.py:308
  4.3 2.7 %collective-permute-start.1 = (f32[5,2,16,128]{3,2,1,0:T(8,128)S(1)}, f32[5,2,16,128]{3,2,1,0:T(8,128)S(1)}, u32[]{:S(2)}, u32[]{:S(2)}) collective-permute-start(f32[5,2,16,128]{3,2,1,0:T(8,128)S(1)} %get-tuple-element.57), channel_id=1, source_target_pairs={{0,224},{32,64},{64,32},{96,128},{128,96},{160,192},{192,160},{224... | collective-permute-start | bytes 245768 | tf_op jit(solution)/shard_map/ppermute | solution.py:308
  7.0 1.6 %collective-permute-start.2 = (f32[5,2,8,128]{3,2,1,0:T(8,128)S(1)}, f32[5,2,8,128]{3,2,1,0:T(8,128)S(1)}, u32[]{:S(2)}, u32[]{:S(2)}) collective-permute-start(f32[5,2,8,128]{3,2,1,0:T(8,128)S(1)} %get-tuple-element.58), channel_id=1, source_target_pairs={{0,4},{4,0},{8,12},{12,8},{16,20},{20,16},{24,28},{28,24},{1,5},{5... | collective-permute-start | bytes 122888 | tf_op jit(solution)/shard_map/ppermute | solution.py:308
  8.6 4.7 %collective-permute-start.3 = (f32[5,2,8,128]{3,2,1,0:T(8,128)S(1)}, f32[5,2,8,128]{3,2,1,0:T(8,128)S(1)}, u32[]{:S(2)}, u32[]{:S(2)}) collective-permute-start(f32[5,2,8,128]{3,2,1,0:T(8,128)S(1)} %get-tuple-element.59), channel_id=1, source_target_pairs={{0,28},{4,8},{8,4},{12,16},{16,12},{20,24},{24,20},{28,0},{1,29},{... | collective-permute-start | bytes 122888 | tf_op jit(solution)/shard_map/ppermute | solution.py:308
  13.3 4.4 %collective-permute-start.5 = (f32[24,128]{1,0:T(8,128)S(1)}, f32[24,128]{1,0:T(8,128)S(1)}, u32[]{:S(2)}, u32[]{:S(2)}) collective-permute-start(f32[24,128]{1,0:T(8,128)S(1)} %get-tuple-element.60), channel_id=1, source_target_pairs={{0,3},{1,2},{2,1},{3,0},{4,7},{5,6},{6,5},{7,4},{8,11},{9,10},{10,... | collective-permute-start | bytes 36872 | tf_op jit(solution)/shard_map/ppermute | solution.py:308
  17.7 0.0 collective-permute-done.r0
  17.7 0.0 collective-permute-start.4
  17.7 0.0 copy-start.4
  17.7 0.0 copy-start.5
  17.7 0.0 copy-start.1
  17.7 0.4 shard_map.96.z_ref
  18.2 0.4 copy-done.3
  18.6 0.5 shard_map.97
  19.1 0.2 collective-permute-done.5.r5
  19.4 0.0 collective-permute-done.2.r2
  19.4 0.0 collective-permute-done.3.r3
  19.4 0.0 collective-permute-done.1.r1
  19.4 0.0 collective-permute-done.4.r4
  19.4 0.1 copy-done.2
  19.5 0.7 shard_map.98
  20.1 0.0 collective-permute-start.6
  20.2 1.6 %collective-permute-start.7 = (f32[5,2,16,128]{3,2,1,0:T(8,128)S(1)}, f32[5,2,16,128]{3,2,1,0:T(8,128)S(1)}, u32[]{:S(2)}, u32[]{:S(2)}) collective-permute-start(f32[5,2,16,128]{3,2,1,0:T(8,128)S(1)} %get-tuple-element.66), channel_id=1, source_target_pairs={{0,224},{32,64},{64,32},{96,128},{128,96},{160,192},{192,160},{224... | collective-permute-start | bytes 245768 | tf_op jit(solution)/shard_map/ppermute | solution.py:308
  21.8 0.0 collective-permute-start.8
  21.8 1.5 %collective-permute-start.9 = (f32[5,2,8,128]{3,2,1,0:T(8,128)S(1)}, f32[5,2,8,128]{3,2,1,0:T(8,128)S(1)}, u32[]{:S(2)}, u32[]{:S(2)}) collective-permute-start(f32[5,2,8,128]{3,2,1,0:T(8,128)S(1)} %get-tuple-element.68), channel_id=1, source_target_pairs={{0,28},{4,8},{8,4},{12,16},{16,12},{20,24},{24,20},{28,0},{1,29},{... | collective-permute-start | bytes 122888 | tf_op jit(solution)/shard_map/ppermute | solution.py:308
  23.3 4.0 %collective-permute-start.11 = (f32[24,128]{1,0:T(8,128)S(1)}, f32[24,128]{1,0:T(8,128)S(1)}, u32[]{:S(2)}, u32[]{:S(2)}) collective-permute-start(f32[24,128]{1,0:T(8,128)S(1)} %get-tuple-element.69), channel_id=1, source_target_pairs={{0,3},{1,2},{2,1},{3,0},{4,7},{5,6},{6,5},{7,4},{8,11},{9,10},{10,... | collective-permute-start | bytes 36872 | tf_op jit(solution)/shard_map/ppermute | solution.py:308
  27.3 0.0 collective-permute-done.6.r0
  27.3 0.0 collective-permute-start.10
  27.3 0.4 shard_map.99.z_ref
  27.8 0.9 %collective-permute-done.11.r5 = f32[24,128]{1,0:T(8,128)S(1)} collective-permute-done((f32[24,128]{1,0:T(8,128)S(1)}, f32[24,128]{1,0:T(8,128)S(1)}, u32[]{:S(2)}, u32[]{:S(2)}) %collective-permute-start.11) | collective-permute-done | bytes 12320 | tf_op jit(solution)/shard_map/ppermute | solution.py:308
  28.7 0.0 collective-permute-done.8.r2
  28.7 0.0 collective-permute-done.9.r3
  28.7 0.0 collective-permute-done.7.r1
  28.7 0.0 collective-permute-done.10.r4
  28.7 0.7 shard_map.100
  29.4 0.0 collective-permute-start.12
  29.5 1.4 %collective-permute-start.13 = (f32[5,2,16,128]{3,2,1,0:T(8,128)S(1)}, f32[5,2,16,128]{3,2,1,0:T(8,128)S(1)}, u32[]{:S(2)}, u32[]{:S(2)}) collective-permute-start(f32[5,2,16,128]{3,2,1,0:T(8,128)S(1)} %get-tuple-element.74), channel_id=1, source_target_pairs={{0,224},{32,64},{64,32},{96,128},{128,96},{160,192},{192,160},{224... | collective-permute-start | bytes 245768 | tf_op jit(solution)/shard_map/ppermute | solution.py:308
  30.9 0.7 collective-permute-start.14
  31.7 0.4 collective-permute-start.15
  32.1 4.4 %collective-permute-start.17 = (f32[24,128]{1,0:T(8,128)S(1)}, f32[24,128]{1,0:T(8,128)S(1)}, u32[]{:S(2)}, u32[]{:S(2)}) collective-permute-start(f32[24,128]{1,0:T(8,128)S(1)} %get-tuple-element.77), channel_id=1, source_target_pairs={{0,3},{1,2},{2,1},{3,0},{4,7},{5,6},{6,5},{7,4},{8,11},{9,10},{10,... | collective-permute-start | bytes 36872 | tf_op jit(solution)/shard_map/ppermute | solution.py:308
  36.4 0.0 collective-permute-done.12.r0
  36.4 0.0 collective-permute-start.16
  36.4 0.4 shard_map.101.z_ref
  36.9 1.2 %collective-permute-done.17.r5 = f32[24,128]{1,0:T(8,128)S(1)} collective-permute-done((f32[24,128]{1,0:T(8,128)S(1)}, f32[24,128]{1,0:T(8,128)S(1)}, u32[]{:S(2)}, u32[]{:S(2)}) %collective-permute-start.17) | collective-permute-done | bytes 12320 | tf_op jit(solution)/shard_map/ppermute | solution.py:308
  38.1 0.0 collective-permute-done.14.r2
  38.1 0.0 collective-permute-done.15.r3
  38.1 0.0 collective-permute-done.13.r1
  38.1 0.7 shard_map.102
  38.8 0.0 collective-permute-start.18
  38.9 1.5 %collective-permute-start.19 = (f32[5,2,16,128]{3,2,1,0:T(8,128)S(1)}, f32[5,2,16,128]{3,2,1,0:T(8,128)S(1)}, u32[]{:S(2)}, u32[]{:S(2)}) collective-permute-start(f32[5,2,16,128]{3,2,1,0:T(8,128)S(1)} %get-tuple-element.82), channel_id=1, source_target_pairs={{0,224},{32,64},{64,32},{96,128},{128,96},{160,192},{192,160},{224... | collective-permute-start | bytes 245768 | tf_op jit(solution)/shard_map/ppermute | solution.py:308
  40.4 1.2 %collective-permute-start.20 = (f32[5,2,8,128]{3,2,1,0:T(8,128)S(1)}, f32[5,2,8,128]{3,2,1,0:T(8,128)S(1)}, u32[]{:S(2)}, u32[]{:S(2)}) collective-permute-start(f32[5,2,8,128]{3,2,1,0:T(8,128)S(1)} %get-tuple-element.83), channel_id=1, source_target_pairs={{0,4},{4,0},{8,12},{12,8},{16,20},{20,16},{24,28},{28,24},{1,5},{5... | collective-permute-start | bytes 122888 | tf_op jit(solution)/shard_map/ppermute | solution.py:308
  41.6 1.2 %collective-permute-start.21 = (f32[5,2,8,128]{3,2,1,0:T(8,128)S(1)}, f32[5,2,8,128]{3,2,1,0:T(8,128)S(1)}, u32[]{:S(2)}, u32[]{:S(2)}) collective-permute-start(f32[5,2,8,128]{3,2,1,0:T(8,128)S(1)} %get-tuple-element.84), channel_id=1, source_target_pairs={{0,28},{4,8},{8,4},{12,16},{16,12},{20,24},{24,20},{28,0},{1,29},{... | collective-permute-start | bytes 122888 | tf_op jit(solution)/shard_map/ppermute | solution.py:308
  42.8 4.4 %collective-permute-start.23 = (f32[24,128]{1,0:T(8,128)S(1)}, f32[24,128]{1,0:T(8,128)S(1)}, u32[]{:S(2)}, u32[]{:S(2)}) collective-permute-start(f32[24,128]{1,0:T(8,128)S(1)} %get-tuple-element.85), channel_id=1, source_target_pairs={{0,3},{1,2},{2,1},{3,0},{4,7},{5,6},{6,5},{7,4},{8,11},{9,10},{10,... | collective-permute-start | bytes 36872 | tf_op jit(solution)/shard_map/ppermute | solution.py:308
  47.2 0.4 shard_map.103.z_ref
  47.6 0.9 %collective-permute-done.23.r5 = f32[24,128]{1,0:T(8,128)S(1)} collective-permute-done((f32[24,128]{1,0:T(8,128)S(1)}, f32[24,128]{1,0:T(8,128)S(1)}, u32[]{:S(2)}, u32[]{:S(2)}) %collective-permute-start.23) | collective-permute-done | bytes 12320 | tf_op jit(solution)/shard_map/ppermute | solution.py:308
  48.6 0.0 collective-permute-done.20.r2
  48.6 0.0 collective-permute-done.21.r3
  48.6 0.0 collective-permute-done.19.r1
  48.6 1.2 %shard_map.104 = (f32[5,128,128]{2,1,0:T(8,128)}, f32[128,96]{1,0:T(8,128)S(1)}) custom-call(f32[5,128,128]{2,1,0:T(8,128)S(1)} %get-tuple-element.78.psi_ref, f32[5,128,128]{2,1,0:T(8,128)S(1)} %shard_map.103.z_ref, f32[5,2,16,128]{3,2,1,0:T(8,128)S(1)} %collective-permute-done.18.r0, f32[5,2,16,128]{3,2,1,0:T(8,128)S(1)} %collective-permute-done.19.r1, ...), custom_call_target="tpu_custom_call" | custom-call | flops 1000000 | bytes 1000000 | tf_op jit(solution)/shard_map/pallas_call | solution.py:287
  49.8 19.0 %all_to_all.5 = f32[128,1,96]{2,1,0:T(1,128)S(1)} all-to-all(f32[128,1,96]{2,1,0:T(1,128)S(1)} %bitcast.27), channel_id=1, replica_groups={{0,2,4,6,8,10,12,14,16,18,20,22,24,26,28,30,32,34,36,38,40,42,44,46,48,..., dimensions={0} | all-to-all | bytes 98304 | tf_op jit(solution)/shard_map/all_to_all | solution.py:348
  68.8 4.0 %collective-permute-start.24 = (f32[8,96]{1,0:T(8,128)S(1)}, f32[8,96]{1,0:T(8,128)S(1)}, u32[]{:S(2)}, u32[]{:S(2)}) collective-permute-start(f32[8,96]{1,0:T(8,128)S(1)} %shard_map.105.own_ref), channel_id=1, source_target_pairs={{0,1},{1,0},{2,3},{3,2},{4,5},{5,4},{6,7},{7,6},{8,9},{9,8},{10,11... | collective-permute-start | bytes 9224 | tf_op jit(solution)/shard_map/ppermute | solution.py:350
  72.8 0.8 %collective-permute-done.24.other_ref = f32[8,96]{1,0:T(8,128)S(1)} collective-permute-done((f32[8,96]{1,0:T(8,128)S(1)}, f32[8,96]{1,0:T(8,128)S(1)}, u32[]{:S(2)}, u32[]{:S(2)}) %collective-permute-start.24) | collective-permute-done | bytes 3104 | tf_op jit(solution)/shard_map/ppermute | solution.py:350
  73.6 0.7 shard_map.106
  (11 shorter events, 0.0 us)
Async XLA Ops:
  2.1 17.3 %copy-start = (bf16[5,5,8,16,128]{4,3,2,1,0:T(8,128)(2,1)S(1)}, bf16[5,5,8,16,128]{4,3,2,1,0:T(8,128)(2,1)}, u32[]{:S(2)}) copy-start(bf16[5,5,8,16,128]{4,3,2,1,0:T(8,128)(2,1)} %param.12) | copy-start | bytes 2457604
  2.1 15.6 %collective-permute-start = (f32[5,2,16,128]{3,2,1,0:T(8,128)S(1)}, f32[5,2,16,128]{3,2,1,0:T(8,128)S(1)}, u32[]{:S(2)}, u32[]{:S(2)}) collective-permute-start(f32[5,2,16,128]{3,2,1,0:T(8,128)S(1)} %get-tuple-element.55), channel_id=1, source_target_pairs={{0,32},{32,0},{64,96},{96,64},{128,160},{160,128},{192,224},{224,1... | collective-permute-start | bytes 245768 | tf_op jit(solution)/shard_map/ppermute | solution.py:308
  4.3 15.1 %collective-permute-start.1 = (f32[5,2,16,128]{3,2,1,0:T(8,128)S(1)}, f32[5,2,16,128]{3,2,1,0:T(8,128)S(1)}, u32[]{:S(2)}, u32[]{:S(2)}) collective-permute-start(f32[5,2,16,128]{3,2,1,0:T(8,128)S(1)} %get-tuple-element.57), channel_id=1, source_target_pairs={{0,224},{32,64},{64,32},{96,128},{128,96},{160,192},{192,160},{224... | collective-permute-start | bytes 245768 | tf_op jit(solution)/shard_map/ppermute | solution.py:308
  7.0 12.4 %collective-permute-start.2 = (f32[5,2,8,128]{3,2,1,0:T(8,128)S(1)}, f32[5,2,8,128]{3,2,1,0:T(8,128)S(1)}, u32[]{:S(2)}, u32[]{:S(2)}) collective-permute-start(f32[5,2,8,128]{3,2,1,0:T(8,128)S(1)} %get-tuple-element.58), channel_id=1, source_target_pairs={{0,4},{4,0},{8,12},{12,8},{16,20},{20,16},{24,28},{28,24},{1,5},{5... | collective-permute-start | bytes 122888 | tf_op jit(solution)/shard_map/ppermute | solution.py:308
  8.6 10.8 %collective-permute-start.3 = (f32[5,2,8,128]{3,2,1,0:T(8,128)S(1)}, f32[5,2,8,128]{3,2,1,0:T(8,128)S(1)}, u32[]{:S(2)}, u32[]{:S(2)}) collective-permute-start(f32[5,2,8,128]{3,2,1,0:T(8,128)S(1)} %get-tuple-element.59), channel_id=1, source_target_pairs={{0,28},{4,8},{8,4},{12,16},{16,12},{20,24},{24,20},{28,0},{1,29},{... | collective-permute-start | bytes 122888 | tf_op jit(solution)/shard_map/ppermute | solution.py:308
  13.3 6.1 %collective-permute-start.5 = (f32[24,128]{1,0:T(8,128)S(1)}, f32[24,128]{1,0:T(8,128)S(1)}, u32[]{:S(2)}, u32[]{:S(2)}) collective-permute-start(f32[24,128]{1,0:T(8,128)S(1)} %get-tuple-element.60), channel_id=1, source_target_pairs={{0,3},{1,2},{2,1},{3,0},{4,7},{5,6},{6,5},{7,4},{8,11},{9,10},{10,... | collective-permute-start | bytes 36872 | tf_op jit(solution)/shard_map/ppermute | solution.py:308
  17.7 1.7 %collective-permute-start.4 = (f32[24,128]{1,0:T(8,128)S(1)}, f32[24,128]{1,0:T(8,128)S(1)}, u32[]{:S(2)}, u32[]{:S(2)}) collective-permute-start(f32[24,128]{1,0:T(8,128)S(1)} %get-tuple-element.60), channel_id=1, source_target_pairs={{0,1},{1,0},{2,3},{3,2},{4,5},{5,4},{6,7},{7,6},{8,9},{9,8},{10,11... | collective-permute-start | bytes 36872 | tf_op jit(solution)/shard_map/ppermute | solution.py:308
  17.7 0.9 %copy-start.3 = (f32[3,10,8,16]{3,2,1,0:T(8,128)S(1)}, f32[3,10,8,16]{3,2,1,0:T(8,128)}, u32[]{:S(2)}) copy-start(f32[3,10,8,16]{3,2,1,0:T(8,128)} %param.13) | copy-start | bytes 46084
  17.7 0.9 %copy-start.4 = (s32[4,8,16]{2,1,0:T(8,128)S(1)}, s32[4,8,16]{2,1,0:T(8,128)}, u32[]{:S(2)}) copy-start(s32[4,8,16]{2,1,0:T(8,128)} %param.14) | copy-start | bytes 6148
  17.7 0.9 %copy-start.5 = (f32[4,8,16]{2,1,0:T(8,128)S(1)}, f32[4,8,16]{2,1,0:T(8,128)}, u32[]{:S(2)}) copy-start(f32[4,8,16]{2,1,0:T(8,128)} %param.15) | copy-start | bytes 6148
  17.7 1.7 %copy-start.1 = (f32[5,8,16,128]{3,2,1,0:T(8,128)S(1)}, f32[5,8,16,128]{3,2,1,0:T(8,128)}, u32[]{:S(2)}) copy-start(f32[5,8,16,128]{3,2,1,0:T(8,128)} %param.9) | copy-start | bytes 983044
  18.6 0.9 %copy-start.2 = (f32[8,16,128]{2,1,0:T(8,128)S(1)}, f32[8,16,128]{2,1,0:T(8,128)}, u32[]{:S(2)}) copy-start(f32[8,16,128]{2,1,0:T(8,128)} %param.10) | copy-start | bytes 196612
  20.1 7.2 %collective-permute-start.6 = (f32[5,2,16,128]{3,2,1,0:T(8,128)S(1)}, f32[5,2,16,128]{3,2,1,0:T(8,128)S(1)}, u32[]{:S(2)}, u32[]{:S(2)}) collective-permute-start(f32[5,2,16,128]{3,2,1,0:T(8,128)S(1)} %get-tuple-element.64), channel_id=1, source_target_pairs={{0,32},{32,0},{64,96},{96,64},{128,160},{160,128},{192,224},{224,1... | collective-permute-start | bytes 245768 | tf_op jit(solution)/shard_map/ppermute | solution.py:308
  20.2 8.5 %collective-permute-start.7 = (f32[5,2,16,128]{3,2,1,0:T(8,128)S(1)}, f32[5,2,16,128]{3,2,1,0:T(8,128)S(1)}, u32[]{:S(2)}, u32[]{:S(2)}) collective-permute-start(f32[5,2,16,128]{3,2,1,0:T(8,128)S(1)} %get-tuple-element.66), channel_id=1, source_target_pairs={{0,224},{32,64},{64,32},{96,128},{128,96},{160,192},{192,160},{224... | collective-permute-start | bytes 245768 | tf_op jit(solution)/shard_map/ppermute | solution.py:308
  21.8 6.9 %collective-permute-start.8 = (f32[5,2,8,128]{3,2,1,0:T(8,128)S(1)}, f32[5,2,8,128]{3,2,1,0:T(8,128)S(1)}, u32[]{:S(2)}, u32[]{:S(2)}) collective-permute-start(f32[5,2,8,128]{3,2,1,0:T(8,128)S(1)} %get-tuple-element.67), channel_id=1, source_target_pairs={{0,4},{4,0},{8,12},{12,8},{16,20},{20,16},{24,28},{28,24},{1,5},{5... | collective-permute-start | bytes 122888 | tf_op jit(solution)/shard_map/ppermute | solution.py:308
  21.8 6.9 %collective-permute-start.9 = (f32[5,2,8,128]{3,2,1,0:T(8,128)S(1)}, f32[5,2,8,128]{3,2,1,0:T(8,128)S(1)}, u32[]{:S(2)}, u32[]{:S(2)}) collective-permute-start(f32[5,2,8,128]{3,2,1,0:T(8,128)S(1)} %get-tuple-element.68), channel_id=1, source_target_pairs={{0,28},{4,8},{8,4},{12,16},{16,12},{20,24},{24,20},{28,0},{1,29},{... | collective-permute-start | bytes 122888 | tf_op jit(solution)/shard_map/ppermute | solution.py:308
  23.3 5.4 %collective-permute-start.11 = (f32[24,128]{1,0:T(8,128)S(1)}, f32[24,128]{1,0:T(8,128)S(1)}, u32[]{:S(2)}, u32[]{:S(2)}) collective-permute-start(f32[24,128]{1,0:T(8,128)S(1)} %get-tuple-element.69), channel_id=1, source_target_pairs={{0,3},{1,2},{2,1},{3,0},{4,7},{5,6},{6,5},{7,4},{8,11},{9,10},{10,... | collective-permute-start | bytes 36872 | tf_op jit(solution)/shard_map/ppermute | solution.py:308
  27.3 1.4 %collective-permute-start.10 = (f32[24,128]{1,0:T(8,128)S(1)}, f32[24,128]{1,0:T(8,128)S(1)}, u32[]{:S(2)}, u32[]{:S(2)}) collective-permute-start(f32[24,128]{1,0:T(8,128)S(1)} %get-tuple-element.69), channel_id=1, source_target_pairs={{0,1},{1,0},{2,3},{3,2},{4,5},{5,4},{6,7},{7,6},{8,9},{9,8},{10,11... | collective-permute-start | bytes 36872 | tf_op jit(solution)/shard_map/ppermute | solution.py:308
  29.4 7.0 %collective-permute-start.12 = (f32[5,2,16,128]{3,2,1,0:T(8,128)S(1)}, f32[5,2,16,128]{3,2,1,0:T(8,128)S(1)}, u32[]{:S(2)}, u32[]{:S(2)}) collective-permute-start(f32[5,2,16,128]{3,2,1,0:T(8,128)S(1)} %get-tuple-element.72), channel_id=1, source_target_pairs={{0,32},{32,0},{64,96},{96,64},{128,160},{160,128},{192,224},{224,1... | collective-permute-start | bytes 245768 | tf_op jit(solution)/shard_map/ppermute | solution.py:308
  29.5 8.7 %collective-permute-start.13 = (f32[5,2,16,128]{3,2,1,0:T(8,128)S(1)}, f32[5,2,16,128]{3,2,1,0:T(8,128)S(1)}, u32[]{:S(2)}, u32[]{:S(2)}) collective-permute-start(f32[5,2,16,128]{3,2,1,0:T(8,128)S(1)} %get-tuple-element.74), channel_id=1, source_target_pairs={{0,224},{32,64},{64,32},{96,128},{128,96},{160,192},{192,160},{224... | collective-permute-start | bytes 245768 | tf_op jit(solution)/shard_map/ppermute | solution.py:308
  30.9 7.2 %collective-permute-start.14 = (f32[5,2,8,128]{3,2,1,0:T(8,128)S(1)}, f32[5,2,8,128]{3,2,1,0:T(8,128)S(1)}, u32[]{:S(2)}, u32[]{:S(2)}) collective-permute-start(f32[5,2,8,128]{3,2,1,0:T(8,128)S(1)} %get-tuple-element.75), channel_id=1, source_target_pairs={{0,4},{4,0},{8,12},{12,8},{16,20},{20,16},{24,28},{28,24},{1,5},{5... | collective-permute-start | bytes 122888 | tf_op jit(solution)/shard_map/ppermute | solution.py:308
  31.7 6.5 %collective-permute-start.15 = (f32[5,2,8,128]{3,2,1,0:T(8,128)S(1)}, f32[5,2,8,128]{3,2,1,0:T(8,128)S(1)}, u32[]{:S(2)}, u32[]{:S(2)}) collective-permute-start(f32[5,2,8,128]{3,2,1,0:T(8,128)S(1)} %get-tuple-element.76), channel_id=1, source_target_pairs={{0,28},{4,8},{8,4},{12,16},{16,12},{20,24},{24,20},{28,0},{1,29},{... | collective-permute-start | bytes 122888 | tf_op jit(solution)/shard_map/ppermute | solution.py:308
  32.1 6.0 %collective-permute-start.17 = (f32[24,128]{1,0:T(8,128)S(1)}, f32[24,128]{1,0:T(8,128)S(1)}, u32[]{:S(2)}, u32[]{:S(2)}) collective-permute-start(f32[24,128]{1,0:T(8,128)S(1)} %get-tuple-element.77), channel_id=1, source_target_pairs={{0,3},{1,2},{2,1},{3,0},{4,7},{5,6},{6,5},{7,4},{8,11},{9,10},{10,... | collective-permute-start | bytes 36872 | tf_op jit(solution)/shard_map/ppermute | solution.py:308
  36.4 1.7 %collective-permute-start.16 = (f32[24,128]{1,0:T(8,128)S(1)}, f32[24,128]{1,0:T(8,128)S(1)}, u32[]{:S(2)}, u32[]{:S(2)}) collective-permute-start(f32[24,128]{1,0:T(8,128)S(1)} %get-tuple-element.77), channel_id=1, source_target_pairs={{0,1},{1,0},{2,3},{3,2},{4,5},{5,4},{6,7},{7,6},{8,9},{9,8},{10,11... | collective-permute-start | bytes 36872 | tf_op jit(solution)/shard_map/ppermute | solution.py:308
  38.8 8.3 %collective-permute-start.18 = (f32[5,2,16,128]{3,2,1,0:T(8,128)S(1)}, f32[5,2,16,128]{3,2,1,0:T(8,128)S(1)}, u32[]{:S(2)}, u32[]{:S(2)}) collective-permute-start(f32[5,2,16,128]{3,2,1,0:T(8,128)S(1)} %get-tuple-element.80), channel_id=1, source_target_pairs={{0,32},{32,0},{64,96},{96,64},{128,160},{160,128},{192,224},{224,1... | collective-permute-start | bytes 245768 | tf_op jit(solution)/shard_map/ppermute | solution.py:308
  38.9 9.7 %collective-permute-start.19 = (f32[5,2,16,128]{3,2,1,0:T(8,128)S(1)}, f32[5,2,16,128]{3,2,1,0:T(8,128)S(1)}, u32[]{:S(2)}, u32[]{:S(2)}) collective-permute-start(f32[5,2,16,128]{3,2,1,0:T(8,128)S(1)} %get-tuple-element.82), channel_id=1, source_target_pairs={{0,224},{32,64},{64,32},{96,128},{128,96},{160,192},{192,160},{224... | collective-permute-start | bytes 245768 | tf_op jit(solution)/shard_map/ppermute | solution.py:308
  40.4 8.2 %collective-permute-start.20 = (f32[5,2,8,128]{3,2,1,0:T(8,128)S(1)}, f32[5,2,8,128]{3,2,1,0:T(8,128)S(1)}, u32[]{:S(2)}, u32[]{:S(2)}) collective-permute-start(f32[5,2,8,128]{3,2,1,0:T(8,128)S(1)} %get-tuple-element.83), channel_id=1, source_target_pairs={{0,4},{4,0},{8,12},{12,8},{16,20},{20,16},{24,28},{28,24},{1,5},{5... | collective-permute-start | bytes 122888 | tf_op jit(solution)/shard_map/ppermute | solution.py:308
  41.6 7.0 %collective-permute-start.21 = (f32[5,2,8,128]{3,2,1,0:T(8,128)S(1)}, f32[5,2,8,128]{3,2,1,0:T(8,128)S(1)}, u32[]{:S(2)}, u32[]{:S(2)}) collective-permute-start(f32[5,2,8,128]{3,2,1,0:T(8,128)S(1)} %get-tuple-element.84), channel_id=1, source_target_pairs={{0,28},{4,8},{8,4},{12,16},{16,12},{20,24},{24,20},{28,0},{1,29},{... | collective-permute-start | bytes 122888 | tf_op jit(solution)/shard_map/ppermute | solution.py:308
  42.8 5.8 %collective-permute-start.23 = (f32[24,128]{1,0:T(8,128)S(1)}, f32[24,128]{1,0:T(8,128)S(1)}, u32[]{:S(2)}, u32[]{:S(2)}) collective-permute-start(f32[24,128]{1,0:T(8,128)S(1)} %get-tuple-element.85), channel_id=1, source_target_pairs={{0,3},{1,2},{2,1},{3,0},{4,7},{5,6},{6,5},{7,4},{8,11},{9,10},{10,... | collective-permute-start | bytes 36872 | tf_op jit(solution)/shard_map/ppermute | solution.py:308
  47.2 1.4 %collective-permute-start.22 = (f32[24,128]{1,0:T(8,128)S(1)}, f32[24,128]{1,0:T(8,128)S(1)}, u32[]{:S(2)}, u32[]{:S(2)}) collective-permute-start(f32[24,128]{1,0:T(8,128)S(1)} %get-tuple-element.85), channel_id=1, source_target_pairs={{0,1},{1,0},{2,3},{3,2},{4,5},{5,4},{6,7},{7,6},{8,9},{9,8},{10,11... | collective-permute-start | bytes 36872 | tf_op jit(solution)/shard_map/ppermute | solution.py:308
  68.8 4.8 %collective-permute-start.24 = (f32[8,96]{1,0:T(8,128)S(1)}, f32[8,96]{1,0:T(8,128)S(1)}, u32[]{:S(2)}, u32[]{:S(2)}) collective-permute-start(f32[8,96]{1,0:T(8,128)S(1)} %shard_map.105.own_ref), channel_id=1, source_target_pairs={{0,1},{1,0},{2,3},{3,2},{4,5},{5,4},{6,7},{7,6},{8,9},{9,8},{10,11... | collective-permute-start | bytes 9224 | tf_op jit(solution)/shard_map/ppermute | solution.py:350

commit v6 on v4

--- a/solution.py
+++ b/solution.py
@@ -15,10 +15,9 @@
 
 
 def pairs(count, odd):
-    table = {}
-    for i in range(0, count, 2):
-        a, b = (i + odd) % count, (i + 1 + odd) % count
-        table[a], table[b] = b, a
+    table = {i: i for i in range(count)}
+    for i in range(odd, count - 1, 2):
+        table[i], table[i + 1] = i + 1, i
     return sorted(table.items())
 
 

time: 73.3 us -> 94.4 us (1.29)
  starting transfers between devices: 38 us -> 56.6 us
  blocking collectives: 22.6 us -> 25.4 us
    ppermute x24, starting transfers between devices: 38 us -> 56.6 us  [swap(): return lax.ppermute(v, axis, pairs(lax.axis_size(axis), odd))]
    all_to_all x1, blocking collectives: 22.6 us -> 25.4 us  [local(): got = lax.all_to_all(slots.reshape(256, 1, 48), AXES, 0, 0).reshape(256, 48)]
  transfers between devices with their start and end apart: 24 -> 24, of which waited for: 4 -> 3; matrix products, arithmetic and copies ran while one was open for 0% -> 0% of each run, Pallas kernels for 3% -> 2%
where the time goes in v6:
time: 94.4 us; the launch traced here: 93.9 us
  starting transfers between devices  56.6 us (60%)
  blocking collectives  25.4 us (27%)
  Pallas kernels  7.75 us (8%)
  waiting for transfers between devices  2.5 us (3%)
  between operations  0.98 us (1%)
    ppermute x24, starting transfers between devices, swap(): return lax.ppermute(v, axis, pairs(lax.axis_size(axis), odd))  56.6 us
    all_to_all x1, blocking collectives, local(): got = lax.all_to_all(slots.reshape(256, 1, 48), AXES, 0, 0).reshape(256, 48)  25.4 us
    pallas_call x11, Pallas kernels, run(): pl.pallas_call(body, out_shape=[jax.ShapeDtypeStruct(s, d) for s, d in ou...  7.75 us
    ppermute x24, waiting for transfers between devices, swap(): return lax.ppermute(v, axis, pairs(lax.axis_size(axis), odd))  2.5 us
  transfers between devices with their start and end apart: 24, of which 3 were waited for; matrix products, arithmetic and copies ran while one was open for 0% of the time, Pallas kernels for 2%

profile of v6, /device:TPU:1, one launch (start us, length us, event | category | flops | bytes accessed | tf_op | source)
XLA Modules:
  0.0 93.9 jit_solution(2649785808726853492)
XLA Ops:
  0.6 1.5 %shard_map.95 = (f32[5,2,16,128]{3,2,1,0:T(8,128)S(1)}, f32[5,2,16,128]{3,2,1,0:T(8,128)S(1)}, f32[5,2,8,128]{3,2,1,0:T(8,128)S(1)}, f32[5,2,8,128]{3,2,1,0:T(8,...) custom-call(f32[5,128,128]{2,1,0:T(8,128)} %bitcast.31, ...), custom_call_target="tpu_custom_call" | custom-call | flops 1000000 | bytes 1000000 | tf_op jit(solution)/shard_map/pallas_call | solution.py:279
  2.1 0.0 copy-start
  2.1 2.1 %collective-permute-start = (f32[5,2,16,128]{3,2,1,0:T(8,128)S(1)}, f32[5,2,16,128]{3,2,1,0:T(8,128)S(1)}, u32[]{:S(2)}, u32[]{:S(2)}) collective-permute-start(f32[5,2,16,128]{3,2,1,0:T(8,128)S(1)} %get-tuple-element.55), channel_id=1, source_target_pairs={{0,32},{32,0},{64,96},{96,64},{128,160},{160,128},{192,224},{224,1... | collective-permute-start | bytes 245768 | tf_op jit(solution)/shard_map/ppermute | solution.py:300
  4.3 0.7 collective-permute-start.1
  4.9 1.7 %collective-permute-start.2 = (f32[5,2,8,128]{3,2,1,0:T(8,128)S(1)}, f32[5,2,8,128]{3,2,1,0:T(8,128)S(1)}, u32[]{:S(2)}, u32[]{:S(2)}) collective-permute-start(f32[5,2,8,128]{3,2,1,0:T(8,128)S(1)} %get-tuple-element.58), channel_id=1, source_target_pairs={{0,4},{4,0},{8,12},{12,8},{16,20},{20,16},{24,28},{28,24},{1,5},{5... | collective-permute-start | bytes 122888 | tf_op jit(solution)/shard_map/ppermute | solution.py:300
  6.6 0.7 collective-permute-start.3
  7.3 5.5 %collective-permute-start.5 = (f32[24,128]{1,0:T(8,128)S(1)}, f32[24,128]{1,0:T(8,128)S(1)}, u32[]{:S(2)}, u32[]{:S(2)}) collective-permute-start(f32[24,128]{1,0:T(8,128)S(1)} %get-tuple-element.60), channel_id=1, source_target_pairs={{0,0},{1,2},{2,1},{3,3},{4,4},{5,6},{6,5},{7,7},{8,8},{9,10},{10,9... | collective-permute-start | bytes 36872 | tf_op jit(solution)/shard_map/ppermute | solution.py:300
  12.8 0.0 collective-permute-done.r0
  12.8 0.1 collective-permute-start.4
  12.9 0.0 copy-start.3
  12.9 0.0 copy-start.4
  12.9 0.0 copy-start.5
  12.9 0.0 copy-start.1
  12.9 0.4 shard_map.96.z_ref
  13.4 0.4 copy-done.3
  13.8 0.6 shard_map.97
  14.4 0.0 collective-permute-done.5.r5
  14.4 0.0 collective-permute-done.2.r2
  14.4 0.0 collective-permute-done.3.r3
  14.4 0.0 collective-permute-done.1.r1
  14.4 0.0 collective-permute-done.4.r4
  14.5 0.2 copy-done.2
  14.7 0.7 shard_map.98
  15.4 3.4 %collective-permute-start.6 = (f32[5,2,16,128]{3,2,1,0:T(8,128)S(1)}, f32[5,2,16,128]{3,2,1,0:T(8,128)S(1)}, u32[]{:S(2)}, u32[]{:S(2)}) collective-permute-start(f32[5,2,16,128]{3,2,1,0:T(8,128)S(1)} %get-tuple-element.64), channel_id=1, source_target_pairs={{0,32},{32,0},{64,96},{96,64},{128,160},{160,128},{192,224},{224,1... | collective-permute-start | bytes 245768 | tf_op jit(solution)/shard_map/ppermute | solution.py:300
  18.8 0.7 collective-permute-start.7
  19.5 4.9 %collective-permute-start.8 = (f32[5,2,8,128]{3,2,1,0:T(8,128)S(1)}, f32[5,2,8,128]{3,2,1,0:T(8,128)S(1)}, u32[]{:S(2)}, u32[]{:S(2)}) collective-permute-start(f32[5,2,8,128]{3,2,1,0:T(8,128)S(1)} %get-tuple-element.67), channel_id=1, source_target_pairs={{0,4},{4,0},{8,12},{12,8},{16,20},{20,16},{24,28},{28,24},{1,5},{5... | collective-permute-start | bytes 122888 | tf_op jit(solution)/shard_map/ppermute | solution.py:300
  24.3 0.7 collective-permute-start.9
  25.0 5.9 %collective-permute-start.11 = (f32[24,128]{1,0:T(8,128)S(1)}, f32[24,128]{1,0:T(8,128)S(1)}, u32[]{:S(2)}, u32[]{:S(2)}) collective-permute-start(f32[24,128]{1,0:T(8,128)S(1)} %get-tuple-element.69), channel_id=1, source_target_pairs={{0,0},{1,2},{2,1},{3,3},{4,4},{5,6},{6,5},{7,7},{8,8},{9,10},{10,9... | collective-permute-start | bytes 36872 | tf_op jit(solution)/shard_map/ppermute | solution.py:300
  30.9 0.0 collective-permute-done.6.r0
  30.9 0.1 collective-permute-start.10
  31.0 0.4 shard_map.99.z_ref
  31.4 0.8 collective-permute-done.11.r5
  32.2 0.0 collective-permute-done.8.r2
  32.2 0.0 collective-permute-done.9.r3
  32.2 0.0 collective-permute-done.7.r1
  32.2 0.0 collective-permute-done.10.r4
  32.3 0.7 shard_map.100
  33.0 3.4 %collective-permute-start.12 = (f32[5,2,16,128]{3,2,1,0:T(8,128)S(1)}, f32[5,2,16,128]{3,2,1,0:T(8,128)S(1)}, u32[]{:S(2)}, u32[]{:S(2)}) collective-permute-start(f32[5,2,16,128]{3,2,1,0:T(8,128)S(1)} %get-tuple-element.72), channel_id=1, source_target_pairs={{0,32},{32,0},{64,96},{96,64},{128,160},{160,128},{192,224},{224,1... | collective-permute-start | bytes 245768 | tf_op jit(solution)/shard_map/ppermute | solution.py:300
  36.4 0.7 collective-permute-start.13
  37.0 5.2 %collective-permute-start.14 = (f32[5,2,8,128]{3,2,1,0:T(8,128)S(1)}, f32[5,2,8,128]{3,2,1,0:T(8,128)S(1)}, u32[]{:S(2)}, u32[]{:S(2)}) collective-permute-start(f32[5,2,8,128]{3,2,1,0:T(8,128)S(1)} %get-tuple-element.75), channel_id=1, source_target_pairs={{0,4},{4,0},{8,12},{12,8},{16,20},{20,16},{24,28},{28,24},{1,5},{5... | collective-permute-start | bytes 122888 | tf_op jit(solution)/shard_map/ppermute | solution.py:300
  42.2 0.7 collective-permute-start.15
  42.9 6.3 %collective-permute-start.17 = (f32[24,128]{1,0:T(8,128)S(1)}, f32[24,128]{1,0:T(8,128)S(1)}, u32[]{:S(2)}, u32[]{:S(2)}) collective-permute-start(f32[24,128]{1,0:T(8,128)S(1)} %get-tuple-element.77), channel_id=1, source_target_pairs={{0,0},{1,2},{2,1},{3,3},{4,4},{5,6},{6,5},{7,7},{8,8},{9,10},{10,9... | collective-permute-start | bytes 36872 | tf_op jit(solution)/shard_map/ppermute | solution.py:300
  49.2 0.0 collective-permute-done.12.r0
  49.2 0.1 collective-permute-start.16
  49.3 0.4 shard_map.101.z_ref
  49.8 0.8 collective-permute-done.17.r5
  50.6 0.0 collective-permute-done.14.r2
  50.6 0.0 collective-permute-done.15.r3
  50.6 0.0 collective-permute-done.13.r1
  50.6 0.0 collective-permute-done.16.r4
  50.6 0.7 shard_map.102
  51.3 3.1 %collective-permute-start.18 = (f32[5,2,16,128]{3,2,1,0:T(8,128)S(1)}, f32[5,2,16,128]{3,2,1,0:T(8,128)S(1)}, u32[]{:S(2)}, u32[]{:S(2)}) collective-permute-start(f32[5,2,16,128]{3,2,1,0:T(8,128)S(1)} %get-tuple-element.80), channel_id=1, source_target_pairs={{0,32},{32,0},{64,96},{96,64},{128,160},{160,128},{192,224},{224,1... | collective-permute-start | bytes 245768 | tf_op jit(solution)/shard_map/ppermute | solution.py:300
  54.5 0.7 collective-permute-start.19
  55.1 3.1 %collective-permute-start.20 = (f32[5,2,8,128]{3,2,1,0:T(8,128)S(1)}, f32[5,2,8,128]{3,2,1,0:T(8,128)S(1)}, u32[]{:S(2)}, u32[]{:S(2)}) collective-permute-start(f32[5,2,8,128]{3,2,1,0:T(8,128)S(1)} %get-tuple-element.83), channel_id=1, source_target_pairs={{0,4},{4,0},{8,12},{12,8},{16,20},{20,16},{24,28},{28,24},{1,5},{5... | collective-permute-start | bytes 122888 | tf_op jit(solution)/shard_map/ppermute | solution.py:300
  58.2 0.7 collective-permute-start.21
  58.9 6.3 %collective-permute-start.23 = (f32[24,128]{1,0:T(8,128)S(1)}, f32[24,128]{1,0:T(8,128)S(1)}, u32[]{:S(2)}, u32[]{:S(2)}) collective-permute-start(f32[24,128]{1,0:T(8,128)S(1)} %get-tuple-element.85), channel_id=1, source_target_pairs={{0,0},{1,2},{2,1},{3,3},{4,4},{5,6},{6,5},{7,7},{8,8},{9,10},{10,9... | collective-permute-start | bytes 36872 | tf_op jit(solution)/shard_map/ppermute | solution.py:300
  65.2 0.0 collective-permute-done.18.r0
  65.2 0.1 collective-permute-start.22
  65.3 0.4 shard_map.103.z_ref
  65.7 0.8 collective-permute-done.23.r5
  66.5 0.0 collective-permute-done.20.r2
  66.6 1.2 %shard_map.104 = (f32[5,128,128]{2,1,0:T(8,128)}, f32[256,48]{1,0:T(8,128)S(1)}) custom-call(f32[5,128,128]{2,1,0:T(8,128)S(1)} %get-tuple-element.78.psi_ref, f32[5,128,128]{2,1,0:T(8,128)S(1)} %shard_map.103.z_ref, f32[5,2,16,128]{3,2,1,0:T(8,128)S(1)} %collective-permute-done.18.r0, f32[5,2,16,128]{3,2,1,0:T(8,128)S(1)} %collective-permute-done.19.r1, ...), custom_call_target="tpu_custom_call" | custom-call | flops 1000000 | bytes 1000000 | tf_op jit(solution)/shard_map/pallas_call | solution.py:279
  67.8 25.4 %all_to_all.5 = f32[256,1,48]{2,1,0:T(1,128)S(1)} all-to-all(f32[256,1,48]{2,1,0:T(1,128)S(1)} %bitcast.26), channel_id=1, replica_groups=mesh['gx'=8,'gy'=8,'wa'=4] {'gx','gy','wa'}, dimensions={0} | all-to-all | bytes 98304 | tf_op jit(solution)/shard_map/all_to_all | solution.py:338
  93.2 0.7 shard_map.105
  (8 shorter events, 0.0 us)
Async XLA Ops:
  2.1 12.3 %copy-start = (bf16[5,5,8,16,128]{4,3,2,1,0:T(8,128)(2,1)S(1)}, bf16[5,5,8,16,128]{4,3,2,1,0:T(8,128)(2,1)}, u32[]{:S(2)}) copy-start(bf16[5,5,8,16,128]{4,3,2,1,0:T(8,128)(2,1)} %param.12) | copy-start | bytes 2457604
  2.1 10.7 %collective-permute-start = (f32[5,2,16,128]{3,2,1,0:T(8,128)S(1)}, f32[5,2,16,128]{3,2,1,0:T(8,128)S(1)}, u32[]{:S(2)}, u32[]{:S(2)}) collective-permute-start(f32[5,2,16,128]{3,2,1,0:T(8,128)S(1)} %get-tuple-element.55), channel_id=1, source_target_pairs={{0,32},{32,0},{64,96},{96,64},{128,160},{160,128},{192,224},{224,1... | collective-permute-start | bytes 245768 | tf_op jit(solution)/shard_map/ppermute | solution.py:300
  4.3 10.2 %collective-permute-start.1 = (f32[5,2,16,128]{3,2,1,0:T(8,128)S(1)}, f32[5,2,16,128]{3,2,1,0:T(8,128)S(1)}, u32[]{:S(2)}, u32[]{:S(2)}) collective-permute-start(f32[5,2,16,128]{3,2,1,0:T(8,128)S(1)} %get-tuple-element.57), channel_id=1, source_target_pairs={{0,0},{32,64},{64,32},{96,128},{128,96},{160,192},{192,160},{224,2... | collective-permute-start | bytes 245768 | tf_op jit(solution)/shard_map/ppermute | solution.py:300
  4.9 9.5 %collective-permute-start.2 = (f32[5,2,8,128]{3,2,1,0:T(8,128)S(1)}, f32[5,2,8,128]{3,2,1,0:T(8,128)S(1)}, u32[]{:S(2)}, u32[]{:S(2)}) collective-permute-start(f32[5,2,8,128]{3,2,1,0:T(8,128)S(1)} %get-tuple-element.58), channel_id=1, source_target_pairs={{0,4},{4,0},{8,12},{12,8},{16,20},{20,16},{24,28},{28,24},{1,5},{5... | collective-permute-start | bytes 122888 | tf_op jit(solution)/shard_map/ppermute | solution.py:300
  6.6 7.8 %collective-permute-start.3 = (f32[5,2,8,128]{3,2,1,0:T(8,128)S(1)}, f32[5,2,8,128]{3,2,1,0:T(8,128)S(1)}, u32[]{:S(2)}, u32[]{:S(2)}) collective-permute-start(f32[5,2,8,128]{3,2,1,0:T(8,128)S(1)} %get-tuple-element.59), channel_id=1, source_target_pairs={{0,0},{4,8},{8,4},{12,16},{16,12},{20,24},{24,20},{28,28},{1,1},{5... | collective-permute-start | bytes 122888 | tf_op jit(solution)/shard_map/ppermute | solution.py:300
  7.3 7.1 %collective-permute-start.5 = (f32[24,128]{1,0:T(8,128)S(1)}, f32[24,128]{1,0:T(8,128)S(1)}, u32[]{:S(2)}, u32[]{:S(2)}) collective-permute-start(f32[24,128]{1,0:T(8,128)S(1)} %get-tuple-element.60), channel_id=1, source_target_pairs={{0,0},{1,2},{2,1},{3,3},{4,4},{5,6},{6,5},{7,7},{8,8},{9,10},{10,9... | collective-permute-start | bytes 36872 | tf_op jit(solution)/shard_map/ppermute | solution.py:300
  12.8 1.6 %collective-permute-start.4 = (f32[24,128]{1,0:T(8,128)S(1)}, f32[24,128]{1,0:T(8,128)S(1)}, u32[]{:S(2)}, u32[]{:S(2)}) collective-permute-start(f32[24,128]{1,0:T(8,128)S(1)} %get-tuple-element.60), channel_id=1, source_target_pairs={{0,1},{1,0},{2,3},{3,2},{4,5},{5,4},{6,7},{7,6},{8,9},{9,8},{10,11... | collective-permute-start | bytes 36872 | tf_op jit(solution)/shard_map/ppermute | solution.py:300
  12.9 0.9 copy-start.3
  12.9 0.9 copy-start.4
  12.9 0.9 copy-start.5
  12.9 1.5 %copy-start.1 = (f32[5,8,16,128]{3,2,1,0:T(8,128)S(1)}, f32[5,8,16,128]{3,2,1,0:T(8,128)}, u32[]{:S(2)}) copy-start(f32[5,8,16,128]{3,2,1,0:T(8,128)} %param.9) | copy-start | bytes 983044
  13.8 0.9 copy-start.2
  15.4 15.5 %collective-permute-start.6 = (f32[5,2,16,128]{3,2,1,0:T(8,128)S(1)}, f32[5,2,16,128]{3,2,1,0:T(8,128)S(1)}, u32[]{:S(2)}, u32[]{:S(2)}) collective-permute-start(f32[5,2,16,128]{3,2,1,0:T(8,128)S(1)} %get-tuple-element.64), channel_id=1, source_target_pairs={{0,32},{32,0},{64,96},{96,64},{128,160},{160,128},{192,224},{224,1... | collective-permute-start | bytes 245768 | tf_op jit(solution)/shard_map/ppermute | solution.py:300
  18.8 13.4 %collective-permute-start.7 = (f32[5,2,16,128]{3,2,1,0:T(8,128)S(1)}, f32[5,2,16,128]{3,2,1,0:T(8,128)S(1)}, u32[]{:S(2)}, u32[]{:S(2)}) collective-permute-start(f32[5,2,16,128]{3,2,1,0:T(8,128)S(1)} %get-tuple-element.66), channel_id=1, source_target_pairs={{0,0},{32,64},{64,32},{96,128},{128,96},{160,192},{192,160},{224,2... | collective-permute-start | bytes 245768 | tf_op jit(solution)/shard_map/ppermute | solution.py:300
  19.5 12.8 %collective-permute-start.8 = (f32[5,2,8,128]{3,2,1,0:T(8,128)S(1)}, f32[5,2,8,128]{3,2,1,0:T(8,128)S(1)}, u32[]{:S(2)}, u32[]{:S(2)}) collective-permute-start(f32[5,2,8,128]{3,2,1,0:T(8,128)S(1)} %get-tuple-element.67), channel_id=1, source_target_pairs={{0,4},{4,0},{8,12},{12,8},{16,20},{20,16},{24,28},{28,24},{1,5},{5... | collective-permute-start | bytes 122888 | tf_op jit(solution)/shard_map/ppermute | solution.py:300
  24.3 7.9 %collective-permute-start.9 = (f32[5,2,8,128]{3,2,1,0:T(8,128)S(1)}, f32[5,2,8,128]{3,2,1,0:T(8,128)S(1)}, u32[]{:S(2)}, u32[]{:S(2)}) collective-permute-start(f32[5,2,8,128]{3,2,1,0:T(8,128)S(1)} %get-tuple-element.68), channel_id=1, source_target_pairs={{0,0},{4,8},{8,4},{12,16},{16,12},{20,24},{24,20},{28,28},{1,1},{5... | collective-permute-start | bytes 122888 | tf_op jit(solution)/shard_map/ppermute | solution.py:300
  25.0 7.2 %collective-permute-start.11 = (f32[24,128]{1,0:T(8,128)S(1)}, f32[24,128]{1,0:T(8,128)S(1)}, u32[]{:S(2)}, u32[]{:S(2)}) collective-permute-start(f32[24,128]{1,0:T(8,128)S(1)} %get-tuple-element.69), channel_id=1, source_target_pairs={{0,0},{1,2},{2,1},{3,3},{4,4},{5,6},{6,5},{7,7},{8,8},{9,10},{10,9... | collective-permute-start | bytes 36872 | tf_op jit(solution)/shard_map/ppermute | solution.py:300
  30.9 1.4 %collective-permute-start.10 = (f32[24,128]{1,0:T(8,128)S(1)}, f32[24,128]{1,0:T(8,128)S(1)}, u32[]{:S(2)}, u32[]{:S(2)}) collective-permute-start(f32[24,128]{1,0:T(8,128)S(1)} %get-tuple-element.69), channel_id=1, source_target_pairs={{0,1},{1,0},{2,3},{3,2},{4,5},{5,4},{6,7},{7,6},{8,9},{9,8},{10,11... | collective-permute-start | bytes 36872 | tf_op jit(solution)/shard_map/ppermute | solution.py:300
  33.0 16.3 %collective-permute-start.12 = (f32[5,2,16,128]{3,2,1,0:T(8,128)S(1)}, f32[5,2,16,128]{3,2,1,0:T(8,128)S(1)}, u32[]{:S(2)}, u32[]{:S(2)}) collective-permute-start(f32[5,2,16,128]{3,2,1,0:T(8,128)S(1)} %get-tuple-element.72), channel_id=1, source_target_pairs={{0,32},{32,0},{64,96},{96,64},{128,160},{160,128},{192,224},{224,1... | collective-permute-start | bytes 245768 | tf_op jit(solution)/shard_map/ppermute | solution.py:300
  36.4 14.2 %collective-permute-start.13 = (f32[5,2,16,128]{3,2,1,0:T(8,128)S(1)}, f32[5,2,16,128]{3,2,1,0:T(8,128)S(1)}, u32[]{:S(2)}, u32[]{:S(2)}) collective-permute-start(f32[5,2,16,128]{3,2,1,0:T(8,128)S(1)} %get-tuple-element.74), channel_id=1, source_target_pairs={{0,0},{32,64},{64,32},{96,128},{128,96},{160,192},{192,160},{224,2... | collective-permute-start | bytes 245768 | tf_op jit(solution)/shard_map/ppermute | solution.py:300
  37.0 13.5 %collective-permute-start.14 = (f32[5,2,8,128]{3,2,1,0:T(8,128)S(1)}, f32[5,2,8,128]{3,2,1,0:T(8,128)S(1)}, u32[]{:S(2)}, u32[]{:S(2)}) collective-permute-start(f32[5,2,8,128]{3,2,1,0:T(8,128)S(1)} %get-tuple-element.75), channel_id=1, source_target_pairs={{0,4},{4,0},{8,12},{12,8},{16,20},{20,16},{24,28},{28,24},{1,5},{5... | collective-permute-start | bytes 122888 | tf_op jit(solution)/shard_map/ppermute | solution.py:300
  42.2 8.3 %collective-permute-start.15 = (f32[5,2,8,128]{3,2,1,0:T(8,128)S(1)}, f32[5,2,8,128]{3,2,1,0:T(8,128)S(1)}, u32[]{:S(2)}, u32[]{:S(2)}) collective-permute-start(f32[5,2,8,128]{3,2,1,0:T(8,128)S(1)} %get-tuple-element.76), channel_id=1, source_target_pairs={{0,0},{4,8},{8,4},{12,16},{16,12},{20,24},{24,20},{28,28},{1,1},{5... | collective-permute-start | bytes 122888 | tf_op jit(solution)/shard_map/ppermute | solution.py:300
  42.9 7.7 %collective-permute-start.17 = (f32[24,128]{1,0:T(8,128)S(1)}, f32[24,128]{1,0:T(8,128)S(1)}, u32[]{:S(2)}, u32[]{:S(2)}) collective-permute-start(f32[24,128]{1,0:T(8,128)S(1)} %get-tuple-element.77), channel_id=1, source_target_pairs={{0,0},{1,2},{2,1},{3,3},{4,4},{5,6},{6,5},{7,7},{8,8},{9,10},{10,9... | collective-permute-start | bytes 36872 | tf_op jit(solution)/shard_map/ppermute | solution.py:300
  49.2 1.4 %collective-permute-start.16 = (f32[24,128]{1,0:T(8,128)S(1)}, f32[24,128]{1,0:T(8,128)S(1)}, u32[]{:S(2)}, u32[]{:S(2)}) collective-permute-start(f32[24,128]{1,0:T(8,128)S(1)} %get-tuple-element.77), channel_id=1, source_target_pairs={{0,1},{1,0},{2,3},{3,2},{4,5},{5,4},{6,7},{7,6},{8,9},{9,8},{10,11... | collective-permute-start | bytes 36872 | tf_op jit(solution)/shard_map/ppermute | solution.py:300
  51.3 13.9 %collective-permute-start.18 = (f32[5,2,16,128]{3,2,1,0:T(8,128)S(1)}, f32[5,2,16,128]{3,2,1,0:T(8,128)S(1)}, u32[]{:S(2)}, u32[]{:S(2)}) collective-permute-start(f32[5,2,16,128]{3,2,1,0:T(8,128)S(1)} %get-tuple-element.80), channel_id=1, source_target_pairs={{0,32},{32,0},{64,96},{96,64},{128,160},{160,128},{192,224},{224,1... | collective-permute-start | bytes 245768 | tf_op jit(solution)/shard_map/ppermute | solution.py:300
  54.5 12.1 %collective-permute-start.19 = (f32[5,2,16,128]{3,2,1,0:T(8,128)S(1)}, f32[5,2,16,128]{3,2,1,0:T(8,128)S(1)}, u32[]{:S(2)}, u32[]{:S(2)}) collective-permute-start(f32[5,2,16,128]{3,2,1,0:T(8,128)S(1)} %get-tuple-element.82), channel_id=1, source_target_pairs={{0,0},{32,64},{64,32},{96,128},{128,96},{160,192},{192,160},{224,2... | collective-permute-start | bytes 245768 | tf_op jit(solution)/shard_map/ppermute | solution.py:300
  55.1 11.4 %collective-permute-start.20 = (f32[5,2,8,128]{3,2,1,0:T(8,128)S(1)}, f32[5,2,8,128]{3,2,1,0:T(8,128)S(1)}, u32[]{:S(2)}, u32[]{:S(2)}) collective-permute-start(f32[5,2,8,128]{3,2,1,0:T(8,128)S(1)} %get-tuple-element.83), channel_id=1, source_target_pairs={{0,4},{4,0},{8,12},{12,8},{16,20},{20,16},{24,28},{28,24},{1,5},{5... | collective-permute-start | bytes 122888 | tf_op jit(solution)/shard_map/ppermute | solution.py:300
  58.2 8.3 %collective-permute-start.21 = (f32[5,2,8,128]{3,2,1,0:T(8,128)S(1)}, f32[5,2,8,128]{3,2,1,0:T(8,128)S(1)}, u32[]{:S(2)}, u32[]{:S(2)}) collective-permute-start(f32[5,2,8,128]{3,2,1,0:T(8,128)S(1)} %get-tuple-element.84), channel_id=1, source_target_pairs={{0,0},{4,8},{8,4},{12,16},{16,12},{20,24},{24,20},{28,28},{1,1},{5... | collective-permute-start | bytes 122888 | tf_op jit(solution)/shard_map/ppermute | solution.py:300
  58.9 7.7 %collective-permute-start.23 = (f32[24,128]{1,0:T(8,128)S(1)}, f32[24,128]{1,0:T(8,128)S(1)}, u32[]{:S(2)}, u32[]{:S(2)}) collective-permute-start(f32[24,128]{1,0:T(8,128)S(1)} %get-tuple-element.85), channel_id=1, source_target_pairs={{0,0},{1,2},{2,1},{3,3},{4,4},{5,6},{6,5},{7,7},{8,8},{9,10},{10,9... | collective-permute-start | bytes 36872 | tf_op jit(solution)/shard_map/ppermute | solution.py:300
  65.2 1.4 %collective-permute-start.22 = (f32[24,128]{1,0:T(8,128)S(1)}, f32[24,128]{1,0:T(8,128)S(1)}, u32[]{:S(2)}, u32[]{:S(2)}) collective-permute-start(f32[24,128]{1,0:T(8,128)S(1)} %get-tuple-element.85), channel_id=1, source_target_pairs={{0,1},{1,0},{2,3},{3,2},{4,5},{5,4},{6,7},{7,6},{8,9},{9,8},{10,11... | collective-permute-start | bytes 36872 | tf_op jit(solution)/shard_map/ppermute | solution.py:300

commit v7 on v4

--- a/solution.py
+++ b/solution.py
@@ -10,6 +10,7 @@
 AXES = ("gx", "gy", "wa")
 FIELDS, NX, NY, NZ = 5, 8, 16, 128
 ROWS = NX * NY
+FAR_ROWS = 96
 F32 = jnp.float32
 VMEM = pl.BlockSpec(memory_space=pltpu.VMEM)
 
@@ -82,12 +83,15 @@
 
 
 def emit_sends(psi_ref, metric_ref, packed_metric, groups, sends):
-    x0, x1, y0, y1, zz = sends
+    x0, x1, y0, y1, zz, far = sends
     lane = iota((8, NZ), 1)
     same, after, before = (packed_metric[8 * i : 8 * i + 8, :] for i in range(3))
     for g, p in enumerate(groups):
         v = same * p + after * lane_roll(p, -1) + before * lane_roll(p, 1)
-        zz[8 * g : 8 * g + 8, :] = jnp.where(lane % 4 < 2, lane_roll(v, -2), lane_roll(v, 2))
+        v = jnp.where(lane % 4 < 2, lane_roll(v, -2), lane_roll(v, 2))
+        zz[8 * g : 8 * g + 8, :] = v
+        far[8 * g : 8 * g + 8, :] = v
+    far[24:, :] = jnp.zeros((FAR_ROWS - 24, NZ), F32)
     even = is_even("gy")
     m4, m6a, m6b = metric_ref[4, edge_rows(15), :], metric_ref[6, edge_rows(14), :], metric_ref[6, edge_rows(15), :]
     m5, m7a, m7b = metric_ref[5, edge_rows(0), :], metric_ref[7, edge_rows(0), :], metric_ref[7, edge_rows(1), :]
@@ -112,7 +116,7 @@
             x1[e, r] = jnp.where(even, low[r], high[r])
 
 
-def first_body(psi_hbm, metric_hbm, x0, x1, y0, y1, zz, packed_metric, psi_ref, metric_ref, sems):
+def first_body(psi_hbm, metric_hbm, x0, x1, y0, y1, zz, far, packed_metric, psi_ref, metric_ref, sems):
     copies = [
         pltpu.make_async_copy(metric_hbm.at[8:12], metric_ref.at[8:12], sems.at[0]),
         pltpu.make_async_copy(psi_hbm, psi_ref, sems.at[1]),
@@ -127,7 +131,7 @@
     groups = pack_edges(psi_ref)
     copies[2].wait()
     copies[3].wait()
-    emit_sends(psi_ref, metric_ref, packed_metric, groups, (x0, x1, y0, y1, zz))
+    emit_sends(psi_ref, metric_ref, packed_metric, groups, (x0, x1, y0, y1, zz, far))
 
 
 def inner_body(psi_ref, metric_ref, z_ref):
@@ -196,9 +200,9 @@
 
 
 def middle_body(psi_ref, z_ref, r0, r1, r2, r3, r4, r5, diag_ref, rhs_ref, jac_ref, metric_ref, packed_metric,
-                new_ref, x0, x1, y0, y1, zz, total_ref):
+                new_ref, x0, x1, y0, y1, zz, far, total_ref):
     update(psi_ref, z_ref, (r0, r1, r2, r3, r4, r5), diag_ref, rhs_ref, jac_ref, new_ref, total_ref)
-    emit_sends(new_ref, metric_ref, packed_metric, pack_edges(new_ref), (x0, x1, y0, y1, zz))
+    emit_sends(new_ref, metric_ref, packed_metric, pack_edges(new_ref), (x0, x1, y0, y1, zz, far))
 
 
 def wall_body(coef_ref, ids_ref, weight_ref, coef_out, weight_out, hot_out, low_out):
@@ -291,19 +295,21 @@
 EDGE_X = ((FIELDS, 2, NY, NZ), F32)
 EDGE_Y = ((FIELDS, 2, NX, NZ), F32)
 EDGE_Z = ((24, NZ), F32)
-SENDS = [EDGE_X, EDGE_X, EDGE_Y, EDGE_Y, EDGE_Z]
+EDGE_FAR = ((FAR_ROWS, NZ), F32)
+SENDS = [EDGE_X, EDGE_X, EDGE_Y, EDGE_Y, EDGE_Z, EDGE_FAR]
 FIELD = ((FIELDS, ROWS, NZ), F32)
 
 
 def exchange(sends):
-    x0, x1, y0, y1, zz = sends
+    x0, x1, y0, y1, zz, far = sends
     def swap(v, axis, odd):
         return lax.ppermute(v, axis, pairs(lax.axis_size(axis), odd))
-    x = swap(x0, "gx", 0), swap(x1, "gx", 1)
+    two_hops = swap(x1, "gx", 1)
+    x = swap(x0, "gx", 0), two_hops
+    far = swap(far, "wa", 1)
     y = swap(y0, "gy", 0), swap(y1, "gy", 1)
-    far = swap(zz, "wa", 1)
-    zz, first = lax.optimization_barrier((zz, x[0]))
-    x = first, x[1]
+    zz, two_hops = lax.optimization_barrier((zz, two_hops))
+    x = x[0], two_hops
     z = swap(zz, "wa", 0), far
     return (*x, *y, *z)
 

time: 73.3 us -> 72.7 us (level)
  transfers between devices with their start and end apart: 24 -> 24, of which waited for: 4 -> 5; matrix products, arithmetic and copies ran while one was open for 0% -> 0% of each run, Pallas kernels for 3% -> 3%
where the time goes in v7:
time: 72.7 us; the launch traced here: 72.5 us
  starting transfers between devices  38.4 us (53%)
  blocking collectives  22.5 us (31%)
  Pallas kernels  7.79 us (11%)
  waiting for transfers between devices  2.61 us (4%)
  between operations  0.78 us (1%)
    ppermute x24, starting transfers between devices, swap(): return lax.ppermute(v, axis, pairs(lax.axis_size(axis), odd))  38.4 us
    all_to_all x1, blocking collectives, local(): got = lax.all_to_all(slots.reshape(256, 1, 48), AXES, 0, 0).reshape(256, 48)  22.5 us
    pallas_call x11, Pallas kernels, run(): pl.pallas_call(body, out_shape=[jax.ShapeDtypeStruct(s, d) for s, d in ou...  7.79 us
    ppermute x24, waiting for transfers between devices, swap(): return lax.ppermute(v, axis, pairs(lax.axis_size(axis), odd))  2.61 us
  transfers between devices with their start and end apart: 24, of which 5 were waited for; matrix products, arithmetic and copies ran while one was open for 0% of the time, Pallas kernels for 3%

profile of v7, /device:TPU:1, one launch (start us, length us, event | category | flops | bytes accessed | tf_op | source)
XLA Modules:
  0.0 72.5 jit_solution(12404630342590491044)
XLA Ops:
  0.6 1.5 %shard_map.95 = (f32[5,2,16,128]{3,2,1,0:T(8,128)S(1)}, f32[5,2,16,128]{3,2,1,0:T(8,128)S(1)}, f32[5,2,8,128]{3,2,1,0:T(8,128)S(1)}, f32[5,2,8,128]{3,2,1,0:T(8,...) custom-call(f32[5,128,128]{2,1,0:T(8,128)} %bitcast.31, ...), custom_call_target="tpu_custom_call" | custom-call | flops 1000000 | bytes 1000000 | tf_op jit(solution)/shard_map/pallas_call | solution.py:284
  2.1 0.0 copy-start
  2.1 4.6 %collective-permute-start.1 = (f32[5,2,16,128]{3,2,1,0:T(8,128)S(1)}, f32[5,2,16,128]{3,2,1,0:T(8,128)S(1)}, u32[]{:S(2)}, u32[]{:S(2)}) collective-permute-start(f32[5,2,16,128]{3,2,1,0:T(8,128)S(1)} %get-tuple-element.60), channel_id=1, source_target_pairs={{0,224},{32,64},{64,32},{96,128},{128,96},{160,192},{192,160},{224... | collective-permute-start | bytes 245768 | tf_op jit(solution)/shard_map/ppermute | solution.py:306
  6.7 0.0 collective-permute-start
  6.7 3.3 %collective-permute-start.5 = (f32[96,128]{1,0:T(8,128)S(1)}, f32[96,128]{1,0:T(8,128)S(1)}, u32[]{:S(2)}, u32[]{:S(2)}) collective-permute-start(f32[96,128]{1,0:T(8,128)S(1)} %get-tuple-element.65), channel_id=1, source_target_pairs={{0,3},{1,2},{2,1},{3,0},{4,7},{5,6},{6,5},{7,4},{8,11},{9,10},{10,... | collective-permute-start | bytes 147464 | tf_op jit(solution)/shard_map/ppermute | solution.py:306
  10.0 1.6 %collective-permute-start.2 = (f32[5,2,8,128]{3,2,1,0:T(8,128)S(1)}, f32[5,2,8,128]{3,2,1,0:T(8,128)S(1)}, u32[]{:S(2)}, u32[]{:S(2)}) collective-permute-start(f32[5,2,8,128]{3,2,1,0:T(8,128)S(1)} %get-tuple-element.62), channel_id=1, source_target_pairs={{0,4},{4,0},{8,12},{12,8},{16,20},{20,16},{24,28},{28,24},{1,5},{5... | collective-permute-start | bytes 122888 | tf_op jit(solution)/shard_map/ppermute | solution.py:306
  11.6 4.7 %collective-permute-start.3 = (f32[5,2,8,128]{3,2,1,0:T(8,128)S(1)}, f32[5,2,8,128]{3,2,1,0:T(8,128)S(1)}, u32[]{:S(2)}, u32[]{:S(2)}) collective-permute-start(f32[5,2,8,128]{3,2,1,0:T(8,128)S(1)} %get-tuple-element.63), channel_id=1, source_target_pairs={{0,28},{4,8},{8,4},{12,16},{16,12},{20,24},{24,20},{28,0},{1,29},{... | collective-permute-start | bytes 122888 | tf_op jit(solution)/shard_map/ppermute | solution.py:306
  16.3 0.0 collective-permute-done.1.r1
  16.3 0.1 collective-permute-start.4
  16.4 0.4 shard_map.96.z_ref
  16.9 0.4 copy-done.3
  17.3 0.0 copy-done.4
  17.3 0.0 copy-done.5
  17.3 0.6 shard_map.97
  17.9 0.0 collective-permute-done.2.r2
  17.9 0.5 collective-permute-done.3.r3
  18.4 0.0 collective-permute-done.5.r5
  18.4 0.0 collective-permute-done.r0
  18.4 0.0 collective-permute-done.4.r4
  18.5 0.7 shard_map.98
  19.2 1.0 %collective-permute-start.7 = (f32[5,2,16,128]{3,2,1,0:T(8,128)S(1)}, f32[5,2,16,128]{3,2,1,0:T(8,128)S(1)}, u32[]{:S(2)}, u32[]{:S(2)}) collective-permute-start(f32[5,2,16,128]{3,2,1,0:T(8,128)S(1)} %get-tuple-element.70), channel_id=1, source_target_pairs={{0,224},{32,64},{64,32},{96,128},{128,96},{160,192},{192,160},{224... | collective-permute-start | bytes 245768 | tf_op jit(solution)/shard_map/ppermute | solution.py:306
  20.1 0.6 collective-permute-start.6
  20.7 1.9 %collective-permute-start.11 = (f32[96,128]{1,0:T(8,128)S(1)}, f32[96,128]{1,0:T(8,128)S(1)}, u32[]{:S(2)}, u32[]{:S(2)}) collective-permute-start(f32[96,128]{1,0:T(8,128)S(1)} %get-tuple-element.75), channel_id=1, source_target_pairs={{0,3},{1,2},{2,1},{3,0},{4,7},{5,6},{6,5},{7,4},{8,11},{9,10},{10,... | collective-permute-start | bytes 147464 | tf_op jit(solution)/shard_map/ppermute | solution.py:306
  22.5 0.0 collective-permute-start.8
  22.5 3.7 %collective-permute-start.9 = (f32[5,2,8,128]{3,2,1,0:T(8,128)S(1)}, f32[5,2,8,128]{3,2,1,0:T(8,128)S(1)}, u32[]{:S(2)}, u32[]{:S(2)}) collective-permute-start(f32[5,2,8,128]{3,2,1,0:T(8,128)S(1)} %get-tuple-element.73), channel_id=1, source_target_pairs={{0,28},{4,8},{8,4},{12,16},{16,12},{20,24},{24,20},{28,0},{1,29},{... | collective-permute-start | bytes 122888 | tf_op jit(solution)/shard_map/ppermute | solution.py:306
  26.3 0.0 collective-permute-done.7.r1
  26.3 0.8 %collective-permute-start.10 = (f32[24,128]{1,0:T(8,128)S(1)}, f32[24,128]{1,0:T(8,128)S(1)}, u32[]{:S(2)}, u32[]{:S(2)}) collective-permute-start(f32[24,128]{1,0:T(8,128)S(1)} %get-tuple-element.74), channel_id=1, source_target_pairs={{0,1},{1,0},{2,3},{3,2},{4,5},{5,4},{6,7},{7,6},{8,9},{9,8},{10,11... | collective-permute-start | bytes 36872 | tf_op jit(solution)/shard_map/ppermute | solution.py:306
  27.0 0.4 shard_map.99.z_ref
  27.5 0.0 collective-permute-done.8.r2
  27.5 0.1 collective-permute-done.9.r3
  27.6 0.0 collective-permute-done.11.r5
  27.6 0.0 collective-permute-done.6.r0
  27.6 0.2 collective-permute-done.10.r4
  27.9 0.7 shard_map.100
  28.6 1.1 %collective-permute-start.13 = (f32[5,2,16,128]{3,2,1,0:T(8,128)S(1)}, f32[5,2,16,128]{3,2,1,0:T(8,128)S(1)}, u32[]{:S(2)}, u32[]{:S(2)}) collective-permute-start(f32[5,2,16,128]{3,2,1,0:T(8,128)S(1)} %get-tuple-element.79), channel_id=1, source_target_pairs={{0,224},{32,64},{64,32},{96,128},{128,96},{160,192},{192,160},{224... | collective-permute-start | bytes 245768 | tf_op jit(solution)/shard_map/ppermute | solution.py:306
  29.6 0.9 %collective-permute-start.12 = (f32[5,2,16,128]{3,2,1,0:T(8,128)S(1)}, f32[5,2,16,128]{3,2,1,0:T(8,128)S(1)}, u32[]{:S(2)}, u32[]{:S(2)}) collective-permute-start(f32[5,2,16,128]{3,2,1,0:T(8,128)S(1)} %get-tuple-element.77), channel_id=1, source_target_pairs={{0,32},{32,0},{64,96},{96,64},{128,160},{160,128},{192,224},{224,1... | collective-permute-start | bytes 245768 | tf_op jit(solution)/shard_map/ppermute | solution.py:306
  30.6 2.5 %collective-permute-start.17 = (f32[96,128]{1,0:T(8,128)S(1)}, f32[96,128]{1,0:T(8,128)S(1)}, u32[]{:S(2)}, u32[]{:S(2)}) collective-permute-start(f32[96,128]{1,0:T(8,128)S(1)} %get-tuple-element.84), channel_id=1, source_target_pairs={{0,3},{1,2},{2,1},{3,0},{4,7},{5,6},{6,5},{7,4},{8,11},{9,10},{10,... | collective-permute-start | bytes 147464 | tf_op jit(solution)/shard_map/ppermute | solution.py:306
  33.0 0.4 collective-permute-start.14
  33.4 3.0 %collective-permute-start.15 = (f32[5,2,8,128]{3,2,1,0:T(8,128)S(1)}, f32[5,2,8,128]{3,2,1,0:T(8,128)S(1)}, u32[]{:S(2)}, u32[]{:S(2)}) collective-permute-start(f32[5,2,8,128]{3,2,1,0:T(8,128)S(1)} %get-tuple-element.82), channel_id=1, source_target_pairs={{0,28},{4,8},{8,4},{12,16},{16,12},{20,24},{24,20},{28,0},{1,29},{... | collective-permute-start | bytes 122888 | tf_op jit(solution)/shard_map/ppermute | solution.py:306
  36.4 0.0 collective-permute-done.13.r1
  36.4 0.6 collective-permute-start.16
  37.0 0.4 shard_map.101.z_ref
  37.4 0.0 collective-permute-done.14.r2
  37.4 0.7 %collective-permute-done.15.r3 = f32[5,2,8,128]{3,2,1,0:T(8,128)S(1)} collective-permute-done((f32[5,2,8,128]{3,2,1,0:T(8,128)S(1)}, f32[5,2,8,128]{3,2,1,0:T(8,128)S(1)}, u32[]{:S(2)}, u32[]{:S(2)}) %collective-permute-start.15) | collective-permute-done | bytes 40992 | tf_op jit(solution)/shard_map/ppermute | solution.py:306
  38.2 0.0 collective-permute-done.17.r5
  38.2 0.0 collective-permute-done.12.r0
  38.2 0.0 collective-permute-done.16.r4
  38.2 0.7 shard_map.102
  38.9 0.9 %collective-permute-start.19 = (f32[5,2,16,128]{3,2,1,0:T(8,128)S(1)}, f32[5,2,16,128]{3,2,1,0:T(8,128)S(1)}, u32[]{:S(2)}, u32[]{:S(2)}) collective-permute-start(f32[5,2,16,128]{3,2,1,0:T(8,128)S(1)} %get-tuple-element.88), channel_id=1, source_target_pairs={{0,224},{32,64},{64,32},{96,128},{128,96},{160,192},{192,160},{224... | collective-permute-start | bytes 245768 | tf_op jit(solution)/shard_map/ppermute | solution.py:306
  39.7 0.8 %collective-permute-start.18 = (f32[5,2,16,128]{3,2,1,0:T(8,128)S(1)}, f32[5,2,16,128]{3,2,1,0:T(8,128)S(1)}, u32[]{:S(2)}, u32[]{:S(2)}) collective-permute-start(f32[5,2,16,128]{3,2,1,0:T(8,128)S(1)} %get-tuple-element.86), channel_id=1, source_target_pairs={{0,32},{32,0},{64,96},{96,64},{128,160},{160,128},{192,224},{224,1... | collective-permute-start | bytes 245768 | tf_op jit(solution)/shard_map/ppermute | solution.py:306
  40.6 2.9 %collective-permute-start.23 = (f32[96,128]{1,0:T(8,128)S(1)}, f32[96,128]{1,0:T(8,128)S(1)}, u32[]{:S(2)}, u32[]{:S(2)}) collective-permute-start(f32[96,128]{1,0:T(8,128)S(1)} %get-tuple-element.93), channel_id=1, source_target_pairs={{0,3},{1,2},{2,1},{3,0},{4,7},{5,6},{6,5},{7,4},{8,11},{9,10},{10,... | collective-permute-start | bytes 147464 | tf_op jit(solution)/shard_map/ppermute | solution.py:306
  43.5 0.0 collective-permute-start.20
  43.5 2.8 %collective-permute-start.21 = (f32[5,2,8,128]{3,2,1,0:T(8,128)S(1)}, f32[5,2,8,128]{3,2,1,0:T(8,128)S(1)}, u32[]{:S(2)}, u32[]{:S(2)}) collective-permute-start(f32[5,2,8,128]{3,2,1,0:T(8,128)S(1)} %get-tuple-element.91), channel_id=1, source_target_pairs={{0,28},{4,8},{8,4},{12,16},{16,12},{20,24},{24,20},{28,0},{1,29},{... | collective-permute-start | bytes 122888 | tf_op jit(solution)/shard_map/ppermute | solution.py:306
  46.3 0.0 collective-permute-done.19.r1
  46.3 0.4 collective-permute-start.22
  46.7 0.4 shard_map.103.z_ref
  47.2 0.0 collective-permute-done.20.r2
  47.2 1.0 %collective-permute-done.21.r3 = f32[5,2,8,128]{3,2,1,0:T(8,128)S(1)} collective-permute-done((f32[5,2,8,128]{3,2,1,0:T(8,128)S(1)}, f32[5,2,8,128]{3,2,1,0:T(8,128)S(1)}, u32[]{:S(2)}, u32[]{:S(2)}) %collective-permute-start.21) | collective-permute-done | bytes 40992 | tf_op jit(solution)/shard_map/ppermute | solution.py:306
  48.1 0.0 collective-permute-done.23.r5
  48.1 0.0 collective-permute-done.18.r0
  48.1 0.0 collective-permute-done.22.r4
  48.1 1.2 %shard_map.104 = (f32[5,128,128]{2,1,0:T(8,128)}, f32[256,48]{1,0:T(8,128)S(1)}) custom-call(f32[5,128,128]{2,1,0:T(8,128)S(1)} %get-tuple-element.85.psi_ref, f32[5,128,128]{2,1,0:T(8,128)S(1)} %shard_map.103.z_ref, f32[5,2,16,128]{3,2,1,0:T(8,128)S(1)} %collective-permute-done.18.r0, f32[5,2,16,128]{3,2,1,0:T(8,128)S(1)} %collective-permute-done.19.r1, ...), custom_call_target="tpu_custom_call" | custom-call | flops 1000000 | bytes 1000000 | tf_op jit(solution)/shard_map/pallas_call | solution.py:284
  49.3 22.5 %all_to_all.5 = f32[256,1,48]{2,1,0:T(1,128)S(1)} all-to-all(f32[256,1,48]{2,1,0:T(1,128)S(1)} %bitcast.26), channel_id=1, replica_groups=mesh['gx'=8,'gy'=8,'wa'=4] {'gx','gy','wa'}, dimensions={0} | all-to-all | bytes 98304 | tf_op jit(solution)/shard_map/all_to_all | solution.py:345
  71.8 0.7 shard_map.105
  (8 shorter events, 0.0 us)
Async XLA Ops:
  2.1 16.3 %copy-start = (bf16[5,5,8,16,128]{4,3,2,1,0:T(8,128)(2,1)S(1)}, bf16[5,5,8,16,128]{4,3,2,1,0:T(8,128)(2,1)}, u32[]{:S(2)}) copy-start(bf16[5,5,8,16,128]{4,3,2,1,0:T(8,128)(2,1)} %param.12) | copy-start | bytes 2457604
  2.1 14.2 %collective-permute-start.1 = (f32[5,2,16,128]{3,2,1,0:T(8,128)S(1)}, f32[5,2,16,128]{3,2,1,0:T(8,128)S(1)}, u32[]{:S(2)}, u32[]{:S(2)}) collective-permute-start(f32[5,2,16,128]{3,2,1,0:T(8,128)S(1)} %get-tuple-element.60), channel_id=1, source_target_pairs={{0,224},{32,64},{64,32},{96,128},{128,96},{160,192},{192,160},{224... | collective-permute-start | bytes 245768 | tf_op jit(solution)/shard_map/ppermute | solution.py:306
  6.7 11.7 %collective-permute-start = (f32[5,2,16,128]{3,2,1,0:T(8,128)S(1)}, f32[5,2,16,128]{3,2,1,0:T(8,128)S(1)}, u32[]{:S(2)}, u32[]{:S(2)}) collective-permute-start(f32[5,2,16,128]{3,2,1,0:T(8,128)S(1)} %get-tuple-element.58), channel_id=1, source_target_pairs={{0,32},{32,0},{64,96},{96,64},{128,160},{160,128},{192,224},{224,1... | collective-permute-start | bytes 245768 | tf_op jit(solution)/shard_map/ppermute | solution.py:306
  6.7 11.7 %collective-permute-start.5 = (f32[96,128]{1,0:T(8,128)S(1)}, f32[96,128]{1,0:T(8,128)S(1)}, u32[]{:S(2)}, u32[]{:S(2)}) collective-permute-start(f32[96,128]{1,0:T(8,128)S(1)} %get-tuple-element.65), channel_id=1, source_target_pairs={{0,3},{1,2},{2,1},{3,0},{4,7},{5,6},{6,5},{7,4},{8,11},{9,10},{10,... | collective-permute-start | bytes 147464 | tf_op jit(solution)/shard_map/ppermute | solution.py:306
  10.0 7.9 %collective-permute-start.2 = (f32[5,2,8,128]{3,2,1,0:T(8,128)S(1)}, f32[5,2,8,128]{3,2,1,0:T(8,128)S(1)}, u32[]{:S(2)}, u32[]{:S(2)}) collective-permute-start(f32[5,2,8,128]{3,2,1,0:T(8,128)S(1)} %get-tuple-element.62), channel_id=1, source_target_pairs={{0,4},{4,0},{8,12},{12,8},{16,20},{20,16},{24,28},{28,24},{1,5},{5... | collective-permute-start | bytes 122888 | tf_op jit(solution)/shard_map/ppermute | solution.py:306
  11.6 6.8 %collective-permute-start.3 = (f32[5,2,8,128]{3,2,1,0:T(8,128)S(1)}, f32[5,2,8,128]{3,2,1,0:T(8,128)S(1)}, u32[]{:S(2)}, u32[]{:S(2)}) collective-permute-start(f32[5,2,8,128]{3,2,1,0:T(8,128)S(1)} %get-tuple-element.63), channel_id=1, source_target_pairs={{0,28},{4,8},{8,4},{12,16},{16,12},{20,24},{24,20},{28,0},{1,29},{... | collective-permute-start | bytes 122888 | tf_op jit(solution)/shard_map/ppermute | solution.py:306
  16.3 2.1 %collective-permute-start.4 = (f32[24,128]{1,0:T(8,128)S(1)}, f32[24,128]{1,0:T(8,128)S(1)}, u32[]{:S(2)}, u32[]{:S(2)}) collective-permute-start(f32[24,128]{1,0:T(8,128)S(1)} %get-tuple-element.64), channel_id=1, source_target_pairs={{0,1},{1,0},{2,3},{3,2},{4,5},{5,4},{6,7},{7,6},{8,9},{9,8},{10,11... | collective-permute-start | bytes 36872 | tf_op jit(solution)/shard_map/ppermute | solution.py:306
  16.4 0.9 %copy-start.3 = (f32[3,10,8,16]{3,2,1,0:T(8,128)S(1)}, f32[3,10,8,16]{3,2,1,0:T(8,128)}, u32[]{:S(2)}) copy-start(f32[3,10,8,16]{3,2,1,0:T(8,128)} %param.13) | copy-start | bytes 46084
  16.4 0.9 %copy-start.4 = (s32[4,8,16]{2,1,0:T(8,128)S(1)}, s32[4,8,16]{2,1,0:T(8,128)}, u32[]{:S(2)}) copy-start(s32[4,8,16]{2,1,0:T(8,128)} %param.14) | copy-start | bytes 6148
  16.4 0.9 %copy-start.5 = (f32[4,8,16]{2,1,0:T(8,128)S(1)}, f32[4,8,16]{2,1,0:T(8,128)}, u32[]{:S(2)}) copy-start(f32[4,8,16]{2,1,0:T(8,128)} %param.15) | copy-start | bytes 6148
  16.4 2.0 %copy-start.1 = (f32[5,8,16,128]{3,2,1,0:T(8,128)S(1)}, f32[5,8,16,128]{3,2,1,0:T(8,128)}, u32[]{:S(2)}) copy-start(f32[5,8,16,128]{3,2,1,0:T(8,128)} %param.9) | copy-start | bytes 983044
  17.3 1.1 %copy-start.2 = (f32[8,16,128]{2,1,0:T(8,128)S(1)}, f32[8,16,128]{2,1,0:T(8,128)}, u32[]{:S(2)}) copy-start(f32[8,16,128]{2,1,0:T(8,128)} %param.10) | copy-start | bytes 196612
  19.2 7.1 %collective-permute-start.7 = (f32[5,2,16,128]{3,2,1,0:T(8,128)S(1)}, f32[5,2,16,128]{3,2,1,0:T(8,128)S(1)}, u32[]{:S(2)}, u32[]{:S(2)}) collective-permute-start(f32[5,2,16,128]{3,2,1,0:T(8,128)S(1)} %get-tuple-element.70), channel_id=1, source_target_pairs={{0,224},{32,64},{64,32},{96,128},{128,96},{160,192},{192,160},{224... | collective-permute-start | bytes 245768 | tf_op jit(solution)/shard_map/ppermute | solution.py:306
  20.1 7.5 %collective-permute-start.6 = (f32[5,2,16,128]{3,2,1,0:T(8,128)S(1)}, f32[5,2,16,128]{3,2,1,0:T(8,128)S(1)}, u32[]{:S(2)}, u32[]{:S(2)}) collective-permute-start(f32[5,2,16,128]{3,2,1,0:T(8,128)S(1)} %get-tuple-element.68), channel_id=1, source_target_pairs={{0,32},{32,0},{64,96},{96,64},{128,160},{160,128},{192,224},{224,1... | collective-permute-start | bytes 245768 | tf_op jit(solution)/shard_map/ppermute | solution.py:306
  20.7 7.0 %collective-permute-start.11 = (f32[96,128]{1,0:T(8,128)S(1)}, f32[96,128]{1,0:T(8,128)S(1)}, u32[]{:S(2)}, u32[]{:S(2)}) collective-permute-start(f32[96,128]{1,0:T(8,128)S(1)} %get-tuple-element.75), channel_id=1, source_target_pairs={{0,3},{1,2},{2,1},{3,0},{4,7},{5,6},{6,5},{7,4},{8,11},{9,10},{10,... | collective-permute-start | bytes 147464 | tf_op jit(solution)/shard_map/ppermute | solution.py:306
  22.5 5.0 %collective-permute-start.8 = (f32[5,2,8,128]{3,2,1,0:T(8,128)S(1)}, f32[5,2,8,128]{3,2,1,0:T(8,128)S(1)}, u32[]{:S(2)}, u32[]{:S(2)}) collective-permute-start(f32[5,2,8,128]{3,2,1,0:T(8,128)S(1)} %get-tuple-element.72), channel_id=1, source_target_pairs={{0,4},{4,0},{8,12},{12,8},{16,20},{20,16},{24,28},{28,24},{1,5},{5... | collective-permute-start | bytes 122888 | tf_op jit(solution)/shard_map/ppermute | solution.py:306
  22.5 5.1 %collective-permute-start.9 = (f32[5,2,8,128]{3,2,1,0:T(8,128)S(1)}, f32[5,2,8,128]{3,2,1,0:T(8,128)S(1)}, u32[]{:S(2)}, u32[]{:S(2)}) collective-permute-start(f32[5,2,8,128]{3,2,1,0:T(8,128)S(1)} %get-tuple-element.73), channel_id=1, source_target_pairs={{0,28},{4,8},{8,4},{12,16},{16,12},{20,24},{24,20},{28,0},{1,29},{... | collective-permute-start | bytes 122888 | tf_op jit(solution)/shard_map/ppermute | solution.py:306
  26.3 1.6 %collective-permute-start.10 = (f32[24,128]{1,0:T(8,128)S(1)}, f32[24,128]{1,0:T(8,128)S(1)}, u32[]{:S(2)}, u32[]{:S(2)}) collective-permute-start(f32[24,128]{1,0:T(8,128)S(1)} %get-tuple-element.74), channel_id=1, source_target_pairs={{0,1},{1,0},{2,3},{3,2},{4,5},{5,4},{6,7},{7,6},{8,9},{9,8},{10,11... | collective-permute-start | bytes 36872 | tf_op jit(solution)/shard_map/ppermute | solution.py:306
  28.6 7.8 %collective-permute-start.13 = (f32[5,2,16,128]{3,2,1,0:T(8,128)S(1)}, f32[5,2,16,128]{3,2,1,0:T(8,128)S(1)}, u32[]{:S(2)}, u32[]{:S(2)}) collective-permute-start(f32[5,2,16,128]{3,2,1,0:T(8,128)S(1)} %get-tuple-element.79), channel_id=1, source_target_pairs={{0,224},{32,64},{64,32},{96,128},{128,96},{160,192},{192,160},{224... | collective-permute-start | bytes 245768 | tf_op jit(solution)/shard_map/ppermute | solution.py:306
  29.6 8.5 %collective-permute-start.12 = (f32[5,2,16,128]{3,2,1,0:T(8,128)S(1)}, f32[5,2,16,128]{3,2,1,0:T(8,128)S(1)}, u32[]{:S(2)}, u32[]{:S(2)}) collective-permute-start(f32[5,2,16,128]{3,2,1,0:T(8,128)S(1)} %get-tuple-element.77), channel_id=1, source_target_pairs={{0,32},{32,0},{64,96},{96,64},{128,160},{160,128},{192,224},{224,1... | collective-permute-start | bytes 245768 | tf_op jit(solution)/shard_map/ppermute | solution.py:306
  30.6 7.6 %collective-permute-start.17 = (f32[96,128]{1,0:T(8,128)S(1)}, f32[96,128]{1,0:T(8,128)S(1)}, u32[]{:S(2)}, u32[]{:S(2)}) collective-permute-start(f32[96,128]{1,0:T(8,128)S(1)} %get-tuple-element.84), channel_id=1, source_target_pairs={{0,3},{1,2},{2,1},{3,0},{4,7},{5,6},{6,5},{7,4},{8,11},{9,10},{10,... | collective-permute-start | bytes 147464 | tf_op jit(solution)/shard_map/ppermute | solution.py:306
  33.0 4.4 %collective-permute-start.14 = (f32[5,2,8,128]{3,2,1,0:T(8,128)S(1)}, f32[5,2,8,128]{3,2,1,0:T(8,128)S(1)}, u32[]{:S(2)}, u32[]{:S(2)}) collective-permute-start(f32[5,2,8,128]{3,2,1,0:T(8,128)S(1)} %get-tuple-element.81), channel_id=1, source_target_pairs={{0,4},{4,0},{8,12},{12,8},{16,20},{20,16},{24,28},{28,24},{1,5},{5... | collective-permute-start | bytes 122888 | tf_op jit(solution)/shard_map/ppermute | solution.py:306
  33.4 4.7 %collective-permute-start.15 = (f32[5,2,8,128]{3,2,1,0:T(8,128)S(1)}, f32[5,2,8,128]{3,2,1,0:T(8,128)S(1)}, u32[]{:S(2)}, u32[]{:S(2)}) collective-permute-start(f32[5,2,8,128]{3,2,1,0:T(8,128)S(1)} %get-tuple-element.82), channel_id=1, source_target_pairs={{0,28},{4,8},{8,4},{12,16},{16,12},{20,24},{24,20},{28,0},{1,29},{... | collective-permute-start | bytes 122888 | tf_op jit(solution)/shard_map/ppermute | solution.py:306
  36.4 1.8 %collective-permute-start.16 = (f32[24,128]{1,0:T(8,128)S(1)}, f32[24,128]{1,0:T(8,128)S(1)}, u32[]{:S(2)}, u32[]{:S(2)}) collective-permute-start(f32[24,128]{1,0:T(8,128)S(1)} %get-tuple-element.83), channel_id=1, source_target_pairs={{0,1},{1,0},{2,3},{3,2},{4,5},{5,4},{6,7},{7,6},{8,9},{9,8},{10,11... | collective-permute-start | bytes 36872 | tf_op jit(solution)/shard_map/ppermute | solution.py:306
  38.9 7.4 %collective-permute-start.19 = (f32[5,2,16,128]{3,2,1,0:T(8,128)S(1)}, f32[5,2,16,128]{3,2,1,0:T(8,128)S(1)}, u32[]{:S(2)}, u32[]{:S(2)}) collective-permute-start(f32[5,2,16,128]{3,2,1,0:T(8,128)S(1)} %get-tuple-element.88), channel_id=1, source_target_pairs={{0,224},{32,64},{64,32},{96,128},{128,96},{160,192},{192,160},{224... | collective-permute-start | bytes 245768 | tf_op jit(solution)/shard_map/ppermute | solution.py:306
  39.7 8.4 %collective-permute-start.18 = (f32[5,2,16,128]{3,2,1,0:T(8,128)S(1)}, f32[5,2,16,128]{3,2,1,0:T(8,128)S(1)}, u32[]{:S(2)}, u32[]{:S(2)}) collective-permute-start(f32[5,2,16,128]{3,2,1,0:T(8,128)S(1)} %get-tuple-element.86), channel_id=1, source_target_pairs={{0,32},{32,0},{64,96},{96,64},{128,160},{160,128},{192,224},{224,1... | collective-permute-start | bytes 245768 | tf_op jit(solution)/shard_map/ppermute | solution.py:306
  40.6 7.5 %collective-permute-start.23 = (f32[96,128]{1,0:T(8,128)S(1)}, f32[96,128]{1,0:T(8,128)S(1)}, u32[]{:S(2)}, u32[]{:S(2)}) collective-permute-start(f32[96,128]{1,0:T(8,128)S(1)} %get-tuple-element.93), channel_id=1, source_target_pairs={{0,3},{1,2},{2,1},{3,0},{4,7},{5,6},{6,5},{7,4},{8,11},{9,10},{10,... | collective-permute-start | bytes 147464 | tf_op jit(solution)/shard_map/ppermute | solution.py:306
  43.5 3.7 %collective-permute-start.20 = (f32[5,2,8,128]{3,2,1,0:T(8,128)S(1)}, f32[5,2,8,128]{3,2,1,0:T(8,128)S(1)}, u32[]{:S(2)}, u32[]{:S(2)}) collective-permute-start(f32[5,2,8,128]{3,2,1,0:T(8,128)S(1)} %get-tuple-element.90), channel_id=1, source_target_pairs={{0,4},{4,0},{8,12},{12,8},{16,20},{20,16},{24,28},{28,24},{1,5},{5... | collective-permute-start | bytes 122888 | tf_op jit(solution)/shard_map/ppermute | solution.py:306
  43.5 4.6 %collective-permute-start.21 = (f32[5,2,8,128]{3,2,1,0:T(8,128)S(1)}, f32[5,2,8,128]{3,2,1,0:T(8,128)S(1)}, u32[]{:S(2)}, u32[]{:S(2)}) collective-permute-start(f32[5,2,8,128]{3,2,1,0:T(8,128)S(1)} %get-tuple-element.91), channel_id=1, source_target_pairs={{0,28},{4,8},{8,4},{12,16},{16,12},{20,24},{24,20},{28,0},{1,29},{... | collective-permute-start | bytes 122888 | tf_op jit(solution)/shard_map/ppermute | solution.py:306
  46.3 1.8 %collective-permute-start.22 = (f32[24,128]{1,0:T(8,128)S(1)}, f32[24,128]{1,0:T(8,128)S(1)}, u32[]{:S(2)}, u32[]{:S(2)}) collective-permute-start(f32[24,128]{1,0:T(8,128)S(1)} %get-tuple-element.92), channel_id=1, source_target_pairs={{0,1},{1,0},{2,3},{3,2},{4,5},{5,4},{6,7},{7,6},{8,9},{9,8},{10,11... | collective-permute-start | bytes 36872 | tf_op jit(solution)/shard_map/ppermute | solution.py:306

commit v8 on v7

--- a/solution.py
+++ b/solution.py
@@ -134,7 +134,17 @@
     emit_sends(psi_ref, metric_ref, packed_metric, groups, (x0, x1, y0, y1, zz, far))
 
 
-def inner_body(psi_ref, metric_ref, z_ref):
+def coupled(jac_ref, s, zs):
+    out = []
+    for f in range(FIELDS):
+        c = jac_ref[f, s, :].astype(F32) * zs[0]
+        for e in range(1, FIELDS):
+            c = c + jac_ref[FIELDS * e + f, s, :].astype(F32) * zs[e]
+        out.append(c)
+    return out
+
+
+def inner_body(psi_ref, metric_ref, diag_ref, rhs_ref, jac_ref, base_ref):
     lane, row = iota((NY, NZ), 1), iota((NY, NZ), 0)
     for x in range(NX):
         s = slab(x)
@@ -144,6 +154,7 @@
             (8, lane < NZ - 1), (9, lane >= 1), (10, lane < NZ - 2), (11, lane >= 2),
         ):
             ms.append(jnp.where(keep, metric_ref[o, s, :], 0.0))
+        zs = []
         for e in range(FIELDS):
             q = psi_ref[e, s, :]
             total = row_roll(ms[0] * q, 1) + row_roll(ms[1] * q, -1)
@@ -153,7 +164,12 @@
             for o, step in enumerate((1, -1, 2, -2)):
                 if 0 <= x - step < NX:
                     total = total + metric_ref[o, slab(x - step), :] * psi_ref[e, slab(x - step), :]
-            z_ref[e, s, :] = total
+            zs.append(total)
+        d = diag_ref[s, :]
+        scale = OMEGA / d
+        for f, c in enumerate(coupled(jac_ref, s, zs)):
+            q = psi_ref[f, s, :]
+            base_ref[f, s, :] = q + (rhs_ref[f, s, :] - d * q + c) * scale
 
 
 def from_sides(axis, first, second):
@@ -164,44 +180,42 @@
     return jnp.where(index > 0, below, 0.0), jnp.where(index < lax.axis_size(axis) - 1, above, 0.0)
 
 
-def update(psi_ref, z_ref, received, diag_ref, rhs_ref, jac_ref, new_ref, total_ref):
+def update(base_ref, received, diag_ref, jac_ref, new_ref, rows_ref):
     x0, x1, y0, y1, z0, z1 = received
     lane8 = iota((8, NZ), 1)
     edge = (lane8 < 2) | (lane8 >= NZ - 2)
+    row = iota((NY, NZ), 0)
+    outer = (row < 2) | (row >= NY - 2)
+    walls = []
     for g in range((FIELDS + 1) // 2):
-        rows = slice(8 * g, 8 * g + 8)
-        below, above = from_sides("wa", z0[rows, :], z1[rows, :])
-        both = jnp.where(lane8 % 4 >= 2, below, above)
-        for e in range(2 * g, min(2 * g + 2, FIELDS)):
-            for x in range(NX):
-                for t in range(2):
-                    shift = -(2 + 64 * (e % 2) + 4 * (2 * x + t))
-                    total_ref[e, tile_rows(x, t), :] = z_ref[e, tile_rows(x, t), :] + jnp.where(edge, lane_roll(both, shift), 0.0)
+        below, above = from_sides("wa", z0[8 * g : 8 * g + 8, :], z1[8 * g : 8 * g + 8, :])
+        walls.append(jnp.where(lane8 % 4 >= 2, below, above))
     for e in range(FIELDS):
         for r in range(2):
-            below, above = from_sides("gx", x0[e, r], x1[e, r])
-            total_ref[e, slab(r), :] += below
-            total_ref[e, slab(NX - 2 + r), :] += above
-        for r in range(2):
             below, above = from_sides("gy", y0[e, r], y1[e, r])
-            total_ref[e, edge_rows(r), :] += below
-            total_ref[e, edge_rows(NY - 2 + r), :] += above
+            rows_ref[e, edge_rows(r), :] = below
+            rows_ref[e, edge_rows(NY - 2 + r), :] = above
     for x in range(NX):
         s = slab(x)
-        d = diag_ref[s, :]
-        scale = OMEGA / d
-        zs = [total_ref[e, s, :] for e in range(FIELDS)]
-        for f in range(FIELDS):
-            c = jac_ref[f, s, :].astype(F32) * zs[0]
-            for e in range(1, FIELDS):
-                c = c + jac_ref[FIELDS * e + f, s, :].astype(F32) * zs[e]
-            q = psi_ref[f, s, :]
-            new_ref[f, s, :] = q + (rhs_ref[f, s, :] - d * q + c) * scale
-
-
-def middle_body(psi_ref, z_ref, r0, r1, r2, r3, r4, r5, diag_ref, rhs_ref, jac_ref, metric_ref, packed_metric,
-                new_ref, x0, x1, y0, y1, zz, far, total_ref):
-    update(psi_ref, z_ref, (r0, r1, r2, r3, r4, r5), diag_ref, rhs_ref, jac_ref, new_ref, total_ref)
+        zs = []
+        for e in range(FIELDS):
+            tiles = [
+                jnp.where(edge, lane_roll(walls[e // 2], -(2 + 64 * (e % 2) + 4 * (2 * x + t))), 0.0) for t in range(2)
+            ]
+            total = jnp.concatenate(tiles, axis=0) + jnp.where(outer, rows_ref[e, s, :], 0.0)
+            if x < 2:
+                total = total + from_sides("gx", x0[e, x], x1[e, x])[0]
+            if x >= NX - 2:
+                total = total + from_sides("gx", x0[e, x - NX + 2], x1[e, x - NX + 2])[1]
+            zs.append(total)
+        scale = OMEGA / diag_ref[s, :]
+        for f, c in enumerate(coupled(jac_ref, s, zs)):
+            new_ref[f, s, :] = base_ref[f, s, :] + c * scale
+
+
+def middle_body(base_ref, r0, r1, r2, r3, r4, r5, diag_ref, jac_ref, metric_ref, packed_metric,
+                new_ref, x0, x1, y0, y1, zz, far, rows_ref):
+    update(base_ref, (r0, r1, r2, r3, r4, r5), diag_ref, jac_ref, new_ref, rows_ref)
     emit_sends(new_ref, metric_ref, packed_metric, pack_edges(new_ref), (x0, x1, y0, y1, zz, far))
 
 
@@ -239,9 +253,9 @@
         hot_out[:, NZ * s : NZ * s + NZ] = jnp.where(hit, 1.0, 0.0).astype(jnp.bfloat16)
 
 
-def last_body(psi_ref, z_ref, r0, r1, r2, r3, r4, r5, diag_ref, rhs_ref, jac_ref, coef_ref, weight_ref, hot_ref, low_ref,
-              out_hbm, slots_ref, new_ref, total_ref, high_part, low_part, sem):
-    update(psi_ref, z_ref, (r0, r1, r2, r3, r4, r5), diag_ref, rhs_ref, jac_ref, new_ref, total_ref)
+def last_body(base_ref, r0, r1, r2, r3, r4, r5, diag_ref, jac_ref, coef_ref, weight_ref, hot_ref, low_ref,
+              out_hbm, slots_ref, new_ref, rows_ref, high_part, low_part, sem):
+    update(base_ref, (r0, r1, r2, r3, r4, r5), diag_ref, jac_ref, new_ref, rows_ref)
     copy = pltpu.make_async_copy(new_ref, out_hbm, sem)
     copy.start()
     lane = iota((8, NZ), 1)
@@ -323,6 +337,7 @@
     *sends, packed_metric, psi, metric = run(
         first_body, (psi, metric), SENDS + [((24, NZ), F32), FIELD, ((12, ROWS, NZ), F32)], sems=[(4,)], far=(0, 1)
     )
+    jac, rhs, diag, packed_metric = lax.optimization_barrier((jac, rhs, diag, packed_metric))
     wall = run(
         wall_body,
         (wall_coef.reshape(30 * NX, NY), ffd_ids.reshape(4 * NX, NY), ffd_weight.reshape(4 * NX, NY)),
@@ -330,16 +345,16 @@
     )
     for step in range(SWEEPS):
         received = exchange(sends)
-        (z,) = run(inner_body, (psi, metric), [FIELD])
-        if step == 0:
-            z, wall = lax.optimization_barrier((z, wall))
+        (base,) = run(inner_body, (psi, metric, diag, rhs, jac), [FIELD])
+        if step == 1:
+            base, wall = lax.optimization_barrier((base, wall))
         if step < SWEEPS - 1:
             psi, *sends = run(
-                middle_body, (psi, z, *received, diag, rhs, jac, metric, packed_metric), [FIELD] + SENDS, scratch=[FIELD]
+                middle_body, (base, *received, diag, jac, metric, packed_metric), [FIELD] + SENDS, scratch=[FIELD]
             )
         else:
             psi, slots = run(
-                last_body, (psi, z, *received, diag, rhs, jac, *wall), [FIELD, ((256, 48), F32)],
+                last_body, (base, *received, diag, jac, *wall), [FIELD, ((256, 48), F32)],
                 scratch=[FIELD, FIELD, ((48, 512), jnp.bfloat16), ((48, 512), jnp.bfloat16)], sems=[()], far_outs=(0,),
             )
     got = lax.all_to_all(slots.reshape(256, 1, 48), AXES, 0, 0).reshape(256, 48)

time: 72.7 us -> 72.7 us (level)
  waiting for transfers between devices: 2.61 us -> 1.58 us
  Pallas kernels: 7.79 us -> 8.76 us
    ppermute x24, waiting for transfers between devices: 2.61 us -> 1.58 us  [swap(): return lax.ppermute(v, axis, pairs(lax.axis_size(axis), odd))]
    pallas_call x11, Pallas kernels: 7.79 us -> 8.76 us  [run(): pl.pallas_call(body, out_shape=[jax.ShapeDtypeStruct(s, d) for s, d in ou...]
  transfers between devices with their start and end apart: 24 -> 24, of which waited for: 5 -> 3; matrix products, arithmetic and copies ran while one was open for 0% -> 0% of each run, Pallas kernels for 3% -> 4%
where the time goes in v8:
time: 72.7 us; the launch traced here: 72.6 us
  starting transfers between devices  38.1 us (52%)
  blocking collectives  22.3 us (31%)
  Pallas kernels  8.76 us (12%)
  waiting for transfers between devices  1.58 us (2%)
  local copies, waits for them, and re-layouts  1 us (1%)
  between operations  0.81 us (1%)
    ppermute x24, starting transfers between devices, swap(): return lax.ppermute(v, axis, pairs(lax.axis_size(axis), odd))  38.1 us
    all_to_all x1, blocking collectives, local(): got = lax.all_to_all(slots.reshape(256, 1, 48), AXES, 0, 0).reshape(256, 48)  22.3 us
    pallas_call x11, Pallas kernels, run(): pl.pallas_call(body, out_shape=[jax.ShapeDtypeStruct(s, d) for s, d in ou...  8.76 us
    ppermute x24, waiting for transfers between devices, swap(): return lax.ppermute(v, axis, pairs(lax.axis_size(axis), odd))  1.58 us
  transfers between devices with their start and end apart: 24, of which 3 were waited for; matrix products, arithmetic and copies ran while one was open for 0% of the time, Pallas kernels for 4%

profile of v8, /device:TPU:1, one launch (start us, length us, event | category | flops | bytes accessed | tf_op | source)
XLA Modules:
  0.0 72.6 jit_solution(2244375638896753686)
XLA Ops:
  0.7 1.6 %shard_map.95 = (f32[5,2,16,128]{3,2,1,0:T(8,128)S(1)}, f32[5,2,16,128]{3,2,1,0:T(8,128)S(1)}, f32[5,2,8,128]{3,2,1,0:T(8,128)S(1)}, f32[5,2,8,128]{3,2,1,0:T(8,...) custom-call(f32[5,128,128]{2,1,0:T(8,128)} %bitcast.39, ...), custom_call_target="tpu_custom_call" | custom-call | flops 1000000 | bytes 1000000 | tf_op jit(solution)/shard_map/pallas_call | solution.py:298
  2.2 4.6 %collective-permute-start.1 = (f32[5,2,16,128]{3,2,1,0:T(8,128)S(1)}, f32[5,2,16,128]{3,2,1,0:T(8,128)S(1)}, u32[]{:S(2)}, u32[]{:S(2)}) collective-permute-start(f32[5,2,16,128]{3,2,1,0:T(8,128)S(1)} %get-tuple-element.63), channel_id=1, source_target_pairs={{0,224},{32,64},{64,32},{96,128},{128,96},{160,192},{192,160},{224... | collective-permute-start | bytes 245768 | tf_op jit(solution)/shard_map/ppermute | solution.py:320
  6.8 0.0 collective-permute-start
  6.8 3.3 %collective-permute-start.5 = (f32[96,128]{1,0:T(8,128)S(1)}, f32[96,128]{1,0:T(8,128)S(1)}, u32[]{:S(2)}, u32[]{:S(2)}) collective-permute-start(f32[96,128]{1,0:T(8,128)S(1)} %get-tuple-element.68), channel_id=1, source_target_pairs={{0,3},{1,2},{2,1},{3,0},{4,7},{5,6},{6,5},{7,4},{8,11},{9,10},{10,... | collective-permute-start | bytes 147464 | tf_op jit(solution)/shard_map/ppermute | solution.py:320
  10.1 1.6 %collective-permute-start.2 = (f32[5,2,8,128]{3,2,1,0:T(8,128)S(1)}, f32[5,2,8,128]{3,2,1,0:T(8,128)S(1)}, u32[]{:S(2)}, u32[]{:S(2)}) collective-permute-start(f32[5,2,8,128]{3,2,1,0:T(8,128)S(1)} %get-tuple-element.65), channel_id=1, source_target_pairs={{0,4},{4,0},{8,12},{12,8},{16,20},{20,16},{24,28},{28,24},{1,5},{5... | collective-permute-start | bytes 122888 | tf_op jit(solution)/shard_map/ppermute | solution.py:320
  11.7 4.7 %collective-permute-start.3 = (f32[5,2,8,128]{3,2,1,0:T(8,128)S(1)}, f32[5,2,8,128]{3,2,1,0:T(8,128)S(1)}, u32[]{:S(2)}, u32[]{:S(2)}) collective-permute-start(f32[5,2,8,128]{3,2,1,0:T(8,128)S(1)} %get-tuple-element.66), channel_id=1, source_target_pairs={{0,28},{4,8},{8,4},{12,16},{16,12},{20,24},{24,20},{28,0},{1,29},{... | collective-permute-start | bytes 122888 | tf_op jit(solution)/shard_map/ppermute | solution.py:320
  16.4 0.0 collective-permute-done.1.r1
  16.4 0.1 collective-permute-start.4
  16.5 1.0 %copy-done.1 = f32[5,8,16,128]{3,2,1,0:T(8,128)S(1)} copy-done((f32[5,8,16,128]{3,2,1,0:T(8,128)S(1)}, f32[5,8,16,128]{3,2,1,0:T(8,128)}, u32[]{:S(2)}) %copy-start.1) | copy-done | bytes 327704
  17.5 0.6 shard_map.96.base_ref
  18.1 0.0 copy-start.4
  18.1 0.0 collective-permute-done.2.r2
  18.2 0.3 collective-permute-done.3.r3
  18.5 0.0 collective-permute-done.5.r5
  18.5 0.0 collective-permute-done.r0
  18.5 0.0 collective-permute-done.4.r4
  18.5 0.0 copy-start.6
  18.5 0.0 copy-start.2
  18.5 0.7 shard_map.97
  19.2 1.0 %collective-permute-start.7 = (f32[5,2,16,128]{3,2,1,0:T(8,128)S(1)}, f32[5,2,16,128]{3,2,1,0:T(8,128)S(1)}, u32[]{:S(2)}, u32[]{:S(2)}) collective-permute-start(f32[5,2,16,128]{3,2,1,0:T(8,128)S(1)} %get-tuple-element.78), channel_id=1, source_target_pairs={{0,224},{32,64},{64,32},{96,128},{128,96},{160,192},{192,160},{224... | collective-permute-start | bytes 245768 | tf_op jit(solution)/shard_map/ppermute | solution.py:320
  20.1 0.6 collective-permute-start.6
  20.7 1.8 %collective-permute-start.11 = (f32[96,128]{1,0:T(8,128)S(1)}, f32[96,128]{1,0:T(8,128)S(1)}, u32[]{:S(2)}, u32[]{:S(2)}) collective-permute-start(f32[96,128]{1,0:T(8,128)S(1)} %get-tuple-element.83), channel_id=1, source_target_pairs={{0,3},{1,2},{2,1},{3,0},{4,7},{5,6},{6,5},{7,4},{8,11},{9,10},{10,... | collective-permute-start | bytes 147464 | tf_op jit(solution)/shard_map/ppermute | solution.py:320
  22.5 0.0 collective-permute-start.8
  22.5 3.7 %collective-permute-start.9 = (f32[5,2,8,128]{3,2,1,0:T(8,128)S(1)}, f32[5,2,8,128]{3,2,1,0:T(8,128)S(1)}, u32[]{:S(2)}, u32[]{:S(2)}) collective-permute-start(f32[5,2,8,128]{3,2,1,0:T(8,128)S(1)} %get-tuple-element.81), channel_id=1, source_target_pairs={{0,28},{4,8},{8,4},{12,16},{16,12},{20,24},{24,20},{28,0},{1,29},{... | collective-permute-start | bytes 122888 | tf_op jit(solution)/shard_map/ppermute | solution.py:320
  26.3 0.0 collective-permute-done.7.r1
  26.3 0.8 %collective-permute-start.10 = (f32[24,128]{1,0:T(8,128)S(1)}, f32[24,128]{1,0:T(8,128)S(1)}, u32[]{:S(2)}, u32[]{:S(2)}) collective-permute-start(f32[24,128]{1,0:T(8,128)S(1)} %get-tuple-element.82), channel_id=1, source_target_pairs={{0,1},{1,0},{2,3},{3,2},{4,5},{5,4},{6,7},{7,6},{8,9},{9,8},{10,11... | collective-permute-start | bytes 36872 | tf_op jit(solution)/shard_map/ppermute | solution.py:320
  27.1 0.6 shard_map.99
  27.6 0.7 shard_map.98.base_ref
  28.3 0.0 collective-permute-done.8.r2
  28.3 0.0 collective-permute-done.9.r3
  28.3 0.0 collective-permute-done.11.r5
  28.4 0.0 collective-permute-done.6.r0
  28.4 0.0 collective-permute-done.10.r4
  28.4 0.7 shard_map.100
  29.0 1.0 %collective-permute-start.13 = (f32[5,2,16,128]{3,2,1,0:T(8,128)S(1)}, f32[5,2,16,128]{3,2,1,0:T(8,128)S(1)}, u32[]{:S(2)}, u32[]{:S(2)}) collective-permute-start(f32[5,2,16,128]{3,2,1,0:T(8,128)S(1)} %get-tuple-element.87), channel_id=1, source_target_pairs={{0,224},{32,64},{64,32},{96,128},{128,96},{160,192},{192,160},{224... | collective-permute-start | bytes 245768 | tf_op jit(solution)/shard_map/ppermute | solution.py:320
  30.1 0.5 collective-permute-start.12
  30.6 2.5 %collective-permute-start.17 = (f32[96,128]{1,0:T(8,128)S(1)}, f32[96,128]{1,0:T(8,128)S(1)}, u32[]{:S(2)}, u32[]{:S(2)}) collective-permute-start(f32[96,128]{1,0:T(8,128)S(1)} %get-tuple-element.92), channel_id=1, source_target_pairs={{0,3},{1,2},{2,1},{3,0},{4,7},{5,6},{6,5},{7,4},{8,11},{9,10},{10,... | collective-permute-start | bytes 147464 | tf_op jit(solution)/shard_map/ppermute | solution.py:320
  33.0 0.4 collective-permute-start.14
  33.4 3.0 %collective-permute-start.15 = (f32[5,2,8,128]{3,2,1,0:T(8,128)S(1)}, f32[5,2,8,128]{3,2,1,0:T(8,128)S(1)}, u32[]{:S(2)}, u32[]{:S(2)}) collective-permute-start(f32[5,2,8,128]{3,2,1,0:T(8,128)S(1)} %get-tuple-element.90), channel_id=1, source_target_pairs={{0,28},{4,8},{8,4},{12,16},{16,12},{20,24},{24,20},{28,0},{1,29},{... | collective-permute-start | bytes 122888 | tf_op jit(solution)/shard_map/ppermute | solution.py:320
  36.4 0.0 collective-permute-done.13.r1
  36.4 0.8 %collective-permute-start.16 = (f32[24,128]{1,0:T(8,128)S(1)}, f32[24,128]{1,0:T(8,128)S(1)}, u32[]{:S(2)}, u32[]{:S(2)}) collective-permute-start(f32[24,128]{1,0:T(8,128)S(1)} %get-tuple-element.91), channel_id=1, source_target_pairs={{0,1},{1,0},{2,3},{3,2},{4,5},{5,4},{6,7},{7,6},{8,9},{9,8},{10,11... | collective-permute-start | bytes 36872 | tf_op jit(solution)/shard_map/ppermute | solution.py:320
  37.2 0.7 shard_map.101.base_ref
  37.8 0.0 collective-permute-done.14.r2
  37.9 0.5 collective-permute-done.15.r3
  38.4 0.0 collective-permute-done.17.r5
  38.4 0.0 collective-permute-done.12.r0
  38.4 0.0 collective-permute-done.16.r4
  38.4 0.7 shard_map.102
  39.1 0.7 collective-permute-start.19
  39.7 0.9 %collective-permute-start.18 = (f32[5,2,16,128]{3,2,1,0:T(8,128)S(1)}, f32[5,2,16,128]{3,2,1,0:T(8,128)S(1)}, u32[]{:S(2)}, u32[]{:S(2)}) collective-permute-start(f32[5,2,16,128]{3,2,1,0:T(8,128)S(1)} %get-tuple-element.94), channel_id=1, source_target_pairs={{0,32},{32,0},{64,96},{96,64},{128,160},{160,128},{192,224},{224,1... | collective-permute-start | bytes 245768 | tf_op jit(solution)/shard_map/ppermute | solution.py:320
  40.6 2.8 %collective-permute-start.23 = (f32[96,128]{1,0:T(8,128)S(1)}, f32[96,128]{1,0:T(8,128)S(1)}, u32[]{:S(2)}, u32[]{:S(2)}) collective-permute-start(f32[96,128]{1,0:T(8,128)S(1)} %get-tuple-element.101), channel_id=1, source_target_pairs={{0,3},{1,2},{2,1},{3,0},{4,7},{5,6},{6,5},{7,4},{8,11},{9,10},{10,... | collective-permute-start | bytes 147464 | tf_op jit(solution)/shard_map/ppermute | solution.py:320
  43.4 0.0 collective-permute-start.20
  43.4 2.9 %collective-permute-start.21 = (f32[5,2,8,128]{3,2,1,0:T(8,128)S(1)}, f32[5,2,8,128]{3,2,1,0:T(8,128)S(1)}, u32[]{:S(2)}, u32[]{:S(2)}) collective-permute-start(f32[5,2,8,128]{3,2,1,0:T(8,128)S(1)} %get-tuple-element.99), channel_id=1, source_target_pairs={{0,28},{4,8},{8,4},{12,16},{16,12},{20,24},{24,20},{28,0},{1,29},{... | collective-permute-start | bytes 122888 | tf_op jit(solution)/shard_map/ppermute | solution.py:320
  46.3 0.0 collective-permute-done.19.r1
  46.3 0.6 collective-permute-start.22
  46.9 0.7 shard_map.103.base_ref
  47.6 0.0 collective-permute-done.20.r2
  47.6 0.7 collective-permute-done.21.r3
  48.2 0.0 collective-permute-done.23.r5
  48.2 0.0 collective-permute-done.18.r0
  48.2 0.0 collective-permute-done.22.r4
  48.2 1.3 %shard_map.104 = (f32[5,128,128]{2,1,0:T(8,128)}, f32[256,48]{1,0:T(8,128)S(1)}) custom-call(f32[5,128,128]{2,1,0:T(8,128)S(1)} %shard_map.103.base_ref, f32[5,2,16,128]{3,2,1,0:T(8,128)S(1)} %collective-permute-done.18.r0, f32[5,2,16,128]{3,2,1,0:T(8,128)S(1)} %collective-permute-done.19.r1, f32[5,2,8,128]{3,2,1,0:T(8,128)S(1)} %collective-permute-done.20.r2, ...), custom_call_target="tpu_custom_call" | custom-call | flops 1000000 | bytes 1000000 | tf_op jit(solution)/shard_map/pallas_call | solution.py:298
  49.6 22.3 %all_to_all.5 = f32[256,1,48]{2,1,0:T(1,128)S(1)} all-to-all(f32[256,1,48]{2,1,0:T(1,128)S(1)} %bitcast.34), channel_id=1, replica_groups=mesh['gx'=8,'gy'=8,'wa'=4] {'gx','gy','wa'}, dimensions={0} | all-to-all | bytes 98304 | tf_op jit(solution)/shard_map/all_to_all | solution.py:360
  71.9 0.7 shard_map.105
  (10 shorter events, 0.0 us)
Async XLA Ops:
  0.6 15.9 %copy-start = (bf16[5,5,8,16,128]{4,3,2,1,0:T(8,128)(2,1)S(1)}, bf16[5,5,8,16,128]{4,3,2,1,0:T(8,128)(2,1)}, u32[]{:S(2)}) copy-start(bf16[5,5,8,16,128]{4,3,2,1,0:T(8,128)(2,1)} %param.12) | copy-start | bytes 2457604
  0.6 15.9 %copy-start.3 = (f32[8,16,128]{2,1,0:T(8,128)S(1)}, f32[8,16,128]{2,1,0:T(8,128)}, u32[]{:S(2)}) copy-start(f32[8,16,128]{2,1,0:T(8,128)} %param.10) | copy-start | bytes 196612
  2.2 14.2 %collective-permute-start.1 = (f32[5,2,16,128]{3,2,1,0:T(8,128)S(1)}, f32[5,2,16,128]{3,2,1,0:T(8,128)S(1)}, u32[]{:S(2)}, u32[]{:S(2)}) collective-permute-start(f32[5,2,16,128]{3,2,1,0:T(8,128)S(1)} %get-tuple-element.63), channel_id=1, source_target_pairs={{0,224},{32,64},{64,32},{96,128},{128,96},{160,192},{192,160},{224... | collective-permute-start | bytes 245768 | tf_op jit(solution)/shard_map/ppermute | solution.py:320
  6.8 11.7 %collective-permute-start = (f32[5,2,16,128]{3,2,1,0:T(8,128)S(1)}, f32[5,2,16,128]{3,2,1,0:T(8,128)S(1)}, u32[]{:S(2)}, u32[]{:S(2)}) collective-permute-start(f32[5,2,16,128]{3,2,1,0:T(8,128)S(1)} %get-tuple-element.61), channel_id=1, source_target_pairs={{0,32},{32,0},{64,96},{96,64},{128,160},{160,128},{192,224},{224,1... | collective-permute-start | bytes 245768 | tf_op jit(solution)/shard_map/ppermute | solution.py:320
  6.8 11.7 %collective-permute-start.5 = (f32[96,128]{1,0:T(8,128)S(1)}, f32[96,128]{1,0:T(8,128)S(1)}, u32[]{:S(2)}, u32[]{:S(2)}) collective-permute-start(f32[96,128]{1,0:T(8,128)S(1)} %get-tuple-element.68), channel_id=1, source_target_pairs={{0,3},{1,2},{2,1},{3,0},{4,7},{5,6},{6,5},{7,4},{8,11},{9,10},{10,... | collective-permute-start | bytes 147464 | tf_op jit(solution)/shard_map/ppermute | solution.py:320
  10.1 8.1 %collective-permute-start.2 = (f32[5,2,8,128]{3,2,1,0:T(8,128)S(1)}, f32[5,2,8,128]{3,2,1,0:T(8,128)S(1)}, u32[]{:S(2)}, u32[]{:S(2)}) collective-permute-start(f32[5,2,8,128]{3,2,1,0:T(8,128)S(1)} %get-tuple-element.65), channel_id=1, source_target_pairs={{0,4},{4,0},{8,12},{12,8},{16,20},{20,16},{24,28},{28,24},{1,5},{5... | collective-permute-start | bytes 122888 | tf_op jit(solution)/shard_map/ppermute | solution.py:320
  11.7 6.8 %collective-permute-start.3 = (f32[5,2,8,128]{3,2,1,0:T(8,128)S(1)}, f32[5,2,8,128]{3,2,1,0:T(8,128)S(1)}, u32[]{:S(2)}, u32[]{:S(2)}) collective-permute-start(f32[5,2,8,128]{3,2,1,0:T(8,128)S(1)} %get-tuple-element.66), channel_id=1, source_target_pairs={{0,28},{4,8},{8,4},{12,16},{16,12},{20,24},{24,20},{28,0},{1,29},{... | collective-permute-start | bytes 122888 | tf_op jit(solution)/shard_map/ppermute | solution.py:320
  16.4 2.1 %collective-permute-start.4 = (f32[24,128]{1,0:T(8,128)S(1)}, f32[24,128]{1,0:T(8,128)S(1)}, u32[]{:S(2)}, u32[]{:S(2)}) collective-permute-start(f32[24,128]{1,0:T(8,128)S(1)} %get-tuple-element.67), channel_id=1, source_target_pairs={{0,1},{1,0},{2,3},{3,2},{4,5},{5,4},{6,7},{7,6},{8,9},{9,8},{10,11... | collective-permute-start | bytes 36872 | tf_op jit(solution)/shard_map/ppermute | solution.py:320
  16.5 1.0 %copy-start.1 = (f32[5,8,16,128]{3,2,1,0:T(8,128)S(1)}, f32[5,8,16,128]{3,2,1,0:T(8,128)}, u32[]{:S(2)}) copy-start(f32[5,8,16,128]{3,2,1,0:T(8,128)} %param.9) | copy-start | bytes 983044
  18.1 8.9 %copy-start.4 = (f32[3,10,8,16]{3,2,1,0:T(8,128)S(1)}, f32[3,10,8,16]{3,2,1,0:T(8,128)}, u32[]{:S(2)}) copy-start(f32[3,10,8,16]{3,2,1,0:T(8,128)} %param.13) | copy-start | bytes 46084
  18.5 8.6 %copy-start.6 = (f32[4,8,16]{2,1,0:T(8,128)S(1)}, f32[4,8,16]{2,1,0:T(8,128)}, u32[]{:S(2)}) copy-start(f32[4,8,16]{2,1,0:T(8,128)} %param.15) | copy-start | bytes 6148
  18.5 9.1 %copy-start.2 = (f32[5,8,16,128]{3,2,1,0:T(8,128)S(1)}, f32[5,8,16,128]{3,2,1,0:T(8,128)}, u32[]{:S(2)}) copy-start(f32[5,8,16,128]{3,2,1,0:T(8,128)} %param.9) | copy-start | bytes 983044
  19.2 7.9 %copy-start.5 = (s32[4,8,16]{2,1,0:T(8,128)S(1)}, s32[4,8,16]{2,1,0:T(8,128)}, u32[]{:S(2)}) copy-start(s32[4,8,16]{2,1,0:T(8,128)} %param.14) | copy-start | bytes 6148
  19.2 7.1 %collective-permute-start.7 = (f32[5,2,16,128]{3,2,1,0:T(8,128)S(1)}, f32[5,2,16,128]{3,2,1,0:T(8,128)S(1)}, u32[]{:S(2)}, u32[]{:S(2)}) collective-permute-start(f32[5,2,16,128]{3,2,1,0:T(8,128)S(1)} %get-tuple-element.78), channel_id=1, source_target_pairs={{0,224},{32,64},{64,32},{96,128},{128,96},{160,192},{192,160},{224... | collective-permute-start | bytes 245768 | tf_op jit(solution)/shard_map/ppermute | solution.py:320
  20.1 8.2 %collective-permute-start.6 = (f32[5,2,16,128]{3,2,1,0:T(8,128)S(1)}, f32[5,2,16,128]{3,2,1,0:T(8,128)S(1)}, u32[]{:S(2)}, u32[]{:S(2)}) collective-permute-start(f32[5,2,16,128]{3,2,1,0:T(8,128)S(1)} %get-tuple-element.76), channel_id=1, source_target_pairs={{0,32},{32,0},{64,96},{96,64},{128,160},{160,128},{192,224},{224,1... | collective-permute-start | bytes 245768 | tf_op jit(solution)/shard_map/ppermute | solution.py:320
  20.7 7.6 %collective-permute-start.11 = (f32[96,128]{1,0:T(8,128)S(1)}, f32[96,128]{1,0:T(8,128)S(1)}, u32[]{:S(2)}, u32[]{:S(2)}) collective-permute-start(f32[96,128]{1,0:T(8,128)S(1)} %get-tuple-element.83), channel_id=1, source_target_pairs={{0,3},{1,2},{2,1},{3,0},{4,7},{5,6},{6,5},{7,4},{8,11},{9,10},{10,... | collective-permute-start | bytes 147464 | tf_op jit(solution)/shard_map/ppermute | solution.py:320
  22.5 5.8 %collective-permute-start.8 = (f32[5,2,8,128]{3,2,1,0:T(8,128)S(1)}, f32[5,2,8,128]{3,2,1,0:T(8,128)S(1)}, u32[]{:S(2)}, u32[]{:S(2)}) collective-permute-start(f32[5,2,8,128]{3,2,1,0:T(8,128)S(1)} %get-tuple-element.80), channel_id=1, source_target_pairs={{0,4},{4,0},{8,12},{12,8},{16,20},{20,16},{24,28},{28,24},{1,5},{5... | collective-permute-start | bytes 122888 | tf_op jit(solution)/shard_map/ppermute | solution.py:320
  22.5 5.8 %collective-permute-start.9 = (f32[5,2,8,128]{3,2,1,0:T(8,128)S(1)}, f32[5,2,8,128]{3,2,1,0:T(8,128)S(1)}, u32[]{:S(2)}, u32[]{:S(2)}) collective-permute-start(f32[5,2,8,128]{3,2,1,0:T(8,128)S(1)} %get-tuple-element.81), channel_id=1, source_target_pairs={{0,28},{4,8},{8,4},{12,16},{16,12},{20,24},{24,20},{28,0},{1,29},{... | collective-permute-start | bytes 122888 | tf_op jit(solution)/shard_map/ppermute | solution.py:320
  26.3 2.1 %collective-permute-start.10 = (f32[24,128]{1,0:T(8,128)S(1)}, f32[24,128]{1,0:T(8,128)S(1)}, u32[]{:S(2)}, u32[]{:S(2)}) collective-permute-start(f32[24,128]{1,0:T(8,128)S(1)} %get-tuple-element.82), channel_id=1, source_target_pairs={{0,1},{1,0},{2,3},{3,2},{4,5},{5,4},{6,7},{7,6},{8,9},{9,8},{10,11... | collective-permute-start | bytes 36872 | tf_op jit(solution)/shard_map/ppermute | solution.py:320
  29.0 7.4 %collective-permute-start.13 = (f32[5,2,16,128]{3,2,1,0:T(8,128)S(1)}, f32[5,2,16,128]{3,2,1,0:T(8,128)S(1)}, u32[]{:S(2)}, u32[]{:S(2)}) collective-permute-start(f32[5,2,16,128]{3,2,1,0:T(8,128)S(1)} %get-tuple-element.87), channel_id=1, source_target_pairs={{0,224},{32,64},{64,32},{96,128},{128,96},{160,192},{192,160},{224... | collective-permute-start | bytes 245768 | tf_op jit(solution)/shard_map/ppermute | solution.py:320
  30.1 8.3 %collective-permute-start.12 = (f32[5,2,16,128]{3,2,1,0:T(8,128)S(1)}, f32[5,2,16,128]{3,2,1,0:T(8,128)S(1)}, u32[]{:S(2)}, u32[]{:S(2)}) collective-permute-start(f32[5,2,16,128]{3,2,1,0:T(8,128)S(1)} %get-tuple-element.85), channel_id=1, source_target_pairs={{0,32},{32,0},{64,96},{96,64},{128,160},{160,128},{192,224},{224,1... | collective-permute-start | bytes 245768 | tf_op jit(solution)/shard_map/ppermute | solution.py:320
  30.6 7.8 %collective-permute-start.17 = (f32[96,128]{1,0:T(8,128)S(1)}, f32[96,128]{1,0:T(8,128)S(1)}, u32[]{:S(2)}, u32[]{:S(2)}) collective-permute-start(f32[96,128]{1,0:T(8,128)S(1)} %get-tuple-element.92), channel_id=1, source_target_pairs={{0,3},{1,2},{2,1},{3,0},{4,7},{5,6},{6,5},{7,4},{8,11},{9,10},{10,... | collective-permute-start | bytes 147464 | tf_op jit(solution)/shard_map/ppermute | solution.py:320
  33.0 4.8 %collective-permute-start.14 = (f32[5,2,8,128]{3,2,1,0:T(8,128)S(1)}, f32[5,2,8,128]{3,2,1,0:T(8,128)S(1)}, u32[]{:S(2)}, u32[]{:S(2)}) collective-permute-start(f32[5,2,8,128]{3,2,1,0:T(8,128)S(1)} %get-tuple-element.89), channel_id=1, source_target_pairs={{0,4},{4,0},{8,12},{12,8},{16,20},{20,16},{24,28},{28,24},{1,5},{5... | collective-permute-start | bytes 122888 | tf_op jit(solution)/shard_map/ppermute | solution.py:320
  33.4 5.0 %collective-permute-start.15 = (f32[5,2,8,128]{3,2,1,0:T(8,128)S(1)}, f32[5,2,8,128]{3,2,1,0:T(8,128)S(1)}, u32[]{:S(2)}, u32[]{:S(2)}) collective-permute-start(f32[5,2,8,128]{3,2,1,0:T(8,128)S(1)} %get-tuple-element.90), channel_id=1, source_target_pairs={{0,28},{4,8},{8,4},{12,16},{16,12},{20,24},{24,20},{28,0},{1,29},{... | collective-permute-start | bytes 122888 | tf_op jit(solution)/shard_map/ppermute | solution.py:320
  36.4 2.0 %collective-permute-start.16 = (f32[24,128]{1,0:T(8,128)S(1)}, f32[24,128]{1,0:T(8,128)S(1)}, u32[]{:S(2)}, u32[]{:S(2)}) collective-permute-start(f32[24,128]{1,0:T(8,128)S(1)} %get-tuple-element.91), channel_id=1, source_target_pairs={{0,1},{1,0},{2,3},{3,2},{4,5},{5,4},{6,7},{7,6},{8,9},{9,8},{10,11... | collective-permute-start | bytes 36872 | tf_op jit(solution)/shard_map/ppermute | solution.py:320
  39.1 7.3 %collective-permute-start.19 = (f32[5,2,16,128]{3,2,1,0:T(8,128)S(1)}, f32[5,2,16,128]{3,2,1,0:T(8,128)S(1)}, u32[]{:S(2)}, u32[]{:S(2)}) collective-permute-start(f32[5,2,16,128]{3,2,1,0:T(8,128)S(1)} %get-tuple-element.96), channel_id=1, source_target_pairs={{0,224},{32,64},{64,32},{96,128},{128,96},{160,192},{192,160},{224... | collective-permute-start | bytes 245768 | tf_op jit(solution)/shard_map/ppermute | solution.py:320
  39.7 8.5 %collective-permute-start.18 = (f32[5,2,16,128]{3,2,1,0:T(8,128)S(1)}, f32[5,2,16,128]{3,2,1,0:T(8,128)S(1)}, u32[]{:S(2)}, u32[]{:S(2)}) collective-permute-start(f32[5,2,16,128]{3,2,1,0:T(8,128)S(1)} %get-tuple-element.94), channel_id=1, source_target_pairs={{0,32},{32,0},{64,96},{96,64},{128,160},{160,128},{192,224},{224,1... | collective-permute-start | bytes 245768 | tf_op jit(solution)/shard_map/ppermute | solution.py:320
  40.6 7.6 %collective-permute-start.23 = (f32[96,128]{1,0:T(8,128)S(1)}, f32[96,128]{1,0:T(8,128)S(1)}, u32[]{:S(2)}, u32[]{:S(2)}) collective-permute-start(f32[96,128]{1,0:T(8,128)S(1)} %get-tuple-element.101), channel_id=1, source_target_pairs={{0,3},{1,2},{2,1},{3,0},{4,7},{5,6},{6,5},{7,4},{8,11},{9,10},{10,... | collective-permute-start | bytes 147464 | tf_op jit(solution)/shard_map/ppermute | solution.py:320
  43.4 4.2 %collective-permute-start.20 = (f32[5,2,8,128]{3,2,1,0:T(8,128)S(1)}, f32[5,2,8,128]{3,2,1,0:T(8,128)S(1)}, u32[]{:S(2)}, u32[]{:S(2)}) collective-permute-start(f32[5,2,8,128]{3,2,1,0:T(8,128)S(1)} %get-tuple-element.98), channel_id=1, source_target_pairs={{0,4},{4,0},{8,12},{12,8},{16,20},{20,16},{24,28},{28,24},{1,5},{5... | collective-permute-start | bytes 122888 | tf_op jit(solution)/shard_map/ppermute | solution.py:320
  43.4 4.8 %collective-permute-start.21 = (f32[5,2,8,128]{3,2,1,0:T(8,128)S(1)}, f32[5,2,8,128]{3,2,1,0:T(8,128)S(1)}, u32[]{:S(2)}, u32[]{:S(2)}) collective-permute-start(f32[5,2,8,128]{3,2,1,0:T(8,128)S(1)} %get-tuple-element.99), channel_id=1, source_target_pairs={{0,28},{4,8},{8,4},{12,16},{16,12},{20,24},{24,20},{28,0},{1,29},{... | collective-permute-start | bytes 122888 | tf_op jit(solution)/shard_map/ppermute | solution.py:320
  46.3 1.9 %collective-permute-start.22 = (f32[24,128]{1,0:T(8,128)S(1)}, f32[24,128]{1,0:T(8,128)S(1)}, u32[]{:S(2)}, u32[]{:S(2)}) collective-permute-start(f32[24,128]{1,0:T(8,128)S(1)} %get-tuple-element.100), channel_id=1, source_target_pairs={{0,1},{1,0},{2,3},{3,2},{4,5},{5,4},{6,7},{7,6},{8,9},{9,8},{10,11... | collective-permute-start | bytes 36872 | tf_op jit(solution)/shard_map/ppermute | solution.py:320

commit v9 on v7

--- a/solution.py
+++ b/solution.py
@@ -10,7 +10,7 @@
 AXES = ("gx", "gy", "wa")
 FIELDS, NX, NY, NZ = 5, 8, 16, 128
 ROWS = NX * NY
-FAR_ROWS = 96
+FAR_ROWS = 88
 F32 = jnp.float32
 VMEM = pl.BlockSpec(memory_space=pltpu.VMEM)
 
@@ -305,11 +305,11 @@
     def swap(v, axis, odd):
         return lax.ppermute(v, axis, pairs(lax.axis_size(axis), odd))
     two_hops = swap(x1, "gx", 1)
-    x = swap(x0, "gx", 0), two_hops
+    one_hop = swap(x0, "gx", 0)
     far = swap(far, "wa", 1)
     y = swap(y0, "gy", 0), swap(y1, "gy", 1)
-    zz, two_hops = lax.optimization_barrier((zz, two_hops))
-    x = x[0], two_hops
+    zz, one_hop = lax.optimization_barrier((zz, one_hop))
+    x = one_hop, two_hops
     z = swap(zz, "wa", 0), far
     return (*x, *y, *z)
 

time: 72.7 us -> 72.7 us (level)
  starting transfers between devices: 38.4 us -> 36.2 us
  waiting for transfers between devices: 2.61 us -> 4.62 us
    ppermute x24, starting transfers between devices: 38.4 us -> 36.2 us  [swap(): return lax.ppermute(v, axis, pairs(lax.axis_size(axis), odd))]
    ppermute x24, waiting for transfers between devices: 2.61 us -> 4.62 us  [swap(): return lax.ppermute(v, axis, pairs(lax.axis_size(axis), odd))]
where the time goes in v9:
time: 72.7 us; the launch traced here: 72.5 us
  starting transfers between devices  36.2 us (50%)
  blocking collectives  22.4 us (31%)
  Pallas kernels  7.84 us (11%)
  waiting for transfers between devices  4.62 us (6%)
  between operations  0.81 us (1%)
    ppermute x24, starting transfers between devices, swap(): return lax.ppermute(v, axis, pairs(lax.axis_size(axis), odd))  36.2 us
    all_to_all x1, blocking collectives, local(): got = lax.all_to_all(slots.reshape(256, 1, 48), AXES, 0, 0).reshape(256, 48)  22.4 us
    pallas_call x11, Pallas kernels, run(): pl.pallas_call(body, out_shape=[jax.ShapeDtypeStruct(s, d) for s, d in ou...  7.84 us
    ppermute x24, waiting for transfers between devices, swap(): return lax.ppermute(v, axis, pairs(lax.axis_size(axis), odd))  4.62 us
  transfers between devices with their start and end apart: 24, of which 5 were waited for; matrix products, arithmetic and copies ran while one was open for 0% of the time, Pallas kernels for 3%

profile of v9, /device:TPU:1, one launch (start us, length us, event | category | flops | bytes accessed | tf_op | source)
XLA Modules:
  0.0 72.5 jit_solution(10093465231889647146)
XLA Ops:
  0.6 1.5 %shard_map.95 = (f32[5,2,16,128]{3,2,1,0:T(8,128)S(1)}, f32[5,2,16,128]{3,2,1,0:T(8,128)S(1)}, f32[5,2,8,128]{3,2,1,0:T(8,128)S(1)}, f32[5,2,8,128]{3,2,1,0:T(8,...) custom-call(f32[5,128,128]{2,1,0:T(8,128)} %bitcast.31, ...), custom_call_target="tpu_custom_call" | custom-call | flops 1000000 | bytes 1000000 | tf_op jit(solution)/shard_map/pallas_call | solution.py:284
  2.1 0.0 copy-start
  2.1 2.1 %collective-permute-start = (f32[5,2,16,128]{3,2,1,0:T(8,128)S(1)}, f32[5,2,16,128]{3,2,1,0:T(8,128)S(1)}, u32[]{:S(2)}, u32[]{:S(2)}) collective-permute-start(f32[5,2,16,128]{3,2,1,0:T(8,128)S(1)} %get-tuple-element.59), channel_id=1, source_target_pairs={{0,32},{32,0},{64,96},{96,64},{128,160},{160,128},{192,224},{224,1... | collective-permute-start | bytes 245768 | tf_op jit(solution)/shard_map/ppermute | solution.py:306
  4.3 2.7 %collective-permute-start.1 = (f32[5,2,16,128]{3,2,1,0:T(8,128)S(1)}, f32[5,2,16,128]{3,2,1,0:T(8,128)S(1)}, u32[]{:S(2)}, u32[]{:S(2)}) collective-permute-start(f32[5,2,16,128]{3,2,1,0:T(8,128)S(1)} %get-tuple-element.61), channel_id=1, source_target_pairs={{0,224},{32,64},{64,32},{96,128},{128,96},{160,192},{192,160},{224... | collective-permute-start | bytes 245768 | tf_op jit(solution)/shard_map/ppermute | solution.py:306
  7.0 3.9 %collective-permute-start.5 = (f32[88,128]{1,0:T(8,128)S(1)}, f32[88,128]{1,0:T(8,128)S(1)}, u32[]{:S(2)}, u32[]{:S(2)}) collective-permute-start(f32[88,128]{1,0:T(8,128)S(1)} %get-tuple-element.65), channel_id=1, source_target_pairs={{0,3},{1,2},{2,1},{3,0},{4,7},{5,6},{6,5},{7,4},{8,11},{9,10},{10,... | collective-permute-start | bytes 135176 | tf_op jit(solution)/shard_map/ppermute | solution.py:306
  10.8 1.6 %collective-permute-start.2 = (f32[5,2,8,128]{3,2,1,0:T(8,128)S(1)}, f32[5,2,8,128]{3,2,1,0:T(8,128)S(1)}, u32[]{:S(2)}, u32[]{:S(2)}) collective-permute-start(f32[5,2,8,128]{3,2,1,0:T(8,128)S(1)} %get-tuple-element.62), channel_id=1, source_target_pairs={{0,4},{4,0},{8,12},{12,8},{16,20},{20,16},{24,28},{28,24},{1,5},{5... | collective-permute-start | bytes 122888 | tf_op jit(solution)/shard_map/ppermute | solution.py:306
  12.5 4.7 %collective-permute-start.3 = (f32[5,2,8,128]{3,2,1,0:T(8,128)S(1)}, f32[5,2,8,128]{3,2,1,0:T(8,128)S(1)}, u32[]{:S(2)}, u32[]{:S(2)}) collective-permute-start(f32[5,2,8,128]{3,2,1,0:T(8,128)S(1)} %get-tuple-element.63), channel_id=1, source_target_pairs={{0,28},{4,8},{8,4},{12,16},{16,12},{20,24},{24,20},{28,0},{1,29},{... | collective-permute-start | bytes 122888 | tf_op jit(solution)/shard_map/ppermute | solution.py:306
  17.1 0.0 collective-permute-done.r0
  17.1 0.0 collective-permute-start.4
  17.1 0.0 copy-start.4
  17.2 0.0 copy-start.5
  17.2 0.0 copy-start.1
  17.2 0.4 shard_map.96.z_ref
  17.6 0.4 copy-done.3
  18.0 0.6 shard_map.97
  18.6 0.0 collective-permute-done.2.r2
  18.6 0.1 collective-permute-done.3.r3
  18.7 0.0 collective-permute-done.5.r5
  18.7 0.0 collective-permute-done.1.r1
  18.7 0.0 collective-permute-done.4.r4
  18.8 0.2 copy-done.2
  18.9 0.7 shard_map.98
  19.6 0.0 collective-permute-start.6
  19.7 1.6 %collective-permute-start.7 = (f32[5,2,16,128]{3,2,1,0:T(8,128)S(1)}, f32[5,2,16,128]{3,2,1,0:T(8,128)S(1)}, u32[]{:S(2)}, u32[]{:S(2)}) collective-permute-start(f32[5,2,16,128]{3,2,1,0:T(8,128)S(1)} %get-tuple-element.71), channel_id=1, source_target_pairs={{0,224},{32,64},{64,32},{96,128},{128,96},{160,192},{192,160},{224... | collective-permute-start | bytes 245768 | tf_op jit(solution)/shard_map/ppermute | solution.py:306
  21.3 1.5 %collective-permute-start.11 = (f32[88,128]{1,0:T(8,128)S(1)}, f32[88,128]{1,0:T(8,128)S(1)}, u32[]{:S(2)}, u32[]{:S(2)}) collective-permute-start(f32[88,128]{1,0:T(8,128)S(1)} %get-tuple-element.75), channel_id=1, source_target_pairs={{0,3},{1,2},{2,1},{3,0},{4,7},{5,6},{6,5},{7,4},{8,11},{9,10},{10,... | collective-permute-start | bytes 135176 | tf_op jit(solution)/shard_map/ppermute | solution.py:306
  22.8 0.0 collective-permute-start.8
  22.8 2.9 %collective-permute-start.9 = (f32[5,2,8,128]{3,2,1,0:T(8,128)S(1)}, f32[5,2,8,128]{3,2,1,0:T(8,128)S(1)}, u32[]{:S(2)}, u32[]{:S(2)}) collective-permute-start(f32[5,2,8,128]{3,2,1,0:T(8,128)S(1)} %get-tuple-element.73), channel_id=1, source_target_pairs={{0,28},{4,8},{8,4},{12,16},{16,12},{20,24},{24,20},{28,0},{1,29},{... | collective-permute-start | bytes 122888 | tf_op jit(solution)/shard_map/ppermute | solution.py:306
  25.6 0.0 collective-permute-done.6.r0
  25.6 0.0 collective-permute-start.10
  25.6 0.4 shard_map.99.z_ref
  26.1 0.2 collective-permute-done.8.r2
  26.3 1.2 %collective-permute-done.9.r3 = f32[5,2,8,128]{3,2,1,0:T(8,128)S(1)} collective-permute-done((f32[5,2,8,128]{3,2,1,0:T(8,128)S(1)}, f32[5,2,8,128]{3,2,1,0:T(8,128)S(1)}, u32[]{:S(2)}, u32[]{:S(2)}) %collective-permute-start.9) | collective-permute-done | bytes 40992 | tf_op jit(solution)/shard_map/ppermute | solution.py:306
  27.5 0.0 collective-permute-done.11.r5
  27.5 0.0 collective-permute-done.7.r1
  27.5 0.0 collective-permute-done.10.r4
  27.5 0.7 shard_map.100
  28.2 0.1 collective-permute-start.12
  28.4 2.3 %collective-permute-start.13 = (f32[5,2,16,128]{3,2,1,0:T(8,128)S(1)}, f32[5,2,16,128]{3,2,1,0:T(8,128)S(1)}, u32[]{:S(2)}, u32[]{:S(2)}) collective-permute-start(f32[5,2,16,128]{3,2,1,0:T(8,128)S(1)} %get-tuple-element.80), channel_id=1, source_target_pairs={{0,224},{32,64},{64,32},{96,128},{128,96},{160,192},{192,160},{224... | collective-permute-start | bytes 245768 | tf_op jit(solution)/shard_map/ppermute | solution.py:306
  30.7 3.4 %collective-permute-start.17 = (f32[88,128]{1,0:T(8,128)S(1)}, f32[88,128]{1,0:T(8,128)S(1)}, u32[]{:S(2)}, u32[]{:S(2)}) collective-permute-start(f32[88,128]{1,0:T(8,128)S(1)} %get-tuple-element.84), channel_id=1, source_target_pairs={{0,3},{1,2},{2,1},{3,0},{4,7},{5,6},{6,5},{7,4},{8,11},{9,10},{10,... | collective-permute-start | bytes 135176 | tf_op jit(solution)/shard_map/ppermute | solution.py:306
  34.1 0.0 collective-permute-start.14
  34.1 3.0 %collective-permute-start.15 = (f32[5,2,8,128]{3,2,1,0:T(8,128)S(1)}, f32[5,2,8,128]{3,2,1,0:T(8,128)S(1)}, u32[]{:S(2)}, u32[]{:S(2)}) collective-permute-start(f32[5,2,8,128]{3,2,1,0:T(8,128)S(1)} %get-tuple-element.82), channel_id=1, source_target_pairs={{0,28},{4,8},{8,4},{12,16},{16,12},{20,24},{24,20},{28,0},{1,29},{... | collective-permute-start | bytes 122888 | tf_op jit(solution)/shard_map/ppermute | solution.py:306
  37.1 0.0 collective-permute-done.12.r0
  37.1 0.0 collective-permute-start.16
  37.1 0.4 shard_map.101.z_ref
  37.6 0.0 collective-permute-done.14.r2
  37.6 1.5 %collective-permute-done.15.r3 = f32[5,2,8,128]{3,2,1,0:T(8,128)S(1)} collective-permute-done((f32[5,2,8,128]{3,2,1,0:T(8,128)S(1)}, f32[5,2,8,128]{3,2,1,0:T(8,128)S(1)}, u32[]{:S(2)}, u32[]{:S(2)}) %collective-permute-start.15) | collective-permute-done | bytes 40992 | tf_op jit(solution)/shard_map/ppermute | solution.py:306
  39.1 0.0 collective-permute-done.17.r5
  39.1 0.0 collective-permute-done.13.r1
  39.1 0.0 collective-permute-done.16.r4
  39.1 0.7 shard_map.102
  39.8 0.0 collective-permute-start.18
  39.9 1.4 %collective-permute-start.19 = (f32[5,2,16,128]{3,2,1,0:T(8,128)S(1)}, f32[5,2,16,128]{3,2,1,0:T(8,128)S(1)}, u32[]{:S(2)}, u32[]{:S(2)}) collective-permute-start(f32[5,2,16,128]{3,2,1,0:T(8,128)S(1)} %get-tuple-element.89), channel_id=1, source_target_pairs={{0,224},{32,64},{64,32},{96,128},{128,96},{160,192},{192,160},{224... | collective-permute-start | bytes 245768 | tf_op jit(solution)/shard_map/ppermute | solution.py:306
  41.2 1.8 %collective-permute-start.23 = (f32[88,128]{1,0:T(8,128)S(1)}, f32[88,128]{1,0:T(8,128)S(1)}, u32[]{:S(2)}, u32[]{:S(2)}) collective-permute-start(f32[88,128]{1,0:T(8,128)S(1)} %get-tuple-element.93), channel_id=1, source_target_pairs={{0,3},{1,2},{2,1},{3,0},{4,7},{5,6},{6,5},{7,4},{8,11},{9,10},{10,... | collective-permute-start | bytes 135176 | tf_op jit(solution)/shard_map/ppermute | solution.py:306
  43.0 0.0 collective-permute-start.20
  43.0 3.0 %collective-permute-start.21 = (f32[5,2,8,128]{3,2,1,0:T(8,128)S(1)}, f32[5,2,8,128]{3,2,1,0:T(8,128)S(1)}, u32[]{:S(2)}, u32[]{:S(2)}) collective-permute-start(f32[5,2,8,128]{3,2,1,0:T(8,128)S(1)} %get-tuple-element.91), channel_id=1, source_target_pairs={{0,28},{4,8},{8,4},{12,16},{16,12},{20,24},{24,20},{28,0},{1,29},{... | collective-permute-start | bytes 122888 | tf_op jit(solution)/shard_map/ppermute | solution.py:306
  46.1 0.0 collective-permute-done.18.r0
  46.1 0.1 collective-permute-start.22
  46.2 0.4 shard_map.103.z_ref
  46.6 0.0 collective-permute-done.20.r2
  46.6 1.6 %collective-permute-done.21.r3 = f32[5,2,8,128]{3,2,1,0:T(8,128)S(1)} collective-permute-done((f32[5,2,8,128]{3,2,1,0:T(8,128)S(1)}, f32[5,2,8,128]{3,2,1,0:T(8,128)S(1)}, u32[]{:S(2)}, u32[]{:S(2)}) %collective-permute-start.21) | collective-permute-done | bytes 40992 | tf_op jit(solution)/shard_map/ppermute | solution.py:306
  48.2 0.0 collective-permute-done.23.r5
  48.2 1.2 %shard_map.104 = (f32[5,128,128]{2,1,0:T(8,128)}, f32[256,48]{1,0:T(8,128)S(1)}) custom-call(f32[5,128,128]{2,1,0:T(8,128)S(1)} %get-tuple-element.85.psi_ref, f32[5,128,128]{2,1,0:T(8,128)S(1)} %shard_map.103.z_ref, f32[5,2,16,128]{3,2,1,0:T(8,128)S(1)} %collective-permute-done.18.r0, f32[5,2,16,128]{3,2,1,0:T(8,128)S(1)} %collective-permute-done.19.r1, ...), custom_call_target="tpu_custom_call" | custom-call | flops 1000000 | bytes 1000000 | tf_op jit(solution)/shard_map/pallas_call | solution.py:284
  49.4 22.4 %all_to_all.5 = f32[256,1,48]{2,1,0:T(1,128)S(1)} all-to-all(f32[256,1,48]{2,1,0:T(1,128)S(1)} %bitcast.26), channel_id=1, replica_groups=mesh['gx'=8,'gy'=8,'wa'=4] {'gx','gy','wa'}, dimensions={0} | all-to-all | bytes 98304 | tf_op jit(solution)/shard_map/all_to_all | solution.py:345
  71.8 0.7 shard_map.105
  (8 shorter events, 0.0 us)
Async XLA Ops:
  2.1 16.6 %copy-start = (bf16[5,5,8,16,128]{4,3,2,1,0:T(8,128)(2,1)S(1)}, bf16[5,5,8,16,128]{4,3,2,1,0:T(8,128)(2,1)}, u32[]{:S(2)}) copy-start(bf16[5,5,8,16,128]{4,3,2,1,0:T(8,128)(2,1)} %param.12) | copy-start | bytes 2457604
  2.1 15.0 %collective-permute-start = (f32[5,2,16,128]{3,2,1,0:T(8,128)S(1)}, f32[5,2,16,128]{3,2,1,0:T(8,128)S(1)}, u32[]{:S(2)}, u32[]{:S(2)}) collective-permute-start(f32[5,2,16,128]{3,2,1,0:T(8,128)S(1)} %get-tuple-element.59), channel_id=1, source_target_pairs={{0,32},{32,0},{64,96},{96,64},{128,160},{160,128},{192,224},{224,1... | collective-permute-start | bytes 245768 | tf_op jit(solution)/shard_map/ppermute | solution.py:306
  4.3 14.5 %collective-permute-start.1 = (f32[5,2,16,128]{3,2,1,0:T(8,128)S(1)}, f32[5,2,16,128]{3,2,1,0:T(8,128)S(1)}, u32[]{:S(2)}, u32[]{:S(2)}) collective-permute-start(f32[5,2,16,128]{3,2,1,0:T(8,128)S(1)} %get-tuple-element.61), channel_id=1, source_target_pairs={{0,224},{32,64},{64,32},{96,128},{128,96},{160,192},{192,160},{224... | collective-permute-start | bytes 245768 | tf_op jit(solution)/shard_map/ppermute | solution.py:306
  7.0 11.8 %collective-permute-start.5 = (f32[88,128]{1,0:T(8,128)S(1)}, f32[88,128]{1,0:T(8,128)S(1)}, u32[]{:S(2)}, u32[]{:S(2)}) collective-permute-start(f32[88,128]{1,0:T(8,128)S(1)} %get-tuple-element.65), channel_id=1, source_target_pairs={{0,3},{1,2},{2,1},{3,0},{4,7},{5,6},{6,5},{7,4},{8,11},{9,10},{10,... | collective-permute-start | bytes 135176 | tf_op jit(solution)/shard_map/ppermute | solution.py:306
  10.8 7.8 %collective-permute-start.2 = (f32[5,2,8,128]{3,2,1,0:T(8,128)S(1)}, f32[5,2,8,128]{3,2,1,0:T(8,128)S(1)}, u32[]{:S(2)}, u32[]{:S(2)}) collective-permute-start(f32[5,2,8,128]{3,2,1,0:T(8,128)S(1)} %get-tuple-element.62), channel_id=1, source_target_pairs={{0,4},{4,0},{8,12},{12,8},{16,20},{20,16},{24,28},{28,24},{1,5},{5... | collective-permute-start | bytes 122888 | tf_op jit(solution)/shard_map/ppermute | solution.py:306
  12.5 6.3 %collective-permute-start.3 = (f32[5,2,8,128]{3,2,1,0:T(8,128)S(1)}, f32[5,2,8,128]{3,2,1,0:T(8,128)S(1)}, u32[]{:S(2)}, u32[]{:S(2)}) collective-permute-start(f32[5,2,8,128]{3,2,1,0:T(8,128)S(1)} %get-tuple-element.63), channel_id=1, source_target_pairs={{0,28},{4,8},{8,4},{12,16},{16,12},{20,24},{24,20},{28,0},{1,29},{... | collective-permute-start | bytes 122888 | tf_op jit(solution)/shard_map/ppermute | solution.py:306
  17.1 1.6 %collective-permute-start.4 = (f32[24,128]{1,0:T(8,128)S(1)}, f32[24,128]{1,0:T(8,128)S(1)}, u32[]{:S(2)}, u32[]{:S(2)}) collective-permute-start(f32[24,128]{1,0:T(8,128)S(1)} %get-tuple-element.64), channel_id=1, source_target_pairs={{0,1},{1,0},{2,3},{3,2},{4,5},{5,4},{6,7},{7,6},{8,9},{9,8},{10,11... | collective-permute-start | bytes 36872 | tf_op jit(solution)/shard_map/ppermute | solution.py:306
  17.1 0.9 %copy-start.3 = (f32[3,10,8,16]{3,2,1,0:T(8,128)S(1)}, f32[3,10,8,16]{3,2,1,0:T(8,128)}, u32[]{:S(2)}) copy-start(f32[3,10,8,16]{3,2,1,0:T(8,128)} %param.13) | copy-start | bytes 46084
  17.1 0.9 %copy-start.4 = (s32[4,8,16]{2,1,0:T(8,128)S(1)}, s32[4,8,16]{2,1,0:T(8,128)}, u32[]{:S(2)}) copy-start(s32[4,8,16]{2,1,0:T(8,128)} %param.14) | copy-start | bytes 6148
  17.2 0.9 %copy-start.5 = (f32[4,8,16]{2,1,0:T(8,128)S(1)}, f32[4,8,16]{2,1,0:T(8,128)}, u32[]{:S(2)}) copy-start(f32[4,8,16]{2,1,0:T(8,128)} %param.15) | copy-start | bytes 6148
  17.2 1.6 %copy-start.1 = (f32[5,8,16,128]{3,2,1,0:T(8,128)S(1)}, f32[5,8,16,128]{3,2,1,0:T(8,128)}, u32[]{:S(2)}) copy-start(f32[5,8,16,128]{3,2,1,0:T(8,128)} %param.9) | copy-start | bytes 983044
  18.0 0.9 %copy-start.2 = (f32[8,16,128]{2,1,0:T(8,128)S(1)}, f32[8,16,128]{2,1,0:T(8,128)}, u32[]{:S(2)}) copy-start(f32[8,16,128]{2,1,0:T(8,128)} %param.10) | copy-start | bytes 196612
  19.6 6.0 %collective-permute-start.6 = (f32[5,2,16,128]{3,2,1,0:T(8,128)S(1)}, f32[5,2,16,128]{3,2,1,0:T(8,128)S(1)}, u32[]{:S(2)}, u32[]{:S(2)}) collective-permute-start(f32[5,2,16,128]{3,2,1,0:T(8,128)S(1)} %get-tuple-element.69), channel_id=1, source_target_pairs={{0,32},{32,0},{64,96},{96,64},{128,160},{160,128},{192,224},{224,1... | collective-permute-start | bytes 245768 | tf_op jit(solution)/shard_map/ppermute | solution.py:306
  19.7 7.9 %collective-permute-start.7 = (f32[5,2,16,128]{3,2,1,0:T(8,128)S(1)}, f32[5,2,16,128]{3,2,1,0:T(8,128)S(1)}, u32[]{:S(2)}, u32[]{:S(2)}) collective-permute-start(f32[5,2,16,128]{3,2,1,0:T(8,128)S(1)} %get-tuple-element.71), channel_id=1, source_target_pairs={{0,224},{32,64},{64,32},{96,128},{128,96},{160,192},{192,160},{224... | collective-permute-start | bytes 245768 | tf_op jit(solution)/shard_map/ppermute | solution.py:306
  21.3 6.2 %collective-permute-start.11 = (f32[88,128]{1,0:T(8,128)S(1)}, f32[88,128]{1,0:T(8,128)S(1)}, u32[]{:S(2)}, u32[]{:S(2)}) collective-permute-start(f32[88,128]{1,0:T(8,128)S(1)} %get-tuple-element.75), channel_id=1, source_target_pairs={{0,3},{1,2},{2,1},{3,0},{4,7},{5,6},{6,5},{7,4},{8,11},{9,10},{10,... | collective-permute-start | bytes 135176 | tf_op jit(solution)/shard_map/ppermute | solution.py:306
  22.8 3.5 %collective-permute-start.8 = (f32[5,2,8,128]{3,2,1,0:T(8,128)S(1)}, f32[5,2,8,128]{3,2,1,0:T(8,128)S(1)}, u32[]{:S(2)}, u32[]{:S(2)}) collective-permute-start(f32[5,2,8,128]{3,2,1,0:T(8,128)S(1)} %get-tuple-element.72), channel_id=1, source_target_pairs={{0,4},{4,0},{8,12},{12,8},{16,20},{20,16},{24,28},{28,24},{1,5},{5... | collective-permute-start | bytes 122888 | tf_op jit(solution)/shard_map/ppermute | solution.py:306
  22.8 4.7 %collective-permute-start.9 = (f32[5,2,8,128]{3,2,1,0:T(8,128)S(1)}, f32[5,2,8,128]{3,2,1,0:T(8,128)S(1)}, u32[]{:S(2)}, u32[]{:S(2)}) collective-permute-start(f32[5,2,8,128]{3,2,1,0:T(8,128)S(1)} %get-tuple-element.73), channel_id=1, source_target_pairs={{0,28},{4,8},{8,4},{12,16},{16,12},{20,24},{24,20},{28,0},{1,29},{... | collective-permute-start | bytes 122888 | tf_op jit(solution)/shard_map/ppermute | solution.py:306
  25.6 1.9 %collective-permute-start.10 = (f32[24,128]{1,0:T(8,128)S(1)}, f32[24,128]{1,0:T(8,128)S(1)}, u32[]{:S(2)}, u32[]{:S(2)}) collective-permute-start(f32[24,128]{1,0:T(8,128)S(1)} %get-tuple-element.74), channel_id=1, source_target_pairs={{0,1},{1,0},{2,3},{3,2},{4,5},{5,4},{6,7},{7,6},{8,9},{9,8},{10,11... | collective-permute-start | bytes 36872 | tf_op jit(solution)/shard_map/ppermute | solution.py:306
  28.2 8.9 %collective-permute-start.12 = (f32[5,2,16,128]{3,2,1,0:T(8,128)S(1)}, f32[5,2,16,128]{3,2,1,0:T(8,128)S(1)}, u32[]{:S(2)}, u32[]{:S(2)}) collective-permute-start(f32[5,2,16,128]{3,2,1,0:T(8,128)S(1)} %get-tuple-element.78), channel_id=1, source_target_pairs={{0,32},{32,0},{64,96},{96,64},{128,160},{160,128},{192,224},{224,1... | collective-permute-start | bytes 245768 | tf_op jit(solution)/shard_map/ppermute | solution.py:306
  28.4 10.7 %collective-permute-start.13 = (f32[5,2,16,128]{3,2,1,0:T(8,128)S(1)}, f32[5,2,16,128]{3,2,1,0:T(8,128)S(1)}, u32[]{:S(2)}, u32[]{:S(2)}) collective-permute-start(f32[5,2,16,128]{3,2,1,0:T(8,128)S(1)} %get-tuple-element.80), channel_id=1, source_target_pairs={{0,224},{32,64},{64,32},{96,128},{128,96},{160,192},{192,160},{224... | collective-permute-start | bytes 245768 | tf_op jit(solution)/shard_map/ppermute | solution.py:306
  30.7 8.4 %collective-permute-start.17 = (f32[88,128]{1,0:T(8,128)S(1)}, f32[88,128]{1,0:T(8,128)S(1)}, u32[]{:S(2)}, u32[]{:S(2)}) collective-permute-start(f32[88,128]{1,0:T(8,128)S(1)} %get-tuple-element.84), channel_id=1, source_target_pairs={{0,3},{1,2},{2,1},{3,0},{4,7},{5,6},{6,5},{7,4},{8,11},{9,10},{10,... | collective-permute-start | bytes 135176 | tf_op jit(solution)/shard_map/ppermute | solution.py:306
  34.1 3.5 %collective-permute-start.14 = (f32[5,2,8,128]{3,2,1,0:T(8,128)S(1)}, f32[5,2,8,128]{3,2,1,0:T(8,128)S(1)}, u32[]{:S(2)}, u32[]{:S(2)}) collective-permute-start(f32[5,2,8,128]{3,2,1,0:T(8,128)S(1)} %get-tuple-element.81), channel_id=1, source_target_pairs={{0,4},{4,0},{8,12},{12,8},{16,20},{20,16},{24,28},{28,24},{1,5},{5... | collective-permute-start | bytes 122888 | tf_op jit(solution)/shard_map/ppermute | solution.py:306
  34.1 5.0 %collective-permute-start.15 = (f32[5,2,8,128]{3,2,1,0:T(8,128)S(1)}, f32[5,2,8,128]{3,2,1,0:T(8,128)S(1)}, u32[]{:S(2)}, u32[]{:S(2)}) collective-permute-start(f32[5,2,8,128]{3,2,1,0:T(8,128)S(1)} %get-tuple-element.82), channel_id=1, source_target_pairs={{0,28},{4,8},{8,4},{12,16},{16,12},{20,24},{24,20},{28,0},{1,29},{... | collective-permute-start | bytes 122888 | tf_op jit(solution)/shard_map/ppermute | solution.py:306
  37.1 2.0 %collective-permute-start.16 = (f32[24,128]{1,0:T(8,128)S(1)}, f32[24,128]{1,0:T(8,128)S(1)}, u32[]{:S(2)}, u32[]{:S(2)}) collective-permute-start(f32[24,128]{1,0:T(8,128)S(1)} %get-tuple-element.83), channel_id=1, source_target_pairs={{0,1},{1,0},{2,3},{3,2},{4,5},{5,4},{6,7},{7,6},{8,9},{9,8},{10,11... | collective-permute-start | bytes 36872 | tf_op jit(solution)/shard_map/ppermute | solution.py:306
  39.8 6.3 %collective-permute-start.18 = (f32[5,2,16,128]{3,2,1,0:T(8,128)S(1)}, f32[5,2,16,128]{3,2,1,0:T(8,128)S(1)}, u32[]{:S(2)}, u32[]{:S(2)}) collective-permute-start(f32[5,2,16,128]{3,2,1,0:T(8,128)S(1)} %get-tuple-element.87), channel_id=1, source_target_pairs={{0,32},{32,0},{64,96},{96,64},{128,160},{160,128},{192,224},{224,1... | collective-permute-start | bytes 245768 | tf_op jit(solution)/shard_map/ppermute | solution.py:306
  39.9 8.3 %collective-permute-start.19 = (f32[5,2,16,128]{3,2,1,0:T(8,128)S(1)}, f32[5,2,16,128]{3,2,1,0:T(8,128)S(1)}, u32[]{:S(2)}, u32[]{:S(2)}) collective-permute-start(f32[5,2,16,128]{3,2,1,0:T(8,128)S(1)} %get-tuple-element.89), channel_id=1, source_target_pairs={{0,224},{32,64},{64,32},{96,128},{128,96},{160,192},{192,160},{224... | collective-permute-start | bytes 245768 | tf_op jit(solution)/shard_map/ppermute | solution.py:306
  41.2 7.0 %collective-permute-start.23 = (f32[88,128]{1,0:T(8,128)S(1)}, f32[88,128]{1,0:T(8,128)S(1)}, u32[]{:S(2)}, u32[]{:S(2)}) collective-permute-start(f32[88,128]{1,0:T(8,128)S(1)} %get-tuple-element.93), channel_id=1, source_target_pairs={{0,3},{1,2},{2,1},{3,0},{4,7},{5,6},{6,5},{7,4},{8,11},{9,10},{10,... | collective-permute-start | bytes 135176 | tf_op jit(solution)/shard_map/ppermute | solution.py:306
  43.0 3.6 %collective-permute-start.20 = (f32[5,2,8,128]{3,2,1,0:T(8,128)S(1)}, f32[5,2,8,128]{3,2,1,0:T(8,128)S(1)}, u32[]{:S(2)}, u32[]{:S(2)}) collective-permute-start(f32[5,2,8,128]{3,2,1,0:T(8,128)S(1)} %get-tuple-element.90), channel_id=1, source_target_pairs={{0,4},{4,0},{8,12},{12,8},{16,20},{20,16},{24,28},{28,24},{1,5},{5... | collective-permute-start | bytes 122888 | tf_op jit(solution)/shard_map/ppermute | solution.py:306
  43.0 5.1 %collective-permute-start.21 = (f32[5,2,8,128]{3,2,1,0:T(8,128)S(1)}, f32[5,2,8,128]{3,2,1,0:T(8,128)S(1)}, u32[]{:S(2)}, u32[]{:S(2)}) collective-permute-start(f32[5,2,8,128]{3,2,1,0:T(8,128)S(1)} %get-tuple-element.91), channel_id=1, source_target_pairs={{0,28},{4,8},{8,4},{12,16},{16,12},{20,24},{24,20},{28,0},{1,29},{... | collective-permute-start | bytes 122888 | tf_op jit(solution)/shard_map/ppermute | solution.py:306
  46.1 2.1 %collective-permute-start.22 = (f32[24,128]{1,0:T(8,128)S(1)}, f32[24,128]{1,0:T(8,128)S(1)}, u32[]{:S(2)}, u32[]{:S(2)}) collective-permute-start(f32[24,128]{1,0:T(8,128)S(1)} %get-tuple-element.92), channel_id=1, source_target_pairs={{0,1},{1,0},{2,3},{3,2},{4,5},{5,4},{6,7},{7,6},{8,9},{9,8},{10,11... | collective-permute-start | bytes 36872 | tf_op jit(solution)/shard_map/ppermute | solution.py:306

commit v10 on v8

--- a/solution.py
+++ b/solution.py
@@ -10,7 +10,8 @@
 AXES = ("gx", "gy", "wa")
 FIELDS, NX, NY, NZ = 5, 8, 16, 128
 ROWS = NX * NY
-FAR_ROWS = 96
+FAR_ROWS = 88
+OUTER_ROWS = (0, 1, NY - 2, NY - 1)
 F32 = jnp.float32
 VMEM = pl.BlockSpec(memory_space=pltpu.VMEM)
 
@@ -82,7 +83,7 @@
         out_ref[8 * i : 8 * i + 8, :] = v + lane_roll(v, 64)
 
 
-def emit_sends(psi_ref, metric_ref, packed_metric, groups, sends):
+def emit_sends(psi_ref, metric_ref, packed_metric, groups, sends, rows=None):
     x0, x1, y0, y1, zz, far = sends
     lane = iota((8, NZ), 1)
     same, after, before = (packed_metric[8 * i : 8 * i + 8, :] for i in range(3))
@@ -96,8 +97,7 @@
     m4, m6a, m6b = metric_ref[4, edge_rows(15), :], metric_ref[6, edge_rows(14), :], metric_ref[6, edge_rows(15), :]
     m5, m7a, m7b = metric_ref[5, edge_rows(0), :], metric_ref[7, edge_rows(0), :], metric_ref[7, edge_rows(1), :]
     for e in range(FIELDS):
-        q14, q15 = psi_ref[e, edge_rows(14), :], psi_ref[e, edge_rows(15), :]
-        q0, q1 = psi_ref[e, edge_rows(0), :], psi_ref[e, edge_rows(1), :]
+        q0, q1, q14, q15 = rows[e] if rows else [psi_ref[e, edge_rows(y), :] for y in OUTER_ROWS]
         high = (m4 * q15 + m6a * q14, m6b * q15)
         low = (m7a * q0, m5 * q0 + m7b * q1)
         for r in range(2):
@@ -134,6 +134,14 @@
     emit_sends(psi_ref, metric_ref, packed_metric, groups, (x0, x1, y0, y1, zz, far))
 
 
+def from_sides(axis, first, second):
+    index = lax.axis_index(axis)
+    even = index % 2 == 0
+    below = jnp.where(even, second, first)
+    above = jnp.where(even, first, second)
+    return jnp.where(index > 0, below, 0.0), jnp.where(index < lax.axis_size(axis) - 1, above, 0.0)
+
+
 def coupled(jac_ref, s, zs):
     out = []
     for f in range(FIELDS):
@@ -144,7 +152,13 @@
     return out
 
 
-def inner_body(psi_ref, metric_ref, diag_ref, rhs_ref, jac_ref, base_ref):
+def window_body(psi_ref, metric_ref, diag_ref, rhs_ref, jac_ref, x0, x1, z0, z1, base_ref):
+    lane8 = iota((8, NZ), 1)
+    edge = (lane8 < 2) | (lane8 >= NZ - 2)
+    walls = []
+    for g in range((FIELDS + 1) // 2):
+        below, above = from_sides("wa", z0[8 * g : 8 * g + 8, :], z1[8 * g : 8 * g + 8, :])
+        walls.append(jnp.where(lane8 % 4 >= 2, below, above))
     lane, row = iota((NY, NZ), 1), iota((NY, NZ), 0)
     for x in range(NX):
         s = slab(x)
@@ -164,6 +178,14 @@
             for o, step in enumerate((1, -1, 2, -2)):
                 if 0 <= x - step < NX:
                     total = total + metric_ref[o, slab(x - step), :] * psi_ref[e, slab(x - step), :]
+            tiles = [
+                jnp.where(edge, lane_roll(walls[e // 2], -(2 + 64 * (e % 2) + 4 * (2 * x + t))), 0.0) for t in range(2)
+            ]
+            total = total + jnp.concatenate(tiles, axis=0)
+            if x < 2:
+                total = total + from_sides("gx", x0[e, x], x1[e, x])[0]
+            if x >= NX - 2:
+                total = total + from_sides("gx", x0[e, x - NX + 2], x1[e, x - NX + 2])[1]
             zs.append(total)
         d = diag_ref[s, :]
         scale = OMEGA / d
@@ -172,51 +194,40 @@
             base_ref[f, s, :] = q + (rhs_ref[f, s, :] - d * q + c) * scale
 
 
-def from_sides(axis, first, second):
-    index = lax.axis_index(axis)
-    even = index % 2 == 0
-    below = jnp.where(even, second, first)
-    above = jnp.where(even, first, second)
-    return jnp.where(index > 0, below, 0.0), jnp.where(index < lax.axis_size(axis) - 1, above, 0.0)
-
-
-def update(base_ref, received, diag_ref, jac_ref, new_ref, rows_ref):
-    x0, x1, y0, y1, z0, z1 = received
-    lane8 = iota((8, NZ), 1)
-    edge = (lane8 < 2) | (lane8 >= NZ - 2)
-    row = iota((NY, NZ), 0)
-    outer = (row < 2) | (row >= NY - 2)
-    walls = []
-    for g in range((FIELDS + 1) // 2):
-        below, above = from_sides("wa", z0[8 * g : 8 * g + 8, :], z1[8 * g : 8 * g + 8, :])
-        walls.append(jnp.where(lane8 % 4 >= 2, below, above))
+def rows_body(jac_ref, diag_ref, jac_rows, scale_rows, wide):
+    for k in range(FIELDS * FIELDS):
+        for x in range(NX):
+            wide[k, slab(x), :] = jac_ref[k, slab(x), :].astype(F32)
+    for i, y in enumerate(OUTER_ROWS):
+        scale_rows[i] = OMEGA / diag_ref[edge_rows(y), :]
+        for k in range(FIELDS * FIELDS):
+            jac_rows[4 * k + i] = wide[k, edge_rows(y), :]
+
+
+def finish(base_ref, y0, y1, jac_rows, scale_rows, new_ref):
+    zs = []
     for e in range(FIELDS):
-        for r in range(2):
-            below, above = from_sides("gy", y0[e, r], y1[e, r])
-            rows_ref[e, edge_rows(r), :] = below
-            rows_ref[e, edge_rows(NY - 2 + r), :] = above
-    for x in range(NX):
-        s = slab(x)
-        zs = []
-        for e in range(FIELDS):
-            tiles = [
-                jnp.where(edge, lane_roll(walls[e // 2], -(2 + 64 * (e % 2) + 4 * (2 * x + t))), 0.0) for t in range(2)
-            ]
-            total = jnp.concatenate(tiles, axis=0) + jnp.where(outer, rows_ref[e, s, :], 0.0)
-            if x < 2:
-                total = total + from_sides("gx", x0[e, x], x1[e, x])[0]
-            if x >= NX - 2:
-                total = total + from_sides("gx", x0[e, x - NX + 2], x1[e, x - NX + 2])[1]
-            zs.append(total)
-        scale = OMEGA / diag_ref[s, :]
-        for f, c in enumerate(coupled(jac_ref, s, zs)):
-            new_ref[f, s, :] = base_ref[f, s, :] + c * scale
-
-
-def middle_body(base_ref, r0, r1, r2, r3, r4, r5, diag_ref, jac_ref, metric_ref, packed_metric,
-                new_ref, x0, x1, y0, y1, zz, far, rows_ref):
-    update(base_ref, (r0, r1, r2, r3, r4, r5), diag_ref, jac_ref, new_ref, rows_ref)
-    emit_sends(new_ref, metric_ref, packed_metric, pack_edges(new_ref), (x0, x1, y0, y1, zz, far))
+        sides = [from_sides("gy", y0[e, r], y1[e, r]) for r in range(2)]
+        zs.append([sides[0][0], sides[1][0], sides[0][1], sides[1][1]])
+    rows = []
+    for f in range(FIELDS):
+        new_ref[f] = base_ref[f]
+        mine = []
+        for i, y in enumerate(OUTER_ROWS):
+            c = jac_rows[4 * f + i] * zs[0][i]
+            for e in range(1, FIELDS):
+                c = c + jac_rows[4 * (FIELDS * e + f) + i] * zs[e][i]
+            mine.append(base_ref[f, edge_rows(y), :] + c * scale_rows[i])
+        for i, y in enumerate(OUTER_ROWS):
+            new_ref[f, edge_rows(y), :] = mine[i]
+        rows.append(mine)
+    return rows
+
+
+def middle_body(base_ref, y_even, y_odd, jac_rows, scale_rows, metric_ref, packed_metric,
+                new_ref, x0, x1, y0, y1, zz, far):
+    rows = finish(base_ref, y_even, y_odd, jac_rows, scale_rows, new_ref)
+    emit_sends(new_ref, metric_ref, packed_metric, pack_edges(new_ref), (x0, x1, y0, y1, zz, far), rows)
 
 
 def wall_body(coef_ref, ids_ref, weight_ref, coef_out, weight_out, hot_out, low_out):
@@ -253,9 +264,9 @@
         hot_out[:, NZ * s : NZ * s + NZ] = jnp.where(hit, 1.0, 0.0).astype(jnp.bfloat16)
 
 
-def last_body(base_ref, r0, r1, r2, r3, r4, r5, diag_ref, jac_ref, coef_ref, weight_ref, hot_ref, low_ref,
-              out_hbm, slots_ref, new_ref, rows_ref, high_part, low_part, sem):
-    update(base_ref, (r0, r1, r2, r3, r4, r5), diag_ref, jac_ref, new_ref, rows_ref)
+def last_body(base_ref, y_even, y_odd, jac_rows, scale_rows, coef_ref, weight_ref, hot_ref, low_ref,
+              out_hbm, slots_ref, new_ref, high_part, low_part, sem):
+    finish(base_ref, y_even, y_odd, jac_rows, scale_rows, new_ref)
     copy = pltpu.make_async_copy(new_ref, out_hbm, sem)
     copy.start()
     lane = iota((8, NZ), 1)
@@ -319,11 +330,11 @@
     def swap(v, axis, odd):
         return lax.ppermute(v, axis, pairs(lax.axis_size(axis), odd))
     two_hops = swap(x1, "gx", 1)
-    x = swap(x0, "gx", 0), two_hops
+    one_hop = swap(x0, "gx", 0)
     far = swap(far, "wa", 1)
     y = swap(y0, "gy", 0), swap(y1, "gy", 1)
-    zz, two_hops = lax.optimization_barrier((zz, two_hops))
-    x = x[0], two_hops
+    zz, one_hop = lax.optimization_barrier((zz, one_hop))
+    x = one_hop, two_hops
     z = swap(zz, "wa", 0), far
     return (*x, *y, *z)
 
@@ -337,25 +348,26 @@
     *sends, packed_metric, psi, metric = run(
         first_body, (psi, metric), SENDS + [((24, NZ), F32), FIELD, ((12, ROWS, NZ), F32)], sems=[(4,)], far=(0, 1)
     )
-    jac, rhs, diag, packed_metric = lax.optimization_barrier((jac, rhs, diag, packed_metric))
     wall = run(
         wall_body,
         (wall_coef.reshape(30 * NX, NY), ffd_ids.reshape(4 * NX, NY), ffd_weight.reshape(4 * NX, NY)),
         [((3, 24, NZ), F32), ((8, NZ), F32), ((256, 512), jnp.bfloat16), ((8, NZ), jnp.int32)],
     )
+    rows = run(
+        rows_body, (jac, diag), [((4 * FIELDS * FIELDS, NX, NZ), F32), ((4, NX, NZ), F32)],
+        scratch=[((FIELDS * FIELDS, ROWS, NZ), F32)],
+    )
     for step in range(SWEEPS):
-        received = exchange(sends)
-        (base,) = run(inner_body, (psi, metric, diag, rhs, jac), [FIELD])
+        x_even, x_odd, y_even, y_odd, z_even, z_odd = exchange(sends)
+        (base,) = run(window_body, (psi, metric, diag, rhs, jac, x_even, x_odd, z_even, z_odd), [FIELD])
         if step == 1:
             base, wall = lax.optimization_barrier((base, wall))
         if step < SWEEPS - 1:
-            psi, *sends = run(
-                middle_body, (base, *received, diag, jac, metric, packed_metric), [FIELD] + SENDS, scratch=[FIELD]
-            )
+            psi, *sends = run(middle_body, (base, y_even, y_odd, *rows, metric, packed_metric), [FIELD] + SENDS)
         else:
             psi, slots = run(
-                last_body, (base, *received, diag, jac, *wall), [FIELD, ((256, 48), F32)],
-                scratch=[FIELD, FIELD, ((48, 512), jnp.bfloat16), ((48, 512), jnp.bfloat16)], sems=[()], far_outs=(0,),
+                last_body, (base, y_even, y_odd, *rows, *wall), [FIELD, ((256, 48), F32)],
+                scratch=[FIELD, ((48, 512), jnp.bfloat16), ((48, 512), jnp.bfloat16)], sems=[()], far_outs=(0,),
             )
     got = lax.all_to_all(slots.reshape(256, 1, 48), AXES, 0, 0).reshape(256, 48)
     (grad,) = run(sum_body, (got,), [((3, 16), F32)])

time: 72.7 us -> 71.6 us (0.985)
  waiting for transfers between devices: 1.58 us -> 3.67 us
  starting transfers between devices: 38.1 us -> 36.4 us
  local copies, waits for them, and re-layouts: 1 us -> 0.03 us
    ppermute x24, waiting for transfers between devices: 1.58 us -> 3.67 us  [swap(): return lax.ppermute(v, axis, pairs(lax.axis_size(axis), odd))]
    ppermute x24, starting transfers between devices: 38.1 us -> 36.4 us  [swap(): return lax.ppermute(v, axis, pairs(lax.axis_size(axis), odd))]
    unnamed x14 -> x12, local copies, waits for them, and re-layouts: 1 us -> 0.03 us
    pallas_call x11 -> x12, Pallas kernels: 8.76 us -> 8.38 us  [run(): pl.pallas_call(body, out_shape=[jax.ShapeDtypeStruct(s, d) for s, d in ou...]
  transfers between devices with their start and end apart: 24 -> 24, of which waited for: 3 -> 6; matrix products, arithmetic and copies ran while one was open for 0% -> 0% of each run, Pallas kernels for 4% -> 5%
where the time goes in v10:
time: 71.6 us; the launch traced here: 71.5 us
  starting transfers between devices  36.4 us (51%)
  blocking collectives  22.2 us (31%)
  Pallas kernels  8.38 us (12%)
  waiting for transfers between devices  3.67 us (5%)
  between operations  0.86 us (1%)
    ppermute x24, starting transfers between devices, swap(): return lax.ppermute(v, axis, pairs(lax.axis_size(axis), odd))  36.4 us
    all_to_all x1, blocking collectives, local(): got = lax.all_to_all(slots.reshape(256, 1, 48), AXES, 0, 0).reshape(256, 48)  22.2 us
    pallas_call x12, Pallas kernels, run(): pl.pallas_call(body, out_shape=[jax.ShapeDtypeStruct(s, d) for s, d in ou...  8.38 us
    ppermute x24, waiting for transfers between devices, swap(): return lax.ppermute(v, axis, pairs(lax.axis_size(axis), odd))  3.67 us
  transfers between devices with their start and end apart: 24, of which 6 were waited for; matrix products, arithmetic and copies ran while one was open for 0% of the time, Pallas kernels for 5%

profile of v10, /device:TPU:1, one launch (start us, length us, event | category | flops | bytes accessed | tf_op | source)
XLA Modules:
  0.0 71.5 jit_solution(11610035660476244647)
XLA Ops:
  0.7 1.6 %shard_map.95 = (f32[5,2,16,128]{3,2,1,0:T(8,128)S(1)}, f32[5,2,16,128]{3,2,1,0:T(8,128)S(1)}, f32[5,2,8,128]{3,2,1,0:T(8,128)S(1)}, f32[5,2,8,128]{3,2,1,0:T(8,...) custom-call(f32[5,128,128]{2,1,0:T(8,128)} %bitcast.33, ...), custom_call_target="tpu_custom_call" | custom-call | flops 1000000 | bytes 1000000 | tf_op jit(solution)/shard_map/pallas_call | solution.py:309
  2.2 2.1 %collective-permute-start = (f32[5,2,16,128]{3,2,1,0:T(8,128)S(1)}, f32[5,2,16,128]{3,2,1,0:T(8,128)S(1)}, u32[]{:S(2)}, u32[]{:S(2)}) collective-permute-start(f32[5,2,16,128]{3,2,1,0:T(8,128)S(1)} %get-tuple-element.56), channel_id=1, source_target_pairs={{0,32},{32,0},{64,96},{96,64},{128,160},{160,128},{192,224},{224,1... | collective-permute-start | bytes 245768 | tf_op jit(solution)/shard_map/ppermute | solution.py:331
  4.3 2.7 %collective-permute-start.1 = (f32[5,2,16,128]{3,2,1,0:T(8,128)S(1)}, f32[5,2,16,128]{3,2,1,0:T(8,128)S(1)}, u32[]{:S(2)}, u32[]{:S(2)}) collective-permute-start(f32[5,2,16,128]{3,2,1,0:T(8,128)S(1)} %get-tuple-element.58), channel_id=1, source_target_pairs={{0,224},{32,64},{64,32},{96,128},{128,96},{160,192},{192,160},{224... | collective-permute-start | bytes 245768 | tf_op jit(solution)/shard_map/ppermute | solution.py:331
  7.0 3.9 %collective-permute-start.3 = (f32[88,128]{1,0:T(8,128)S(1)}, f32[88,128]{1,0:T(8,128)S(1)}, u32[]{:S(2)}, u32[]{:S(2)}) collective-permute-start(f32[88,128]{1,0:T(8,128)S(1)} %get-tuple-element.60), channel_id=1, source_target_pairs={{0,3},{1,2},{2,1},{3,0},{4,7},{5,6},{6,5},{7,4},{8,11},{9,10},{10,... | collective-permute-start | bytes 135176 | tf_op jit(solution)/shard_map/ppermute | solution.py:331
  10.9 1.6 %collective-permute-start.4 = (f32[5,2,8,128]{3,2,1,0:T(8,128)S(1)}, f32[5,2,8,128]{3,2,1,0:T(8,128)S(1)}, u32[]{:S(2)}, u32[]{:S(2)}) collective-permute-start(f32[5,2,8,128]{3,2,1,0:T(8,128)S(1)} %get-tuple-element.61), channel_id=1, source_target_pairs={{0,4},{4,0},{8,12},{12,8},{16,20},{20,16},{24,28},{28,24},{1,5},{5... | collective-permute-start | bytes 122888 | tf_op jit(solution)/shard_map/ppermute | solution.py:331
  12.5 4.7 %collective-permute-start.5 = (f32[5,2,8,128]{3,2,1,0:T(8,128)S(1)}, f32[5,2,8,128]{3,2,1,0:T(8,128)S(1)}, u32[]{:S(2)}, u32[]{:S(2)}) collective-permute-start(f32[5,2,8,128]{3,2,1,0:T(8,128)S(1)} %get-tuple-element.62), channel_id=1, source_target_pairs={{0,28},{4,8},{8,4},{12,16},{16,12},{20,24},{24,20},{28,0},{1,29},{... | collective-permute-start | bytes 122888 | tf_op jit(solution)/shard_map/ppermute | solution.py:331
  17.2 0.0 collective-permute-done.x0
  17.2 0.0 collective-permute-start.2
  17.2 0.0 copy-start.1
  17.2 0.3 shard_map.97
  17.5 0.0 collective-permute-done.3.z1
  17.5 0.0 collective-permute-done.1.x1
  17.5 0.8 %collective-permute-done.2.z0 = f32[24,128]{1,0:T(8,128)S(1)} collective-permute-done((f32[24,128]{1,0:T(8,128)S(1)}, f32[24,128]{1,0:T(8,128)S(1)}, u32[]{:S(2)}, u32[]{:S(2)}) %collective-permute-start.2) | collective-permute-done | bytes 12320 | tf_op jit(solution)/shard_map/ppermute | solution.py:331
  18.4 0.7 %shard_map.96.base_ref = f32[5,128,128]{2,1,0:T(8,128)S(1)} custom-call(f32[5,128,128]{2,1,0:T(8,128)S(1)} %get-tuple-element.53.psi_ref, f32[12,128,128]{2,1,0:T(8,128)S(1)} %get-tuple-element.54.metric_ref, f32[128,128]{1,0:T(8,128)S(1)} %bitcast.23, f32[5,128,128]{2,1,0:T(8,128)S(1)} %bitcast.18, bf16[25,128,128]{2,1,0:T(8,128)(2,1)S(1)} %bitcast.14, ...), custom_call_target="tpu_custom_call" | custom-call | flops 1000000 | bytes 1000000 | tf_op jit(solution)/shard_map/pallas_call | solution.py:309
  19.1 0.0 collective-permute-done.4.y_even
  19.2 0.0 collective-permute-done.5.y_odd
  19.2 0.0 copy-start.3
  19.2 0.0 copy-start.5
  19.2 0.4 shard_map.98
  19.6 0.0 collective-permute-start.6
  19.6 1.6 %collective-permute-start.7 = (f32[5,2,16,128]{3,2,1,0:T(8,128)S(1)}, f32[5,2,16,128]{3,2,1,0:T(8,128)S(1)}, u32[]{:S(2)}, u32[]{:S(2)}) collective-permute-start(f32[5,2,16,128]{3,2,1,0:T(8,128)S(1)} %get-tuple-element.70), channel_id=1, source_target_pairs={{0,224},{32,64},{64,32},{96,128},{128,96},{160,192},{192,160},{224... | collective-permute-start | bytes 245768 | tf_op jit(solution)/shard_map/ppermute | solution.py:331
  21.3 1.2 %collective-permute-start.9 = (f32[88,128]{1,0:T(8,128)S(1)}, f32[88,128]{1,0:T(8,128)S(1)}, u32[]{:S(2)}, u32[]{:S(2)}) collective-permute-start(f32[88,128]{1,0:T(8,128)S(1)} %get-tuple-element.72), channel_id=1, source_target_pairs={{0,3},{1,2},{2,1},{3,0},{4,7},{5,6},{6,5},{7,4},{8,11},{9,10},{10,... | collective-permute-start | bytes 135176 | tf_op jit(solution)/shard_map/ppermute | solution.py:331
  22.5 0.0 collective-permute-start.10
  22.5 3.2 %collective-permute-start.11 = (f32[5,2,8,128]{3,2,1,0:T(8,128)S(1)}, f32[5,2,8,128]{3,2,1,0:T(8,128)S(1)}, u32[]{:S(2)}, u32[]{:S(2)}) collective-permute-start(f32[5,2,8,128]{3,2,1,0:T(8,128)S(1)} %get-tuple-element.79), channel_id=1, source_target_pairs={{0,28},{4,8},{8,4},{12,16},{16,12},{20,24},{24,20},{28,0},{1,29},{... | collective-permute-start | bytes 122888 | tf_op jit(solution)/shard_map/ppermute | solution.py:331
  25.6 0.0 collective-permute-done.6.x0
  25.6 0.0 collective-permute-start.8
  25.7 0.6 shard_map.100
  26.2 0.6 collective-permute-done.9.z1
  26.8 0.0 collective-permute-done.7.x1
  26.8 0.0 collective-permute-done.8.z0
  26.9 0.8 %shard_map.99.base_ref = f32[5,128,128]{2,1,0:T(8,128)S(1)} custom-call(f32[5,128,128]{2,1,0:T(8,128)S(1)} %get-tuple-element.66.psi_ref, f32[12,128,128]{2,1,0:T(8,128)S(1)} %get-tuple-element.54.metric_ref, f32[128,128]{1,0:T(8,128)S(1)} %bitcast.24, f32[5,128,128]{2,1,0:T(8,128)S(1)} %bitcast.19, bf16[25,128,128]{2,1,0:T(8,128)(2,1)S(1)} %bitcast.15, ...), custom_call_target="tpu_custom_call" | custom-call | flops 1000000 | bytes 1000000 | tf_op jit(solution)/shard_map/pallas_call | solution.py:309
  27.6 0.0 collective-permute-done.10.y_even
  27.6 0.0 collective-permute-done.11.y_odd
  27.6 0.4 shard_map.101
  28.0 0.1 collective-permute-start.12
  28.2 2.1 %collective-permute-start.13 = (f32[5,2,16,128]{3,2,1,0:T(8,128)S(1)}, f32[5,2,16,128]{3,2,1,0:T(8,128)S(1)}, u32[]{:S(2)}, u32[]{:S(2)}) collective-permute-start(f32[5,2,16,128]{3,2,1,0:T(8,128)S(1)} %get-tuple-element.84), channel_id=1, source_target_pairs={{0,224},{32,64},{64,32},{96,128},{128,96},{160,192},{192,160},{224... | collective-permute-start | bytes 245768 | tf_op jit(solution)/shard_map/ppermute | solution.py:331
  30.3 3.2 %collective-permute-start.15 = (f32[88,128]{1,0:T(8,128)S(1)}, f32[88,128]{1,0:T(8,128)S(1)}, u32[]{:S(2)}, u32[]{:S(2)}) collective-permute-start(f32[88,128]{1,0:T(8,128)S(1)} %get-tuple-element.86), channel_id=1, source_target_pairs={{0,3},{1,2},{2,1},{3,0},{4,7},{5,6},{6,5},{7,4},{8,11},{9,10},{10,... | collective-permute-start | bytes 135176 | tf_op jit(solution)/shard_map/ppermute | solution.py:331
  33.5 0.2 collective-permute-start.16
  33.7 2.8 %collective-permute-start.17 = (f32[5,2,8,128]{3,2,1,0:T(8,128)S(1)}, f32[5,2,8,128]{3,2,1,0:T(8,128)S(1)}, u32[]{:S(2)}, u32[]{:S(2)}) collective-permute-start(f32[5,2,8,128]{3,2,1,0:T(8,128)S(1)} %get-tuple-element.88), channel_id=1, source_target_pairs={{0,28},{4,8},{8,4},{12,16},{16,12},{20,24},{24,20},{28,0},{1,29},{... | collective-permute-start | bytes 122888 | tf_op jit(solution)/shard_map/ppermute | solution.py:331
  36.5 0.0 collective-permute-done.12.x0
  36.5 0.0 collective-permute-start.14
  36.5 0.2 collective-permute-done.15.z1
  36.7 0.0 collective-permute-done.13.x1
  36.7 1.0 %collective-permute-done.14.z0 = f32[24,128]{1,0:T(8,128)S(1)} collective-permute-done((f32[24,128]{1,0:T(8,128)S(1)}, f32[24,128]{1,0:T(8,128)S(1)}, u32[]{:S(2)}, u32[]{:S(2)}) %collective-permute-start.14) | collective-permute-done | bytes 12320 | tf_op jit(solution)/shard_map/ppermute | solution.py:331
  37.7 0.8 %shard_map.102.base_ref = f32[5,128,128]{2,1,0:T(8,128)S(1)} custom-call(f32[5,128,128]{2,1,0:T(8,128)S(1)} %get-tuple-element.80.psi_ref, f32[12,128,128]{2,1,0:T(8,128)S(1)} %get-tuple-element.54.metric_ref, f32[128,128]{1,0:T(8,128)S(1)} %bitcast.25, f32[5,128,128]{2,1,0:T(8,128)S(1)} %bitcast.20, bf16[25,128,128]{2,1,0:T(8,128)(2,1)S(1)} %bitcast.16, ...), custom_call_target="tpu_custom_call" | custom-call | flops 1000000 | bytes 1000000 | tf_op jit(solution)/shard_map/pallas_call | solution.py:309
  38.5 0.0 collective-permute-done.16.y_even
  38.5 0.0 collective-permute-done.17.y_odd
  38.5 0.4 shard_map.103
  38.9 0.0 collective-permute-start.18
  38.9 1.8 %collective-permute-start.19 = (f32[5,2,16,128]{3,2,1,0:T(8,128)S(1)}, f32[5,2,16,128]{3,2,1,0:T(8,128)S(1)}, u32[]{:S(2)}, u32[]{:S(2)}) collective-permute-start(f32[5,2,16,128]{3,2,1,0:T(8,128)S(1)} %get-tuple-element.93), channel_id=1, source_target_pairs={{0,224},{32,64},{64,32},{96,128},{128,96},{160,192},{192,160},{224... | collective-permute-start | bytes 245768 | tf_op jit(solution)/shard_map/ppermute | solution.py:331
  40.8 1.6 %collective-permute-start.21 = (f32[88,128]{1,0:T(8,128)S(1)}, f32[88,128]{1,0:T(8,128)S(1)}, u32[]{:S(2)}, u32[]{:S(2)}) collective-permute-start(f32[88,128]{1,0:T(8,128)S(1)} %get-tuple-element.95), channel_id=1, source_target_pairs={{0,3},{1,2},{2,1},{3,0},{4,7},{5,6},{6,5},{7,4},{8,11},{9,10},{10,... | collective-permute-start | bytes 135176 | tf_op jit(solution)/shard_map/ppermute | solution.py:331
  42.4 0.2 collective-permute-start.22
  42.6 2.9 %collective-permute-start.23 = (f32[5,2,8,128]{3,2,1,0:T(8,128)S(1)}, f32[5,2,8,128]{3,2,1,0:T(8,128)S(1)}, u32[]{:S(2)}, u32[]{:S(2)}) collective-permute-start(f32[5,2,8,128]{3,2,1,0:T(8,128)S(1)} %get-tuple-element.97), channel_id=1, source_target_pairs={{0,28},{4,8},{8,4},{12,16},{16,12},{20,24},{24,20},{28,0},{1,29},{... | collective-permute-start | bytes 122888 | tf_op jit(solution)/shard_map/ppermute | solution.py:331
  45.5 0.0 collective-permute-done.18.x0
  45.5 0.2 collective-permute-start.20
  45.7 0.4 collective-permute-done.21.z1
  46.1 0.0 collective-permute-done.19.x1
  46.1 0.6 collective-permute-done.20.z0
  46.7 0.8 %shard_map.104.base_ref = f32[5,128,128]{2,1,0:T(8,128)S(1)} custom-call(f32[5,128,128]{2,1,0:T(8,128)S(1)} %get-tuple-element.89.psi_ref, f32[12,128,128]{2,1,0:T(8,128)S(1)} %get-tuple-element.54.metric_ref, f32[128,128]{1,0:T(8,128)S(1)} %bitcast.26, f32[5,128,128]{2,1,0:T(8,128)S(1)} %bitcast.21, bf16[25,128,128]{2,1,0:T(8,128)(2,1)S(1)} %bitcast.17, ...), custom_call_target="tpu_custom_call" | custom-call | flops 1000000 | bytes 1000000 | tf_op jit(solution)/shard_map/pallas_call | solution.py:309
  47.4 0.0 collective-permute-done.22.y_even
  47.4 0.0 collective-permute-done.23.y_odd
  47.5 1.1 %shard_map.105 = (f32[5,128,128]{2,1,0:T(8,128)}, f32[256,48]{1,0:T(8,128)S(1)}) custom-call(f32[5,128,128]{2,1,0:T(8,128)S(1)} %shard_map.104.base_ref, f32[5,2,8,128]{3,2,1,0:T(8,128)S(1)} %collective-permute-done.22.y_even, f32[5,2,8,128]{3,2,1,0:T(8,128)S(1)} %collective-permute-done.23.y_odd, f32[100,8,128]{2,1,0:T(8,128)S(1)} %get-tuple-element.63.jac_rows, ...), custom_call_target="tpu_custom_call" | custom-call | flops 1000000 | bytes 1000000 | tf_op jit(solution)/shard_map/pallas_call | solution.py:309
  48.6 22.2 %all_to_all.5 = f32[256,1,48]{2,1,0:T(1,128)S(1)} all-to-all(f32[256,1,48]{2,1,0:T(1,128)S(1)} %bitcast.28), channel_id=1, replica_groups=mesh['gx'=8,'gy'=8,'wa'=4] {'gx','gy','wa'}, dimensions={0} | all-to-all | bytes 98304 | tf_op jit(solution)/shard_map/all_to_all | solution.py:372
  70.8 0.7 shard_map.106
  (9 shorter events, 0.0 us)
Async XLA Ops:
  0.6 16.6 %copy-start = (bf16[5,5,8,16,128]{4,3,2,1,0:T(8,128)(2,1)S(1)}, bf16[5,5,8,16,128]{4,3,2,1,0:T(8,128)(2,1)}, u32[]{:S(2)}) copy-start(bf16[5,5,8,16,128]{4,3,2,1,0:T(8,128)(2,1)} %param.12) | copy-start | bytes 2457604
  0.6 16.6 %copy-start.2 = (f32[8,16,128]{2,1,0:T(8,128)S(1)}, f32[8,16,128]{2,1,0:T(8,128)}, u32[]{:S(2)}) copy-start(f32[8,16,128]{2,1,0:T(8,128)} %param.10) | copy-start | bytes 196612
  2.2 15.0 %collective-permute-start = (f32[5,2,16,128]{3,2,1,0:T(8,128)S(1)}, f32[5,2,16,128]{3,2,1,0:T(8,128)S(1)}, u32[]{:S(2)}, u32[]{:S(2)}) collective-permute-start(f32[5,2,16,128]{3,2,1,0:T(8,128)S(1)} %get-tuple-element.56), channel_id=1, source_target_pairs={{0,32},{32,0},{64,96},{96,64},{128,160},{160,128},{192,224},{224,1... | collective-permute-start | bytes 245768 | tf_op jit(solution)/shard_map/ppermute | solution.py:331
  4.3 13.2 %collective-permute-start.1 = (f32[5,2,16,128]{3,2,1,0:T(8,128)S(1)}, f32[5,2,16,128]{3,2,1,0:T(8,128)S(1)}, u32[]{:S(2)}, u32[]{:S(2)}) collective-permute-start(f32[5,2,16,128]{3,2,1,0:T(8,128)S(1)} %get-tuple-element.58), channel_id=1, source_target_pairs={{0,224},{32,64},{64,32},{96,128},{128,96},{160,192},{192,160},{224... | collective-permute-start | bytes 245768 | tf_op jit(solution)/shard_map/ppermute | solution.py:331
  7.0 10.5 %collective-permute-start.3 = (f32[88,128]{1,0:T(8,128)S(1)}, f32[88,128]{1,0:T(8,128)S(1)}, u32[]{:S(2)}, u32[]{:S(2)}) collective-permute-start(f32[88,128]{1,0:T(8,128)S(1)} %get-tuple-element.60), channel_id=1, source_target_pairs={{0,3},{1,2},{2,1},{3,0},{4,7},{5,6},{6,5},{7,4},{8,11},{9,10},{10,... | collective-permute-start | bytes 135176 | tf_op jit(solution)/shard_map/ppermute | solution.py:331
  10.9 8.2 %collective-permute-start.4 = (f32[5,2,8,128]{3,2,1,0:T(8,128)S(1)}, f32[5,2,8,128]{3,2,1,0:T(8,128)S(1)}, u32[]{:S(2)}, u32[]{:S(2)}) collective-permute-start(f32[5,2,8,128]{3,2,1,0:T(8,128)S(1)} %get-tuple-element.61), channel_id=1, source_target_pairs={{0,4},{4,0},{8,12},{12,8},{16,20},{20,16},{24,28},{28,24},{1,5},{5... | collective-permute-start | bytes 122888 | tf_op jit(solution)/shard_map/ppermute | solution.py:331
  12.5 6.6 %collective-permute-start.5 = (f32[5,2,8,128]{3,2,1,0:T(8,128)S(1)}, f32[5,2,8,128]{3,2,1,0:T(8,128)S(1)}, u32[]{:S(2)}, u32[]{:S(2)}) collective-permute-start(f32[5,2,8,128]{3,2,1,0:T(8,128)S(1)} %get-tuple-element.62), channel_id=1, source_target_pairs={{0,28},{4,8},{8,4},{12,16},{16,12},{20,24},{24,20},{28,0},{1,29},{... | collective-permute-start | bytes 122888 | tf_op jit(solution)/shard_map/ppermute | solution.py:331
  17.2 1.2 %collective-permute-start.2 = (f32[24,128]{1,0:T(8,128)S(1)}, f32[24,128]{1,0:T(8,128)S(1)}, u32[]{:S(2)}, u32[]{:S(2)}) collective-permute-start(f32[24,128]{1,0:T(8,128)S(1)} %get-tuple-element.59), channel_id=1, source_target_pairs={{0,1},{1,0},{2,3},{3,2},{4,5},{5,4},{6,7},{7,6},{8,9},{9,8},{10,11... | collective-permute-start | bytes 36872 | tf_op jit(solution)/shard_map/ppermute | solution.py:331
  17.2 1.2 %copy-start.1 = (f32[5,8,16,128]{3,2,1,0:T(8,128)S(1)}, f32[5,8,16,128]{3,2,1,0:T(8,128)}, u32[]{:S(2)}) copy-start(f32[5,8,16,128]{3,2,1,0:T(8,128)} %param.9) | copy-start | bytes 983044
  19.2 6.5 %copy-start.3 = (f32[3,10,8,16]{3,2,1,0:T(8,128)S(1)}, f32[3,10,8,16]{3,2,1,0:T(8,128)}, u32[]{:S(2)}) copy-start(f32[3,10,8,16]{3,2,1,0:T(8,128)} %param.13) | copy-start | bytes 46084
  19.2 6.5 %copy-start.5 = (f32[4,8,16]{2,1,0:T(8,128)S(1)}, f32[4,8,16]{2,1,0:T(8,128)}, u32[]{:S(2)}) copy-start(f32[4,8,16]{2,1,0:T(8,128)} %param.15) | copy-start | bytes 6148
  19.6 6.1 %copy-start.4 = (s32[4,8,16]{2,1,0:T(8,128)S(1)}, s32[4,8,16]{2,1,0:T(8,128)}, u32[]{:S(2)}) copy-start(s32[4,8,16]{2,1,0:T(8,128)} %param.14) | copy-start | bytes 6148
  19.6 6.1 %collective-permute-start.6 = (f32[5,2,16,128]{3,2,1,0:T(8,128)S(1)}, f32[5,2,16,128]{3,2,1,0:T(8,128)S(1)}, u32[]{:S(2)}, u32[]{:S(2)}) collective-permute-start(f32[5,2,16,128]{3,2,1,0:T(8,128)S(1)} %get-tuple-element.68), channel_id=1, source_target_pairs={{0,32},{32,0},{64,96},{96,64},{128,160},{160,128},{192,224},{224,1... | collective-permute-start | bytes 245768 | tf_op jit(solution)/shard_map/ppermute | solution.py:331
  19.6 7.2 %collective-permute-start.7 = (f32[5,2,16,128]{3,2,1,0:T(8,128)S(1)}, f32[5,2,16,128]{3,2,1,0:T(8,128)S(1)}, u32[]{:S(2)}, u32[]{:S(2)}) collective-permute-start(f32[5,2,16,128]{3,2,1,0:T(8,128)S(1)} %get-tuple-element.70), channel_id=1, source_target_pairs={{0,224},{32,64},{64,32},{96,128},{128,96},{160,192},{192,160},{224... | collective-permute-start | bytes 245768 | tf_op jit(solution)/shard_map/ppermute | solution.py:331
  21.3 5.6 %collective-permute-start.9 = (f32[88,128]{1,0:T(8,128)S(1)}, f32[88,128]{1,0:T(8,128)S(1)}, u32[]{:S(2)}, u32[]{:S(2)}) collective-permute-start(f32[88,128]{1,0:T(8,128)S(1)} %get-tuple-element.72), channel_id=1, source_target_pairs={{0,3},{1,2},{2,1},{3,0},{4,7},{5,6},{6,5},{7,4},{8,11},{9,10},{10,... | collective-permute-start | bytes 135176 | tf_op jit(solution)/shard_map/ppermute | solution.py:331
  22.5 5.1 %collective-permute-start.10 = (f32[5,2,8,128]{3,2,1,0:T(8,128)S(1)}, f32[5,2,8,128]{3,2,1,0:T(8,128)S(1)}, u32[]{:S(2)}, u32[]{:S(2)}) collective-permute-start(f32[5,2,8,128]{3,2,1,0:T(8,128)S(1)} %get-tuple-element.78), channel_id=1, source_target_pairs={{0,4},{4,0},{8,12},{12,8},{16,20},{20,16},{24,28},{28,24},{1,5},{5... | collective-permute-start | bytes 122888 | tf_op jit(solution)/shard_map/ppermute | solution.py:331
  22.5 5.1 %collective-permute-start.11 = (f32[5,2,8,128]{3,2,1,0:T(8,128)S(1)}, f32[5,2,8,128]{3,2,1,0:T(8,128)S(1)}, u32[]{:S(2)}, u32[]{:S(2)}) collective-permute-start(f32[5,2,8,128]{3,2,1,0:T(8,128)S(1)} %get-tuple-element.79), channel_id=1, source_target_pairs={{0,28},{4,8},{8,4},{12,16},{16,12},{20,24},{24,20},{28,0},{1,29},{... | collective-permute-start | bytes 122888 | tf_op jit(solution)/shard_map/ppermute | solution.py:331
  25.6 1.2 %collective-permute-start.8 = (f32[24,128]{1,0:T(8,128)S(1)}, f32[24,128]{1,0:T(8,128)S(1)}, u32[]{:S(2)}, u32[]{:S(2)}) collective-permute-start(f32[24,128]{1,0:T(8,128)S(1)} %get-tuple-element.71), channel_id=1, source_target_pairs={{0,1},{1,0},{2,3},{3,2},{4,5},{5,4},{6,7},{7,6},{8,9},{9,8},{10,11... | collective-permute-start | bytes 36872 | tf_op jit(solution)/shard_map/ppermute | solution.py:331
  28.0 8.5 %collective-permute-start.12 = (f32[5,2,16,128]{3,2,1,0:T(8,128)S(1)}, f32[5,2,16,128]{3,2,1,0:T(8,128)S(1)}, u32[]{:S(2)}, u32[]{:S(2)}) collective-permute-start(f32[5,2,16,128]{3,2,1,0:T(8,128)S(1)} %get-tuple-element.82), channel_id=1, source_target_pairs={{0,32},{32,0},{64,96},{96,64},{128,160},{160,128},{192,224},{224,1... | collective-permute-start | bytes 245768 | tf_op jit(solution)/shard_map/ppermute | solution.py:331
  28.2 8.6 %collective-permute-start.13 = (f32[5,2,16,128]{3,2,1,0:T(8,128)S(1)}, f32[5,2,16,128]{3,2,1,0:T(8,128)S(1)}, u32[]{:S(2)}, u32[]{:S(2)}) collective-permute-start(f32[5,2,16,128]{3,2,1,0:T(8,128)S(1)} %get-tuple-element.84), channel_id=1, source_target_pairs={{0,224},{32,64},{64,32},{96,128},{128,96},{160,192},{192,160},{224... | collective-permute-start | bytes 245768 | tf_op jit(solution)/shard_map/ppermute | solution.py:331
  30.3 6.5 %collective-permute-start.15 = (f32[88,128]{1,0:T(8,128)S(1)}, f32[88,128]{1,0:T(8,128)S(1)}, u32[]{:S(2)}, u32[]{:S(2)}) collective-permute-start(f32[88,128]{1,0:T(8,128)S(1)} %get-tuple-element.86), channel_id=1, source_target_pairs={{0,3},{1,2},{2,1},{3,0},{4,7},{5,6},{6,5},{7,4},{8,11},{9,10},{10,... | collective-permute-start | bytes 135176 | tf_op jit(solution)/shard_map/ppermute | solution.py:331
  33.5 5.0 %collective-permute-start.16 = (f32[5,2,8,128]{3,2,1,0:T(8,128)S(1)}, f32[5,2,8,128]{3,2,1,0:T(8,128)S(1)}, u32[]{:S(2)}, u32[]{:S(2)}) collective-permute-start(f32[5,2,8,128]{3,2,1,0:T(8,128)S(1)} %get-tuple-element.87), channel_id=1, source_target_pairs={{0,4},{4,0},{8,12},{12,8},{16,20},{20,16},{24,28},{28,24},{1,5},{5... | collective-permute-start | bytes 122888 | tf_op jit(solution)/shard_map/ppermute | solution.py:331
  33.7 4.8 %collective-permute-start.17 = (f32[5,2,8,128]{3,2,1,0:T(8,128)S(1)}, f32[5,2,8,128]{3,2,1,0:T(8,128)S(1)}, u32[]{:S(2)}, u32[]{:S(2)}) collective-permute-start(f32[5,2,8,128]{3,2,1,0:T(8,128)S(1)} %get-tuple-element.88), channel_id=1, source_target_pairs={{0,28},{4,8},{8,4},{12,16},{16,12},{20,24},{24,20},{28,0},{1,29},{... | collective-permute-start | bytes 122888 | tf_op jit(solution)/shard_map/ppermute | solution.py:331
  36.5 1.2 %collective-permute-start.14 = (f32[24,128]{1,0:T(8,128)S(1)}, f32[24,128]{1,0:T(8,128)S(1)}, u32[]{:S(2)}, u32[]{:S(2)}) collective-permute-start(f32[24,128]{1,0:T(8,128)S(1)} %get-tuple-element.85), channel_id=1, source_target_pairs={{0,1},{1,0},{2,3},{3,2},{4,5},{5,4},{6,7},{7,6},{8,9},{9,8},{10,11... | collective-permute-start | bytes 36872 | tf_op jit(solution)/shard_map/ppermute | solution.py:331
  38.9 6.6 %collective-permute-start.18 = (f32[5,2,16,128]{3,2,1,0:T(8,128)S(1)}, f32[5,2,16,128]{3,2,1,0:T(8,128)S(1)}, u32[]{:S(2)}, u32[]{:S(2)}) collective-permute-start(f32[5,2,16,128]{3,2,1,0:T(8,128)S(1)} %get-tuple-element.91), channel_id=1, source_target_pairs={{0,32},{32,0},{64,96},{96,64},{128,160},{160,128},{192,224},{224,1... | collective-permute-start | bytes 245768 | tf_op jit(solution)/shard_map/ppermute | solution.py:331
  38.9 7.1 %collective-permute-start.19 = (f32[5,2,16,128]{3,2,1,0:T(8,128)S(1)}, f32[5,2,16,128]{3,2,1,0:T(8,128)S(1)}, u32[]{:S(2)}, u32[]{:S(2)}) collective-permute-start(f32[5,2,16,128]{3,2,1,0:T(8,128)S(1)} %get-tuple-element.93), channel_id=1, source_target_pairs={{0,224},{32,64},{64,32},{96,128},{128,96},{160,192},{192,160},{224... | collective-permute-start | bytes 245768 | tf_op jit(solution)/shard_map/ppermute | solution.py:331
  40.8 5.3 %collective-permute-start.21 = (f32[88,128]{1,0:T(8,128)S(1)}, f32[88,128]{1,0:T(8,128)S(1)}, u32[]{:S(2)}, u32[]{:S(2)}) collective-permute-start(f32[88,128]{1,0:T(8,128)S(1)} %get-tuple-element.95), channel_id=1, source_target_pairs={{0,3},{1,2},{2,1},{3,0},{4,7},{5,6},{6,5},{7,4},{8,11},{9,10},{10,... | collective-permute-start | bytes 135176 | tf_op jit(solution)/shard_map/ppermute | solution.py:331
  42.4 5.1 %collective-permute-start.22 = (f32[5,2,8,128]{3,2,1,0:T(8,128)S(1)}, f32[5,2,8,128]{3,2,1,0:T(8,128)S(1)}, u32[]{:S(2)}, u32[]{:S(2)}) collective-permute-start(f32[5,2,8,128]{3,2,1,0:T(8,128)S(1)} %get-tuple-element.96), channel_id=1, source_target_pairs={{0,4},{4,0},{8,12},{12,8},{16,20},{20,16},{24,28},{28,24},{1,5},{5... | collective-permute-start | bytes 122888 | tf_op jit(solution)/shard_map/ppermute | solution.py:331
  42.6 4.9 %collective-permute-start.23 = (f32[5,2,8,128]{3,2,1,0:T(8,128)S(1)}, f32[5,2,8,128]{3,2,1,0:T(8,128)S(1)}, u32[]{:S(2)}, u32[]{:S(2)}) collective-permute-start(f32[5,2,8,128]{3,2,1,0:T(8,128)S(1)} %get-tuple-element.97), channel_id=1, source_target_pairs={{0,28},{4,8},{8,4},{12,16},{16,12},{20,24},{24,20},{28,0},{1,29},{... | collective-permute-start | bytes 122888 | tf_op jit(solution)/shard_map/ppermute | solution.py:331
  45.5 1.2 %collective-permute-start.20 = (f32[24,128]{1,0:T(8,128)S(1)}, f32[24,128]{1,0:T(8,128)S(1)}, u32[]{:S(2)}, u32[]{:S(2)}) collective-permute-start(f32[24,128]{1,0:T(8,128)S(1)} %get-tuple-element.94), channel_id=1, source_target_pairs={{0,1},{1,0},{2,3},{3,2},{4,5},{5,4},{6,7},{7,6},{8,9},{9,8},{10,11... | collective-permute-start | bytes 36872 | tf_op jit(solution)/shard_map/ppermute | solution.py:331

commit v11 on v10

--- a/solution.py
+++ b/solution.py
@@ -83,7 +83,7 @@
         out_ref[8 * i : 8 * i + 8, :] = v + lane_roll(v, 64)
 
 
-def emit_sends(psi_ref, metric_ref, packed_metric, groups, sends, rows=None):
+def emit_sends(psi_ref, metric_ref, packed_metric, groups, sends, rows=None, loads=()):
     x0, x1, y0, y1, zz, far = sends
     lane = iota((8, NZ), 1)
     same, after, before = (packed_metric[8 * i : 8 * i + 8, :] for i in range(3))
@@ -93,6 +93,8 @@
         zz[8 * g : 8 * g + 8, :] = v
         far[8 * g : 8 * g + 8, :] = v
     far[24:, :] = jnp.zeros((FAR_ROWS - 24, NZ), F32)
+    for copy in loads[:1]:
+        copy.wait()
     even = is_even("gy")
     m4, m6a, m6b = metric_ref[4, edge_rows(15), :], metric_ref[6, edge_rows(14), :], metric_ref[6, edge_rows(15), :]
     m5, m7a, m7b = metric_ref[5, edge_rows(0), :], metric_ref[7, edge_rows(0), :], metric_ref[7, edge_rows(1), :]
@@ -103,6 +105,8 @@
         for r in range(2):
             y0[e, r] = jnp.where(even, high[r], low[r])
             y1[e, r] = jnp.where(even, low[r], high[r])
+    for copy in loads[1:]:
+        copy.wait()
     even = is_even("gx")
     last, near = slab(NX - 1), slab(NX - 2)
     m0, m2a, m2b = metric_ref[0, last, :], metric_ref[2, near, :], metric_ref[2, last, :]
@@ -129,9 +133,7 @@
     pack_metric(metric_ref, packed_metric)
     copies[1].wait()
     groups = pack_edges(psi_ref)
-    copies[2].wait()
-    copies[3].wait()
-    emit_sends(psi_ref, metric_ref, packed_metric, groups, (x0, x1, y0, y1, zz, far))
+    emit_sends(psi_ref, metric_ref, packed_metric, groups, (x0, x1, y0, y1, zz, far), loads=copies[2:])
 
 
 def from_sides(axis, first, second):
@@ -204,14 +206,15 @@
             jac_rows[4 * k + i] = wide[k, edge_rows(y), :]
 
 
-def finish(base_ref, y0, y1, jac_rows, scale_rows, new_ref):
+def finish(base_ref, y0, y1, jac_rows, scale_rows, new_ref, in_place=True, out=()):
     zs = []
     for e in range(FIELDS):
         sides = [from_sides("gy", y0[e, r], y1[e, r]) for r in range(2)]
         zs.append([sides[0][0], sides[1][0], sides[0][1], sides[1][1]])
     rows = []
     for f in range(FIELDS):
-        new_ref[f] = base_ref[f]
+        if not in_place:
+            new_ref[f] = base_ref[f]
         mine = []
         for i, y in enumerate(OUTER_ROWS):
             c = jac_rows[4 * f + i] * zs[0][i]
@@ -220,6 +223,8 @@
             mine.append(base_ref[f, edge_rows(y), :] + c * scale_rows[i])
         for i, y in enumerate(OUTER_ROWS):
             new_ref[f, edge_rows(y), :] = mine[i]
+        if out:
+            out[f].start()
         rows.append(mine)
     return rows
 
@@ -265,10 +270,9 @@
 
 
 def last_body(base_ref, y_even, y_odd, jac_rows, scale_rows, coef_ref, weight_ref, hot_ref, low_ref,
-              out_hbm, slots_ref, new_ref, high_part, low_part, sem):
-    finish(base_ref, y_even, y_odd, jac_rows, scale_rows, new_ref)
-    copy = pltpu.make_async_copy(new_ref, out_hbm, sem)
-    copy.start()
+              out_hbm, slots_ref, new_ref, high_part, low_part, sems):
+    copies = [pltpu.make_async_copy(new_ref.at[f], out_hbm.at[f], sems.at[f]) for f in range(FIELDS)]
+    finish(base_ref, y_even, y_odd, jac_rows, scale_rows, new_ref, in_place=False, out=copies)
     lane = iota((8, NZ), 1)
     groups = pack_edges(new_ref)
     low = low_ref[...]
@@ -294,7 +298,8 @@
     slots_ref[...] = lax.dot_general(hot, high_part[...], dims, preferred_element_type=F32) + lax.dot_general(
         hot, low_part[...], dims, preferred_element_type=F32
     )
-    copy.wait()
+    for copy in copies:
+        copy.wait()
 
 
 def sum_body(got_ref, out_ref):
@@ -303,7 +308,7 @@
         out_ref[c : c + 1, :] = v[:, 16 * c : 16 * c + 16]
 
 
-def run(body, args, outs, scratch=(), sems=(), far=(), far_outs=()):
+def run(body, args, outs, scratch=(), sems=(), far=(), far_outs=(), aliases=None):
     hbm = pl.BlockSpec(memory_space=pltpu.HBM)
     args = [pltpu.with_memory_space_constraint(v, pltpu.HBM) if i in far else v for i, v in enumerate(args)]
     return pl.pallas_call(
@@ -312,6 +317,7 @@
         in_specs=[hbm if i in far else VMEM for i in range(len(args))],
         out_specs=[hbm if i in far_outs else VMEM for i in range(len(outs))],
         scratch_shapes=[pltpu.VMEM(s, d) for s, d in scratch] + [pltpu.SemaphoreType.DMA(s) for s in sems],
+        input_output_aliases=aliases or {},
         compiler_params=pltpu.CompilerParams(vmem_limit_bytes=24 << 20),
         cost_estimate=pl.CostEstimate(flops=1000000, bytes_accessed=1000000, transcendentals=0),
     )(*args)
@@ -363,11 +369,13 @@
         if step == 1:
             base, wall = lax.optimization_barrier((base, wall))
         if step < SWEEPS - 1:
-            psi, *sends = run(middle_body, (base, y_even, y_odd, *rows, metric, packed_metric), [FIELD] + SENDS)
+            psi, *sends = run(
+                middle_body, (base, y_even, y_odd, *rows, metric, packed_metric), [FIELD] + SENDS, aliases={0: 0}
+            )
         else:
             psi, slots = run(
                 last_body, (base, y_even, y_odd, *rows, *wall), [FIELD, ((256, 48), F32)],
-                scratch=[FIELD, ((48, 512), jnp.bfloat16), ((48, 512), jnp.bfloat16)], sems=[()], far_outs=(0,),
+                scratch=[FIELD, ((48, 512), jnp.bfloat16), ((48, 512), jnp.bfloat16)], sems=[(FIELDS,)], far_outs=(0,),
             )
     got = lax.all_to_all(slots.reshape(256, 1, 48), AXES, 0, 0).reshape(256, 48)
     (grad,) = run(sum_body, (got,), [((3, 16), F32)])

time: 71.6 us -> 71.5 us (level)
  transfers between devices with their start and end apart: 24 -> 24, of which waited for: 6 -> 7; matrix products, arithmetic and copies ran while one was open for 0% -> 0% of each run, Pallas kernels for 5% -> 5%
where the time goes in v11:
time: 71.5 us; the launch traced here: 71.3 us
  starting transfers between devices  36.4 us (51%)
  blocking collectives  22.2 us (31%)
  Pallas kernels  8.15 us (11%)
  waiting for transfers between devices  3.73 us (5%)
  between operations  0.86 us (1%)
    ppermute x24, starting transfers between devices, swap(): return lax.ppermute(v, axis, pairs(lax.axis_size(axis), odd))  36.4 us
    all_to_all x1, blocking collectives, local(): got = lax.all_to_all(slots.reshape(256, 1, 48), AXES, 0, 0).reshape(256, 48)  22.2 us
    pallas_call x12, Pallas kernels, run(): pl.pallas_call(body, out_shape=[jax.ShapeDtypeStruct(s, d) for s, d in ou...  8.15 us
    ppermute x24, waiting for transfers between devices, swap(): return lax.ppermute(v, axis, pairs(lax.axis_size(axis), odd))  3.73 us
  transfers between devices with their start and end apart: 24, of which 7 were waited for; matrix products, arithmetic and copies ran while one was open for 0% of the time, Pallas kernels for 5%

profile of v11, /device:TPU:1, one launch (start us, length us, event | category | flops | bytes accessed | tf_op | source)
XLA Modules:
  0.0 71.3 jit_solution(12139845651010699480)
XLA Ops:
  0.7 1.6 %shard_map.95 = (f32[5,2,16,128]{3,2,1,0:T(8,128)S(1)}, f32[5,2,16,128]{3,2,1,0:T(8,128)S(1)}, f32[5,2,8,128]{3,2,1,0:T(8,128)S(1)}, f32[5,2,8,128]{3,2,1,0:T(8,...) custom-call(f32[5,128,128]{2,1,0:T(8,128)} %bitcast.33, ...), custom_call_target="tpu_custom_call" | custom-call | flops 1000000 | bytes 1000000 | tf_op jit(solution)/shard_map/pallas_call | solution.py:314
  2.3 2.1 %collective-permute-start = (f32[5,2,16,128]{3,2,1,0:T(8,128)S(1)}, f32[5,2,16,128]{3,2,1,0:T(8,128)S(1)}, u32[]{:S(2)}, u32[]{:S(2)}) collective-permute-start(f32[5,2,16,128]{3,2,1,0:T(8,128)S(1)} %get-tuple-element.56), channel_id=1, source_target_pairs={{0,32},{32,0},{64,96},{96,64},{128,160},{160,128},{192,224},{224,1... | collective-permute-start | bytes 245768 | tf_op jit(solution)/shard_map/ppermute | solution.py:337
  4.4 2.7 %collective-permute-start.1 = (f32[5,2,16,128]{3,2,1,0:T(8,128)S(1)}, f32[5,2,16,128]{3,2,1,0:T(8,128)S(1)}, u32[]{:S(2)}, u32[]{:S(2)}) collective-permute-start(f32[5,2,16,128]{3,2,1,0:T(8,128)S(1)} %get-tuple-element.58), channel_id=1, source_target_pairs={{0,224},{32,64},{64,32},{96,128},{128,96},{160,192},{192,160},{224... | collective-permute-start | bytes 245768 | tf_op jit(solution)/shard_map/ppermute | solution.py:337
  7.1 3.9 %collective-permute-start.3 = (f32[88,128]{1,0:T(8,128)S(1)}, f32[88,128]{1,0:T(8,128)S(1)}, u32[]{:S(2)}, u32[]{:S(2)}) collective-permute-start(f32[88,128]{1,0:T(8,128)S(1)} %get-tuple-element.60), channel_id=1, source_target_pairs={{0,3},{1,2},{2,1},{3,0},{4,7},{5,6},{6,5},{7,4},{8,11},{9,10},{10,... | collective-permute-start | bytes 135176 | tf_op jit(solution)/shard_map/ppermute | solution.py:337
  11.0 1.6 %collective-permute-start.4 = (f32[5,2,8,128]{3,2,1,0:T(8,128)S(1)}, f32[5,2,8,128]{3,2,1,0:T(8,128)S(1)}, u32[]{:S(2)}, u32[]{:S(2)}) collective-permute-start(f32[5,2,8,128]{3,2,1,0:T(8,128)S(1)} %get-tuple-element.61), channel_id=1, source_target_pairs={{0,4},{4,0},{8,12},{12,8},{16,20},{20,16},{24,28},{28,24},{1,5},{5... | collective-permute-start | bytes 122888 | tf_op jit(solution)/shard_map/ppermute | solution.py:337
  12.6 4.7 %collective-permute-start.5 = (f32[5,2,8,128]{3,2,1,0:T(8,128)S(1)}, f32[5,2,8,128]{3,2,1,0:T(8,128)S(1)}, u32[]{:S(2)}, u32[]{:S(2)}) collective-permute-start(f32[5,2,8,128]{3,2,1,0:T(8,128)S(1)} %get-tuple-element.62), channel_id=1, source_target_pairs={{0,28},{4,8},{8,4},{12,16},{16,12},{20,24},{24,20},{28,0},{1,29},{... | collective-permute-start | bytes 122888 | tf_op jit(solution)/shard_map/ppermute | solution.py:337
  17.3 0.0 collective-permute-done.x0
  17.3 0.0 collective-permute-start.2
  17.3 0.0 copy-start.1
  17.3 0.3 shard_map.97
  17.6 0.0 collective-permute-done.3.z1
  17.6 0.0 collective-permute-done.1.x1
  17.6 0.8 %collective-permute-done.2.z0 = f32[24,128]{1,0:T(8,128)S(1)} collective-permute-done((f32[24,128]{1,0:T(8,128)S(1)}, f32[24,128]{1,0:T(8,128)S(1)}, u32[]{:S(2)}, u32[]{:S(2)}) %collective-permute-start.2) | collective-permute-done | bytes 12320 | tf_op jit(solution)/shard_map/ppermute | solution.py:337
  18.5 0.7 %shard_map.96.base_ref = f32[5,128,128]{2,1,0:T(8,128)S(1)} custom-call(f32[5,128,128]{2,1,0:T(8,128)S(1)} %get-tuple-element.53.psi_ref, f32[12,128,128]{2,1,0:T(8,128)S(1)} %get-tuple-element.54.metric_ref, f32[128,128]{1,0:T(8,128)S(1)} %bitcast.23, f32[5,128,128]{2,1,0:T(8,128)S(1)} %bitcast.18, bf16[25,128,128]{2,1,0:T(8,128)(2,1)S(1)} %bitcast.14, ...), custom_call_target="tpu_custom_call" | custom-call | flops 1000000 | bytes 1000000 | tf_op jit(solution)/shard_map/pallas_call | solution.py:314
  19.2 0.0 collective-permute-done.4.y_even
  19.2 0.0 collective-permute-done.5.y_odd
  19.2 0.0 copy-start.3
  19.2 0.0 copy-start.5
  19.3 0.4 shard_map.98
  19.7 0.0 collective-permute-start.6
  19.7 1.6 %collective-permute-start.7 = (f32[5,2,16,128]{3,2,1,0:T(8,128)S(1)}, f32[5,2,16,128]{3,2,1,0:T(8,128)S(1)}, u32[]{:S(2)}, u32[]{:S(2)}) collective-permute-start(f32[5,2,16,128]{3,2,1,0:T(8,128)S(1)} %get-tuple-element.70), channel_id=1, source_target_pairs={{0,224},{32,64},{64,32},{96,128},{128,96},{160,192},{192,160},{224... | collective-permute-start | bytes 245768 | tf_op jit(solution)/shard_map/ppermute | solution.py:337
  21.4 1.2 %collective-permute-start.9 = (f32[88,128]{1,0:T(8,128)S(1)}, f32[88,128]{1,0:T(8,128)S(1)}, u32[]{:S(2)}, u32[]{:S(2)}) collective-permute-start(f32[88,128]{1,0:T(8,128)S(1)} %get-tuple-element.72), channel_id=1, source_target_pairs={{0,3},{1,2},{2,1},{3,0},{4,7},{5,6},{6,5},{7,4},{8,11},{9,10},{10,... | collective-permute-start | bytes 135176 | tf_op jit(solution)/shard_map/ppermute | solution.py:337
  22.6 0.0 collective-permute-start.10
  22.6 3.2 %collective-permute-start.11 = (f32[5,2,8,128]{3,2,1,0:T(8,128)S(1)}, f32[5,2,8,128]{3,2,1,0:T(8,128)S(1)}, u32[]{:S(2)}, u32[]{:S(2)}) collective-permute-start(f32[5,2,8,128]{3,2,1,0:T(8,128)S(1)} %get-tuple-element.79), channel_id=1, source_target_pairs={{0,28},{4,8},{8,4},{12,16},{16,12},{20,24},{24,20},{28,0},{1,29},{... | collective-permute-start | bytes 122888 | tf_op jit(solution)/shard_map/ppermute | solution.py:337
  25.7 0.0 collective-permute-done.6.x0
  25.7 0.0 collective-permute-start.8
  25.8 0.6 shard_map.100
  26.3 0.6 collective-permute-done.9.z1
  26.9 0.0 collective-permute-done.7.x1
  26.9 0.0 collective-permute-done.8.z0
  26.9 0.7 shard_map.99.base_ref
  27.6 0.0 collective-permute-done.10.y_even
  27.7 0.0 collective-permute-done.11.y_odd
  27.7 0.4 shard_map.101
  28.1 0.1 collective-permute-start.12
  28.2 2.1 %collective-permute-start.13 = (f32[5,2,16,128]{3,2,1,0:T(8,128)S(1)}, f32[5,2,16,128]{3,2,1,0:T(8,128)S(1)}, u32[]{:S(2)}, u32[]{:S(2)}) collective-permute-start(f32[5,2,16,128]{3,2,1,0:T(8,128)S(1)} %get-tuple-element.84), channel_id=1, source_target_pairs={{0,224},{32,64},{64,32},{96,128},{128,96},{160,192},{192,160},{224... | collective-permute-start | bytes 245768 | tf_op jit(solution)/shard_map/ppermute | solution.py:337
  30.3 3.2 %collective-permute-start.15 = (f32[88,128]{1,0:T(8,128)S(1)}, f32[88,128]{1,0:T(8,128)S(1)}, u32[]{:S(2)}, u32[]{:S(2)}) collective-permute-start(f32[88,128]{1,0:T(8,128)S(1)} %get-tuple-element.86), channel_id=1, source_target_pairs={{0,3},{1,2},{2,1},{3,0},{4,7},{5,6},{6,5},{7,4},{8,11},{9,10},{10,... | collective-permute-start | bytes 135176 | tf_op jit(solution)/shard_map/ppermute | solution.py:337
  33.5 0.2 collective-permute-start.16
  33.8 2.8 %collective-permute-start.17 = (f32[5,2,8,128]{3,2,1,0:T(8,128)S(1)}, f32[5,2,8,128]{3,2,1,0:T(8,128)S(1)}, u32[]{:S(2)}, u32[]{:S(2)}) collective-permute-start(f32[5,2,8,128]{3,2,1,0:T(8,128)S(1)} %get-tuple-element.88), channel_id=1, source_target_pairs={{0,28},{4,8},{8,4},{12,16},{16,12},{20,24},{24,20},{28,0},{1,29},{... | collective-permute-start | bytes 122888 | tf_op jit(solution)/shard_map/ppermute | solution.py:337
  36.6 0.0 collective-permute-done.12.x0
  36.6 0.0 collective-permute-start.14
  36.6 0.2 collective-permute-done.15.z1
  36.8 0.0 collective-permute-done.13.x1
  36.8 1.0 %collective-permute-done.14.z0 = f32[24,128]{1,0:T(8,128)S(1)} collective-permute-done((f32[24,128]{1,0:T(8,128)S(1)}, f32[24,128]{1,0:T(8,128)S(1)}, u32[]{:S(2)}, u32[]{:S(2)}) %collective-permute-start.14) | collective-permute-done | bytes 12320 | tf_op jit(solution)/shard_map/ppermute | solution.py:337
  37.8 0.7 shard_map.102.base_ref
  38.5 0.0 collective-permute-done.16.y_even
  38.5 0.0 collective-permute-done.17.y_odd
  38.5 0.4 shard_map.103
  38.9 0.0 collective-permute-start.18
  39.0 1.8 %collective-permute-start.19 = (f32[5,2,16,128]{3,2,1,0:T(8,128)S(1)}, f32[5,2,16,128]{3,2,1,0:T(8,128)S(1)}, u32[]{:S(2)}, u32[]{:S(2)}) collective-permute-start(f32[5,2,16,128]{3,2,1,0:T(8,128)S(1)} %get-tuple-element.93), channel_id=1, source_target_pairs={{0,224},{32,64},{64,32},{96,128},{128,96},{160,192},{192,160},{224... | collective-permute-start | bytes 245768 | tf_op jit(solution)/shard_map/ppermute | solution.py:337
  40.8 1.6 %collective-permute-start.21 = (f32[88,128]{1,0:T(8,128)S(1)}, f32[88,128]{1,0:T(8,128)S(1)}, u32[]{:S(2)}, u32[]{:S(2)}) collective-permute-start(f32[88,128]{1,0:T(8,128)S(1)} %get-tuple-element.95), channel_id=1, source_target_pairs={{0,3},{1,2},{2,1},{3,0},{4,7},{5,6},{6,5},{7,4},{8,11},{9,10},{10,... | collective-permute-start | bytes 135176 | tf_op jit(solution)/shard_map/ppermute | solution.py:337
  42.4 0.2 collective-permute-start.22
  42.6 2.9 %collective-permute-start.23 = (f32[5,2,8,128]{3,2,1,0:T(8,128)S(1)}, f32[5,2,8,128]{3,2,1,0:T(8,128)S(1)}, u32[]{:S(2)}, u32[]{:S(2)}) collective-permute-start(f32[5,2,8,128]{3,2,1,0:T(8,128)S(1)} %get-tuple-element.97), channel_id=1, source_target_pairs={{0,28},{4,8},{8,4},{12,16},{16,12},{20,24},{24,20},{28,0},{1,29},{... | collective-permute-start | bytes 122888 | tf_op jit(solution)/shard_map/ppermute | solution.py:337
  45.5 0.0 collective-permute-done.18.x0
  45.5 0.2 collective-permute-start.20
  45.7 0.4 collective-permute-done.21.z1
  46.1 0.0 collective-permute-done.19.x1
  46.1 0.6 collective-permute-done.20.z0
  46.7 0.8 %shard_map.104.base_ref = f32[5,128,128]{2,1,0:T(8,128)S(1)} custom-call(f32[5,128,128]{2,1,0:T(8,128)S(1)} %get-tuple-element.89.psi_ref, f32[12,128,128]{2,1,0:T(8,128)S(1)} %get-tuple-element.54.metric_ref, f32[128,128]{1,0:T(8,128)S(1)} %bitcast.26, f32[5,128,128]{2,1,0:T(8,128)S(1)} %bitcast.21, bf16[25,128,128]{2,1,0:T(8,128)(2,1)S(1)} %bitcast.17, ...), custom_call_target="tpu_custom_call" | custom-call | flops 1000000 | bytes 1000000 | tf_op jit(solution)/shard_map/pallas_call | solution.py:314
  47.5 0.0 collective-permute-done.22.y_even
  47.5 0.1 collective-permute-done.23.y_odd
  47.5 0.9 %shard_map.105 = (f32[5,128,128]{2,1,0:T(8,128)}, f32[256,48]{1,0:T(8,128)S(1)}) custom-call(f32[5,128,128]{2,1,0:T(8,128)S(1)} %shard_map.104.base_ref, f32[5,2,8,128]{3,2,1,0:T(8,128)S(1)} %collective-permute-done.22.y_even, f32[5,2,8,128]{3,2,1,0:T(8,128)S(1)} %collective-permute-done.23.y_odd, f32[100,8,128]{2,1,0:T(8,128)S(1)} %get-tuple-element.63.jac_rows, ...), custom_call_target="tpu_custom_call" | custom-call | flops 1000000 | bytes 1000000 | tf_op jit(solution)/shard_map/pallas_call | solution.py:314
  48.4 22.2 %all_to_all.5 = f32[256,1,48]{2,1,0:T(1,128)S(1)} all-to-all(f32[256,1,48]{2,1,0:T(1,128)S(1)} %bitcast.28), channel_id=1, replica_groups=mesh['gx'=8,'gy'=8,'wa'=4] {'gx','gy','wa'}, dimensions={0} | all-to-all | bytes 98304 | tf_op jit(solution)/shard_map/all_to_all | solution.py:380
  70.6 0.7 shard_map.106
  (9 shorter events, 0.0 us)
Async XLA Ops:
  0.6 16.7 %copy-start = (bf16[5,5,8,16,128]{4,3,2,1,0:T(8,128)(2,1)S(1)}, bf16[5,5,8,16,128]{4,3,2,1,0:T(8,128)(2,1)}, u32[]{:S(2)}) copy-start(bf16[5,5,8,16,128]{4,3,2,1,0:T(8,128)(2,1)} %param.12) | copy-start | bytes 2457604
  0.6 16.7 %copy-start.2 = (f32[8,16,128]{2,1,0:T(8,128)S(1)}, f32[8,16,128]{2,1,0:T(8,128)}, u32[]{:S(2)}) copy-start(f32[8,16,128]{2,1,0:T(8,128)} %param.10) | copy-start | bytes 196612
  2.3 15.0 %collective-permute-start = (f32[5,2,16,128]{3,2,1,0:T(8,128)S(1)}, f32[5,2,16,128]{3,2,1,0:T(8,128)S(1)}, u32[]{:S(2)}, u32[]{:S(2)}) collective-permute-start(f32[5,2,16,128]{3,2,1,0:T(8,128)S(1)} %get-tuple-element.56), channel_id=1, source_target_pairs={{0,32},{32,0},{64,96},{96,64},{128,160},{160,128},{192,224},{224,1... | collective-permute-start | bytes 245768 | tf_op jit(solution)/shard_map/ppermute | solution.py:337
  4.4 13.2 %collective-permute-start.1 = (f32[5,2,16,128]{3,2,1,0:T(8,128)S(1)}, f32[5,2,16,128]{3,2,1,0:T(8,128)S(1)}, u32[]{:S(2)}, u32[]{:S(2)}) collective-permute-start(f32[5,2,16,128]{3,2,1,0:T(8,128)S(1)} %get-tuple-element.58), channel_id=1, source_target_pairs={{0,224},{32,64},{64,32},{96,128},{128,96},{160,192},{192,160},{224... | collective-permute-start | bytes 245768 | tf_op jit(solution)/shard_map/ppermute | solution.py:337
  7.1 10.5 %collective-permute-start.3 = (f32[88,128]{1,0:T(8,128)S(1)}, f32[88,128]{1,0:T(8,128)S(1)}, u32[]{:S(2)}, u32[]{:S(2)}) collective-permute-start(f32[88,128]{1,0:T(8,128)S(1)} %get-tuple-element.60), channel_id=1, source_target_pairs={{0,3},{1,2},{2,1},{3,0},{4,7},{5,6},{6,5},{7,4},{8,11},{9,10},{10,... | collective-permute-start | bytes 135176 | tf_op jit(solution)/shard_map/ppermute | solution.py:337
  11.0 8.2 %collective-permute-start.4 = (f32[5,2,8,128]{3,2,1,0:T(8,128)S(1)}, f32[5,2,8,128]{3,2,1,0:T(8,128)S(1)}, u32[]{:S(2)}, u32[]{:S(2)}) collective-permute-start(f32[5,2,8,128]{3,2,1,0:T(8,128)S(1)} %get-tuple-element.61), channel_id=1, source_target_pairs={{0,4},{4,0},{8,12},{12,8},{16,20},{20,16},{24,28},{28,24},{1,5},{5... | collective-permute-start | bytes 122888 | tf_op jit(solution)/shard_map/ppermute | solution.py:337
  12.6 6.6 %collective-permute-start.5 = (f32[5,2,8,128]{3,2,1,0:T(8,128)S(1)}, f32[5,2,8,128]{3,2,1,0:T(8,128)S(1)}, u32[]{:S(2)}, u32[]{:S(2)}) collective-permute-start(f32[5,2,8,128]{3,2,1,0:T(8,128)S(1)} %get-tuple-element.62), channel_id=1, source_target_pairs={{0,28},{4,8},{8,4},{12,16},{16,12},{20,24},{24,20},{28,0},{1,29},{... | collective-permute-start | bytes 122888 | tf_op jit(solution)/shard_map/ppermute | solution.py:337
  17.3 1.2 %collective-permute-start.2 = (f32[24,128]{1,0:T(8,128)S(1)}, f32[24,128]{1,0:T(8,128)S(1)}, u32[]{:S(2)}, u32[]{:S(2)}) collective-permute-start(f32[24,128]{1,0:T(8,128)S(1)} %get-tuple-element.59), channel_id=1, source_target_pairs={{0,1},{1,0},{2,3},{3,2},{4,5},{5,4},{6,7},{7,6},{8,9},{9,8},{10,11... | collective-permute-start | bytes 36872 | tf_op jit(solution)/shard_map/ppermute | solution.py:337
  17.3 1.2 %copy-start.1 = (f32[5,8,16,128]{3,2,1,0:T(8,128)S(1)}, f32[5,8,16,128]{3,2,1,0:T(8,128)}, u32[]{:S(2)}) copy-start(f32[5,8,16,128]{3,2,1,0:T(8,128)} %param.9) | copy-start | bytes 983044
  19.2 6.5 %copy-start.3 = (f32[3,10,8,16]{3,2,1,0:T(8,128)S(1)}, f32[3,10,8,16]{3,2,1,0:T(8,128)}, u32[]{:S(2)}) copy-start(f32[3,10,8,16]{3,2,1,0:T(8,128)} %param.13) | copy-start | bytes 46084
  19.2 6.5 %copy-start.5 = (f32[4,8,16]{2,1,0:T(8,128)S(1)}, f32[4,8,16]{2,1,0:T(8,128)}, u32[]{:S(2)}) copy-start(f32[4,8,16]{2,1,0:T(8,128)} %param.15) | copy-start | bytes 6148
  19.7 6.1 %copy-start.4 = (s32[4,8,16]{2,1,0:T(8,128)S(1)}, s32[4,8,16]{2,1,0:T(8,128)}, u32[]{:S(2)}) copy-start(s32[4,8,16]{2,1,0:T(8,128)} %param.14) | copy-start | bytes 6148
  19.7 6.1 %collective-permute-start.6 = (f32[5,2,16,128]{3,2,1,0:T(8,128)S(1)}, f32[5,2,16,128]{3,2,1,0:T(8,128)S(1)}, u32[]{:S(2)}, u32[]{:S(2)}) collective-permute-start(f32[5,2,16,128]{3,2,1,0:T(8,128)S(1)} %get-tuple-element.68), channel_id=1, source_target_pairs={{0,32},{32,0},{64,96},{96,64},{128,160},{160,128},{192,224},{224,1... | collective-permute-start | bytes 245768 | tf_op jit(solution)/shard_map/ppermute | solution.py:337
  19.7 7.2 %collective-permute-start.7 = (f32[5,2,16,128]{3,2,1,0:T(8,128)S(1)}, f32[5,2,16,128]{3,2,1,0:T(8,128)S(1)}, u32[]{:S(2)}, u32[]{:S(2)}) collective-permute-start(f32[5,2,16,128]{3,2,1,0:T(8,128)S(1)} %get-tuple-element.70), channel_id=1, source_target_pairs={{0,224},{32,64},{64,32},{96,128},{128,96},{160,192},{192,160},{224... | collective-permute-start | bytes 245768 | tf_op jit(solution)/shard_map/ppermute | solution.py:337
  21.4 5.6 %collective-permute-start.9 = (f32[88,128]{1,0:T(8,128)S(1)}, f32[88,128]{1,0:T(8,128)S(1)}, u32[]{:S(2)}, u32[]{:S(2)}) collective-permute-start(f32[88,128]{1,0:T(8,128)S(1)} %get-tuple-element.72), channel_id=1, source_target_pairs={{0,3},{1,2},{2,1},{3,0},{4,7},{5,6},{6,5},{7,4},{8,11},{9,10},{10,... | collective-permute-start | bytes 135176 | tf_op jit(solution)/shard_map/ppermute | solution.py:337
  22.6 5.1 %collective-permute-start.10 = (f32[5,2,8,128]{3,2,1,0:T(8,128)S(1)}, f32[5,2,8,128]{3,2,1,0:T(8,128)S(1)}, u32[]{:S(2)}, u32[]{:S(2)}) collective-permute-start(f32[5,2,8,128]{3,2,1,0:T(8,128)S(1)} %get-tuple-element.78), channel_id=1, source_target_pairs={{0,4},{4,0},{8,12},{12,8},{16,20},{20,16},{24,28},{28,24},{1,5},{5... | collective-permute-start | bytes 122888 | tf_op jit(solution)/shard_map/ppermute | solution.py:337
  22.6 5.1 %collective-permute-start.11 = (f32[5,2,8,128]{3,2,1,0:T(8,128)S(1)}, f32[5,2,8,128]{3,2,1,0:T(8,128)S(1)}, u32[]{:S(2)}, u32[]{:S(2)}) collective-permute-start(f32[5,2,8,128]{3,2,1,0:T(8,128)S(1)} %get-tuple-element.79), channel_id=1, source_target_pairs={{0,28},{4,8},{8,4},{12,16},{16,12},{20,24},{24,20},{28,0},{1,29},{... | collective-permute-start | bytes 122888 | tf_op jit(solution)/shard_map/ppermute | solution.py:337
  25.7 1.2 %collective-permute-start.8 = (f32[24,128]{1,0:T(8,128)S(1)}, f32[24,128]{1,0:T(8,128)S(1)}, u32[]{:S(2)}, u32[]{:S(2)}) collective-permute-start(f32[24,128]{1,0:T(8,128)S(1)} %get-tuple-element.71), channel_id=1, source_target_pairs={{0,1},{1,0},{2,3},{3,2},{4,5},{5,4},{6,7},{7,6},{8,9},{9,8},{10,11... | collective-permute-start | bytes 36872 | tf_op jit(solution)/shard_map/ppermute | solution.py:337
  28.1 8.5 %collective-permute-start.12 = (f32[5,2,16,128]{3,2,1,0:T(8,128)S(1)}, f32[5,2,16,128]{3,2,1,0:T(8,128)S(1)}, u32[]{:S(2)}, u32[]{:S(2)}) collective-permute-start(f32[5,2,16,128]{3,2,1,0:T(8,128)S(1)} %get-tuple-element.82), channel_id=1, source_target_pairs={{0,32},{32,0},{64,96},{96,64},{128,160},{160,128},{192,224},{224,1... | collective-permute-start | bytes 245768 | tf_op jit(solution)/shard_map/ppermute | solution.py:337
  28.2 8.6 %collective-permute-start.13 = (f32[5,2,16,128]{3,2,1,0:T(8,128)S(1)}, f32[5,2,16,128]{3,2,1,0:T(8,128)S(1)}, u32[]{:S(2)}, u32[]{:S(2)}) collective-permute-start(f32[5,2,16,128]{3,2,1,0:T(8,128)S(1)} %get-tuple-element.84), channel_id=1, source_target_pairs={{0,224},{32,64},{64,32},{96,128},{128,96},{160,192},{192,160},{224... | collective-permute-start | bytes 245768 | tf_op jit(solution)/shard_map/ppermute | solution.py:337
  30.3 6.5 %collective-permute-start.15 = (f32[88,128]{1,0:T(8,128)S(1)}, f32[88,128]{1,0:T(8,128)S(1)}, u32[]{:S(2)}, u32[]{:S(2)}) collective-permute-start(f32[88,128]{1,0:T(8,128)S(1)} %get-tuple-element.86), channel_id=1, source_target_pairs={{0,3},{1,2},{2,1},{3,0},{4,7},{5,6},{6,5},{7,4},{8,11},{9,10},{10,... | collective-permute-start | bytes 135176 | tf_op jit(solution)/shard_map/ppermute | solution.py:337
  33.5 4.9 %collective-permute-start.16 = (f32[5,2,8,128]{3,2,1,0:T(8,128)S(1)}, f32[5,2,8,128]{3,2,1,0:T(8,128)S(1)}, u32[]{:S(2)}, u32[]{:S(2)}) collective-permute-start(f32[5,2,8,128]{3,2,1,0:T(8,128)S(1)} %get-tuple-element.87), channel_id=1, source_target_pairs={{0,4},{4,0},{8,12},{12,8},{16,20},{20,16},{24,28},{28,24},{1,5},{5... | collective-permute-start | bytes 122888 | tf_op jit(solution)/shard_map/ppermute | solution.py:337
  33.8 4.7 %collective-permute-start.17 = (f32[5,2,8,128]{3,2,1,0:T(8,128)S(1)}, f32[5,2,8,128]{3,2,1,0:T(8,128)S(1)}, u32[]{:S(2)}, u32[]{:S(2)}) collective-permute-start(f32[5,2,8,128]{3,2,1,0:T(8,128)S(1)} %get-tuple-element.88), channel_id=1, source_target_pairs={{0,28},{4,8},{8,4},{12,16},{16,12},{20,24},{24,20},{28,0},{1,29},{... | collective-permute-start | bytes 122888 | tf_op jit(solution)/shard_map/ppermute | solution.py:337
  36.6 1.2 %collective-permute-start.14 = (f32[24,128]{1,0:T(8,128)S(1)}, f32[24,128]{1,0:T(8,128)S(1)}, u32[]{:S(2)}, u32[]{:S(2)}) collective-permute-start(f32[24,128]{1,0:T(8,128)S(1)} %get-tuple-element.85), channel_id=1, source_target_pairs={{0,1},{1,0},{2,3},{3,2},{4,5},{5,4},{6,7},{7,6},{8,9},{9,8},{10,11... | collective-permute-start | bytes 36872 | tf_op jit(solution)/shard_map/ppermute | solution.py:337
  38.9 6.6 %collective-permute-start.18 = (f32[5,2,16,128]{3,2,1,0:T(8,128)S(1)}, f32[5,2,16,128]{3,2,1,0:T(8,128)S(1)}, u32[]{:S(2)}, u32[]{:S(2)}) collective-permute-start(f32[5,2,16,128]{3,2,1,0:T(8,128)S(1)} %get-tuple-element.91), channel_id=1, source_target_pairs={{0,32},{32,0},{64,96},{96,64},{128,160},{160,128},{192,224},{224,1... | collective-permute-start | bytes 245768 | tf_op jit(solution)/shard_map/ppermute | solution.py:337
  39.0 7.1 %collective-permute-start.19 = (f32[5,2,16,128]{3,2,1,0:T(8,128)S(1)}, f32[5,2,16,128]{3,2,1,0:T(8,128)S(1)}, u32[]{:S(2)}, u32[]{:S(2)}) collective-permute-start(f32[5,2,16,128]{3,2,1,0:T(8,128)S(1)} %get-tuple-element.93), channel_id=1, source_target_pairs={{0,224},{32,64},{64,32},{96,128},{128,96},{160,192},{192,160},{224... | collective-permute-start | bytes 245768 | tf_op jit(solution)/shard_map/ppermute | solution.py:337
  40.8 5.3 %collective-permute-start.21 = (f32[88,128]{1,0:T(8,128)S(1)}, f32[88,128]{1,0:T(8,128)S(1)}, u32[]{:S(2)}, u32[]{:S(2)}) collective-permute-start(f32[88,128]{1,0:T(8,128)S(1)} %get-tuple-element.95), channel_id=1, source_target_pairs={{0,3},{1,2},{2,1},{3,0},{4,7},{5,6},{6,5},{7,4},{8,11},{9,10},{10,... | collective-permute-start | bytes 135176 | tf_op jit(solution)/shard_map/ppermute | solution.py:337
  42.4 5.0 %collective-permute-start.22 = (f32[5,2,8,128]{3,2,1,0:T(8,128)S(1)}, f32[5,2,8,128]{3,2,1,0:T(8,128)S(1)}, u32[]{:S(2)}, u32[]{:S(2)}) collective-permute-start(f32[5,2,8,128]{3,2,1,0:T(8,128)S(1)} %get-tuple-element.96), channel_id=1, source_target_pairs={{0,4},{4,0},{8,12},{12,8},{16,20},{20,16},{24,28},{28,24},{1,5},{5... | collective-permute-start | bytes 122888 | tf_op jit(solution)/shard_map/ppermute | solution.py:337
  42.6 4.9 %collective-permute-start.23 = (f32[5,2,8,128]{3,2,1,0:T(8,128)S(1)}, f32[5,2,8,128]{3,2,1,0:T(8,128)S(1)}, u32[]{:S(2)}, u32[]{:S(2)}) collective-permute-start(f32[5,2,8,128]{3,2,1,0:T(8,128)S(1)} %get-tuple-element.97), channel_id=1, source_target_pairs={{0,28},{4,8},{8,4},{12,16},{16,12},{20,24},{24,20},{28,0},{1,29},{... | collective-permute-start | bytes 122888 | tf_op jit(solution)/shard_map/ppermute | solution.py:337
  45.5 1.2 %collective-permute-start.20 = (f32[24,128]{1,0:T(8,128)S(1)}, f32[24,128]{1,0:T(8,128)S(1)}, u32[]{:S(2)}, u32[]{:S(2)}) collective-permute-start(f32[24,128]{1,0:T(8,128)S(1)} %get-tuple-element.94), channel_id=1, source_target_pairs={{0,1},{1,0},{2,3},{3,2},{4,5},{5,4},{6,7},{7,6},{8,9},{9,8},{10,11... | collective-permute-start | bytes 36872 | tf_op jit(solution)/shard_map/ppermute | solution.py:337

commit v12 on v11

--- a/solution.py
+++ b/solution.py
@@ -12,6 +12,7 @@
 ROWS = NX * NY
 FAR_ROWS = 88
 OUTER_ROWS = (0, 1, NY - 2, NY - 1)
+SPAN_METRICS = ((4, NY - 1), (6, NY - 2), (6, NY - 1), (5, 0), (7, 0), (7, 1))
 F32 = jnp.float32
 VMEM = pl.BlockSpec(memory_space=pltpu.VMEM)
 
@@ -83,7 +84,7 @@
         out_ref[8 * i : 8 * i + 8, :] = v + lane_roll(v, 64)
 
 
-def emit_sends(psi_ref, metric_ref, packed_metric, groups, sends, rows=None, loads=()):
+def emit_sends(psi_ref, metric_ref, packed_metric, groups, sends, rows=None, loads=(), metric_rows=None):
     x0, x1, y0, y1, zz, far = sends
     lane = iota((8, NZ), 1)
     same, after, before = (packed_metric[8 * i : 8 * i + 8, :] for i in range(3))
@@ -96,8 +97,10 @@
     for copy in loads[:1]:
         copy.wait()
     even = is_even("gy")
-    m4, m6a, m6b = metric_ref[4, edge_rows(15), :], metric_ref[6, edge_rows(14), :], metric_ref[6, edge_rows(15), :]
-    m5, m7a, m7b = metric_ref[5, edge_rows(0), :], metric_ref[7, edge_rows(0), :], metric_ref[7, edge_rows(1), :]
+    if metric_rows is None:
+        m4, m6a, m6b, m5, m7a, m7b = (metric_ref[o, edge_rows(y), :] for o, y in SPAN_METRICS)
+    else:
+        m4, m6a, m6b, m5, m7a, m7b = (metric_rows[i] for i in range(6))
     for e in range(FIELDS):
         q0, q1, q14, q15 = rows[e] if rows else [psi_ref[e, edge_rows(y), :] for y in OUTER_ROWS]
         high = (m4 * q15 + m6a * q14, m6b * q15)
@@ -154,7 +157,7 @@
     return out
 
 
-def window_body(psi_ref, metric_ref, diag_ref, rhs_ref, jac_ref, x0, x1, z0, z1, base_ref):
+def window_body(psi_ref, metric_ref, diag_ref, rhs_ref, jac_ref, x0, x1, z0, z1, base_ref, rows_ref):
     lane8 = iota((8, NZ), 1)
     edge = (lane8 < 2) | (lane8 >= NZ - 2)
     walls = []
@@ -194,19 +197,24 @@
         for f, c in enumerate(coupled(jac_ref, s, zs)):
             q = psi_ref[f, s, :]
             base_ref[f, s, :] = q + (rhs_ref[f, s, :] - d * q + c) * scale
-
-
-def rows_body(jac_ref, diag_ref, jac_rows, scale_rows, wide):
+    for f in range(FIELDS):
+        for i, y in enumerate(OUTER_ROWS):
+            rows_ref[4 * f + i] = base_ref[f, edge_rows(y), :]
+
+
+def rows_body(jac_ref, diag_ref, metric_ref, jac_rows, metric_rows, wide):
+    for i, (o, y) in enumerate(SPAN_METRICS):
+        metric_rows[i] = metric_ref[o, edge_rows(y), :]
     for k in range(FIELDS * FIELDS):
         for x in range(NX):
             wide[k, slab(x), :] = jac_ref[k, slab(x), :].astype(F32)
     for i, y in enumerate(OUTER_ROWS):
-        scale_rows[i] = OMEGA / diag_ref[edge_rows(y), :]
+        scale = OMEGA / diag_ref[edge_rows(y), :]
         for k in range(FIELDS * FIELDS):
-            jac_rows[4 * k + i] = wide[k, edge_rows(y), :]
-
-
-def finish(base_ref, y0, y1, jac_rows, scale_rows, new_ref, in_place=True, out=()):
+            jac_rows[4 * k + i] = wide[k, edge_rows(y), :] * scale
+
+
+def finish(base_ref, base_rows, y0, y1, jac_rows, new_ref, in_place=True, out=()):
     zs = []
     for e in range(FIELDS):
         sides = [from_sides("gy", y0[e, r], y1[e, r]) for r in range(2)]
@@ -217,10 +225,10 @@
             new_ref[f] = base_ref[f]
         mine = []
         for i, y in enumerate(OUTER_ROWS):
-            c = jac_rows[4 * f + i] * zs[0][i]
+            c = base_rows[4 * f + i] + jac_rows[4 * f + i] * zs[0][i]
             for e in range(1, FIELDS):
                 c = c + jac_rows[4 * (FIELDS * e + f) + i] * zs[e][i]
-            mine.append(base_ref[f, edge_rows(y), :] + c * scale_rows[i])
+            mine.append(c)
         for i, y in enumerate(OUTER_ROWS):
             new_ref[f, edge_rows(y), :] = mine[i]
         if out:
@@ -229,10 +237,11 @@
     return rows
 
 
-def middle_body(base_ref, y_even, y_odd, jac_rows, scale_rows, metric_ref, packed_metric,
+def middle_body(base_ref, base_rows, y_even, y_odd, jac_rows, metric_rows, metric_ref, packed_metric,
                 new_ref, x0, x1, y0, y1, zz, far):
-    rows = finish(base_ref, y_even, y_odd, jac_rows, scale_rows, new_ref)
-    emit_sends(new_ref, metric_ref, packed_metric, pack_edges(new_ref), (x0, x1, y0, y1, zz, far), rows)
+    rows = finish(base_ref, base_rows, y_even, y_odd, jac_rows, new_ref)
+    sends = (x0, x1, y0, y1, zz, far)
+    emit_sends(new_ref, metric_ref, packed_metric, pack_edges(new_ref), sends, rows, metric_rows=metric_rows)
 
 
 def wall_body(coef_ref, ids_ref, weight_ref, coef_out, weight_out, hot_out, low_out):
@@ -269,10 +278,10 @@
         hot_out[:, NZ * s : NZ * s + NZ] = jnp.where(hit, 1.0, 0.0).astype(jnp.bfloat16)
 
 
-def last_body(base_ref, y_even, y_odd, jac_rows, scale_rows, coef_ref, weight_ref, hot_ref, low_ref,
+def last_body(base_ref, base_rows, y_even, y_odd, jac_rows, coef_ref, weight_ref, hot_ref, low_ref,
               out_hbm, slots_ref, new_ref, high_part, low_part, sems):
     copies = [pltpu.make_async_copy(new_ref.at[f], out_hbm.at[f], sems.at[f]) for f in range(FIELDS)]
-    finish(base_ref, y_even, y_odd, jac_rows, scale_rows, new_ref, in_place=False, out=copies)
+    finish(base_ref, base_rows, y_even, y_odd, jac_rows, new_ref, in_place=False, out=copies)
     lane = iota((8, NZ), 1)
     groups = pack_edges(new_ref)
     low = low_ref[...]
@@ -359,22 +368,24 @@
         (wall_coef.reshape(30 * NX, NY), ffd_ids.reshape(4 * NX, NY), ffd_weight.reshape(4 * NX, NY)),
         [((3, 24, NZ), F32), ((8, NZ), F32), ((256, 512), jnp.bfloat16), ((8, NZ), jnp.int32)],
     )
-    rows = run(
-        rows_body, (jac, diag), [((4 * FIELDS * FIELDS, NX, NZ), F32), ((4, NX, NZ), F32)],
+    jac_rows, metric_rows = run(
+        rows_body, (jac, diag, metric), [((4 * FIELDS * FIELDS, NX, NZ), F32), ((6, NX, NZ), F32)],
         scratch=[((FIELDS * FIELDS, ROWS, NZ), F32)],
     )
     for step in range(SWEEPS):
         x_even, x_odd, y_even, y_odd, z_even, z_odd = exchange(sends)
-        (base,) = run(window_body, (psi, metric, diag, rhs, jac, x_even, x_odd, z_even, z_odd), [FIELD])
+        base, rows = run(
+            window_body, (psi, metric, diag, rhs, jac, x_even, x_odd, z_even, z_odd), [FIELD, ((4 * FIELDS, NX, NZ), F32)]
+        )
         if step == 1:
             base, wall = lax.optimization_barrier((base, wall))
         if step < SWEEPS - 1:
             psi, *sends = run(
-                middle_body, (base, y_even, y_odd, *rows, metric, packed_metric), [FIELD] + SENDS, aliases={0: 0}
+                middle_body, (base, rows, y_even, y_odd, jac_rows, metric_rows, metric, packed_metric), [FIELD] + SENDS, aliases={0: 0}
             )
         else:
             psi, slots = run(
-                last_body, (base, y_even, y_odd, *rows, *wall), [FIELD, ((256, 48), F32)],
+                last_body, (base, rows, y_even, y_odd, jac_rows, *wall), [FIELD, ((256, 48), F32)],
                 scratch=[FIELD, ((48, 512), jnp.bfloat16), ((48, 512), jnp.bfloat16)], sems=[(FIELDS,)], far_outs=(0,),
             )
     got = lax.all_to_all(slots.reshape(256, 1, 48), AXES, 0, 0).reshape(256, 48)

time: 71.5 us -> 71.3 us (level)
  transfers between devices with their start and end apart: 24 -> 24, of which waited for: 7 -> 6; matrix products, arithmetic and copies ran while one was open for 0% -> 0% of each run, Pallas kernels for 5% -> 6%
where the time goes in v12:
time: 71.3 us; the launch traced here: 71.1 us
  starting transfers between devices  36.3 us (51%)
  blocking collectives  22.2 us (31%)
  Pallas kernels  8.18 us (11%)
  waiting for transfers between devices  3.55 us (5%)
  between operations  0.87 us (1%)
    ppermute x24, starting transfers between devices, swap(): return lax.ppermute(v, axis, pairs(lax.axis_size(axis), odd))  36.3 us
    all_to_all x1, blocking collectives, local(): got = lax.all_to_all(slots.reshape(256, 1, 48), AXES, 0, 0).reshape(256, 48)  22.2 us
    pallas_call x12, Pallas kernels, run(): pl.pallas_call(body, out_shape=[jax.ShapeDtypeStruct(s, d) for s, d in ou...  8.18 us
    ppermute x24, waiting for transfers between devices, swap(): return lax.ppermute(v, axis, pairs(lax.axis_size(axis), odd))  3.55 us
  transfers between devices with their start and end apart: 24, of which 6 were waited for; matrix products, arithmetic and copies ran while one was open for 0% of the time, Pallas kernels for 6%

profile of v12, /device:TPU:1, one launch (start us, length us, event | category | flops | bytes accessed | tf_op | source)
XLA Modules:
  0.0 71.1 jit_solution(4306446230271744672)
XLA Ops:
  0.7 1.6 %shard_map.95 = (f32[5,2,16,128]{3,2,1,0:T(8,128)S(1)}, f32[5,2,16,128]{3,2,1,0:T(8,128)S(1)}, f32[5,2,8,128]{3,2,1,0:T(8,128)S(1)}, f32[5,2,8,128]{3,2,1,0:T(8,...) custom-call(f32[5,128,128]{2,1,0:T(8,128)} %bitcast.33, ...), custom_call_target="tpu_custom_call" | custom-call | flops 1000000 | bytes 1000000 | tf_op jit(solution)/shard_map/pallas_call | solution.py:323
  2.3 2.1 %collective-permute-start = (f32[5,2,16,128]{3,2,1,0:T(8,128)S(1)}, f32[5,2,16,128]{3,2,1,0:T(8,128)S(1)}, u32[]{:S(2)}, u32[]{:S(2)}) collective-permute-start(f32[5,2,16,128]{3,2,1,0:T(8,128)S(1)} %get-tuple-element.64), channel_id=1, source_target_pairs={{0,32},{32,0},{64,96},{96,64},{128,160},{160,128},{192,224},{224,1... | collective-permute-start | bytes 245768 | tf_op jit(solution)/shard_map/ppermute | solution.py:346
  4.4 2.7 %collective-permute-start.1 = (f32[5,2,16,128]{3,2,1,0:T(8,128)S(1)}, f32[5,2,16,128]{3,2,1,0:T(8,128)S(1)}, u32[]{:S(2)}, u32[]{:S(2)}) collective-permute-start(f32[5,2,16,128]{3,2,1,0:T(8,128)S(1)} %get-tuple-element.66), channel_id=1, source_target_pairs={{0,224},{32,64},{64,32},{96,128},{128,96},{160,192},{192,160},{224... | collective-permute-start | bytes 245768 | tf_op jit(solution)/shard_map/ppermute | solution.py:346
  7.1 3.9 %collective-permute-start.3 = (f32[88,128]{1,0:T(8,128)S(1)}, f32[88,128]{1,0:T(8,128)S(1)}, u32[]{:S(2)}, u32[]{:S(2)}) collective-permute-start(f32[88,128]{1,0:T(8,128)S(1)} %get-tuple-element.68), channel_id=1, source_target_pairs={{0,3},{1,2},{2,1},{3,0},{4,7},{5,6},{6,5},{7,4},{8,11},{9,10},{10,... | collective-permute-start | bytes 135176 | tf_op jit(solution)/shard_map/ppermute | solution.py:346
  11.0 1.6 %collective-permute-start.4 = (f32[5,2,8,128]{3,2,1,0:T(8,128)S(1)}, f32[5,2,8,128]{3,2,1,0:T(8,128)S(1)}, u32[]{:S(2)}, u32[]{:S(2)}) collective-permute-start(f32[5,2,8,128]{3,2,1,0:T(8,128)S(1)} %get-tuple-element.71), channel_id=1, source_target_pairs={{0,4},{4,0},{8,12},{12,8},{16,20},{20,16},{24,28},{28,24},{1,5},{5... | collective-permute-start | bytes 122888 | tf_op jit(solution)/shard_map/ppermute | solution.py:346
  12.6 4.7 %collective-permute-start.5 = (f32[5,2,8,128]{3,2,1,0:T(8,128)S(1)}, f32[5,2,8,128]{3,2,1,0:T(8,128)S(1)}, u32[]{:S(2)}, u32[]{:S(2)}) collective-permute-start(f32[5,2,8,128]{3,2,1,0:T(8,128)S(1)} %get-tuple-element.72), channel_id=1, source_target_pairs={{0,28},{4,8},{8,4},{12,16},{16,12},{20,24},{24,20},{28,0},{1,29},{... | collective-permute-start | bytes 122888 | tf_op jit(solution)/shard_map/ppermute | solution.py:346
  17.3 0.0 collective-permute-done.x0
  17.3 0.0 collective-permute-start.2
  17.3 0.0 copy-start.1
  17.3 0.3 shard_map.97
  17.6 0.0 collective-permute-done.3.z1
  17.6 0.0 collective-permute-done.1.x1
  17.6 0.8 %collective-permute-done.2.z0 = f32[24,128]{1,0:T(8,128)S(1)} collective-permute-done((f32[24,128]{1,0:T(8,128)S(1)}, f32[24,128]{1,0:T(8,128)S(1)}, u32[]{:S(2)}, u32[]{:S(2)}) %collective-permute-start.2) | collective-permute-done | bytes 12320 | tf_op jit(solution)/shard_map/ppermute | solution.py:346
  18.5 0.8 %shard_map.96 = (f32[5,128,128]{2,1,0:T(8,128)S(1)}, f32[20,8,128]{2,1,0:T(8,128)S(1)}) custom-call(f32[5,128,128]{2,1,0:T(8,128)S(1)} %get-tuple-element.61.psi_ref, f32[12,128,128]{2,1,0:T(8,128)S(1)} %get-tuple-element.62.metric_ref, f32[128,128]{1,0:T(8,128)S(1)} %bitcast.23, f32[5,128,128]{2,1,0:T(8,128)S(1)} %bitcast.18, ...), custom_call_target="tpu_custom_call" | custom-call | flops 1000000 | bytes 1000000 | tf_op jit(solution)/shard_map/pallas_call | solution.py:323
  19.3 0.0 collective-permute-done.4.y_even
  19.3 0.0 collective-permute-done.5.y_odd
  19.3 0.0 copy-start.3
  19.3 0.0 copy-start.5
  19.3 0.3 shard_map.98
  19.7 0.0 collective-permute-start.6
  19.7 1.6 %collective-permute-start.7 = (f32[5,2,16,128]{3,2,1,0:T(8,128)S(1)}, f32[5,2,16,128]{3,2,1,0:T(8,128)S(1)}, u32[]{:S(2)}, u32[]{:S(2)}) collective-permute-start(f32[5,2,16,128]{3,2,1,0:T(8,128)S(1)} %get-tuple-element.80), channel_id=1, source_target_pairs={{0,224},{32,64},{64,32},{96,128},{128,96},{160,192},{192,160},{224... | collective-permute-start | bytes 245768 | tf_op jit(solution)/shard_map/ppermute | solution.py:346
  21.3 1.2 %collective-permute-start.9 = (f32[88,128]{1,0:T(8,128)S(1)}, f32[88,128]{1,0:T(8,128)S(1)}, u32[]{:S(2)}, u32[]{:S(2)}) collective-permute-start(f32[88,128]{1,0:T(8,128)S(1)} %get-tuple-element.82), channel_id=1, source_target_pairs={{0,3},{1,2},{2,1},{3,0},{4,7},{5,6},{6,5},{7,4},{8,11},{9,10},{10,... | collective-permute-start | bytes 135176 | tf_op jit(solution)/shard_map/ppermute | solution.py:346
  22.5 0.0 collective-permute-start.10
  22.5 3.2 %collective-permute-start.11 = (f32[5,2,8,128]{3,2,1,0:T(8,128)S(1)}, f32[5,2,8,128]{3,2,1,0:T(8,128)S(1)}, u32[]{:S(2)}, u32[]{:S(2)}) collective-permute-start(f32[5,2,8,128]{3,2,1,0:T(8,128)S(1)} %get-tuple-element.91), channel_id=1, source_target_pairs={{0,28},{4,8},{8,4},{12,16},{16,12},{20,24},{24,20},{28,0},{1,29},{... | collective-permute-start | bytes 122888 | tf_op jit(solution)/shard_map/ppermute | solution.py:346
  25.7 0.0 collective-permute-done.6.x0
  25.7 0.0 collective-permute-start.8
  25.7 0.6 shard_map.100
  26.3 0.6 collective-permute-done.9.z1
  26.9 0.0 collective-permute-done.7.x1
  26.9 0.0 collective-permute-done.8.z0
  26.9 0.8 %shard_map.99 = (f32[5,128,128]{2,1,0:T(8,128)S(1)}, f32[20,8,128]{2,1,0:T(8,128)S(1)}) custom-call(f32[5,128,128]{2,1,0:T(8,128)S(1)} %get-tuple-element.76.psi_ref, f32[12,128,128]{2,1,0:T(8,128)S(1)} %get-tuple-element.62.metric_ref, f32[128,128]{1,0:T(8,128)S(1)} %bitcast.24, f32[5,128,128]{2,1,0:T(8,128)S(1)} %bitcast.19, ...), custom_call_target="tpu_custom_call" | custom-call | flops 1000000 | bytes 1000000 | tf_op jit(solution)/shard_map/pallas_call | solution.py:323
  27.7 0.0 collective-permute-done.10.y_even
  27.7 0.0 collective-permute-done.11.y_odd
  27.7 0.3 shard_map.101
  28.1 0.1 collective-permute-start.12
  28.2 2.1 %collective-permute-start.13 = (f32[5,2,16,128]{3,2,1,0:T(8,128)S(1)}, f32[5,2,16,128]{3,2,1,0:T(8,128)S(1)}, u32[]{:S(2)}, u32[]{:S(2)}) collective-permute-start(f32[5,2,16,128]{3,2,1,0:T(8,128)S(1)} %get-tuple-element.96), channel_id=1, source_target_pairs={{0,224},{32,64},{64,32},{96,128},{128,96},{160,192},{192,160},{224... | collective-permute-start | bytes 245768 | tf_op jit(solution)/shard_map/ppermute | solution.py:346
  30.3 3.1 %collective-permute-start.15 = (f32[88,128]{1,0:T(8,128)S(1)}, f32[88,128]{1,0:T(8,128)S(1)}, u32[]{:S(2)}, u32[]{:S(2)}) collective-permute-start(f32[88,128]{1,0:T(8,128)S(1)} %get-tuple-element.98), channel_id=1, source_target_pairs={{0,3},{1,2},{2,1},{3,0},{4,7},{5,6},{6,5},{7,4},{8,11},{9,10},{10,... | collective-permute-start | bytes 135176 | tf_op jit(solution)/shard_map/ppermute | solution.py:346
  33.4 0.3 collective-permute-start.16
  33.7 2.8 %collective-permute-start.17 = (f32[5,2,8,128]{3,2,1,0:T(8,128)S(1)}, f32[5,2,8,128]{3,2,1,0:T(8,128)S(1)}, u32[]{:S(2)}, u32[]{:S(2)}) collective-permute-start(f32[5,2,8,128]{3,2,1,0:T(8,128)S(1)} %get-tuple-element.102), channel_id=1, source_target_pairs={{0,28},{4,8},{8,4},{12,16},{16,12},{20,24},{24,20},{28,0},{1,29},{... | collective-permute-start | bytes 122888 | tf_op jit(solution)/shard_map/ppermute | solution.py:346
  36.5 0.0 collective-permute-done.12.x0
  36.5 0.0 collective-permute-start.14
  36.5 0.3 collective-permute-done.15.z1
  36.8 0.0 collective-permute-done.13.x1
  36.8 0.9 %collective-permute-done.14.z0 = f32[24,128]{1,0:T(8,128)S(1)} collective-permute-done((f32[24,128]{1,0:T(8,128)S(1)}, f32[24,128]{1,0:T(8,128)S(1)}, u32[]{:S(2)}, u32[]{:S(2)}) %collective-permute-start.14) | collective-permute-done | bytes 12320 | tf_op jit(solution)/shard_map/ppermute | solution.py:346
  37.7 0.8 %shard_map.102 = (f32[5,128,128]{2,1,0:T(8,128)S(1)}, f32[20,8,128]{2,1,0:T(8,128)S(1)}) custom-call(f32[5,128,128]{2,1,0:T(8,128)S(1)} %get-tuple-element.92.psi_ref, f32[12,128,128]{2,1,0:T(8,128)S(1)} %get-tuple-element.62.metric_ref, f32[128,128]{1,0:T(8,128)S(1)} %bitcast.25, f32[5,128,128]{2,1,0:T(8,128)S(1)} %bitcast.20, ...), custom_call_target="tpu_custom_call" | custom-call | flops 1000000 | bytes 1000000 | tf_op jit(solution)/shard_map/pallas_call | solution.py:323
  38.4 0.0 collective-permute-done.16.y_even
  38.4 0.0 collective-permute-done.17.y_odd
  38.5 0.4 shard_map.103
  38.8 0.0 collective-permute-start.18
  38.9 1.9 %collective-permute-start.19 = (f32[5,2,16,128]{3,2,1,0:T(8,128)S(1)}, f32[5,2,16,128]{3,2,1,0:T(8,128)S(1)}, u32[]{:S(2)}, u32[]{:S(2)}) collective-permute-start(f32[5,2,16,128]{3,2,1,0:T(8,128)S(1)} %get-tuple-element.107), channel_id=1, source_target_pairs={{0,224},{32,64},{64,32},{96,128},{128,96},{160,192},{192,160},{224... | collective-permute-start | bytes 245768 | tf_op jit(solution)/shard_map/ppermute | solution.py:346
  40.7 1.5 %collective-permute-start.21 = (f32[88,128]{1,0:T(8,128)S(1)}, f32[88,128]{1,0:T(8,128)S(1)}, u32[]{:S(2)}, u32[]{:S(2)}) collective-permute-start(f32[88,128]{1,0:T(8,128)S(1)} %get-tuple-element.109), channel_id=1, source_target_pairs={{0,3},{1,2},{2,1},{3,0},{4,7},{5,6},{6,5},{7,4},{8,11},{9,10},{10,... | collective-permute-start | bytes 135176 | tf_op jit(solution)/shard_map/ppermute | solution.py:346
  42.2 0.4 collective-permute-start.22
  42.6 2.9 %collective-permute-start.23 = (f32[5,2,8,128]{3,2,1,0:T(8,128)S(1)}, f32[5,2,8,128]{3,2,1,0:T(8,128)S(1)}, u32[]{:S(2)}, u32[]{:S(2)}) collective-permute-start(f32[5,2,8,128]{3,2,1,0:T(8,128)S(1)} %get-tuple-element.113), channel_id=1, source_target_pairs={{0,28},{4,8},{8,4},{12,16},{16,12},{20,24},{24,20},{28,0},{1,29},{... | collective-permute-start | bytes 122888 | tf_op jit(solution)/shard_map/ppermute | solution.py:346
  45.4 0.0 collective-permute-done.18.x0
  45.4 0.3 collective-permute-start.20
  45.7 0.3 collective-permute-done.21.z1
  46.0 0.0 collective-permute-done.19.x1
  46.0 0.6 collective-permute-done.20.z0
  46.6 0.8 %shard_map.104 = (f32[5,128,128]{2,1,0:T(8,128)S(1)}, f32[20,8,128]{2,1,0:T(8,128)S(1)}) custom-call(f32[5,128,128]{2,1,0:T(8,128)S(1)} %get-tuple-element.103.psi_ref, f32[12,128,128]{2,1,0:T(8,128)S(1)} %get-tuple-element.62.metric_ref, f32[128,128]{1,0:T(8,128)S(1)} %bitcast.26, f32[5,128,128]{2,1,0:T(8,128)S(1)} %bitcast.21, ...), custom_call_target="tpu_custom_call" | custom-call | flops 1000000 | bytes 1000000 | tf_op jit(solution)/shard_map/pallas_call | solution.py:323
  47.4 0.0 collective-permute-done.22.y_even
  47.4 0.0 collective-permute-done.23.y_odd
  47.4 0.9 %shard_map.105 = (f32[5,128,128]{2,1,0:T(8,128)}, f32[256,48]{1,0:T(8,128)S(1)}) custom-call(f32[5,128,128]{2,1,0:T(8,128)S(1)} %get-tuple-element.110.base_ref, f32[20,8,128]{2,1,0:T(8,128)S(1)} %get-tuple-element.111.base_rows, f32[5,2,8,128]{3,2,1,0:T(8,128)S(1)} %collective-permute-done.22.y_even, f32[5,2,8,128]{3,2,1,0:T(8,128)S(1)} %collective-permute-done.23.y_odd, ...), custom_call_target="tpu_custom_call" | custom-call | flops 1000000 | bytes 1000000 | tf_op jit(solution)/shard_map/pallas_call | solution.py:323
  48.3 22.2 %all_to_all.5 = f32[256,1,48]{2,1,0:T(1,128)S(1)} all-to-all(f32[256,1,48]{2,1,0:T(1,128)S(1)} %bitcast.28), channel_id=1, replica_groups=mesh['gx'=8,'gy'=8,'wa'=4] {'gx','gy','wa'}, dimensions={0} | all-to-all | bytes 98304 | tf_op jit(solution)/shard_map/all_to_all | solution.py:391
  70.5 0.7 shard_map.106
  (9 shorter events, 0.0 us)
Async XLA Ops:
  0.6 16.7 %copy-start = (bf16[5,5,8,16,128]{4,3,2,1,0:T(8,128)(2,1)S(1)}, bf16[5,5,8,16,128]{4,3,2,1,0:T(8,128)(2,1)}, u32[]{:S(2)}) copy-start(bf16[5,5,8,16,128]{4,3,2,1,0:T(8,128)(2,1)} %param.12) | copy-start | bytes 2457604
  0.6 16.7 %copy-start.2 = (f32[8,16,128]{2,1,0:T(8,128)S(1)}, f32[8,16,128]{2,1,0:T(8,128)}, u32[]{:S(2)}) copy-start(f32[8,16,128]{2,1,0:T(8,128)} %param.10) | copy-start | bytes 196612
  2.3 15.0 %collective-permute-start = (f32[5,2,16,128]{3,2,1,0:T(8,128)S(1)}, f32[5,2,16,128]{3,2,1,0:T(8,128)S(1)}, u32[]{:S(2)}, u32[]{:S(2)}) collective-permute-start(f32[5,2,16,128]{3,2,1,0:T(8,128)S(1)} %get-tuple-element.64), channel_id=1, source_target_pairs={{0,32},{32,0},{64,96},{96,64},{128,160},{160,128},{192,224},{224,1... | collective-permute-start | bytes 245768 | tf_op jit(solution)/shard_map/ppermute | solution.py:346
  4.4 13.2 %collective-permute-start.1 = (f32[5,2,16,128]{3,2,1,0:T(8,128)S(1)}, f32[5,2,16,128]{3,2,1,0:T(8,128)S(1)}, u32[]{:S(2)}, u32[]{:S(2)}) collective-permute-start(f32[5,2,16,128]{3,2,1,0:T(8,128)S(1)} %get-tuple-element.66), channel_id=1, source_target_pairs={{0,224},{32,64},{64,32},{96,128},{128,96},{160,192},{192,160},{224... | collective-permute-start | bytes 245768 | tf_op jit(solution)/shard_map/ppermute | solution.py:346
  7.1 10.5 %collective-permute-start.3 = (f32[88,128]{1,0:T(8,128)S(1)}, f32[88,128]{1,0:T(8,128)S(1)}, u32[]{:S(2)}, u32[]{:S(2)}) collective-permute-start(f32[88,128]{1,0:T(8,128)S(1)} %get-tuple-element.68), channel_id=1, source_target_pairs={{0,3},{1,2},{2,1},{3,0},{4,7},{5,6},{6,5},{7,4},{8,11},{9,10},{10,... | collective-permute-start | bytes 135176 | tf_op jit(solution)/shard_map/ppermute | solution.py:346
  11.0 8.3 %collective-permute-start.4 = (f32[5,2,8,128]{3,2,1,0:T(8,128)S(1)}, f32[5,2,8,128]{3,2,1,0:T(8,128)S(1)}, u32[]{:S(2)}, u32[]{:S(2)}) collective-permute-start(f32[5,2,8,128]{3,2,1,0:T(8,128)S(1)} %get-tuple-element.71), channel_id=1, source_target_pairs={{0,4},{4,0},{8,12},{12,8},{16,20},{20,16},{24,28},{28,24},{1,5},{5... | collective-permute-start | bytes 122888 | tf_op jit(solution)/shard_map/ppermute | solution.py:346
  12.6 6.7 %collective-permute-start.5 = (f32[5,2,8,128]{3,2,1,0:T(8,128)S(1)}, f32[5,2,8,128]{3,2,1,0:T(8,128)S(1)}, u32[]{:S(2)}, u32[]{:S(2)}) collective-permute-start(f32[5,2,8,128]{3,2,1,0:T(8,128)S(1)} %get-tuple-element.72), channel_id=1, source_target_pairs={{0,28},{4,8},{8,4},{12,16},{16,12},{20,24},{24,20},{28,0},{1,29},{... | collective-permute-start | bytes 122888 | tf_op jit(solution)/shard_map/ppermute | solution.py:346
  17.3 1.2 %collective-permute-start.2 = (f32[24,128]{1,0:T(8,128)S(1)}, f32[24,128]{1,0:T(8,128)S(1)}, u32[]{:S(2)}, u32[]{:S(2)}) collective-permute-start(f32[24,128]{1,0:T(8,128)S(1)} %get-tuple-element.67), channel_id=1, source_target_pairs={{0,1},{1,0},{2,3},{3,2},{4,5},{5,4},{6,7},{7,6},{8,9},{9,8},{10,11... | collective-permute-start | bytes 36872 | tf_op jit(solution)/shard_map/ppermute | solution.py:346
  17.3 1.2 %copy-start.1 = (f32[5,8,16,128]{3,2,1,0:T(8,128)S(1)}, f32[5,8,16,128]{3,2,1,0:T(8,128)}, u32[]{:S(2)}) copy-start(f32[5,8,16,128]{3,2,1,0:T(8,128)} %param.9) | copy-start | bytes 983044
  19.3 6.4 %copy-start.3 = (f32[3,10,8,16]{3,2,1,0:T(8,128)S(1)}, f32[3,10,8,16]{3,2,1,0:T(8,128)}, u32[]{:S(2)}) copy-start(f32[3,10,8,16]{3,2,1,0:T(8,128)} %param.13) | copy-start | bytes 46084
  19.3 6.4 %copy-start.5 = (f32[4,8,16]{2,1,0:T(8,128)S(1)}, f32[4,8,16]{2,1,0:T(8,128)}, u32[]{:S(2)}) copy-start(f32[4,8,16]{2,1,0:T(8,128)} %param.15) | copy-start | bytes 6148
  19.6 6.1 %copy-start.4 = (s32[4,8,16]{2,1,0:T(8,128)S(1)}, s32[4,8,16]{2,1,0:T(8,128)}, u32[]{:S(2)}) copy-start(s32[4,8,16]{2,1,0:T(8,128)} %param.14) | copy-start | bytes 6148
  19.7 6.1 %collective-permute-start.6 = (f32[5,2,16,128]{3,2,1,0:T(8,128)S(1)}, f32[5,2,16,128]{3,2,1,0:T(8,128)S(1)}, u32[]{:S(2)}, u32[]{:S(2)}) collective-permute-start(f32[5,2,16,128]{3,2,1,0:T(8,128)S(1)} %get-tuple-element.78), channel_id=1, source_target_pairs={{0,32},{32,0},{64,96},{96,64},{128,160},{160,128},{192,224},{224,1... | collective-permute-start | bytes 245768 | tf_op jit(solution)/shard_map/ppermute | solution.py:346
  19.7 7.2 %collective-permute-start.7 = (f32[5,2,16,128]{3,2,1,0:T(8,128)S(1)}, f32[5,2,16,128]{3,2,1,0:T(8,128)S(1)}, u32[]{:S(2)}, u32[]{:S(2)}) collective-permute-start(f32[5,2,16,128]{3,2,1,0:T(8,128)S(1)} %get-tuple-element.80), channel_id=1, source_target_pairs={{0,224},{32,64},{64,32},{96,128},{128,96},{160,192},{192,160},{224... | collective-permute-start | bytes 245768 | tf_op jit(solution)/shard_map/ppermute | solution.py:346
  21.3 5.6 %collective-permute-start.9 = (f32[88,128]{1,0:T(8,128)S(1)}, f32[88,128]{1,0:T(8,128)S(1)}, u32[]{:S(2)}, u32[]{:S(2)}) collective-permute-start(f32[88,128]{1,0:T(8,128)S(1)} %get-tuple-element.82), channel_id=1, source_target_pairs={{0,3},{1,2},{2,1},{3,0},{4,7},{5,6},{6,5},{7,4},{8,11},{9,10},{10,... | collective-permute-start | bytes 135176 | tf_op jit(solution)/shard_map/ppermute | solution.py:346
  22.5 5.2 %collective-permute-start.10 = (f32[5,2,8,128]{3,2,1,0:T(8,128)S(1)}, f32[5,2,8,128]{3,2,1,0:T(8,128)S(1)}, u32[]{:S(2)}, u32[]{:S(2)}) collective-permute-start(f32[5,2,8,128]{3,2,1,0:T(8,128)S(1)} %get-tuple-element.90), channel_id=1, source_target_pairs={{0,4},{4,0},{8,12},{12,8},{16,20},{20,16},{24,28},{28,24},{1,5},{5... | collective-permute-start | bytes 122888 | tf_op jit(solution)/shard_map/ppermute | solution.py:346
  22.5 5.2 %collective-permute-start.11 = (f32[5,2,8,128]{3,2,1,0:T(8,128)S(1)}, f32[5,2,8,128]{3,2,1,0:T(8,128)S(1)}, u32[]{:S(2)}, u32[]{:S(2)}) collective-permute-start(f32[5,2,8,128]{3,2,1,0:T(8,128)S(1)} %get-tuple-element.91), channel_id=1, source_target_pairs={{0,28},{4,8},{8,4},{12,16},{16,12},{20,24},{24,20},{28,0},{1,29},{... | collective-permute-start | bytes 122888 | tf_op jit(solution)/shard_map/ppermute | solution.py:346
  25.7 1.2 %collective-permute-start.8 = (f32[24,128]{1,0:T(8,128)S(1)}, f32[24,128]{1,0:T(8,128)S(1)}, u32[]{:S(2)}, u32[]{:S(2)}) collective-permute-start(f32[24,128]{1,0:T(8,128)S(1)} %get-tuple-element.81), channel_id=1, source_target_pairs={{0,1},{1,0},{2,3},{3,2},{4,5},{5,4},{6,7},{7,6},{8,9},{9,8},{10,11... | collective-permute-start | bytes 36872 | tf_op jit(solution)/shard_map/ppermute | solution.py:346
  28.1 8.4 %collective-permute-start.12 = (f32[5,2,16,128]{3,2,1,0:T(8,128)S(1)}, f32[5,2,16,128]{3,2,1,0:T(8,128)S(1)}, u32[]{:S(2)}, u32[]{:S(2)}) collective-permute-start(f32[5,2,16,128]{3,2,1,0:T(8,128)S(1)} %get-tuple-element.94), channel_id=1, source_target_pairs={{0,32},{32,0},{64,96},{96,64},{128,160},{160,128},{192,224},{224,1... | collective-permute-start | bytes 245768 | tf_op jit(solution)/shard_map/ppermute | solution.py:346
  28.2 8.6 %collective-permute-start.13 = (f32[5,2,16,128]{3,2,1,0:T(8,128)S(1)}, f32[5,2,16,128]{3,2,1,0:T(8,128)S(1)}, u32[]{:S(2)}, u32[]{:S(2)}) collective-permute-start(f32[5,2,16,128]{3,2,1,0:T(8,128)S(1)} %get-tuple-element.96), channel_id=1, source_target_pairs={{0,224},{32,64},{64,32},{96,128},{128,96},{160,192},{192,160},{224... | collective-permute-start | bytes 245768 | tf_op jit(solution)/shard_map/ppermute | solution.py:346
  30.3 6.5 %collective-permute-start.15 = (f32[88,128]{1,0:T(8,128)S(1)}, f32[88,128]{1,0:T(8,128)S(1)}, u32[]{:S(2)}, u32[]{:S(2)}) collective-permute-start(f32[88,128]{1,0:T(8,128)S(1)} %get-tuple-element.98), channel_id=1, source_target_pairs={{0,3},{1,2},{2,1},{3,0},{4,7},{5,6},{6,5},{7,4},{8,11},{9,10},{10,... | collective-permute-start | bytes 135176 | tf_op jit(solution)/shard_map/ppermute | solution.py:346
  33.4 5.0 %collective-permute-start.16 = (f32[5,2,8,128]{3,2,1,0:T(8,128)S(1)}, f32[5,2,8,128]{3,2,1,0:T(8,128)S(1)}, u32[]{:S(2)}, u32[]{:S(2)}) collective-permute-start(f32[5,2,8,128]{3,2,1,0:T(8,128)S(1)} %get-tuple-element.101), channel_id=1, source_target_pairs={{0,4},{4,0},{8,12},{12,8},{16,20},{20,16},{24,28},{28,24},{1,5},{5... | collective-permute-start | bytes 122888 | tf_op jit(solution)/shard_map/ppermute | solution.py:346
  33.7 4.7 %collective-permute-start.17 = (f32[5,2,8,128]{3,2,1,0:T(8,128)S(1)}, f32[5,2,8,128]{3,2,1,0:T(8,128)S(1)}, u32[]{:S(2)}, u32[]{:S(2)}) collective-permute-start(f32[5,2,8,128]{3,2,1,0:T(8,128)S(1)} %get-tuple-element.102), channel_id=1, source_target_pairs={{0,28},{4,8},{8,4},{12,16},{16,12},{20,24},{24,20},{28,0},{1,29},{... | collective-permute-start | bytes 122888 | tf_op jit(solution)/shard_map/ppermute | solution.py:346
  36.5 1.2 %collective-permute-start.14 = (f32[24,128]{1,0:T(8,128)S(1)}, f32[24,128]{1,0:T(8,128)S(1)}, u32[]{:S(2)}, u32[]{:S(2)}) collective-permute-start(f32[24,128]{1,0:T(8,128)S(1)} %get-tuple-element.97), channel_id=1, source_target_pairs={{0,1},{1,0},{2,3},{3,2},{4,5},{5,4},{6,7},{7,6},{8,9},{9,8},{10,11... | collective-permute-start | bytes 36872 | tf_op jit(solution)/shard_map/ppermute | solution.py:346
  38.8 6.6 %collective-permute-start.18 = (f32[5,2,16,128]{3,2,1,0:T(8,128)S(1)}, f32[5,2,16,128]{3,2,1,0:T(8,128)S(1)}, u32[]{:S(2)}, u32[]{:S(2)}) collective-permute-start(f32[5,2,16,128]{3,2,1,0:T(8,128)S(1)} %get-tuple-element.105), channel_id=1, source_target_pairs={{0,32},{32,0},{64,96},{96,64},{128,160},{160,128},{192,224},{224,1... | collective-permute-start | bytes 245768 | tf_op jit(solution)/shard_map/ppermute | solution.py:346
  38.9 7.1 %collective-permute-start.19 = (f32[5,2,16,128]{3,2,1,0:T(8,128)S(1)}, f32[5,2,16,128]{3,2,1,0:T(8,128)S(1)}, u32[]{:S(2)}, u32[]{:S(2)}) collective-permute-start(f32[5,2,16,128]{3,2,1,0:T(8,128)S(1)} %get-tuple-element.107), channel_id=1, source_target_pairs={{0,224},{32,64},{64,32},{96,128},{128,96},{160,192},{192,160},{224... | collective-permute-start | bytes 245768 | tf_op jit(solution)/shard_map/ppermute | solution.py:346
  40.7 5.3 %collective-permute-start.21 = (f32[88,128]{1,0:T(8,128)S(1)}, f32[88,128]{1,0:T(8,128)S(1)}, u32[]{:S(2)}, u32[]{:S(2)}) collective-permute-start(f32[88,128]{1,0:T(8,128)S(1)} %get-tuple-element.109), channel_id=1, source_target_pairs={{0,3},{1,2},{2,1},{3,0},{4,7},{5,6},{6,5},{7,4},{8,11},{9,10},{10,... | collective-permute-start | bytes 135176 | tf_op jit(solution)/shard_map/ppermute | solution.py:346
  42.2 5.2 %collective-permute-start.22 = (f32[5,2,8,128]{3,2,1,0:T(8,128)S(1)}, f32[5,2,8,128]{3,2,1,0:T(8,128)S(1)}, u32[]{:S(2)}, u32[]{:S(2)}) collective-permute-start(f32[5,2,8,128]{3,2,1,0:T(8,128)S(1)} %get-tuple-element.112), channel_id=1, source_target_pairs={{0,4},{4,0},{8,12},{12,8},{16,20},{20,16},{24,28},{28,24},{1,5},{5... | collective-permute-start | bytes 122888 | tf_op jit(solution)/shard_map/ppermute | solution.py:346
  42.6 4.8 %collective-permute-start.23 = (f32[5,2,8,128]{3,2,1,0:T(8,128)S(1)}, f32[5,2,8,128]{3,2,1,0:T(8,128)S(1)}, u32[]{:S(2)}, u32[]{:S(2)}) collective-permute-start(f32[5,2,8,128]{3,2,1,0:T(8,128)S(1)} %get-tuple-element.113), channel_id=1, source_target_pairs={{0,28},{4,8},{8,4},{12,16},{16,12},{20,24},{24,20},{28,0},{1,29},{... | collective-permute-start | bytes 122888 | tf_op jit(solution)/shard_map/ppermute | solution.py:346
  45.4 1.2 %collective-permute-start.20 = (f32[24,128]{1,0:T(8,128)S(1)}, f32[24,128]{1,0:T(8,128)S(1)}, u32[]{:S(2)}, u32[]{:S(2)}) collective-permute-start(f32[24,128]{1,0:T(8,128)S(1)} %get-tuple-element.108), channel_id=1, source_target_pairs={{0,1},{1,0},{2,3},{3,2},{4,5},{5,4},{6,7},{7,6},{8,9},{9,8},{10,11... | collective-permute-start | bytes 36872 | tf_op jit(solution)/shard_map/ppermute | solution.py:346

commit v13 on v12

--- a/solution.py
+++ b/solution.py
@@ -71,15 +71,16 @@
 def pack_metric(metric_ref, out_ref):
     lane = iota((8, NZ), 1)
     same = jnp.zeros((8, NZ), F32)
-    after = jnp.zeros((8, NZ), F32)
-    before = jnp.zeros((8, NZ), F32)
+    near = jnp.zeros((8, NZ), F32)
     for x in range(NX):
         for t in range(2):
             j, rows = 4 * (2 * x + t), tile_rows(x, t)
             v = jnp.where(lane >= NZ - 2, metric_ref[10, rows, :], jnp.where(lane < 2, metric_ref[11, rows, :], 0.0))
             same = same + lane_roll(v, 2 + j)
-            after = after + lane_roll(jnp.where(lane == NZ - 1, metric_ref[8, rows, :], 0.0), 1 + j)
-            before = before + lane_roll(jnp.where(lane == 0, metric_ref[9, rows, :], 0.0), 3 + j)
+            v = jnp.where(lane == NZ - 1, metric_ref[8, rows, :], jnp.where(lane == 0, metric_ref[9, rows, :], 0.0))
+            near = near + lane_roll(v, 2 + j)
+    after = jnp.where(lane % 4 == 0, lane_roll(near, -1), 0.0)
+    before = jnp.where(lane % 4 == 3, lane_roll(near, 1), 0.0)
     for i, v in enumerate((same, after, before)):
         out_ref[8 * i : 8 * i + 8, :] = v + lane_roll(v, 64)
 
@@ -279,7 +280,7 @@
 
 
 def last_body(base_ref, base_rows, y_even, y_odd, jac_rows, coef_ref, weight_ref, hot_ref, low_ref,
-              out_hbm, slots_ref, new_ref, high_part, low_part, sems):
+              out_hbm, slots_ref, new_ref, parts, sems):
     copies = [pltpu.make_async_copy(new_ref.at[f], out_hbm.at[f], sems.at[f]) for f in range(FIELDS)]
     finish(base_ref, base_rows, y_even, y_odd, jac_rows, new_ref, in_place=False, out=copies)
     lane = iota((8, NZ), 1)
@@ -299,14 +300,12 @@
             here = point == jnp.broadcast_to(low[s : s + 1, :], (16, NZ))
             w = jnp.where(here, jnp.broadcast_to(v[s : s + 1, :], (16, NZ)), 0.0)
             top = w.astype(jnp.bfloat16)
-            at = (slice(16 * c, 16 * c + 16), slice(NZ * s, NZ * s + NZ))
-            high_part[at] = top
-            low_part[at] = (w - top.astype(F32)).astype(jnp.bfloat16)
-    hot = hot_ref[...]
-    dims = (((1,), (1,)), ((), ()))
-    slots_ref[...] = lax.dot_general(hot, high_part[...], dims, preferred_element_type=F32) + lax.dot_general(
-        hot, low_part[...], dims, preferred_element_type=F32
-    )
+            columns = slice(NZ * s, NZ * s + NZ)
+            parts[16 * c : 16 * c + 16, columns] = top
+            parts[NZ + 16 * c : NZ + 16 * c + 16, columns] = (w - top.astype(F32)).astype(jnp.bfloat16)
+    parts[48:NZ, :] = jnp.zeros((NZ - 48, 512), jnp.bfloat16)
+    both = lax.dot_general(hot_ref[...], parts[...], (((1,), (1,)), ((), ())), preferred_element_type=F32)
+    slots_ref[...] = both[:, :48] + both[:, NZ : NZ + 48]
     for copy in copies:
         copy.wait()
 
@@ -386,7 +385,7 @@
         else:
             psi, slots = run(
                 last_body, (base, rows, y_even, y_odd, jac_rows, *wall), [FIELD, ((256, 48), F32)],
-                scratch=[FIELD, ((48, 512), jnp.bfloat16), ((48, 512), jnp.bfloat16)], sems=[(FIELDS,)], far_outs=(0,),
+                scratch=[FIELD, ((NZ + 48, 512), jnp.bfloat16)], sems=[(FIELDS,)], far_outs=(0,),
             )
     got = lax.all_to_all(slots.reshape(256, 1, 48), AXES, 0, 0).reshape(256, 48)
     (grad,) = run(sum_body, (got,), [((3, 16), F32)])

time: 71.3 us -> 71.3 us (level)
  no operation moved by 1% of the time
where the time goes in v13:
time: 71.3 us; the launch traced here: 71.1 us
  starting transfers between devices  36.3 us (51%)
  blocking collectives  22.2 us (31%)
  Pallas kernels  8.2 us (12%)
  waiting for transfers between devices  3.54 us (5%)
  between operations  0.87 us (1%)
    ppermute x24, starting transfers between devices, swap(): return lax.ppermute(v, axis, pairs(lax.axis_size(axis), odd))  36.3 us
    all_to_all x1, blocking collectives, local(): got = lax.all_to_all(slots.reshape(256, 1, 48), AXES, 0, 0).reshape(256, 48)  22.2 us
    pallas_call x12, Pallas kernels, run(): pl.pallas_call(body, out_shape=[jax.ShapeDtypeStruct(s, d) for s, d in ou...  8.2 us
    ppermute x24, waiting for transfers between devices, swap(): return lax.ppermute(v, axis, pairs(lax.axis_size(axis), odd))  3.54 us
  transfers between devices with their start and end apart: 24, of which 6 were waited for; matrix products, arithmetic and copies ran while one was open for 0% of the time, Pallas kernels for 6%

profile of v13, /device:TPU:1, one launch (start us, length us, event | category | flops | bytes accessed | tf_op | source)
XLA Modules:
  0.0 71.1 jit_solution(18312781519611357335)
XLA Ops:
  0.7 1.7 %shard_map.95 = (f32[5,2,16,128]{3,2,1,0:T(8,128)S(1)}, f32[5,2,16,128]{3,2,1,0:T(8,128)S(1)}, f32[5,2,8,128]{3,2,1,0:T(8,128)S(1)}, f32[5,2,8,128]{3,2,1,0:T(8,...) custom-call(f32[5,128,128]{2,1,0:T(8,128)} %bitcast.33, ...), custom_call_target="tpu_custom_call" | custom-call | flops 1000000 | bytes 1000000 | tf_op jit(solution)/shard_map/pallas_call | solution.py:322
  2.3 2.1 %collective-permute-start = (f32[5,2,16,128]{3,2,1,0:T(8,128)S(1)}, f32[5,2,16,128]{3,2,1,0:T(8,128)S(1)}, u32[]{:S(2)}, u32[]{:S(2)}) collective-permute-start(f32[5,2,16,128]{3,2,1,0:T(8,128)S(1)} %get-tuple-element.64), channel_id=1, source_target_pairs={{0,32},{32,0},{64,96},{96,64},{128,160},{160,128},{192,224},{224,1... | collective-permute-start | bytes 245768 | tf_op jit(solution)/shard_map/ppermute | solution.py:345
  4.4 2.7 %collective-permute-start.1 = (f32[5,2,16,128]{3,2,1,0:T(8,128)S(1)}, f32[5,2,16,128]{3,2,1,0:T(8,128)S(1)}, u32[]{:S(2)}, u32[]{:S(2)}) collective-permute-start(f32[5,2,16,128]{3,2,1,0:T(8,128)S(1)} %get-tuple-element.66), channel_id=1, source_target_pairs={{0,224},{32,64},{64,32},{96,128},{128,96},{160,192},{192,160},{224... | collective-permute-start | bytes 245768 | tf_op jit(solution)/shard_map/ppermute | solution.py:345
  7.1 3.9 %collective-permute-start.3 = (f32[88,128]{1,0:T(8,128)S(1)}, f32[88,128]{1,0:T(8,128)S(1)}, u32[]{:S(2)}, u32[]{:S(2)}) collective-permute-start(f32[88,128]{1,0:T(8,128)S(1)} %get-tuple-element.68), channel_id=1, source_target_pairs={{0,3},{1,2},{2,1},{3,0},{4,7},{5,6},{6,5},{7,4},{8,11},{9,10},{10,... | collective-permute-start | bytes 135176 | tf_op jit(solution)/shard_map/ppermute | solution.py:345
  11.0 1.6 %collective-permute-start.4 = (f32[5,2,8,128]{3,2,1,0:T(8,128)S(1)}, f32[5,2,8,128]{3,2,1,0:T(8,128)S(1)}, u32[]{:S(2)}, u32[]{:S(2)}) collective-permute-start(f32[5,2,8,128]{3,2,1,0:T(8,128)S(1)} %get-tuple-element.71), channel_id=1, source_target_pairs={{0,4},{4,0},{8,12},{12,8},{16,20},{20,16},{24,28},{28,24},{1,5},{5... | collective-permute-start | bytes 122888 | tf_op jit(solution)/shard_map/ppermute | solution.py:345
  12.6 4.7 %collective-permute-start.5 = (f32[5,2,8,128]{3,2,1,0:T(8,128)S(1)}, f32[5,2,8,128]{3,2,1,0:T(8,128)S(1)}, u32[]{:S(2)}, u32[]{:S(2)}) collective-permute-start(f32[5,2,8,128]{3,2,1,0:T(8,128)S(1)} %get-tuple-element.72), channel_id=1, source_target_pairs={{0,28},{4,8},{8,4},{12,16},{16,12},{20,24},{24,20},{28,0},{1,29},{... | collective-permute-start | bytes 122888 | tf_op jit(solution)/shard_map/ppermute | solution.py:345
  17.3 0.0 collective-permute-done.x0
  17.3 0.0 collective-permute-start.2
  17.3 0.0 copy-start.1
  17.3 0.3 shard_map.97
  17.6 0.0 collective-permute-done.3.z1
  17.7 0.0 collective-permute-done.1.x1
  17.7 0.8 %collective-permute-done.2.z0 = f32[24,128]{1,0:T(8,128)S(1)} collective-permute-done((f32[24,128]{1,0:T(8,128)S(1)}, f32[24,128]{1,0:T(8,128)S(1)}, u32[]{:S(2)}, u32[]{:S(2)}) %collective-permute-start.2) | collective-permute-done | bytes 12320 | tf_op jit(solution)/shard_map/ppermute | solution.py:345
  18.5 0.8 %shard_map.96 = (f32[5,128,128]{2,1,0:T(8,128)S(1)}, f32[20,8,128]{2,1,0:T(8,128)S(1)}) custom-call(f32[5,128,128]{2,1,0:T(8,128)S(1)} %get-tuple-element.61.psi_ref, f32[12,128,128]{2,1,0:T(8,128)S(1)} %get-tuple-element.62.metric_ref, f32[128,128]{1,0:T(8,128)S(1)} %bitcast.23, f32[5,128,128]{2,1,0:T(8,128)S(1)} %bitcast.18, ...), custom_call_target="tpu_custom_call" | custom-call | flops 1000000 | bytes 1000000 | tf_op jit(solution)/shard_map/pallas_call | solution.py:322
  19.3 0.0 collective-permute-done.4.y_even
  19.3 0.0 collective-permute-done.5.y_odd
  19.3 0.0 copy-start.3
  19.3 0.0 copy-start.5
  19.3 0.3 shard_map.98
  19.7 0.0 collective-permute-start.6
  19.7 1.6 %collective-permute-start.7 = (f32[5,2,16,128]{3,2,1,0:T(8,128)S(1)}, f32[5,2,16,128]{3,2,1,0:T(8,128)S(1)}, u32[]{:S(2)}, u32[]{:S(2)}) collective-permute-start(f32[5,2,16,128]{3,2,1,0:T(8,128)S(1)} %get-tuple-element.80), channel_id=1, source_target_pairs={{0,224},{32,64},{64,32},{96,128},{128,96},{160,192},{192,160},{224... | collective-permute-start | bytes 245768 | tf_op jit(solution)/shard_map/ppermute | solution.py:345
  21.4 1.2 %collective-permute-start.9 = (f32[88,128]{1,0:T(8,128)S(1)}, f32[88,128]{1,0:T(8,128)S(1)}, u32[]{:S(2)}, u32[]{:S(2)}) collective-permute-start(f32[88,128]{1,0:T(8,128)S(1)} %get-tuple-element.82), channel_id=1, source_target_pairs={{0,3},{1,2},{2,1},{3,0},{4,7},{5,6},{6,5},{7,4},{8,11},{9,10},{10,... | collective-permute-start | bytes 135176 | tf_op jit(solution)/shard_map/ppermute | solution.py:345
  22.5 0.0 collective-permute-start.10
  22.5 3.2 %collective-permute-start.11 = (f32[5,2,8,128]{3,2,1,0:T(8,128)S(1)}, f32[5,2,8,128]{3,2,1,0:T(8,128)S(1)}, u32[]{:S(2)}, u32[]{:S(2)}) collective-permute-start(f32[5,2,8,128]{3,2,1,0:T(8,128)S(1)} %get-tuple-element.91), channel_id=1, source_target_pairs={{0,28},{4,8},{8,4},{12,16},{16,12},{20,24},{24,20},{28,0},{1,29},{... | collective-permute-start | bytes 122888 | tf_op jit(solution)/shard_map/ppermute | solution.py:345
  25.7 0.0 collective-permute-done.6.x0
  25.7 0.0 collective-permute-start.8
  25.8 0.6 shard_map.100
  26.4 0.6 collective-permute-done.9.z1
  27.0 0.0 collective-permute-done.7.x1
  27.0 0.0 collective-permute-done.8.z0
  27.0 0.8 %shard_map.99 = (f32[5,128,128]{2,1,0:T(8,128)S(1)}, f32[20,8,128]{2,1,0:T(8,128)S(1)}) custom-call(f32[5,128,128]{2,1,0:T(8,128)S(1)} %get-tuple-element.76.psi_ref, f32[12,128,128]{2,1,0:T(8,128)S(1)} %get-tuple-element.62.metric_ref, f32[128,128]{1,0:T(8,128)S(1)} %bitcast.24, f32[5,128,128]{2,1,0:T(8,128)S(1)} %bitcast.19, ...), custom_call_target="tpu_custom_call" | custom-call | flops 1000000 | bytes 1000000 | tf_op jit(solution)/shard_map/pallas_call | solution.py:322
  27.7 0.0 collective-permute-done.10.y_even
  27.8 0.0 collective-permute-done.11.y_odd
  27.8 0.3 shard_map.101
  28.1 0.1 collective-permute-start.12
  28.2 2.1 %collective-permute-start.13 = (f32[5,2,16,128]{3,2,1,0:T(8,128)S(1)}, f32[5,2,16,128]{3,2,1,0:T(8,128)S(1)}, u32[]{:S(2)}, u32[]{:S(2)}) collective-permute-start(f32[5,2,16,128]{3,2,1,0:T(8,128)S(1)} %get-tuple-element.96), channel_id=1, source_target_pairs={{0,224},{32,64},{64,32},{96,128},{128,96},{160,192},{192,160},{224... | collective-permute-start | bytes 245768 | tf_op jit(solution)/shard_map/ppermute | solution.py:345
  30.3 3.1 %collective-permute-start.15 = (f32[88,128]{1,0:T(8,128)S(1)}, f32[88,128]{1,0:T(8,128)S(1)}, u32[]{:S(2)}, u32[]{:S(2)}) collective-permute-start(f32[88,128]{1,0:T(8,128)S(1)} %get-tuple-element.98), channel_id=1, source_target_pairs={{0,3},{1,2},{2,1},{3,0},{4,7},{5,6},{6,5},{7,4},{8,11},{9,10},{10,... | collective-permute-start | bytes 135176 | tf_op jit(solution)/shard_map/ppermute | solution.py:345
  33.5 0.3 collective-permute-start.16
  33.8 2.8 %collective-permute-start.17 = (f32[5,2,8,128]{3,2,1,0:T(8,128)S(1)}, f32[5,2,8,128]{3,2,1,0:T(8,128)S(1)}, u32[]{:S(2)}, u32[]{:S(2)}) collective-permute-start(f32[5,2,8,128]{3,2,1,0:T(8,128)S(1)} %get-tuple-element.102), channel_id=1, source_target_pairs={{0,28},{4,8},{8,4},{12,16},{16,12},{20,24},{24,20},{28,0},{1,29},{... | collective-permute-start | bytes 122888 | tf_op jit(solution)/shard_map/ppermute | solution.py:345
  36.5 0.0 collective-permute-done.12.x0
  36.5 0.0 collective-permute-start.14
  36.5 0.3 collective-permute-done.15.z1
  36.8 0.0 collective-permute-done.13.x1
  36.8 0.9 %collective-permute-done.14.z0 = f32[24,128]{1,0:T(8,128)S(1)} collective-permute-done((f32[24,128]{1,0:T(8,128)S(1)}, f32[24,128]{1,0:T(8,128)S(1)}, u32[]{:S(2)}, u32[]{:S(2)}) %collective-permute-start.14) | collective-permute-done | bytes 12320 | tf_op jit(solution)/shard_map/ppermute | solution.py:345
  37.7 0.8 %shard_map.102 = (f32[5,128,128]{2,1,0:T(8,128)S(1)}, f32[20,8,128]{2,1,0:T(8,128)S(1)}) custom-call(f32[5,128,128]{2,1,0:T(8,128)S(1)} %get-tuple-element.92.psi_ref, f32[12,128,128]{2,1,0:T(8,128)S(1)} %get-tuple-element.62.metric_ref, f32[128,128]{1,0:T(8,128)S(1)} %bitcast.25, f32[5,128,128]{2,1,0:T(8,128)S(1)} %bitcast.20, ...), custom_call_target="tpu_custom_call" | custom-call | flops 1000000 | bytes 1000000 | tf_op jit(solution)/shard_map/pallas_call | solution.py:322
  38.5 0.0 collective-permute-done.16.y_even
  38.5 0.0 collective-permute-done.17.y_odd
  38.5 0.4 shard_map.103
  38.9 0.0 collective-permute-start.18
  38.9 1.9 %collective-permute-start.19 = (f32[5,2,16,128]{3,2,1,0:T(8,128)S(1)}, f32[5,2,16,128]{3,2,1,0:T(8,128)S(1)}, u32[]{:S(2)}, u32[]{:S(2)}) collective-permute-start(f32[5,2,16,128]{3,2,1,0:T(8,128)S(1)} %get-tuple-element.107), channel_id=1, source_target_pairs={{0,224},{32,64},{64,32},{96,128},{128,96},{160,192},{192,160},{224... | collective-permute-start | bytes 245768 | tf_op jit(solution)/shard_map/ppermute | solution.py:345
  40.8 1.5 %collective-permute-start.21 = (f32[88,128]{1,0:T(8,128)S(1)}, f32[88,128]{1,0:T(8,128)S(1)}, u32[]{:S(2)}, u32[]{:S(2)}) collective-permute-start(f32[88,128]{1,0:T(8,128)S(1)} %get-tuple-element.109), channel_id=1, source_target_pairs={{0,3},{1,2},{2,1},{3,0},{4,7},{5,6},{6,5},{7,4},{8,11},{9,10},{10,... | collective-permute-start | bytes 135176 | tf_op jit(solution)/shard_map/ppermute | solution.py:345
  42.2 0.4 collective-permute-start.22
  42.6 2.9 %collective-permute-start.23 = (f32[5,2,8,128]{3,2,1,0:T(8,128)S(1)}, f32[5,2,8,128]{3,2,1,0:T(8,128)S(1)}, u32[]{:S(2)}, u32[]{:S(2)}) collective-permute-start(f32[5,2,8,128]{3,2,1,0:T(8,128)S(1)} %get-tuple-element.113), channel_id=1, source_target_pairs={{0,28},{4,8},{8,4},{12,16},{16,12},{20,24},{24,20},{28,0},{1,29},{... | collective-permute-start | bytes 122888 | tf_op jit(solution)/shard_map/ppermute | solution.py:345
  45.5 0.0 collective-permute-done.18.x0
  45.5 0.3 collective-permute-start.20
  45.7 0.3 collective-permute-done.21.z1
  46.0 0.0 collective-permute-done.19.x1
  46.0 0.6 collective-permute-done.20.z0
  46.6 0.8 %shard_map.104 = (f32[5,128,128]{2,1,0:T(8,128)S(1)}, f32[20,8,128]{2,1,0:T(8,128)S(1)}) custom-call(f32[5,128,128]{2,1,0:T(8,128)S(1)} %get-tuple-element.103.psi_ref, f32[12,128,128]{2,1,0:T(8,128)S(1)} %get-tuple-element.62.metric_ref, f32[128,128]{1,0:T(8,128)S(1)} %bitcast.26, f32[5,128,128]{2,1,0:T(8,128)S(1)} %bitcast.21, ...), custom_call_target="tpu_custom_call" | custom-call | flops 1000000 | bytes 1000000 | tf_op jit(solution)/shard_map/pallas_call | solution.py:322
  47.4 0.0 collective-permute-done.22.y_even
  47.4 0.0 collective-permute-done.23.y_odd
  47.4 0.8 %shard_map.105 = (f32[5,128,128]{2,1,0:T(8,128)}, f32[256,48]{1,0:T(8,128)S(1)}) custom-call(f32[5,128,128]{2,1,0:T(8,128)S(1)} %get-tuple-element.110.base_ref, f32[20,8,128]{2,1,0:T(8,128)S(1)} %get-tuple-element.111.base_rows, f32[5,2,8,128]{3,2,1,0:T(8,128)S(1)} %collective-permute-done.22.y_even, f32[5,2,8,128]{3,2,1,0:T(8,128)S(1)} %collective-permute-done.23.y_odd, ...), custom_call_target="tpu_custom_call" | custom-call | flops 1000000 | bytes 1000000 | tf_op jit(solution)/shard_map/pallas_call | solution.py:322
  48.3 22.2 %all_to_all.5 = f32[256,1,48]{2,1,0:T(1,128)S(1)} all-to-all(f32[256,1,48]{2,1,0:T(1,128)S(1)} %bitcast.28), channel_id=1, replica_groups=mesh['gx'=8,'gy'=8,'wa'=4] {'gx','gy','wa'}, dimensions={0} | all-to-all | bytes 98304 | tf_op jit(solution)/shard_map/all_to_all | solution.py:390
  70.5 0.7 shard_map.106
  (9 shorter events, 0.0 us)
Async XLA Ops:
  0.6 16.7 %copy-start = (bf16[5,5,8,16,128]{4,3,2,1,0:T(8,128)(2,1)S(1)}, bf16[5,5,8,16,128]{4,3,2,1,0:T(8,128)(2,1)}, u32[]{:S(2)}) copy-start(bf16[5,5,8,16,128]{4,3,2,1,0:T(8,128)(2,1)} %param.12) | copy-start | bytes 2457604
  0.6 16.7 %copy-start.2 = (f32[8,16,128]{2,1,0:T(8,128)S(1)}, f32[8,16,128]{2,1,0:T(8,128)}, u32[]{:S(2)}) copy-start(f32[8,16,128]{2,1,0:T(8,128)} %param.10) | copy-start | bytes 196612
  2.3 15.0 %collective-permute-start = (f32[5,2,16,128]{3,2,1,0:T(8,128)S(1)}, f32[5,2,16,128]{3,2,1,0:T(8,128)S(1)}, u32[]{:S(2)}, u32[]{:S(2)}) collective-permute-start(f32[5,2,16,128]{3,2,1,0:T(8,128)S(1)} %get-tuple-element.64), channel_id=1, source_target_pairs={{0,32},{32,0},{64,96},{96,64},{128,160},{160,128},{192,224},{224,1... | collective-permute-start | bytes 245768 | tf_op jit(solution)/shard_map/ppermute | solution.py:345
  4.4 13.2 %collective-permute-start.1 = (f32[5,2,16,128]{3,2,1,0:T(8,128)S(1)}, f32[5,2,16,128]{3,2,1,0:T(8,128)S(1)}, u32[]{:S(2)}, u32[]{:S(2)}) collective-permute-start(f32[5,2,16,128]{3,2,1,0:T(8,128)S(1)} %get-tuple-element.66), channel_id=1, source_target_pairs={{0,224},{32,64},{64,32},{96,128},{128,96},{160,192},{192,160},{224... | collective-permute-start | bytes 245768 | tf_op jit(solution)/shard_map/ppermute | solution.py:345
  7.1 10.5 %collective-permute-start.3 = (f32[88,128]{1,0:T(8,128)S(1)}, f32[88,128]{1,0:T(8,128)S(1)}, u32[]{:S(2)}, u32[]{:S(2)}) collective-permute-start(f32[88,128]{1,0:T(8,128)S(1)} %get-tuple-element.68), channel_id=1, source_target_pairs={{0,3},{1,2},{2,1},{3,0},{4,7},{5,6},{6,5},{7,4},{8,11},{9,10},{10,... | collective-permute-start | bytes 135176 | tf_op jit(solution)/shard_map/ppermute | solution.py:345
  11.0 8.3 %collective-permute-start.4 = (f32[5,2,8,128]{3,2,1,0:T(8,128)S(1)}, f32[5,2,8,128]{3,2,1,0:T(8,128)S(1)}, u32[]{:S(2)}, u32[]{:S(2)}) collective-permute-start(f32[5,2,8,128]{3,2,1,0:T(8,128)S(1)} %get-tuple-element.71), channel_id=1, source_target_pairs={{0,4},{4,0},{8,12},{12,8},{16,20},{20,16},{24,28},{28,24},{1,5},{5... | collective-permute-start | bytes 122888 | tf_op jit(solution)/shard_map/ppermute | solution.py:345
  12.6 6.7 %collective-permute-start.5 = (f32[5,2,8,128]{3,2,1,0:T(8,128)S(1)}, f32[5,2,8,128]{3,2,1,0:T(8,128)S(1)}, u32[]{:S(2)}, u32[]{:S(2)}) collective-permute-start(f32[5,2,8,128]{3,2,1,0:T(8,128)S(1)} %get-tuple-element.72), channel_id=1, source_target_pairs={{0,28},{4,8},{8,4},{12,16},{16,12},{20,24},{24,20},{28,0},{1,29},{... | collective-permute-start | bytes 122888 | tf_op jit(solution)/shard_map/ppermute | solution.py:345
  17.3 1.2 %collective-permute-start.2 = (f32[24,128]{1,0:T(8,128)S(1)}, f32[24,128]{1,0:T(8,128)S(1)}, u32[]{:S(2)}, u32[]{:S(2)}) collective-permute-start(f32[24,128]{1,0:T(8,128)S(1)} %get-tuple-element.67), channel_id=1, source_target_pairs={{0,1},{1,0},{2,3},{3,2},{4,5},{5,4},{6,7},{7,6},{8,9},{9,8},{10,11... | collective-permute-start | bytes 36872 | tf_op jit(solution)/shard_map/ppermute | solution.py:345
  17.3 1.2 %copy-start.1 = (f32[5,8,16,128]{3,2,1,0:T(8,128)S(1)}, f32[5,8,16,128]{3,2,1,0:T(8,128)}, u32[]{:S(2)}) copy-start(f32[5,8,16,128]{3,2,1,0:T(8,128)} %param.9) | copy-start | bytes 983044
  19.3 6.4 %copy-start.3 = (f32[3,10,8,16]{3,2,1,0:T(8,128)S(1)}, f32[3,10,8,16]{3,2,1,0:T(8,128)}, u32[]{:S(2)}) copy-start(f32[3,10,8,16]{3,2,1,0:T(8,128)} %param.13) | copy-start | bytes 46084
  19.3 6.4 %copy-start.5 = (f32[4,8,16]{2,1,0:T(8,128)S(1)}, f32[4,8,16]{2,1,0:T(8,128)}, u32[]{:S(2)}) copy-start(f32[4,8,16]{2,1,0:T(8,128)} %param.15) | copy-start | bytes 6148
  19.7 6.1 %copy-start.4 = (s32[4,8,16]{2,1,0:T(8,128)S(1)}, s32[4,8,16]{2,1,0:T(8,128)}, u32[]{:S(2)}) copy-start(s32[4,8,16]{2,1,0:T(8,128)} %param.14) | copy-start | bytes 6148
  19.7 6.1 %collective-permute-start.6 = (f32[5,2,16,128]{3,2,1,0:T(8,128)S(1)}, f32[5,2,16,128]{3,2,1,0:T(8,128)S(1)}, u32[]{:S(2)}, u32[]{:S(2)}) collective-permute-start(f32[5,2,16,128]{3,2,1,0:T(8,128)S(1)} %get-tuple-element.78), channel_id=1, source_target_pairs={{0,32},{32,0},{64,96},{96,64},{128,160},{160,128},{192,224},{224,1... | collective-permute-start | bytes 245768 | tf_op jit(solution)/shard_map/ppermute | solution.py:345
  19.7 7.2 %collective-permute-start.7 = (f32[5,2,16,128]{3,2,1,0:T(8,128)S(1)}, f32[5,2,16,128]{3,2,1,0:T(8,128)S(1)}, u32[]{:S(2)}, u32[]{:S(2)}) collective-permute-start(f32[5,2,16,128]{3,2,1,0:T(8,128)S(1)} %get-tuple-element.80), channel_id=1, source_target_pairs={{0,224},{32,64},{64,32},{96,128},{128,96},{160,192},{192,160},{224... | collective-permute-start | bytes 245768 | tf_op jit(solution)/shard_map/ppermute | solution.py:345
  21.4 5.6 %collective-permute-start.9 = (f32[88,128]{1,0:T(8,128)S(1)}, f32[88,128]{1,0:T(8,128)S(1)}, u32[]{:S(2)}, u32[]{:S(2)}) collective-permute-start(f32[88,128]{1,0:T(8,128)S(1)} %get-tuple-element.82), channel_id=1, source_target_pairs={{0,3},{1,2},{2,1},{3,0},{4,7},{5,6},{6,5},{7,4},{8,11},{9,10},{10,... | collective-permute-start | bytes 135176 | tf_op jit(solution)/shard_map/ppermute | solution.py:345
  22.5 5.2 %collective-permute-start.10 = (f32[5,2,8,128]{3,2,1,0:T(8,128)S(1)}, f32[5,2,8,128]{3,2,1,0:T(8,128)S(1)}, u32[]{:S(2)}, u32[]{:S(2)}) collective-permute-start(f32[5,2,8,128]{3,2,1,0:T(8,128)S(1)} %get-tuple-element.90), channel_id=1, source_target_pairs={{0,4},{4,0},{8,12},{12,8},{16,20},{20,16},{24,28},{28,24},{1,5},{5... | collective-permute-start | bytes 122888 | tf_op jit(solution)/shard_map/ppermute | solution.py:345
  22.5 5.2 %collective-permute-start.11 = (f32[5,2,8,128]{3,2,1,0:T(8,128)S(1)}, f32[5,2,8,128]{3,2,1,0:T(8,128)S(1)}, u32[]{:S(2)}, u32[]{:S(2)}) collective-permute-start(f32[5,2,8,128]{3,2,1,0:T(8,128)S(1)} %get-tuple-element.91), channel_id=1, source_target_pairs={{0,28},{4,8},{8,4},{12,16},{16,12},{20,24},{24,20},{28,0},{1,29},{... | collective-permute-start | bytes 122888 | tf_op jit(solution)/shard_map/ppermute | solution.py:345
  25.7 1.2 %collective-permute-start.8 = (f32[24,128]{1,0:T(8,128)S(1)}, f32[24,128]{1,0:T(8,128)S(1)}, u32[]{:S(2)}, u32[]{:S(2)}) collective-permute-start(f32[24,128]{1,0:T(8,128)S(1)} %get-tuple-element.81), channel_id=1, source_target_pairs={{0,1},{1,0},{2,3},{3,2},{4,5},{5,4},{6,7},{7,6},{8,9},{9,8},{10,11... | collective-permute-start | bytes 36872 | tf_op jit(solution)/shard_map/ppermute | solution.py:345
  28.1 8.4 %collective-permute-start.12 = (f32[5,2,16,128]{3,2,1,0:T(8,128)S(1)}, f32[5,2,16,128]{3,2,1,0:T(8,128)S(1)}, u32[]{:S(2)}, u32[]{:S(2)}) collective-permute-start(f32[5,2,16,128]{3,2,1,0:T(8,128)S(1)} %get-tuple-element.94), channel_id=1, source_target_pairs={{0,32},{32,0},{64,96},{96,64},{128,160},{160,128},{192,224},{224,1... | collective-permute-start | bytes 245768 | tf_op jit(solution)/shard_map/ppermute | solution.py:345
  28.2 8.6 %collective-permute-start.13 = (f32[5,2,16,128]{3,2,1,0:T(8,128)S(1)}, f32[5,2,16,128]{3,2,1,0:T(8,128)S(1)}, u32[]{:S(2)}, u32[]{:S(2)}) collective-permute-start(f32[5,2,16,128]{3,2,1,0:T(8,128)S(1)} %get-tuple-element.96), channel_id=1, source_target_pairs={{0,224},{32,64},{64,32},{96,128},{128,96},{160,192},{192,160},{224... | collective-permute-start | bytes 245768 | tf_op jit(solution)/shard_map/ppermute | solution.py:345
  30.3 6.5 %collective-permute-start.15 = (f32[88,128]{1,0:T(8,128)S(1)}, f32[88,128]{1,0:T(8,128)S(1)}, u32[]{:S(2)}, u32[]{:S(2)}) collective-permute-start(f32[88,128]{1,0:T(8,128)S(1)} %get-tuple-element.98), channel_id=1, source_target_pairs={{0,3},{1,2},{2,1},{3,0},{4,7},{5,6},{6,5},{7,4},{8,11},{9,10},{10,... | collective-permute-start | bytes 135176 | tf_op jit(solution)/shard_map/ppermute | solution.py:345
  33.5 5.0 %collective-permute-start.16 = (f32[5,2,8,128]{3,2,1,0:T(8,128)S(1)}, f32[5,2,8,128]{3,2,1,0:T(8,128)S(1)}, u32[]{:S(2)}, u32[]{:S(2)}) collective-permute-start(f32[5,2,8,128]{3,2,1,0:T(8,128)S(1)} %get-tuple-element.101), channel_id=1, source_target_pairs={{0,4},{4,0},{8,12},{12,8},{16,20},{20,16},{24,28},{28,24},{1,5},{5... | collective-permute-start | bytes 122888 | tf_op jit(solution)/shard_map/ppermute | solution.py:345
  33.8 4.7 %collective-permute-start.17 = (f32[5,2,8,128]{3,2,1,0:T(8,128)S(1)}, f32[5,2,8,128]{3,2,1,0:T(8,128)S(1)}, u32[]{:S(2)}, u32[]{:S(2)}) collective-permute-start(f32[5,2,8,128]{3,2,1,0:T(8,128)S(1)} %get-tuple-element.102), channel_id=1, source_target_pairs={{0,28},{4,8},{8,4},{12,16},{16,12},{20,24},{24,20},{28,0},{1,29},{... | collective-permute-start | bytes 122888 | tf_op jit(solution)/shard_map/ppermute | solution.py:345
  36.5 1.2 %collective-permute-start.14 = (f32[24,128]{1,0:T(8,128)S(1)}, f32[24,128]{1,0:T(8,128)S(1)}, u32[]{:S(2)}, u32[]{:S(2)}) collective-permute-start(f32[24,128]{1,0:T(8,128)S(1)} %get-tuple-element.97), channel_id=1, source_target_pairs={{0,1},{1,0},{2,3},{3,2},{4,5},{5,4},{6,7},{7,6},{8,9},{9,8},{10,11... | collective-permute-start | bytes 36872 | tf_op jit(solution)/shard_map/ppermute | solution.py:345
  38.9 6.6 %collective-permute-start.18 = (f32[5,2,16,128]{3,2,1,0:T(8,128)S(1)}, f32[5,2,16,128]{3,2,1,0:T(8,128)S(1)}, u32[]{:S(2)}, u32[]{:S(2)}) collective-permute-start(f32[5,2,16,128]{3,2,1,0:T(8,128)S(1)} %get-tuple-element.105), channel_id=1, source_target_pairs={{0,32},{32,0},{64,96},{96,64},{128,160},{160,128},{192,224},{224,1... | collective-permute-start | bytes 245768 | tf_op jit(solution)/shard_map/ppermute | solution.py:345
  38.9 7.1 %collective-permute-start.19 = (f32[5,2,16,128]{3,2,1,0:T(8,128)S(1)}, f32[5,2,16,128]{3,2,1,0:T(8,128)S(1)}, u32[]{:S(2)}, u32[]{:S(2)}) collective-permute-start(f32[5,2,16,128]{3,2,1,0:T(8,128)S(1)} %get-tuple-element.107), channel_id=1, source_target_pairs={{0,224},{32,64},{64,32},{96,128},{128,96},{160,192},{192,160},{224... | collective-permute-start | bytes 245768 | tf_op jit(solution)/shard_map/ppermute | solution.py:345
  40.8 5.3 %collective-permute-start.21 = (f32[88,128]{1,0:T(8,128)S(1)}, f32[88,128]{1,0:T(8,128)S(1)}, u32[]{:S(2)}, u32[]{:S(2)}) collective-permute-start(f32[88,128]{1,0:T(8,128)S(1)} %get-tuple-element.109), channel_id=1, source_target_pairs={{0,3},{1,2},{2,1},{3,0},{4,7},{5,6},{6,5},{7,4},{8,11},{9,10},{10,... | collective-permute-start | bytes 135176 | tf_op jit(solution)/shard_map/ppermute | solution.py:345
  42.2 5.2 %collective-permute-start.22 = (f32[5,2,8,128]{3,2,1,0:T(8,128)S(1)}, f32[5,2,8,128]{3,2,1,0:T(8,128)S(1)}, u32[]{:S(2)}, u32[]{:S(2)}) collective-permute-start(f32[5,2,8,128]{3,2,1,0:T(8,128)S(1)} %get-tuple-element.112), channel_id=1, source_target_pairs={{0,4},{4,0},{8,12},{12,8},{16,20},{20,16},{24,28},{28,24},{1,5},{5... | collective-permute-start | bytes 122888 | tf_op jit(solution)/shard_map/ppermute | solution.py:345
  42.6 4.8 %collective-permute-start.23 = (f32[5,2,8,128]{3,2,1,0:T(8,128)S(1)}, f32[5,2,8,128]{3,2,1,0:T(8,128)S(1)}, u32[]{:S(2)}, u32[]{:S(2)}) collective-permute-start(f32[5,2,8,128]{3,2,1,0:T(8,128)S(1)} %get-tuple-element.113), channel_id=1, source_target_pairs={{0,28},{4,8},{8,4},{12,16},{16,12},{20,24},{24,20},{28,0},{1,29},{... | collective-permute-start | bytes 122888 | tf_op jit(solution)/shard_map/ppermute | solution.py:345
  45.5 1.2 %collective-permute-start.20 = (f32[24,128]{1,0:T(8,128)S(1)}, f32[24,128]{1,0:T(8,128)S(1)}, u32[]{:S(2)}, u32[]{:S(2)}) collective-permute-start(f32[24,128]{1,0:T(8,128)S(1)} %get-tuple-element.108), channel_id=1, source_target_pairs={{0,1},{1,0},{2,3},{3,2},{4,5},{5,4},{6,7},{7,6},{8,9},{9,8},{10,11... | collective-permute-start | bytes 36872 | tf_op jit(solution)/shard_map/ppermute | solution.py:345

commit v14 on v12

--- a/solution.py
+++ b/solution.py
@@ -10,7 +10,7 @@
 AXES = ("gx", "gy", "wa")
 FIELDS, NX, NY, NZ = 5, 8, 16, 128
 ROWS = NX * NY
-FAR_ROWS = 88
+FAR_ROWS = 160
 OUTER_ROWS = (0, 1, NY - 2, NY - 1)
 SPAN_METRICS = ((4, NY - 1), (6, NY - 2), (6, NY - 1), (5, 0), (7, 0), (7, 1))
 F32 = jnp.float32
@@ -345,10 +345,10 @@
     def swap(v, axis, odd):
         return lax.ppermute(v, axis, pairs(lax.axis_size(axis), odd))
     two_hops = swap(x1, "gx", 1)
+    far = swap(far, "wa", 1)
     one_hop = swap(x0, "gx", 0)
-    far = swap(far, "wa", 1)
     y = swap(y0, "gy", 0), swap(y1, "gy", 1)
-    zz, one_hop = lax.optimization_barrier((zz, one_hop))
+    zz, two_hops = lax.optimization_barrier((zz, two_hops))
     x = one_hop, two_hops
     z = swap(zz, "wa", 0), far
     return (*x, *y, *z)

time: 71.3 us -> 75.4 us (1.058)
  starting transfers between devices: 36.3 us -> 39.8 us
    ppermute x24, starting transfers between devices: 36.3 us -> 39.8 us  [swap(): return lax.ppermute(v, axis, pairs(lax.axis_size(axis), odd))]
  transfers between devices with their start and end apart: 24 -> 24, of which waited for: 6 -> 5; matrix products, arithmetic and copies ran while one was open for 0% -> 0% of each run, Pallas kernels for 6% -> 5%
where the time goes in v14:
time: 75.4 us; the launch traced here: 75.2 us
  starting transfers between devices  39.8 us (53%)
  blocking collectives  22.8 us (30%)
  Pallas kernels  8.21 us (11%)
  waiting for transfers between devices  3.62 us (5%)
  between operations  0.8 us (1%)
    ppermute x24, starting transfers between devices, swap(): return lax.ppermute(v, axis, pairs(lax.axis_size(axis), odd))  39.8 us
    all_to_all x1, blocking collectives, local(): got = lax.all_to_all(slots.reshape(256, 1, 48), AXES, 0, 0).reshape(256, 48)  22.8 us
    pallas_call x12, Pallas kernels, run(): pl.pallas_call(body, out_shape=[jax.ShapeDtypeStruct(s, d) for s, d in ou...  8.21 us
    ppermute x24, waiting for transfers between devices, swap(): return lax.ppermute(v, axis, pairs(lax.axis_size(axis), odd))  3.62 us
  transfers between devices with their start and end apart: 24, of which 5 were waited for; matrix products, arithmetic and copies ran while one was open for 0% of the time, Pallas kernels for 5%

profile of v14, /device:TPU:1, one launch (start us, length us, event | category | flops | bytes accessed | tf_op | source)
XLA Modules:
  0.0 75.2 jit_solution(13912675563976246979)
XLA Ops:
  0.6 0.0 copy-start
  0.6 0.0 copy-start.2
  0.7 1.6 %shard_map.95 = (f32[5,2,16,128]{3,2,1,0:T(8,128)S(1)}, f32[5,2,16,128]{3,2,1,0:T(8,128)S(1)}, f32[5,2,8,128]{3,2,1,0:T(8,128)S(1)}, f32[5,2,8,128]{3,2,1,0:T(8,...) custom-call(f32[5,128,128]{2,1,0:T(8,128)} %bitcast.33, ...), custom_call_target="tpu_custom_call" | custom-call | flops 1000000 | bytes 1000000 | tf_op jit(solution)/shard_map/pallas_call | solution.py:323
  2.3 4.6 %collective-permute-start.1 = (f32[5,2,16,128]{3,2,1,0:T(8,128)S(1)}, f32[5,2,16,128]{3,2,1,0:T(8,128)S(1)}, u32[]{:S(2)}, u32[]{:S(2)}) collective-permute-start(f32[5,2,16,128]{3,2,1,0:T(8,128)S(1)} %get-tuple-element.65), channel_id=1, source_target_pairs={{0,224},{32,64},{64,32},{96,128},{128,96},{160,192},{192,160},{224... | collective-permute-start | bytes 245768 | tf_op jit(solution)/shard_map/ppermute | solution.py:346
  6.9 0.0 collective-permute-start
  6.9 3.3 %collective-permute-start.3 = (f32[160,128]{1,0:T(8,128)S(1)}, f32[160,128]{1,0:T(8,128)S(1)}, u32[]{:S(2)}, u32[]{:S(2)}) collective-permute-start(f32[160,128]{1,0:T(8,128)S(1)} %get-tuple-element.68), channel_id=1, source_target_pairs={{0,3},{1,2},{2,1},{3,0},{4,7},{5,6},{6,5},{7,4},{8,11},{9,10},{10,... | collective-permute-start | bytes 245768 | tf_op jit(solution)/shard_map/ppermute | solution.py:346
  10.2 1.6 %collective-permute-start.4 = (f32[5,2,8,128]{3,2,1,0:T(8,128)S(1)}, f32[5,2,8,128]{3,2,1,0:T(8,128)S(1)}, u32[]{:S(2)}, u32[]{:S(2)}) collective-permute-start(f32[5,2,8,128]{3,2,1,0:T(8,128)S(1)} %get-tuple-element.71), channel_id=1, source_target_pairs={{0,4},{4,0},{8,12},{12,8},{16,20},{20,16},{24,28},{28,24},{1,5},{5... | collective-permute-start | bytes 122888 | tf_op jit(solution)/shard_map/ppermute | solution.py:346
  11.8 4.7 %collective-permute-start.5 = (f32[5,2,8,128]{3,2,1,0:T(8,128)S(1)}, f32[5,2,8,128]{3,2,1,0:T(8,128)S(1)}, u32[]{:S(2)}, u32[]{:S(2)}) collective-permute-start(f32[5,2,8,128]{3,2,1,0:T(8,128)S(1)} %get-tuple-element.72), channel_id=1, source_target_pairs={{0,28},{4,8},{8,4},{12,16},{16,12},{20,24},{24,20},{28,0},{1,29},{... | collective-permute-start | bytes 122888 | tf_op jit(solution)/shard_map/ppermute | solution.py:346
  16.5 0.0 collective-permute-done.1.x1
  16.5 0.1 collective-permute-start.2
  16.6 0.3 shard_map.97
  16.9 0.0 collective-permute-done.x0
  16.9 0.0 collective-permute-done.3.z1
  16.9 0.7 collective-permute-done.2.z0
  17.6 0.8 %shard_map.96 = (f32[5,128,128]{2,1,0:T(8,128)S(1)}, f32[20,8,128]{2,1,0:T(8,128)S(1)}) custom-call(f32[5,128,128]{2,1,0:T(8,128)S(1)} %get-tuple-element.61.psi_ref, f32[12,128,128]{2,1,0:T(8,128)S(1)} %get-tuple-element.62.metric_ref, f32[128,128]{1,0:T(8,128)S(1)} %bitcast.23, f32[5,128,128]{2,1,0:T(8,128)S(1)} %bitcast.18, ...), custom_call_target="tpu_custom_call" | custom-call | flops 1000000 | bytes 1000000 | tf_op jit(solution)/shard_map/pallas_call | solution.py:323
  18.4 0.0 collective-permute-done.4.y_even
  18.4 0.1 collective-permute-done.5.y_odd
  18.6 0.3 shard_map.98
  18.9 1.3 %collective-permute-start.7 = (f32[5,2,16,128]{3,2,1,0:T(8,128)S(1)}, f32[5,2,16,128]{3,2,1,0:T(8,128)S(1)}, u32[]{:S(2)}, u32[]{:S(2)}) collective-permute-start(f32[5,2,16,128]{3,2,1,0:T(8,128)S(1)} %get-tuple-element.79), channel_id=1, source_target_pairs={{0,224},{32,64},{64,32},{96,128},{128,96},{160,192},{192,160},{224... | collective-permute-start | bytes 245768 | tf_op jit(solution)/shard_map/ppermute | solution.py:346
  20.2 0.6 collective-permute-start.6
  20.7 1.7 %collective-permute-start.9 = (f32[160,128]{1,0:T(8,128)S(1)}, f32[160,128]{1,0:T(8,128)S(1)}, u32[]{:S(2)}, u32[]{:S(2)}) collective-permute-start(f32[160,128]{1,0:T(8,128)S(1)} %get-tuple-element.82), channel_id=1, source_target_pairs={{0,3},{1,2},{2,1},{3,0},{4,7},{5,6},{6,5},{7,4},{8,11},{9,10},{10,... | collective-permute-start | bytes 245768 | tf_op jit(solution)/shard_map/ppermute | solution.py:346
  22.4 0.0 collective-permute-start.10
  22.4 3.9 %collective-permute-start.11 = (f32[5,2,8,128]{3,2,1,0:T(8,128)S(1)}, f32[5,2,8,128]{3,2,1,0:T(8,128)S(1)}, u32[]{:S(2)}, u32[]{:S(2)}) collective-permute-start(f32[5,2,8,128]{3,2,1,0:T(8,128)S(1)} %get-tuple-element.91), channel_id=1, source_target_pairs={{0,28},{4,8},{8,4},{12,16},{16,12},{20,24},{24,20},{28,0},{1,29},{... | collective-permute-start | bytes 122888 | tf_op jit(solution)/shard_map/ppermute | solution.py:346
  26.3 0.0 collective-permute-done.7.x1
  26.3 0.6 collective-permute-start.8
  26.9 0.0 copy-done.5
  26.9 0.6 shard_map.100
  27.5 0.0 collective-permute-done.6.x0
  27.5 0.6 collective-permute-done.9.z1
  28.1 0.0 collective-permute-done.8.z0
  28.1 0.8 %shard_map.99 = (f32[5,128,128]{2,1,0:T(8,128)S(1)}, f32[20,8,128]{2,1,0:T(8,128)S(1)}) custom-call(f32[5,128,128]{2,1,0:T(8,128)S(1)} %get-tuple-element.76.psi_ref, f32[12,128,128]{2,1,0:T(8,128)S(1)} %get-tuple-element.62.metric_ref, f32[128,128]{1,0:T(8,128)S(1)} %bitcast.24, f32[5,128,128]{2,1,0:T(8,128)S(1)} %bitcast.19, ...), custom_call_target="tpu_custom_call" | custom-call | flops 1000000 | bytes 1000000 | tf_op jit(solution)/shard_map/pallas_call | solution.py:323
  28.9 0.0 collective-permute-done.10.y_even
  29.0 0.0 collective-permute-done.11.y_odd
  29.0 0.3 shard_map.101
  29.3 1.0 %collective-permute-start.13 = (f32[5,2,16,128]{3,2,1,0:T(8,128)S(1)}, f32[5,2,16,128]{3,2,1,0:T(8,128)S(1)}, u32[]{:S(2)}, u32[]{:S(2)}) collective-permute-start(f32[5,2,16,128]{3,2,1,0:T(8,128)S(1)} %get-tuple-element.95), channel_id=1, source_target_pairs={{0,224},{32,64},{64,32},{96,128},{128,96},{160,192},{192,160},{224... | collective-permute-start | bytes 245768 | tf_op jit(solution)/shard_map/ppermute | solution.py:346
  30.3 1.3 %collective-permute-start.12 = (f32[5,2,16,128]{3,2,1,0:T(8,128)S(1)}, f32[5,2,16,128]{3,2,1,0:T(8,128)S(1)}, u32[]{:S(2)}, u32[]{:S(2)}) collective-permute-start(f32[5,2,16,128]{3,2,1,0:T(8,128)S(1)} %get-tuple-element.93), channel_id=1, source_target_pairs={{0,32},{32,0},{64,96},{96,64},{128,160},{160,128},{192,224},{224,1... | collective-permute-start | bytes 245768 | tf_op jit(solution)/shard_map/ppermute | solution.py:346
  31.5 2.2 %collective-permute-start.15 = (f32[160,128]{1,0:T(8,128)S(1)}, f32[160,128]{1,0:T(8,128)S(1)}, u32[]{:S(2)}, u32[]{:S(2)}) collective-permute-start(f32[160,128]{1,0:T(8,128)S(1)} %get-tuple-element.98), channel_id=1, source_target_pairs={{0,3},{1,2},{2,1},{3,0},{4,7},{5,6},{6,5},{7,4},{8,11},{9,10},{10,... | collective-permute-start | bytes 245768 | tf_op jit(solution)/shard_map/ppermute | solution.py:346
  33.7 0.1 collective-permute-start.16
  33.8 4.7 %collective-permute-start.17 = (f32[5,2,8,128]{3,2,1,0:T(8,128)S(1)}, f32[5,2,8,128]{3,2,1,0:T(8,128)S(1)}, u32[]{:S(2)}, u32[]{:S(2)}) collective-permute-start(f32[5,2,8,128]{3,2,1,0:T(8,128)S(1)} %get-tuple-element.102), channel_id=1, source_target_pairs={{0,28},{4,8},{8,4},{12,16},{16,12},{20,24},{24,20},{28,0},{1,29},{... | collective-permute-start | bytes 122888 | tf_op jit(solution)/shard_map/ppermute | solution.py:346
  38.5 0.0 collective-permute-done.13.x1
  38.5 0.4 collective-permute-start.14
  38.9 0.0 collective-permute-done.12.x0
  38.9 0.8 %collective-permute-done.15.z1 = f32[160,128]{1,0:T(8,128)S(1)} collective-permute-done((f32[160,128]{1,0:T(8,128)S(1)}, f32[160,128]{1,0:T(8,128)S(1)}, u32[]{:S(2)}, u32[]{:S(2)}) %collective-permute-start.15) | collective-permute-done | bytes 81952 | tf_op jit(solution)/shard_map/ppermute | solution.py:346
  39.7 0.0 collective-permute-done.14.z0
  39.7 0.8 %shard_map.102 = (f32[5,128,128]{2,1,0:T(8,128)S(1)}, f32[20,8,128]{2,1,0:T(8,128)S(1)}) custom-call(f32[5,128,128]{2,1,0:T(8,128)S(1)} %get-tuple-element.92.psi_ref, f32[12,128,128]{2,1,0:T(8,128)S(1)} %get-tuple-element.62.metric_ref, f32[128,128]{1,0:T(8,128)S(1)} %bitcast.25, f32[5,128,128]{2,1,0:T(8,128)S(1)} %bitcast.20, ...), custom_call_target="tpu_custom_call" | custom-call | flops 1000000 | bytes 1000000 | tf_op jit(solution)/shard_map/pallas_call | solution.py:323
  40.5 0.0 collective-permute-done.16.y_even
  40.5 0.0 collective-permute-done.17.y_odd
  40.5 0.4 shard_map.103
  40.9 0.4 collective-permute-start.19
  41.2 1.0 %collective-permute-start.18 = (f32[5,2,16,128]{3,2,1,0:T(8,128)S(1)}, f32[5,2,16,128]{3,2,1,0:T(8,128)S(1)}, u32[]{:S(2)}, u32[]{:S(2)}) collective-permute-start(f32[5,2,16,128]{3,2,1,0:T(8,128)S(1)} %get-tuple-element.104), channel_id=1, source_target_pairs={{0,32},{32,0},{64,96},{96,64},{128,160},{160,128},{192,224},{224,1... | collective-permute-start | bytes 245768 | tf_op jit(solution)/shard_map/ppermute | solution.py:346
  42.2 2.2 %collective-permute-start.21 = (f32[160,128]{1,0:T(8,128)S(1)}, f32[160,128]{1,0:T(8,128)S(1)}, u32[]{:S(2)}, u32[]{:S(2)}) collective-permute-start(f32[160,128]{1,0:T(8,128)S(1)} %get-tuple-element.109), channel_id=1, source_target_pairs={{0,3},{1,2},{2,1},{3,0},{4,7},{5,6},{6,5},{7,4},{8,11},{9,10},{10,... | collective-permute-start | bytes 245768 | tf_op jit(solution)/shard_map/ppermute | solution.py:346
  44.4 0.0 collective-permute-start.22
  44.4 3.9 %collective-permute-start.23 = (f32[5,2,8,128]{3,2,1,0:T(8,128)S(1)}, f32[5,2,8,128]{3,2,1,0:T(8,128)S(1)}, u32[]{:S(2)}, u32[]{:S(2)}) collective-permute-start(f32[5,2,8,128]{3,2,1,0:T(8,128)S(1)} %get-tuple-element.113), channel_id=1, source_target_pairs={{0,28},{4,8},{8,4},{12,16},{16,12},{20,24},{24,20},{28,0},{1,29},{... | collective-permute-start | bytes 122888 | tf_op jit(solution)/shard_map/ppermute | solution.py:346
  48.3 0.0 collective-permute-done.19.x1
  48.3 0.6 collective-permute-start.20
  48.9 0.0 collective-permute-done.18.x0
  48.9 1.2 %collective-permute-done.21.z1 = f32[160,128]{1,0:T(8,128)S(1)} collective-permute-done((f32[160,128]{1,0:T(8,128)S(1)}, f32[160,128]{1,0:T(8,128)S(1)}, u32[]{:S(2)}, u32[]{:S(2)}) %collective-permute-start.21) | collective-permute-done | bytes 81952 | tf_op jit(solution)/shard_map/ppermute | solution.py:346
  50.1 0.0 collective-permute-done.20.z0
  50.1 0.8 %shard_map.104 = (f32[5,128,128]{2,1,0:T(8,128)S(1)}, f32[20,8,128]{2,1,0:T(8,128)S(1)}) custom-call(f32[5,128,128]{2,1,0:T(8,128)S(1)} %get-tuple-element.103.psi_ref, f32[12,128,128]{2,1,0:T(8,128)S(1)} %get-tuple-element.62.metric_ref, f32[128,128]{1,0:T(8,128)S(1)} %bitcast.26, f32[5,128,128]{2,1,0:T(8,128)S(1)} %bitcast.21, ...), custom_call_target="tpu_custom_call" | custom-call | flops 1000000 | bytes 1000000 | tf_op jit(solution)/shard_map/pallas_call | solution.py:323
  50.9 0.0 collective-permute-done.22.y_even
  50.9 0.0 collective-permute-done.23.y_odd
  50.9 0.9 %shard_map.105 = (f32[5,128,128]{2,1,0:T(8,128)}, f32[256,48]{1,0:T(8,128)S(1)}) custom-call(f32[5,128,128]{2,1,0:T(8,128)S(1)} %get-tuple-element.110.base_ref, f32[20,8,128]{2,1,0:T(8,128)S(1)} %get-tuple-element.111.base_rows, f32[5,2,8,128]{3,2,1,0:T(8,128)S(1)} %collective-permute-done.22.y_even, f32[5,2,8,128]{3,2,1,0:T(8,128)S(1)} %collective-permute-done.23.y_odd, ...), custom_call_target="tpu_custom_call" | custom-call | flops 1000000 | bytes 1000000 | tf_op jit(solution)/shard_map/pallas_call | solution.py:323
  51.8 22.8 %all_to_all.5 = f32[256,1,48]{2,1,0:T(1,128)S(1)} all-to-all(f32[256,1,48]{2,1,0:T(1,128)S(1)} %bitcast.28), channel_id=1, replica_groups=mesh['gx'=8,'gy'=8,'wa'=4] {'gx','gy','wa'}, dimensions={0} | all-to-all | bytes 98304 | tf_op jit(solution)/shard_map/all_to_all | solution.py:391
  74.5 0.7 shard_map.106
  (9 shorter events, 0.0 us)
Async XLA Ops:
  0.6 15.9 %copy-start = (bf16[5,5,8,16,128]{4,3,2,1,0:T(8,128)(2,1)S(1)}, bf16[5,5,8,16,128]{4,3,2,1,0:T(8,128)(2,1)}, u32[]{:S(2)}) copy-start(bf16[5,5,8,16,128]{4,3,2,1,0:T(8,128)(2,1)} %param.12) | copy-start | bytes 2457604
  0.6 15.9 %copy-start.2 = (f32[8,16,128]{2,1,0:T(8,128)S(1)}, f32[8,16,128]{2,1,0:T(8,128)}, u32[]{:S(2)}) copy-start(f32[8,16,128]{2,1,0:T(8,128)} %param.10) | copy-start | bytes 196612
  2.3 14.2 %collective-permute-start.1 = (f32[5,2,16,128]{3,2,1,0:T(8,128)S(1)}, f32[5,2,16,128]{3,2,1,0:T(8,128)S(1)}, u32[]{:S(2)}, u32[]{:S(2)}) collective-permute-start(f32[5,2,16,128]{3,2,1,0:T(8,128)S(1)} %get-tuple-element.65), channel_id=1, source_target_pairs={{0,224},{32,64},{64,32},{96,128},{128,96},{160,192},{192,160},{224... | collective-permute-start | bytes 245768 | tf_op jit(solution)/shard_map/ppermute | solution.py:346
  6.9 10.0 %collective-permute-start = (f32[5,2,16,128]{3,2,1,0:T(8,128)S(1)}, f32[5,2,16,128]{3,2,1,0:T(8,128)S(1)}, u32[]{:S(2)}, u32[]{:S(2)}) collective-permute-start(f32[5,2,16,128]{3,2,1,0:T(8,128)S(1)} %get-tuple-element.63), channel_id=1, source_target_pairs={{0,32},{32,0},{64,96},{96,64},{128,160},{160,128},{192,224},{224,1... | collective-permute-start | bytes 245768 | tf_op jit(solution)/shard_map/ppermute | solution.py:346
  6.9 10.0 %collective-permute-start.3 = (f32[160,128]{1,0:T(8,128)S(1)}, f32[160,128]{1,0:T(8,128)S(1)}, u32[]{:S(2)}, u32[]{:S(2)}) collective-permute-start(f32[160,128]{1,0:T(8,128)S(1)} %get-tuple-element.68), channel_id=1, source_target_pairs={{0,3},{1,2},{2,1},{3,0},{4,7},{5,6},{6,5},{7,4},{8,11},{9,10},{10,... | collective-permute-start | bytes 245768 | tf_op jit(solution)/shard_map/ppermute | solution.py:346
  10.2 8.3 %collective-permute-start.4 = (f32[5,2,8,128]{3,2,1,0:T(8,128)S(1)}, f32[5,2,8,128]{3,2,1,0:T(8,128)S(1)}, u32[]{:S(2)}, u32[]{:S(2)}) collective-permute-start(f32[5,2,8,128]{3,2,1,0:T(8,128)S(1)} %get-tuple-element.71), channel_id=1, source_target_pairs={{0,4},{4,0},{8,12},{12,8},{16,20},{20,16},{24,28},{28,24},{1,5},{5... | collective-permute-start | bytes 122888 | tf_op jit(solution)/shard_map/ppermute | solution.py:346
  11.8 6.8 %collective-permute-start.5 = (f32[5,2,8,128]{3,2,1,0:T(8,128)S(1)}, f32[5,2,8,128]{3,2,1,0:T(8,128)S(1)}, u32[]{:S(2)}, u32[]{:S(2)}) collective-permute-start(f32[5,2,8,128]{3,2,1,0:T(8,128)S(1)} %get-tuple-element.72), channel_id=1, source_target_pairs={{0,28},{4,8},{8,4},{12,16},{16,12},{20,24},{24,20},{28,0},{1,29},{... | collective-permute-start | bytes 122888 | tf_op jit(solution)/shard_map/ppermute | solution.py:346
  16.5 1.2 %collective-permute-start.2 = (f32[24,128]{1,0:T(8,128)S(1)}, f32[24,128]{1,0:T(8,128)S(1)}, u32[]{:S(2)}, u32[]{:S(2)}) collective-permute-start(f32[24,128]{1,0:T(8,128)S(1)} %get-tuple-element.67), channel_id=1, source_target_pairs={{0,1},{1,0},{2,3},{3,2},{4,5},{5,4},{6,7},{7,6},{8,9},{9,8},{10,11... | collective-permute-start | bytes 36872 | tf_op jit(solution)/shard_map/ppermute | solution.py:346
  16.6 1.1 %copy-start.1 = (f32[5,8,16,128]{3,2,1,0:T(8,128)S(1)}, f32[5,8,16,128]{3,2,1,0:T(8,128)}, u32[]{:S(2)}) copy-start(f32[5,8,16,128]{3,2,1,0:T(8,128)} %param.9) | copy-start | bytes 983044
  18.6 8.3 %copy-start.3 = (f32[3,10,8,16]{3,2,1,0:T(8,128)S(1)}, f32[3,10,8,16]{3,2,1,0:T(8,128)}, u32[]{:S(2)}) copy-start(f32[3,10,8,16]{3,2,1,0:T(8,128)} %param.13) | copy-start | bytes 46084
  18.6 8.3 %copy-start.5 = (f32[4,8,16]{2,1,0:T(8,128)S(1)}, f32[4,8,16]{2,1,0:T(8,128)}, u32[]{:S(2)}) copy-start(f32[4,8,16]{2,1,0:T(8,128)} %param.15) | copy-start | bytes 6148
  18.9 8.0 %copy-start.4 = (s32[4,8,16]{2,1,0:T(8,128)S(1)}, s32[4,8,16]{2,1,0:T(8,128)}, u32[]{:S(2)}) copy-start(s32[4,8,16]{2,1,0:T(8,128)} %param.14) | copy-start | bytes 6148
  18.9 7.4 %collective-permute-start.7 = (f32[5,2,16,128]{3,2,1,0:T(8,128)S(1)}, f32[5,2,16,128]{3,2,1,0:T(8,128)S(1)}, u32[]{:S(2)}, u32[]{:S(2)}) collective-permute-start(f32[5,2,16,128]{3,2,1,0:T(8,128)S(1)} %get-tuple-element.79), channel_id=1, source_target_pairs={{0,224},{32,64},{64,32},{96,128},{128,96},{160,192},{192,160},{224... | collective-permute-start | bytes 245768 | tf_op jit(solution)/shard_map/ppermute | solution.py:346
  20.2 7.3 %collective-permute-start.6 = (f32[5,2,16,128]{3,2,1,0:T(8,128)S(1)}, f32[5,2,16,128]{3,2,1,0:T(8,128)S(1)}, u32[]{:S(2)}, u32[]{:S(2)}) collective-permute-start(f32[5,2,16,128]{3,2,1,0:T(8,128)S(1)} %get-tuple-element.77), channel_id=1, source_target_pairs={{0,32},{32,0},{64,96},{96,64},{128,160},{160,128},{192,224},{224,1... | collective-permute-start | bytes 245768 | tf_op jit(solution)/shard_map/ppermute | solution.py:346
  20.7 7.4 %collective-permute-start.9 = (f32[160,128]{1,0:T(8,128)S(1)}, f32[160,128]{1,0:T(8,128)S(1)}, u32[]{:S(2)}, u32[]{:S(2)}) collective-permute-start(f32[160,128]{1,0:T(8,128)S(1)} %get-tuple-element.82), channel_id=1, source_target_pairs={{0,3},{1,2},{2,1},{3,0},{4,7},{5,6},{6,5},{7,4},{8,11},{9,10},{10,... | collective-permute-start | bytes 245768 | tf_op jit(solution)/shard_map/ppermute | solution.py:346
  22.4 6.5 %collective-permute-start.10 = (f32[5,2,8,128]{3,2,1,0:T(8,128)S(1)}, f32[5,2,8,128]{3,2,1,0:T(8,128)S(1)}, u32[]{:S(2)}, u32[]{:S(2)}) collective-permute-start(f32[5,2,8,128]{3,2,1,0:T(8,128)S(1)} %get-tuple-element.90), channel_id=1, source_target_pairs={{0,4},{4,0},{8,12},{12,8},{16,20},{20,16},{24,28},{28,24},{1,5},{5... | collective-permute-start | bytes 122888 | tf_op jit(solution)/shard_map/ppermute | solution.py:346
  22.4 6.5 %collective-permute-start.11 = (f32[5,2,8,128]{3,2,1,0:T(8,128)S(1)}, f32[5,2,8,128]{3,2,1,0:T(8,128)S(1)}, u32[]{:S(2)}, u32[]{:S(2)}) collective-permute-start(f32[5,2,8,128]{3,2,1,0:T(8,128)S(1)} %get-tuple-element.91), channel_id=1, source_target_pairs={{0,28},{4,8},{8,4},{12,16},{16,12},{20,24},{24,20},{28,0},{1,29},{... | collective-permute-start | bytes 122888 | tf_op jit(solution)/shard_map/ppermute | solution.py:346
  26.3 1.8 %collective-permute-start.8 = (f32[24,128]{1,0:T(8,128)S(1)}, f32[24,128]{1,0:T(8,128)S(1)}, u32[]{:S(2)}, u32[]{:S(2)}) collective-permute-start(f32[24,128]{1,0:T(8,128)S(1)} %get-tuple-element.81), channel_id=1, source_target_pairs={{0,1},{1,0},{2,3},{3,2},{4,5},{5,4},{6,7},{7,6},{8,9},{9,8},{10,11... | collective-permute-start | bytes 36872 | tf_op jit(solution)/shard_map/ppermute | solution.py:346
  29.3 9.2 %collective-permute-start.13 = (f32[5,2,16,128]{3,2,1,0:T(8,128)S(1)}, f32[5,2,16,128]{3,2,1,0:T(8,128)S(1)}, u32[]{:S(2)}, u32[]{:S(2)}) collective-permute-start(f32[5,2,16,128]{3,2,1,0:T(8,128)S(1)} %get-tuple-element.95), channel_id=1, source_target_pairs={{0,224},{32,64},{64,32},{96,128},{128,96},{160,192},{192,160},{224... | collective-permute-start | bytes 245768 | tf_op jit(solution)/shard_map/ppermute | solution.py:346
  30.3 8.6 %collective-permute-start.12 = (f32[5,2,16,128]{3,2,1,0:T(8,128)S(1)}, f32[5,2,16,128]{3,2,1,0:T(8,128)S(1)}, u32[]{:S(2)}, u32[]{:S(2)}) collective-permute-start(f32[5,2,16,128]{3,2,1,0:T(8,128)S(1)} %get-tuple-element.93), channel_id=1, source_target_pairs={{0,32},{32,0},{64,96},{96,64},{128,160},{160,128},{192,224},{224,1... | collective-permute-start | bytes 245768 | tf_op jit(solution)/shard_map/ppermute | solution.py:346
  31.5 8.2 %collective-permute-start.15 = (f32[160,128]{1,0:T(8,128)S(1)}, f32[160,128]{1,0:T(8,128)S(1)}, u32[]{:S(2)}, u32[]{:S(2)}) collective-permute-start(f32[160,128]{1,0:T(8,128)S(1)} %get-tuple-element.98), channel_id=1, source_target_pairs={{0,3},{1,2},{2,1},{3,0},{4,7},{5,6},{6,5},{7,4},{8,11},{9,10},{10,... | collective-permute-start | bytes 245768 | tf_op jit(solution)/shard_map/ppermute | solution.py:346
  33.7 6.8 %collective-permute-start.16 = (f32[5,2,8,128]{3,2,1,0:T(8,128)S(1)}, f32[5,2,8,128]{3,2,1,0:T(8,128)S(1)}, u32[]{:S(2)}, u32[]{:S(2)}) collective-permute-start(f32[5,2,8,128]{3,2,1,0:T(8,128)S(1)} %get-tuple-element.101), channel_id=1, source_target_pairs={{0,4},{4,0},{8,12},{12,8},{16,20},{20,16},{24,28},{28,24},{1,5},{5... | collective-permute-start | bytes 122888 | tf_op jit(solution)/shard_map/ppermute | solution.py:346
  33.8 6.7 %collective-permute-start.17 = (f32[5,2,8,128]{3,2,1,0:T(8,128)S(1)}, f32[5,2,8,128]{3,2,1,0:T(8,128)S(1)}, u32[]{:S(2)}, u32[]{:S(2)}) collective-permute-start(f32[5,2,8,128]{3,2,1,0:T(8,128)S(1)} %get-tuple-element.102), channel_id=1, source_target_pairs={{0,28},{4,8},{8,4},{12,16},{16,12},{20,24},{24,20},{28,0},{1,29},{... | collective-permute-start | bytes 122888 | tf_op jit(solution)/shard_map/ppermute | solution.py:346
  38.5 1.2 %collective-permute-start.14 = (f32[24,128]{1,0:T(8,128)S(1)}, f32[24,128]{1,0:T(8,128)S(1)}, u32[]{:S(2)}, u32[]{:S(2)}) collective-permute-start(f32[24,128]{1,0:T(8,128)S(1)} %get-tuple-element.97), channel_id=1, source_target_pairs={{0,1},{1,0},{2,3},{3,2},{4,5},{5,4},{6,7},{7,6},{8,9},{9,8},{10,11... | collective-permute-start | bytes 36872 | tf_op jit(solution)/shard_map/ppermute | solution.py:346
  40.9 7.4 %collective-permute-start.19 = (f32[5,2,16,128]{3,2,1,0:T(8,128)S(1)}, f32[5,2,16,128]{3,2,1,0:T(8,128)S(1)}, u32[]{:S(2)}, u32[]{:S(2)}) collective-permute-start(f32[5,2,16,128]{3,2,1,0:T(8,128)S(1)} %get-tuple-element.106), channel_id=1, source_target_pairs={{0,224},{32,64},{64,32},{96,128},{128,96},{160,192},{192,160},{224... | collective-permute-start | bytes 245768 | tf_op jit(solution)/shard_map/ppermute | solution.py:346
  41.2 7.6 %collective-permute-start.18 = (f32[5,2,16,128]{3,2,1,0:T(8,128)S(1)}, f32[5,2,16,128]{3,2,1,0:T(8,128)S(1)}, u32[]{:S(2)}, u32[]{:S(2)}) collective-permute-start(f32[5,2,16,128]{3,2,1,0:T(8,128)S(1)} %get-tuple-element.104), channel_id=1, source_target_pairs={{0,32},{32,0},{64,96},{96,64},{128,160},{160,128},{192,224},{224,1... | collective-permute-start | bytes 245768 | tf_op jit(solution)/shard_map/ppermute | solution.py:346
  42.2 7.9 %collective-permute-start.21 = (f32[160,128]{1,0:T(8,128)S(1)}, f32[160,128]{1,0:T(8,128)S(1)}, u32[]{:S(2)}, u32[]{:S(2)}) collective-permute-start(f32[160,128]{1,0:T(8,128)S(1)} %get-tuple-element.109), channel_id=1, source_target_pairs={{0,3},{1,2},{2,1},{3,0},{4,7},{5,6},{6,5},{7,4},{8,11},{9,10},{10,... | collective-permute-start | bytes 245768 | tf_op jit(solution)/shard_map/ppermute | solution.py:346
  44.4 6.5 %collective-permute-start.22 = (f32[5,2,8,128]{3,2,1,0:T(8,128)S(1)}, f32[5,2,8,128]{3,2,1,0:T(8,128)S(1)}, u32[]{:S(2)}, u32[]{:S(2)}) collective-permute-start(f32[5,2,8,128]{3,2,1,0:T(8,128)S(1)} %get-tuple-element.112), channel_id=1, source_target_pairs={{0,4},{4,0},{8,12},{12,8},{16,20},{20,16},{24,28},{28,24},{1,5},{5... | collective-permute-start | bytes 122888 | tf_op jit(solution)/shard_map/ppermute | solution.py:346
  44.4 6.5 %collective-permute-start.23 = (f32[5,2,8,128]{3,2,1,0:T(8,128)S(1)}, f32[5,2,8,128]{3,2,1,0:T(8,128)S(1)}, u32[]{:S(2)}, u32[]{:S(2)}) collective-permute-start(f32[5,2,8,128]{3,2,1,0:T(8,128)S(1)} %get-tuple-element.113), channel_id=1, source_target_pairs={{0,28},{4,8},{8,4},{12,16},{16,12},{20,24},{24,20},{28,0},{1,29},{... | collective-permute-start | bytes 122888 | tf_op jit(solution)/shard_map/ppermute | solution.py:346
  48.3 1.8 %collective-permute-start.20 = (f32[24,128]{1,0:T(8,128)S(1)}, f32[24,128]{1,0:T(8,128)S(1)}, u32[]{:S(2)}, u32[]{:S(2)}) collective-permute-start(f32[24,128]{1,0:T(8,128)S(1)} %get-tuple-element.108), channel_id=1, source_target_pairs={{0,1},{1,0},{2,3},{3,2},{4,5},{5,4},{6,7},{7,6},{8,9},{9,8},{10,11... | collective-permute-start | bytes 36872 | tf_op jit(solution)/shard_map/ppermute | solution.py:346
